TPU v7x, 32 devices: a whole 2x2x4 slice. The times are simulated.
32 devices in a mesh: grp: 2 (over y), ctx: 4 (over x, core), head: 4 (over z).
Axes of the slice: x: 2, y: 2, z: 4, core: 2. Of those that a mesh axis runs over, the one named last changes fastest.
Arguments:
- query_codes: bfloat16 [8192, 2048], P(('grp', 'ctx', 'head')), parts along dimension 0, may hold values from -0.5 to 2.5
- key_codes: bfloat16 [8192, 2048], P(('grp', 'ctx', 'head')), parts along dimension 0, may hold values from -0.5 to 2.5
- value_codes: bfloat16 [8192, 4096], P(('grp', 'ctx', 'head')), parts along dimension 0, may hold values from -6 to 6
- block_scales: float32 [64, 3, 8], P(('grp', 'ctx', 'head')), parts along dimension 0, may hold values from 0.25 to 2
- fault_tensor: int32 [64, 8], P(('grp', 'ctx', 'head')), parts along dimension 0, may hold values from 0 to 2
- fault_offset: int32 [64, 8], P(('grp', 'ctx', 'head')), parts along dimension 0, may hold values from 0 to 65535
- fault_bit: int32 [64, 8], P(('grp', 'ctx', 'head')), parts along dimension 0, may hold values from 0 to 3
- input_gate: bfloat16 [8192, 8], P(('grp', 'ctx', 'head')), parts along dimension 0, may hold values from -10 to 104
- forget_gate: bfloat16 [8192, 8], P(('grp', 'ctx', 'head')), parts along dimension 0, may hold values from 0.5 to 15
Outputs:
- hidden_states: bfloat16 [8192, 4096], P(('grp', 'ctx', 'head')), parts along dimension 0
There are 2 independent parts, one for each index of `grp`. A program takes and returns all parts, laid end to end along the dimension named above; each array names one. Nothing has to cross between parts.
All inputs are finite; a program needn't handle non-finite values.
Results may differ from a plain program's by a relative error of at most 0.0057.
Values may be sent and summed in bfloat16 or wider, within the bound.
No kernel may reach another device: no remote copies, remote signals or barrier semaphores. Data moves between devices by JAX's collectives and lax.ppermute only.
A program may use at most 128 MiB of HBM per device.

v0:
```python
import math

import jax
import jax.numpy as jnp
from jax import lax
from jax.sharding import PartitionSpec as P

DK = 256
DV = 512
CH = 256
BLK = 128


NEG_FILL = -1e30


def entering(x, axis, combine, identity):
    peers, mine = (lax.axis_size(axis), lax.axis_index(axis))
    everything = jax.tree.map(lambda part: lax.all_gather(part, axis), x)
    start = jax.tree.map(
        lambda part, zero: jnp.broadcast_to(jnp.asarray(zero, part.dtype), part.shape), x, identity
    )

    def hop(k, before):
        reached = k < mine
        new = combine(before, jax.tree.map(lambda part: part[k], everything))
        return jax.tree.map(lambda a, b: jnp.where(reached, a, b), new, before)

    return lax.fori_loop(0, peers, hop, start)


def dequant(codes, scales, tensor_id, fault_tensor, fault_offset, fault_bit, width):
    rows = codes.shape[0]
    blocks = rows // BLK
    heads = scales.shape[2]
    shaped = codes.reshape(blocks, BLK, heads, width).astype(jnp.float32)
    block_factor = scales[:, tensor_id, :]
    struck = fault_tensor == tensor_id
    token_hit = fault_offset // DV
    column_hit = fault_offset % DV % width
    token_line = jnp.arange(BLK, dtype=jnp.int32)
    column_line = jnp.arange(width, dtype=jnp.int32)
    marked = (
        (token_line[None, :, None, None] == token_hit[:, None, :, None])
        & (column_line[None, None, None, :] == column_hit[:, None, :, None])
        & struck[:, None, :, None]
    )
    flipped = -jnp.exp2(fault_bit.astype(jnp.float32))
    factor = jnp.where(marked, flipped[:, None, :, None], jnp.ones_like(shaped))
    result = shaped * block_factor[:, None, :, None] * factor
    return result.reshape(rows, heads, width).astype(jnp.bfloat16)


def identity_state(groups):
    return (
        jnp.zeros((groups, DK, DV), jnp.float32),
        jnp.zeros((groups, DK), jnp.float32),
        jnp.full((groups,), NEG_FILL, jnp.float32),
        jnp.zeros((groups,), jnp.float32),
    )


def combine(earlier, following):
    peak = jnp.maximum(earlier[2] + following[3], following[2])
    first = jnp.exp(earlier[2] + following[3] - peak)
    second = jnp.exp(following[2] - peak)
    matrix = earlier[0] * first[..., None, None] + following[0] * second[..., None, None]
    normer = earlier[1] * first[..., None] + following[1] * second[..., None]
    return (matrix, normer, peak, earlier[3] + following[3])


def span_terms(lookup_vectors, values, gate_in, log_forget):
    running = jnp.cumsum(log_forget, axis=1)
    total = running[:, -1]
    exponent = total[:, None] - running + gate_in
    peak = jnp.max(exponent, axis=1)
    weights = jnp.exp(exponent - peak[:, None])
    weighted = (lookup_vectors.astype(jnp.float32) * weights[..., None]).astype(jnp.bfloat16)
    matrix = jnp.einsum("csgk,csgv->cgkv", weighted, values, preferred_element_type=jnp.float32)
    normer = jnp.sum(weighted.astype(jnp.float32), axis=1)
    return (matrix, normer, peak, total)


def prefix_states(states, start):

    def advance(carried, element):
        return (combine(carried, element), carried)

    return lax.scan(advance, start, states)


def span_outputs(queries, lookup_vectors, values, gate_in, log_forget, before):
    size = queries.shape[1]
    factor = 1.0 / math.sqrt(DK)
    running = jnp.cumsum(log_forget, axis=1).transpose(0, 2, 1)
    gate_rows = gate_in.transpose(0, 2, 1)
    exponent = running[..., :, None] - running[..., None, :] + gate_rows[..., None, :]
    line = jnp.arange(size, dtype=jnp.int32)
    causal = line[:, None] >= line[None, :]
    exponent = jnp.where(causal, exponent, NEG_FILL)
    inter = running + before[2][..., None]
    row_peak = jnp.maximum(jnp.max(exponent, axis=-1), inter)
    decay = jnp.exp(exponent - row_peak[..., None])
    scores = (
        jnp.einsum("ctgk,csgk->cgts", queries, lookup_vectors, preferred_element_type=jnp.float32)
        * factor
    )
    product = decay * scores
    product_weights = product.astype(jnp.bfloat16)
    numerator = jnp.einsum(
        "cgts,csgv->ctgv", product_weights, values, preferred_element_type=jnp.float32
    )
    lift = jnp.exp(inter - row_peak)
    lifted = (queries.astype(jnp.float32) * (factor * lift).transpose(0, 2, 1)[..., None]).astype(
        jnp.bfloat16
    )
    start_matrix = before[0].astype(jnp.bfloat16)
    numerator = numerator + jnp.einsum(
        "ctgk,cgkv->ctgv", lifted, start_matrix, preferred_element_type=jnp.float32
    )
    denominator = jnp.sum(product, axis=-1) + jnp.einsum(
        "ctgk,cgk->cgt", lifted.astype(jnp.float32), before[1], precision=lax.Precision.HIGHEST
    )
    floor_value = jnp.maximum(jnp.abs(denominator), 1.0)
    return (numerator / floor_value.transpose(0, 2, 1)[..., None]).astype(jnp.bfloat16)


def in_spans(array, width):
    spans = array.shape[0] // CH
    if width == 0:
        return array.reshape(spans, CH, array.shape[1])
    return array.reshape(spans, CH, array.shape[1], width)


def body(
    query_codes,
    key_codes,
    value_codes,
    block_scales,
    fault_tensor,
    fault_offset,
    fault_bit,
    input_gate,
    forget_gate,
):
    queries = dequant(query_codes, block_scales, 0, fault_tensor, fault_offset, fault_bit, DK)
    lookup_vectors = dequant(key_codes, block_scales, 1, fault_tensor, fault_offset, fault_bit, DK)
    values = dequant(value_codes, block_scales, 2, fault_tensor, fault_offset, fault_bit, DV)
    tok_rows = queries.shape[0]
    got_q, got_k, got_v, got_i, got_f = (
        lax.all_to_all(queries, "head", split_axis=1, concat_axis=0, tiled=True),
        lax.all_to_all(lookup_vectors, "head", split_axis=1, concat_axis=0, tiled=True),
        lax.all_to_all(values, "head", split_axis=1, concat_axis=0, tiled=True),
        lax.all_to_all(input_gate, "head", split_axis=1, concat_axis=0, tiled=True),
        lax.all_to_all(forget_gate, "head", split_axis=1, concat_axis=0, tiled=True),
    )
    length = got_q.shape[0]
    groups = got_q.shape[1]
    span_q = in_spans(got_q, DK)
    span_k = in_spans(got_k, DK)
    span_v = in_spans(got_v, DV)
    gate_in = in_spans(got_i.astype(jnp.float32), 0)
    log_forget = in_spans(jax.nn.log_sigmoid(got_f.astype(jnp.float32)), 0)
    terms = span_terms(span_k, span_v, gate_in, log_forget)
    total, before_local = prefix_states(terms, identity_state(groups))
    incoming = entering(total, "ctx", combine, identity_state(groups))
    before = combine(incoming, before_local)
    hidden = span_outputs(span_q, span_k, span_v, gate_in, log_forget, before).reshape(
        length, groups, DV
    )
    hidden_rows = lax.all_to_all(hidden, "head", split_axis=0, concat_axis=1, tiled=True)
    return hidden_rows.reshape(tok_rows, -1)


def solution(mesh):
    placed = (
        P(("grp", "ctx", "head"), None),
        P(("grp", "ctx", "head"), None),
        P(("grp", "ctx", "head"), None),
        P(("grp", "ctx", "head"), None, None),
        P(("grp", "ctx", "head"), None),
        P(("grp", "ctx", "head"), None),
        P(("grp", "ctx", "head"), None),
        P(("grp", "ctx", "head"), None),
        P(("grp", "ctx", "head"), None),
    )
    return jax.shard_map(
        body, mesh=mesh, in_specs=placed, out_specs=P(("grp", "ctx", "head"), None), check_vma=False
    )
```

profile of v0, /device:TPU:0, one launch (start us, length us, event | category | flops | bytes accessed | tf_op | source)
XLA Modules:
  0.0 248.8 jit_solution(14191822384164090131)
XLA Ops:
  6.5 1.4 all_to_all.67
  7.9 6.3 %all-to-all-start.1 = ((bf16[256,4,2]{0,2,1:T(2,128)(2,1)}), bf16[256,4,2]{0,2,1:T(2,128)(2,1)S(1)}, u32[]{:S(2)}, u32[]{:S(2)}) async-start(bf16[256,4,2]{0,2,1:T(2,128)(2,1)} %all_to_all.67), calls=%async_computation.1 | async-start | bytes 8192 | tf_op jit(solution)/shard_map/all_to_all | solution.py:155
  14.9 0.7 slice_bitcast_fusion.1
  16.3 0.7 and_select_fusion
  17.4 1.3 all_to_all.69
  18.7 1.1 all-to-all-done.1
  19.8 4.0 %all-to-all-start.2 = ((bf16[256,4,2]{0,2,1:T(2,128)(2,1)}), bf16[256,4,2]{0,2,1:T(2,128)(2,1)S(1)}, u32[]{:S(2)}, u32[]{:S(2)}) async-start(bf16[256,4,2]{0,2,1:T(2,128)(2,1)} %all_to_all.69), calls=%async_computation.2 | async-start | bytes 8192 | tf_op jit(solution)/shard_map/all_to_all | solution.py:154
  23.9 1.5 convert_element_type.105
  25.6 4.3 %fusion.23 = (bf16[256,8,256]{2,0,1:T(8,128)(2,1)}, bf16[256,8,256]{2,0,1:T(8,128)(2,1)}) fusion(f32[32,8,8,256]{3,2,1,0:T(8,128)S(1)} %bitcast.234, f32[256,8]{0,1:T(8,128)S(1)} %get-tuple-element.445, f32[256,8]{0,1:T(8,128)S(1)} %get-tuple-element.442, pred[256,8]{0,1:T(8,128)(4,1)S(1)} %get-tuple-element.444, ...), kind=kLoop, calls=%fused_computation.48 | loop fusion | flops 5767168 | bytes 6326272 | tf_op jit(solution)/shard_map/convert_element_type | solution.py:51
  29.9 5.1 %all-to-all-start.3 = ((bf16[256,8,256]{2,0,1:T(8,128)(2,1)}), bf16[256,8,256]{2,0,1:T(8,128)(2,1)S(1)}, u32[]{:S(2)}, u32[]{:S(2)}) async-start(bf16[256,8,256]{2,0,1:T(8,128)(2,1)} %get-tuple-element.430), calls=%async_computation.3 | async-start | bytes 2097152 | tf_op jit(solution)/shard_map/all_to_all | solution.py:152
  35.0 4.0 %convert_element_type.102 = f32[256,4096]{1,0:T(8,128)} convert(bf16[256,4096]{1,0:T(8,128)(2,1)} %param.15) | non-fusion elementwise | flops 1048576 | bytes 6291456 | tf_op jit(solution)/shard_map/convert_element_type | solution.py:36
  39.3 4.8 %fusion.17 = bf16[256,8,512]{2,0,1:T(8,128)(2,1)} fusion(f32[32,8,8,512]{3,2,1,0:T(8,128)} %bitcast.230, f32[256,8]{0,1:T(8,128)S(1)} %get-tuple-element.445, f32[256,8]{0,1:T(8,128)S(1)} %get-tuple-element.446, pred[256,8]{0,1:T(8,128)(4,1)S(1)} %broadcast_bitcast_fusion.6, pred[2,8,512]{2,0,1:T(4,128)(4,1)S(1)} %iota_compare_fusion.1, ...), kind=kLoop, calls=%fused_computation.37 | loop fusion | flops 6291456 | bytes 6320128 | tf_op jit(solution)/shard_map/convert_element_type | solution.py:51
  44.2 15.5 %all-to-all-done.3 = bf16[256,8,256]{2,0,1:T(8,128)(2,1)S(1)} async-done(((bf16[256,8,256]{2,0,1:T(8,128)(2,1)}), bf16[256,8,256]{2,0,1:T(8,128)(2,1)S(1)}, u32[]{:S(2)}, u32[]{:S(2)}) %all-to-all-start.3) | async-done | bytes 1048608 | tf_op jit(solution)/shard_map/all_to_all | solution.py:152
  59.6 1.0 copy-done.1
  60.6 3.6 %all-to-all-start = ((bf16[256,8,512]{2,0,1:T(8,128)(2,1)}), bf16[256,8,512]{2,0,1:T(8,128)(2,1)S(1)}, u32[]{:S(2)}, u32[]{:S(2)}) async-start(bf16[256,8,512]{2,0,1:T(8,128)(2,1)} %fusion.17), calls=%async_computation | async-start | bytes 4194304 | tf_op jit(solution)/shard_map/all_to_all | solution.py:153
  64.4 2.4 reduce-window.6
  67.8 1.6 convert_reduce_fusion
  69.4 42.5 %all-to-all-done = bf16[256,8,512]{2,0,1:T(8,128)(2,1)S(1)} async-done(((bf16[256,8,512]{2,0,1:T(8,128)(2,1)}), bf16[256,8,512]{2,0,1:T(8,128)(2,1)S(1)}, u32[]{:S(2)}, u32[]{:S(2)}) %all-to-all-start) | async-done | bytes 2097184 | tf_op jit(solution)/shard_map/all_to_all | solution.py:153
  111.9 4.3 %fusion.32 = f32[4,2,256,512]{3,2,1,0:T(8,128)} fusion(bf16[4,256,2,512]{3,1,2,0:T(8,128)(2,1)S(1)} %bitcast.228, bf16[4,256,2,256]{3,1,2,0:T(8,128)(2,1)} %bitcast.232, f32[4,256,2]{1,2,0:T(2,128)S(1)} %subtract_exponential_fusion.4), kind=kOutput, calls=%fused_computation.63 | convolution fusion | flops 538443776 | bytes 7348224 | tf_op jit(solution)/shard_map/csgk,csgv->cgkv/dot_general | solution.py:79
  116.2 11.4 %while.45 = (s32[]{:T(128)}, f32[2,256,512]{2,1,0:T(8,128)S(1)}, f32[2,256]{1,0:T(2,128)S(1)}, f32[2]{0:T(128)S(1)}, f32[2]{0:T(128)S(1)}, /*index=5*/f32[4,2,25...) while((s32[]{:T(128)}, f32[2,256,512]{2,1,0:T(8,128)S(1)}, ...), condition=%wide.region_6.7_spmd.clone.clone, body=%wide.region_5.6_spmd.clone.sunk.clone | while | flops 1313299 | bytes 5253468 | solution.py:89
  116.2 1.1 bitcast_dynamic-update-slice_fusion.6
  117.3 1.6 fusion.63
  119.1 1.1 bitcast_dynamic-update-slice_fusion.6
  120.2 1.6 fusion.63
  121.9 1.1 bitcast_dynamic-update-slice_fusion.6
  123.1 1.6 fusion.63
  124.8 1.1 bitcast_dynamic-update-slice_fusion.6
  125.9 1.6 fusion.63
  127.7 1.0 copy-done
  128.7 4.3 %all-to-all-start.4 = ((bf16[256,8,256]{2,0,1:T(8,128)(2,1)}), bf16[256,8,256]{2,0,1:T(8,128)(2,1)}, u32[]{:S(2)}, u32[]{:S(2)}) async-start(bf16[256,8,256]{2,0,1:T(8,128)(2,1)} %get-tuple-element.431), calls=%async_computation.4 | async-start | bytes 2097152 | tf_op jit(solution)/shard_map/all_to_all | solution.py:151
  134.8 0.7 fusion.27
  135.5 6.7 %all-reduce.2 = (f32[8]{0:T(128)S(1)}, f32[8]{0:T(128)S(1)}) all-reduce(f32[8]{0:T(128)S(1)} %dynamic-update-slice, f32[8]{0:T(128)S(1)} %dynamic-update-slice.1), channel_id=2, replica_groups=mesh['grp'=2,'ctx'=4,'head'=4] {'ctx'}, use_global_device_ids=true, to_apply=%add | all-reduce | flops 16 | bytes 128
  142.3 5.5 %all-gather.4 = f32[4,2,256]{2,1,0:T(2,128)S(1)} all-gather(f32[1,2,256]{2,1,0:T(2,128)S(1)} %bitcast.241), channel_id=5, replica_groups=mesh['grp'=2,'ctx'=4,'head'=4] {'ctx'}, dimensions={0}, use_global_device_ids=true | all-gather | bytes 10240 | tf_op jit(solution)/shard_map/all_gather | solution.py:19
  147.9 14.7 %all-gather.7.cloned.1.call-done = f32[8,256,512]{2,1,0:T(8,128)} async-done(((f32[2,256,512]{2,1,0:T(8,128)}), f32[8,256,512]{2,1,0:T(8,128)}) %all-gather.7.cloned.1.call-update) | async-done | bytes 4194320 | tf_op jit(solution)/shard_map/all_gather | solution.py:19
  162.6 7.8 %while.46 = (s32[]{:T(128)}, f32[2,256,512]{2,1,0:T(8,128)S(1)}, f32[2,256]{1,0:T(2,128)S(1)}, f32[2]{0:T(128)S(1)}, s32[]{:T(128)}, /*index=5*/f32[4,2]{1,0:T(4...) while((s32[]{:T(128)}, f32[2,256,512]{2,1,0:T(8,128)S(1)}, ...), condition=%wide.region_8.9_spmd.clone.clone, body=%wide.region_7.8_spmd.clone.sunk.clone | while | flops 1313298 | bytes 3152117 | solution.py:29
  162.6 1.8 fusion.66
  164.5 1.8 fusion.66
  166.5 1.8 fusion.66
  168.4 1.8 fusion.66
  170.4 2.4 fusion.47
  172.9 0.8 fusion.30
  173.7 2.6 %fusion.33 = f32[4,2,1,256]{3,2,1,0:T(1,128)S(1)} fusion(bf16[4,256,2,256]{3,1,2,0:T(8,128)(2,1)} %bitcast.29, f32[4,256,2]{1,2,0:T(2,128)S(1)} %get-tuple-element.428, f32[4,2,256,1]{2,1,0,3:T(2,128)S(1)} %add_bitcast_fusion), kind=kOutput, calls=%fused_computation.64 | convolution fusion | flops 7864320 | bytes 1073152 | tf_op jit(solution)/shard_map/ctgk,cgk->cgt/dot_general | solution.py:121
  176.4 2.8 %fusion.18 = bf16[4,256,2,512]{3,1,2,0:T(8,128)(2,1)S(1)} fusion(f32[4,2,512,256]{2,3,1,0:T(8,128)S(1)} %fusion.30, f32[4,2,256,512]{3,2,1,0:T(8,128)S(1)} %copy-done.3, f32[4,256,2]{1,2,0:T(2,128)S(1)} %fusion.38, f32[4,2]{1,0:T(4,128)S(1)} %subtract_exponential_fusion.5, f32[4,2]{1,0:T(4,128)S(1)} %get-tuple-element.420, ...), kind=kOutput, calls=%fused_computation.39 | convolution fusion | flops 545783808 | bytes 12599360 | tf_op jit(solution)/shard_map/ctgk,cgkv->ctgv/dot_general | solution.py:118
  179.5 2.2 copy.75
  181.6 53.0 %all_to_all.86 = bf16[1024,2,512]{2,1,0:T(2,128)(2,1)S(1)} all-to-all(bf16[1024,2,512]{2,1,0:T(2,128)(2,1)S(1)} %copy.75), channel_id=1, replica_groups=mesh['grp'=2,'ctx'=4,'head'=4] {'head'}, dimensions={0} | all-to-all | bytes 4194304 | tf_op jit(solution)/shard_map/all_to_all | solution.py:171
  234.6 1.7 copy.76
  236.3 2.8 %copy.77 = bf16[256,4,2,512]{0,3,2,1:T(8,128)(2,1)S(1)} copy(bf16[256,4,2,512]{3,0,1,2:T(8,128)(2,1)} %bitcast.237) | data formatting | bytes 4194304 | tf_op jit(solution)/shard_map/all_to_all | solution.py:171
  239.1 2.9 %copy.78 = bf16[256,4096]{1,0:T(8,128)(2,1)} copy(bf16[256,4096]{0,1:T(8,128)(2,1)S(1)} %bitcast.238) | data formatting | bytes 4194304 | tf_op jit(solution)/shard_map/reshape | solution.py:172
  (106 shorter events, 6.4 us)
Async XLA Ops:
  6.5 18.8 %copy-start.2 = (bf16[256,2048]{1,0:T(8,128)(2,1)S(1)}, bf16[256,2048]{1,0:T(8,128)(2,1)}, u32[]{:S(2)}) copy-start(bf16[256,2048]{1,0:T(8,128)(2,1)} %param.13) | copy-start | bytes 3145732
  7.9 11.9 %all-to-all-start.1 = ((bf16[256,4,2]{0,2,1:T(2,128)(2,1)}), bf16[256,4,2]{0,2,1:T(2,128)(2,1)S(1)}, u32[]{:S(2)}, u32[]{:S(2)}) async-start(bf16[256,4,2]{0,2,1:T(2,128)(2,1)} %all_to_all.67), calls=%async_computation.1 | async-start | bytes 8192 | tf_op jit(solution)/shard_map/all_to_all | solution.py:155
  19.8 10.1 %all-to-all-start.2 = ((bf16[256,4,2]{0,2,1:T(2,128)(2,1)}), bf16[256,4,2]{0,2,1:T(2,128)(2,1)S(1)}, u32[]{:S(2)}, u32[]{:S(2)}) async-start(bf16[256,4,2]{0,2,1:T(2,128)(2,1)} %all_to_all.69), calls=%async_computation.2 | async-start | bytes 8192 | tf_op jit(solution)/shard_map/all_to_all | solution.py:154
  29.9 29.7 %all-to-all-start.3 = ((bf16[256,8,256]{2,0,1:T(8,128)(2,1)}), bf16[256,8,256]{2,0,1:T(8,128)(2,1)S(1)}, u32[]{:S(2)}, u32[]{:S(2)}) async-start(bf16[256,8,256]{2,0,1:T(8,128)(2,1)} %get-tuple-element.430), calls=%async_computation.3 | async-start | bytes 2097152 | tf_op jit(solution)/shard_map/all_to_all | solution.py:152
  59.6 1.0 copy-start.1
  60.6 51.3 %all-to-all-start = ((bf16[256,8,512]{2,0,1:T(8,128)(2,1)}), bf16[256,8,512]{2,0,1:T(8,128)(2,1)S(1)}, u32[]{:S(2)}, u32[]{:S(2)}) async-start(bf16[256,8,512]{2,0,1:T(8,128)(2,1)} %fusion.17), calls=%async_computation | async-start | bytes 4194304 | tf_op jit(solution)/shard_map/all_to_all | solution.py:153
  64.2 98.3 %all-gather.7.cloned.1.call-start = ((), (), s32[]{:S(2)}) async-start(), calls=%async_computation.6 | async-start | bytes 5242880 | tf_op jit(solution)/shard_map/all_gather | solution.py:19
  127.7 1.0 copy-start
  127.7 5.3 %copy-start.4 = (u32[32]{0:T(128)S(1)}, u32[32]{0:T(128)}, u32[]{:S(2)}) copy-start(u32[32]{0:T(128)} %constant.143) | copy-start | bytes 388
  128.7 41.8 %all-to-all-start.4 = ((bf16[256,8,256]{2,0,1:T(8,128)(2,1)}), bf16[256,8,256]{2,0,1:T(8,128)(2,1)}, u32[]{:S(2)}, u32[]{:S(2)}) async-start(bf16[256,8,256]{2,0,1:T(8,128)(2,1)} %get-tuple-element.431), calls=%async_computation.4 | async-start | bytes 2097152 | tf_op jit(solution)/shard_map/all_to_all | solution.py:151
  172.9 3.5 %copy-start.3 = (f32[4,2,256,512]{3,2,1,0:T(8,128)S(1)}, f32[4,2,256,512]{3,2,1,0:T(8,128)}, u32[]{:S(2)}) copy-start(f32[4,2,256,512]{3,2,1,0:T(8,128)} %get-tuple-element.243) | copy-start | bytes 12582916
Sparse Core Ops, SparseCore 0:
  128.8 33.7 all-gather.6
where the time goes:
time: 250 us; the launch traced here: 249 us
  waiting for transfers between devices  73.8 us (30%)
  blocking collectives  65.2 us (26%)
  other arithmetic  41.4 us (17%)
  starting transfers between devices  23.3 us (9%)
  local copies, waits for them, and re-layouts  17.6 us (7%)
  between operations  14.4 us (6%)
  matrix products  12.9 us (5%)
    all_to_all x1, blocking collectives, body(): lax.all_to_all(hidden, 'head', split_axis=0, concat_axis=1, tiled=True)  53 us
    all_to_all x1, waiting for transfers between devices, body(): lax.all_to_all(values, 'head', split_axis=1, concat_axis=0, tiled=True)  42.5 us
    all_to_all x1, waiting for transfers between devices, body(): lax.all_to_all(lookup_vectors, 'head', split_axis=1, concat_axis=0, tiled...  15.5 us
    all_gather x1, waiting for transfers between devices, entering(): everything = jax.tree.map(lambda part: lax.all_gather(part, axis), x)  14.7 us
    convert_element_type x2, other arithmetic, dequant(): return result.reshape(rows, heads, width).astype(jnp.bfloat16)  9.17 us
    select_n x12, other arithmetic, hop(): return jax.tree.map(lambda a, b: jnp.where(reached, a, b), new, before)  7.68 us
    unnamed x1, blocking collectives  6.69 us
    all_to_all x1, starting transfers between devices, body(): lax.all_to_all(forget_gate, 'head', split_axis=1, concat_axis=0, tiled=True)  6.35 us
  transfers between devices with their start and end apart: 6, of which 4 were waited for; matrix products, arithmetic and copies ran while one was open for 13% of the time, Pallas kernels for 0%

commit v1 on v0

v1 whole, which is shorter than its diff:
```python
import functools
import math

import jax
import jax.numpy as jnp
from jax import lax
from jax.experimental import pallas as pl
from jax.experimental.pallas import tpu as pltpu
from jax.sharding import PartitionSpec as P

DK = 256
DV = 512
CH = 256
BLK = 128
NEG_FILL = -1e30
TAIL = 8
ROWS = DK + TAIL
CHUNKS = (1, 1, 1, 1)

F32 = jnp.float32
BF16 = jnp.bfloat16


def sizes(mesh):
    ctx, head = mesh.shape["ctx"], mesh.shape["head"]
    head_bits, ctx_bits = head.bit_length() - 1, ctx.bit_length() - 1
    assert head == 1 << head_bits and ctx == 1 << ctx_bits and head_bits >= 1
    return head_bits, ctx_bits


def flip(x, bit, head_bits, ctx_bits, last):
    axis, size, b = (
        ("head", 1 << head_bits, bit) if bit < head_bits else ("ctx", 1 << ctx_bits, bit - head_bits)
    )
    pairs = [(i, i ^ (1 << b)) for i in range(size) if not (last and i & (1 << b))]
    return lax.ppermute(x, axis, pairs)


def span_index(head_bits):
    return lax.axis_index("ctx") * (1 << head_bits) + lax.axis_index("head")


def gate_kernel(i_ref, f_ref, run_ref, shift_ref, weight_ref, mf_ref):
    gate = i_ref[...].astype(F32)
    x = f_ref[...].astype(F32)
    log_forget = jnp.minimum(x, 0.0) - jnp.log1p(jnp.exp(-jnp.abs(x)))
    size = x.shape[0]
    row = lax.broadcasted_iota(jnp.int32, (size, size), 0)
    col = lax.broadcasted_iota(jnp.int32, (size, size), 1)
    below = jnp.where(row >= col, 1.0, 0.0).astype(F32)
    running = jnp.dot(below, log_forget, precision=lax.Precision.HIGHEST, preferred_element_type=F32)
    total = running[size - 1 : size, :]
    shift = gate - running
    exponent = total + shift
    peak = jnp.max(exponent, axis=0, keepdims=True)
    run_ref[...] = running
    shift_ref[...] = shift
    weight_ref[...] = jnp.exp(exponent - peak)
    mf_ref[...] = jnp.concatenate([peak, total], axis=0)


def gates(input_gate, forget_gate):
    size, heads = input_gate.shape
    col = jax.ShapeDtypeStruct((size, heads), F32)
    return pl.pallas_call(
        gate_kernel,
        out_shape=(col, col, col, jax.ShapeDtypeStruct((2, heads), F32)),
        name="gates",
    )(input_gate, forget_gate)


def coef_layout(bits):
    at, send = 0, {}
    for b in range(1, bits):
        send[b] = at
        at += 1 + b
    own, other, peak = at, at + bits, at + 2 * bits
    return send, own, other, peak, peak + 1


def coef_kernel(head_bits, bits, tab_ref, out_ref):
    spans = 1 << bits
    me = span_index(head_bits)
    peaks = tab_ref[pl.ds(0, spans, stride=2), :]
    totals = tab_ref[pl.ds(1, spans, stride=2), :]
    j = lax.broadcasted_iota(jnp.int32, (spans, 1), 0) ^ me
    j_row = lax.broadcasted_iota(jnp.int32, (1, spans), 1) ^ me
    upto = jnp.where(j_row <= j, 1.0, 0.0).astype(F32)
    running = jnp.dot(upto, totals, precision=lax.Precision.HIGHEST, preferred_element_type=F32)
    level = peaks - running

    def top(mask):
        return jnp.max(jnp.where(mask, level, NEG_FILL), axis=0, keepdims=True)

    def weight(a, b):
        return jnp.exp(jnp.minimum(a - b, 0.0))

    group = [top((j >> b) == (me >> b)) for b in range(bits)]
    peer = [top((j >> b) == ((me >> b) ^ 1)) for b in range(bits)]
    bit = [((me >> b) & 1) == 1 for b in range(bits)]
    zero = jnp.zeros_like(group[0])
    rows = []
    for b in range(1, bits):
        rows.append(weight(group[0], group[b]))
        rows += [weight(peer[k], group[b]) for k in range(b)]
    mine, theirs = top(j < me), top(j < (me ^ 1))
    rows += [jnp.where(bit[b], weight(peer[b], mine), zero) for b in range(bits)]
    rows.append(jnp.where(bit[0], zero, weight(group[0], theirs)))
    rows += [jnp.where(bit[b], weight(peer[b], theirs), zero) for b in range(1, bits)]
    before = jnp.sum(jnp.where(j < me, totals, 0.0), axis=0, keepdims=True)
    rows.append(jnp.where(me > 0, before + mine, NEG_FILL))
    for r, value in enumerate(rows):
        out_ref[r : r + 1, :] = value


def coefficients(table, head_bits, bits):
    rows = coef_layout(bits)[-1]
    return pl.pallas_call(
        functools.partial(coef_kernel, head_bits, bits),
        out_shape=jax.ShapeDtypeStruct((rows, table.shape[1]), F32),
        name="coefficients",
    )(table)


def pick(ref, h):
    x = ref[...]
    lane = lax.broadcasted_iota(jnp.int32, x.shape, 1)
    return jnp.sum(jnp.where(lane == h, x, 0.0), axis=1, keepdims=True)


def dequant(codes, tensor_id, h, scales, tensors, offsets, bits):
    rows, width = codes.shape
    x = codes.astype(F32)
    row = lax.broadcasted_iota(jnp.int32, (rows, 1), 0)
    col = lax.broadcasted_iota(jnp.int32, (1, width), 1)
    scale = jnp.zeros((rows, 1), F32)
    for b in range(rows // BLK):
        scale = jnp.where(row // BLK == b, scales[b, tensor_id, h], scale)
    x = x * scale
    for b in range(rows // BLK):
        offset = offsets[b, h]
        hit_row = jnp.where(tensors[b, h] == tensor_id, b * BLK + offset // DV, -1)
        hit_col = (offset % DV) % width
        flipped = -(lax.shift_left(jnp.int32(1), bits[b, h]).astype(F32))
        x = jnp.where((row == hit_row) & (col == hit_col), x * flipped, x)
    return x.astype(BF16)


def pack_tail(n):
    high = n.astype(BF16).astype(F32)
    low = (n - high).astype(BF16).astype(F32)
    least = n - high - low
    first = jnp.concatenate([high, low], axis=1)
    second = jnp.concatenate([least, jnp.zeros_like(least)], axis=1)
    row = lax.broadcasted_iota(jnp.int32, (TAIL, DV), 0)
    return jnp.where(row == 0, first, jnp.where(row == 1, second, 0.0)).astype(BF16)


def read_tail(ref, i):
    t = ref[i, DK:ROWS, :].astype(F32)
    return t[0:1, :DK] + t[0:1, DK : 2 * DK] + t[1:2, :DK]


def state_kernel(first, scales, tensors, offsets, fbits, weight_ref, k_ref, v_ref, keep_ref, send_ref):
    own = lax.axis_index("head") & 1
    pair = first + pl.program_id(0)
    for out_ref, side in ((send_ref, 1 - own), (keep_ref, own)):
        h = 2 * pair + side
        info = (h, scales, tensors, offsets, fbits)
        k = dequant(k_ref[:, pl.ds(pl.multiple_of(side * DK, DK), DK)], 1, *info)
        v = dequant(v_ref[:, pl.ds(pl.multiple_of(side * DV, DV), DV)], 2, *info)
        weighted = (k.astype(F32) * pick(weight_ref, h)).astype(BF16)
        matrix = lax.dot_general(weighted, v, (((0,), (0,)), ((), ())), preferred_element_type=F32)
        out_ref[0, :DK, :] = matrix.astype(BF16)
        out_ref[0, DK:ROWS, :] = pack_tail(jnp.sum(weighted.astype(F32), axis=0, keepdims=True))


SMEM = pl.BlockSpec(memory_space=pltpu.SMEM)


def whole(shape):
    return pl.BlockSpec(shape, lambda i: (0,) * len(shape))


STATE = pl.BlockSpec((1, ROWS, DV), lambda i: (i, 0, 0))


def span_states(first, count, small, weight, key_codes, value_codes):
    rows = key_codes.shape[0]
    out = jax.ShapeDtypeStruct((count, ROWS, DV), BF16)
    return pl.pallas_call(
        functools.partial(state_kernel, first),
        grid=(count,),
        in_specs=[SMEM] * 4
        + [
            whole(weight.shape),
            pl.BlockSpec((rows, 2 * DK), lambda i: (0, first + i)),
            pl.BlockSpec((rows, 2 * DV), lambda i: (0, first + i)),
        ],
        out_specs=(STATE, STATE),
        out_shape=(out, out),
        cost_estimate=pl.CostEstimate(
            flops=count * 4 * rows * DK * DV, bytes_accessed=count * rows * 2 * (2 * DK + 4 * DV), transcendentals=0
        ),
        name="span_states",
    )(*small, weight, key_codes, value_codes)


def combined(coefs, h, at, refs):
    total, normer = None, None
    for r, ref in zip(at, refs):
        c = coefs[r, h]
        term, tail = ref[0, :DK, :].astype(F32) * c, read_tail(ref, 0) * c
        total = term if total is None else total + term
        normer = tail if normer is None else normer + tail
    return total, normer


def combine_kernel(first, at, coefs, *refs):
    h = 2 * (first + pl.program_id(0)) + (lax.axis_index("head") & 1)
    total, normer = combined(coefs, h, at, refs[:-1])
    refs[-1][0, :DK, :] = total.astype(BF16)
    refs[-1][0, DK:ROWS, :] = pack_tail(normer)


def combine(first, at, coefs, parts):
    count = parts[0].shape[0]
    return pl.pallas_call(
        functools.partial(combine_kernel, first, at),
        grid=(count,),
        in_specs=[SMEM] + [STATE] * len(parts),
        out_specs=STATE,
        out_shape=jax.ShapeDtypeStruct((count, ROWS, DV), BF16),
        cost_estimate=pl.CostEstimate(
            flops=count * ROWS * DV * 2 * len(parts), bytes_accessed=count * ROWS * DV * 2 * (len(parts) + 1), transcendentals=0
        ),
        name="combine",
    )(coefs, *parts)


def output_kernel(
    first, at, peak_row, has_out, coefs, scales, tensors, offsets, fbits, run_ref, shift_ref, q_ref, k_ref, v_ref, back_ref, *rest
):
    parts, out_ref = rest[: len(at)], rest[-1]
    own = lax.axis_index("head") & 1
    pair = first + pl.program_id(0)
    factor = 1.0 / math.sqrt(DK)
    size = q_ref.shape[0]
    row = lax.broadcasted_iota(jnp.int32, (size, size), 0)
    col = lax.broadcasted_iota(jnp.int32, (size, size), 1)
    for side, mine in ((own, True), (1 - own, False)):
        h = 2 * pair + side
        info = (h, scales, tensors, offsets, fbits)
        if mine:
            start, normer = combined(coefs, h, at, parts)
            start = start.astype(BF16)
        else:
            start, normer = back_ref[0, :DK, :], read_tail(back_ref, 0)
        narrow = pl.ds(pl.multiple_of(side * DK, DK), DK)
        wide = pl.ds(pl.multiple_of(side * DV, DV), DV)
        q = dequant(q_ref[:, narrow], 0, *info)
        k = dequant(k_ref[:, narrow], 1, *info)
        v = dequant(v_ref[:, wide], 2, *info)
        run, shift = pick(run_ref, h), pick(shift_ref, h)
        shift_row = jnp.sum(jnp.where(row == col, shift, 0.0), axis=0, keepdims=True)
        exponent = jnp.where(row >= col, run + shift_row, NEG_FILL)
        inter = run + coefs[peak_row, h]
        row_peak = jnp.maximum(jnp.max(exponent, axis=1, keepdims=True), inter)
        decay = jnp.exp(exponent - row_peak)
        scores = lax.dot_general(q, k, (((1,), (1,)), ((), ())), preferred_element_type=F32) * factor
        product = decay * scores
        lifted = (q.astype(F32) * (factor * jnp.exp(inter - row_peak))).astype(BF16)
        numerator = jnp.dot(product.astype(BF16), v, preferred_element_type=F32)
        numerator = numerator + jnp.dot(lifted, start, preferred_element_type=F32)
        denominator = jnp.sum(product, axis=1, keepdims=True) + jnp.sum(
            lifted.astype(F32) * normer, axis=1, keepdims=True
        )
        out_ref[:, wide] = (numerator / jnp.maximum(jnp.abs(denominator), 1.0)).astype(BF16)


def span_outputs(first, at, peak_row, coefs, small, run, shift, codes, back, parts, before):
    q, k, v = codes
    count, rows = back.shape[0], q.shape[0]
    narrow = pl.BlockSpec((rows, 2 * DK), lambda i: (0, first + i))
    wide = pl.BlockSpec((rows, 2 * DV), lambda i: (0, first + i))
    operands = [coefs, *small, run, shift, q, k, v, back, *parts]
    in_specs = [SMEM] * 5 + [whole(run.shape)] * 2 + [narrow, narrow, wide, STATE] + [STATE] * len(parts)
    aliases = {}
    if before is not None:
        aliases = {len(operands): 0}
        operands.append(before)
        in_specs.append(pl.BlockSpec(memory_space=pl.ANY))
    return pl.pallas_call(
        functools.partial(output_kernel, first, at, peak_row, before is not None),
        grid=(count,),
        in_specs=in_specs,
        out_specs=wide,
        out_shape=jax.ShapeDtypeStruct(v.shape, BF16),
        input_output_aliases=aliases,
        cost_estimate=pl.CostEstimate(
            flops=count * 4 * rows * (rows * DK + rows * DV + DK * DV),
            bytes_accessed=count * (rows * 2 * (4 * DK + 4 * DV) + ROWS * DV * 2 * (1 + len(parts))),
            transcendentals=count * 2 * rows * rows,
        ),
        name="span_outputs",
    )(*operands)


def body(
    head_bits,
    ctx_bits,
    query_codes,
    key_codes,
    value_codes,
    block_scales,
    fault_tensor,
    fault_offset,
    fault_bit,
    input_gate,
    forget_gate,
):
    bits = head_bits + ctx_bits
    assert query_codes.shape[0] == CH
    send_at, own_at, other_at, peak_row, _ = coef_layout(bits)
    small = (block_scales, fault_tensor, fault_offset, fault_bit)
    exchange = functools.partial(flip, head_bits=head_bits, ctx_bits=ctx_bits)
    run, shift, weight, table = gates(input_gate, forget_gate)
    for b in range(bits):
        table = jnp.concatenate([table, exchange(table, b, last=False)], axis=0)
    coefs = coefficients(table, head_bits, bits)

    starts = [sum(CHUNKS[:c]) for c in range(len(CHUNKS))]
    assert 2 * sum(CHUNKS) == input_gate.shape[1]
    out = None
    for first, count in zip(starts, CHUNKS):
        keep, send = span_states(first, count, small, weight, key_codes, value_codes)
        got = [exchange(send, 0, last=False)]
        for b in range(1, bits):
            at = [send_at[b] + r for r in range(b + 1)]
            group = combine(first, at, coefs, [keep, *got])
            got.append(exchange(group, b, last=b == bits - 1))
        at = [other_at + r for r in range(bits)]
        back = exchange(combine(first, at, coefs, [keep, *got[1:]]), 0, last=False)
        at = [own_at + r for r in range(bits)]
        out = span_outputs(
            first, at, peak_row, coefs, small, run, shift, (query_codes, key_codes, value_codes), back, got, out
        )
    return out


def solution(mesh):
    rows = P(("grp", "ctx", "head"), None)
    placed = (rows, rows, rows, P(("grp", "ctx", "head"), None, None)) + (rows,) * 5
    return jax.shard_map(
        functools.partial(body, *sizes(mesh)), mesh=mesh, in_specs=placed, out_specs=rows, check_vma=False
    )
```

time: 250 us -> 149 us (0.60)
  blocking collectives: 65.2 us -> 0 us
  Pallas kernels: 0 us -> 63.4 us
  other arithmetic: 41.4 us -> 0.03 us
  waiting for transfers between devices: 73.8 us -> 35 us
  between operations: 14.4 us -> 0.19 us
  matrix products: 12.9 us -> 0 us
  starting transfers between devices: 23.3 us -> 29.6 us
  local copies, waits for them, and re-layouts: 17.6 us -> 20.1 us
    pallas_call x0 -> x26, Pallas kernels: none -> 63.4 us  [the longest x16 32.6 us: combine(): pl.pallas_call(functools.partial(combine_kernel, first, at), grid=(count,...]
    all_to_all x5 -> x0, waiting for transfers between devices: 59.1 us -> none  [the longest x1 42.5 us: body(): lax.all_to_all(values, 'head', split_axis=1, concat_axis=0, tiled=True)]
    all_to_all x1 -> x0, blocking collectives: 53 us -> none  [body(): lax.all_to_all(hidden, 'head', split_axis=0, concat_axis=1, tiled=True)]
    ppermute x0 -> x24, waiting for transfers between devices: none -> 35 us  [flip(): return lax.ppermute(x, axis, pairs)]
    ppermute x0 -> x24, starting transfers between devices: none -> 29.6 us  [flip(): return lax.ppermute(x, axis, pairs)]
    all_to_all x5 -> x0, starting transfers between devices: 23.3 us -> none  [the longest x1 6.35 us: body(): lax.all_to_all(forget_gate, 'head', split_axis=1, concat_axis=0, tiled=True)]
    unnamed x16 -> x45, local copies, waits for them, and re-layouts: 3.12 us -> 18.3 us
    convert_element_type x6 -> x0, other arithmetic: 14.9 us -> none  [the longest x2 9.17 us: dequant(): return result.reshape(rows, heads, width).astype(jnp.bfloat16)]
  transfers between devices with their start and end apart: 6 -> 24, of which waited for: 4 -> 8; matrix products, arithmetic and copies ran while one was open for 13% -> 2% of each run, Pallas kernels for 0% -> 39%
where the time goes in v1:
time: 149 us; the launch traced here: 148 us
  Pallas kernels  63.4 us (43%)
  waiting for transfers between devices  35 us (23%)
  starting transfers between devices  29.6 us (20%)
  local copies, waits for them, and re-layouts  20.1 us (13%)
    ppermute x24, waiting for transfers between devices, flip(): return lax.ppermute(x, axis, pairs)  35 us
    pallas_call x16, Pallas kernels, combine(): pl.pallas_call(functools.partial(combine_kernel, first, at), grid=(count,...  32.6 us
    ppermute x24, starting transfers between devices, flip(): return lax.ppermute(x, axis, pairs)  29.6 us
    unnamed x45, local copies, waits for them, and re-layouts  18.3 us
    pallas_call x4, Pallas kernels, span_outputs(): pl.pallas_call(functools.partial(output_kernel, first, at, peak_row, befo...  16.2 us
    pallas_call x4, Pallas kernels, span_states(): pl.pallas_call(functools.partial(state_kernel, first), grid=(count,), in_...  11 us
  transfers between devices with their start and end apart: 24, of which 8 were waited for; matrix products, arithmetic and copies ran while one was open for 2% of the time, Pallas kernels for 39%

profile of v1, /device:TPU:0, one launch (start us, length us, event | category | flops | bytes accessed | tf_op | source)
XLA Modules:
  0.0 148.2 jit_solution(12316492986254788338)
XLA Ops:
  0.0 1.4 copy.39.i_ref
  1.4 1.4 copy.40.f_ref
  2.8 2.0 %gates.1 = (f32[256,8]{1,0:T(8,128)}, f32[256,8]{1,0:T(8,128)}, f32[256,8]{1,0:T(8,128)}, f32[2,8]{1,0:T(2,128)}) custom-call(bf16[256,8]{1,0:T(8,128)(2,1)} %copy.39.i_ref, bf16[256,8]{1,0:T(8,128)(2,1)} %copy.40.f_ref), custom_call_target="tpu_custom_call" | custom-call | tf_op jit(solution)/shard_map/gates/pallas_call | solution.py:65
  4.9 3.1 %collective-permute-start = (f32[2,8]{1,0:T(2,128)}, f32[2,8]{1,0:T(2,128)S(1)}, u32[]{:S(2)}, u32[]{:S(2)}) collective-permute-start(f32[2,8]{1,0:T(2,128)} %get-tuple-element.17), channel_id=1, source_target_pairs={{0,1},{1,0},{2,3},{3,2},{4,5},{5,4},{6,7},{7,6},{8,9},{9,8},{10,11... | collective-permute-start | bytes 200 | tf_op jit(solution)/shard_map/ppermute | solution.py:36
  7.9 1.3 copy.48.scales
  9.2 2.8 %span_states.7 = (bf16[1,264,512]{2,1,0:T(8,128)(2,1)}, bf16[1,264,512]{2,1,0:T(8,128)(2,1)}) custom-call(f32[2,3,8]{2,1,0:T(4,128)} %copy.48.scales, s32[2,8]{1,0:T(2,128)} %tensors.15, s32[2,8]{1,0:T(2,128)} %offsets.15, s32[2,8]{1,0:T(2,128)} %fbits.15, f32[256,8]{1,0:T(8,128)} %get-tuple-element.20.weight_ref, bf16[256,2048]{1,0:T(8,128)(2,1)} %k_ref.15, ...), custom_call_target="tpu_custom_call" | custom-call | flops 134217728 | bytes 1310720 | tf_op jit(solution)/shard_map/span_states/pallas_call | solution.py:191
  12.0 2.8 %span_states.6 = (bf16[1,264,512]{2,1,0:T(8,128)(2,1)}, bf16[1,264,512]{2,1,0:T(8,128)(2,1)}) custom-call(f32[2,3,8]{2,1,0:T(4,128)} %copy.48.scales, s32[2,8]{1,0:T(2,128)} %tensors.15, s32[2,8]{1,0:T(2,128)} %offsets.15, s32[2,8]{1,0:T(2,128)} %fbits.15, f32[256,8]{1,0:T(8,128)} %get-tuple-element.20.weight_ref, bf16[256,2048]{1,0:T(8,128)(2,1)} %k_ref.15, ...), custom_call_target="tpu_custom_call" | custom-call | flops 134217728 | bytes 1310720 | tf_op jit(solution)/shard_map/span_states/pallas_call | solution.py:191
  14.7 2.0 %collective-permute-start.14 = (bf16[1,264,512]{2,1,0:T(8,128)(2,1)}, bf16[1,264,512]{2,1,0:T(8,128)(2,1)S(1)}, u32[]{:S(2)}, u32[]{:S(2)}) collective-permute-start(bf16[1,264,512]{2,1,0:T(8,128)(2,1)} %get-tuple-element.26), channel_id=1, source_target_pairs={{0,1},{1,0},{2,3},{3,2},{4,5},{5,4},{6,7},{7,6},{8,9},{9,8},{10,11... | collective-permute-start | bytes 811016 | tf_op jit(solution)/shard_map/ppermute | solution.py:36
  16.7 2.8 %span_states.5 = (bf16[1,264,512]{2,1,0:T(8,128)(2,1)}, bf16[1,264,512]{2,1,0:T(8,128)(2,1)}) custom-call(f32[2,3,8]{2,1,0:T(4,128)} %copy.48.scales, s32[2,8]{1,0:T(2,128)} %tensors.15, s32[2,8]{1,0:T(2,128)} %offsets.15, s32[2,8]{1,0:T(2,128)} %fbits.15, f32[256,8]{1,0:T(8,128)} %get-tuple-element.20.weight_ref, bf16[256,2048]{1,0:T(8,128)(2,1)} %k_ref.15, ...), custom_call_target="tpu_custom_call" | custom-call | flops 134217728 | bytes 1310720 | tf_op jit(solution)/shard_map/span_states/pallas_call | solution.py:191
  19.5 2.8 %span_states.4 = (bf16[1,264,512]{2,1,0:T(8,128)(2,1)}, bf16[1,264,512]{2,1,0:T(8,128)(2,1)}) custom-call(f32[2,3,8]{2,1,0:T(4,128)} %copy.48.scales, s32[2,8]{1,0:T(2,128)} %tensors.15, s32[2,8]{1,0:T(2,128)} %offsets.15, s32[2,8]{1,0:T(2,128)} %fbits.15, f32[256,8]{1,0:T(8,128)} %get-tuple-element.20.weight_ref, bf16[256,2048]{1,0:T(8,128)(2,1)} %k_ref.15, ...), custom_call_target="tpu_custom_call" | custom-call | flops 134217728 | bytes 1310720 | tf_op jit(solution)/shard_map/span_states/pallas_call | solution.py:191
  22.3 3.1 %collective-permute-start.1 = (f32[4,8]{1,0:T(4,128)S(1)}, f32[4,8]{1,0:T(4,128)S(1)}, u32[]{:S(2)}, u32[]{:S(2)}) collective-permute-start(f32[4,8]{1,0:T(4,128)S(1)} %pad_maximum_fusion.2), channel_id=1, source_target_pairs={{0,2},{1,3},{2,0},{3,1},{4,6},{5,7},{6,4},{7,5},{8,10},{9,11},{10,... | collective-permute-start | bytes 392 | tf_op jit(solution)/shard_map/ppermute | solution.py:36
  25.4 1.6 %collective-permute-start.4 = (bf16[1,264,512]{2,1,0:T(8,128)(2,1)}, bf16[1,264,512]{2,1,0:T(8,128)(2,1)S(1)}, u32[]{:S(2)}, u32[]{:S(2)}) collective-permute-start(bf16[1,264,512]{2,1,0:T(8,128)(2,1)} %get-tuple-element.22), channel_id=1, source_target_pairs={{0,1},{1,0},{2,3},{3,2},{4,5},{5,4},{6,7},{7,6},{8,9},{9,8},{10,11... | collective-permute-start | bytes 811016 | tf_op jit(solution)/shard_map/ppermute | solution.py:36
  27.0 3.8 %collective-permute-done.1 = f32[4,8]{1,0:T(4,128)S(1)} collective-permute-done((f32[4,8]{1,0:T(4,128)S(1)}, f32[4,8]{1,0:T(4,128)S(1)}, u32[]{:S(2)}, u32[]{:S(2)}) %collective-permute-start.1) | collective-permute-done | bytes 160 | tf_op jit(solution)/shard_map/ppermute | solution.py:36
  32.0 2.0 %collective-permute-start.3 = (f32[16,8]{1,0:T(8,128)S(1)}, f32[16,8]{1,0:T(8,128)S(1)}, u32[]{:S(2)}, u32[]{:S(2)}) collective-permute-start(f32[16,8]{1,0:T(8,128)S(1)} %pad_maximum_fusion), channel_id=1, source_target_pairs={{0,8},{4,12},{8,0},{12,4},{1,9},{5,13},{9,1},{13,5},{2,10},{6,14},... | collective-permute-start | bytes 1544 | tf_op jit(solution)/shard_map/ppermute | solution.py:36
  34.0 1.7 %collective-permute-done.3 = f32[16,8]{1,0:T(8,128)S(1)} collective-permute-done((f32[16,8]{1,0:T(8,128)S(1)}, f32[16,8]{1,0:T(8,128)S(1)}, u32[]{:S(2)}, u32[]{:S(2)}) %collective-permute-start.3) | collective-permute-done | bytes 544 | tf_op jit(solution)/shard_map/ppermute | solution.py:36
  35.7 1.8 %concatenate.18.tab_ref = f32[32,8]{1,0:T(8,128)} concatenate(f32[2,8]{1,0:T(2,128)S(1)} %copy-done.20, f32[2,8]{1,0:T(2,128)S(1)} %collective-permute-done, f32[4,8]{1,0:T(4,128)S(1)} %collective-permute-done.1, f32[8,8]{1,0:T(8,128)S(1)} %collective-permute-done.2, f32[16,8]{1,0:T(8,128)S(1)} %collective-permute-done.3), dimensions={0} | concatenate | bytes 2048 | tf_op jit(solution)/shard_map/concatenate | solution.py:329
  37.5 1.5 %coefficients.1.coefs = f32[18,8]{1,0:T(8,128)} custom-call(f32[32,8]{1,0:T(8,128)} %concatenate.18.tab_ref), custom_call_target="tpu_custom_call" | custom-call | tf_op jit(solution)/shard_map/coefficients/pallas_call | solution.py:118
  39.7 1.9 %combine.28 = bf16[1,264,512]{2,1,0:T(8,128)(2,1)} custom-call(f32[18,8]{1,0:T(8,128)} %coefficients.1.coefs, bf16[1,264,512]{2,1,0:T(8,128)(2,1)} %get-tuple-element.27.refs_0_, bf16[1,264,512]{2,1,0:T(8,128)(2,1)} %copy-done.6), custom_call_target="tpu_custom_call" | custom-call | flops 540672 | bytes 811008 | tf_op jit(solution)/shard_map/combine/pallas_call | solution.py:228
  41.6 3.3 %collective-permute-start.20 = (bf16[1,264,512]{2,1,0:T(8,128)(2,1)}, bf16[1,264,512]{2,1,0:T(8,128)(2,1)S(1)}, u32[]{:S(2)}, u32[]{:S(2)}) collective-permute-start(bf16[1,264,512]{2,1,0:T(8,128)(2,1)} %combine.28), channel_id=1, source_target_pairs={{0,2},{1,3},{2,0},{3,1},{4,6},{5,7},{6,4},{7,5},{8,10},{9,11},{10,... | collective-permute-start | bytes 811016 | tf_op jit(solution)/shard_map/ppermute | solution.py:36
  45.6 1.9 %combine.24 = bf16[1,264,512]{2,1,0:T(8,128)(2,1)} custom-call(f32[18,8]{1,0:T(8,128)} %coefficients.1.coefs, bf16[1,264,512]{2,1,0:T(8,128)(2,1)} %get-tuple-element.25.refs_0_, bf16[1,264,512]{2,1,0:T(8,128)(2,1)} %copy-done.2), custom_call_target="tpu_custom_call" | custom-call | flops 540672 | bytes 811008 | tf_op jit(solution)/shard_map/combine/pallas_call | solution.py:228
  48.2 1.9 %combine.20 = bf16[1,264,512]{2,1,0:T(8,128)(2,1)} custom-call(f32[18,8]{1,0:T(8,128)} %coefficients.1.coefs, bf16[1,264,512]{2,1,0:T(8,128)(2,1)} %get-tuple-element.23.refs_0_, bf16[1,264,512]{2,1,0:T(8,128)(2,1)} %copy-done), custom_call_target="tpu_custom_call" | custom-call | flops 540672 | bytes 811008 | tf_op jit(solution)/shard_map/combine/pallas_call | solution.py:228
  50.1 2.9 %collective-permute-start.10 = (bf16[1,264,512]{2,1,0:T(8,128)(2,1)}, bf16[1,264,512]{2,1,0:T(8,128)(2,1)S(1)}, u32[]{:S(2)}, u32[]{:S(2)}) collective-permute-start(bf16[1,264,512]{2,1,0:T(8,128)(2,1)} %combine.20), channel_id=1, source_target_pairs={{0,2},{1,3},{2,0},{3,1},{4,6},{5,7},{6,4},{7,5},{8,10},{9,11},{10,... | collective-permute-start | bytes 811016 | tf_op jit(solution)/shard_map/ppermute | solution.py:36
  53.7 1.9 %combine.16 = bf16[1,264,512]{2,1,0:T(8,128)(2,1)} custom-call(f32[18,8]{1,0:T(8,128)} %coefficients.1.coefs, bf16[1,264,512]{2,1,0:T(8,128)(2,1)} %get-tuple-element.21.refs_0_, bf16[1,264,512]{2,1,0:T(8,128)(2,1)} %copy-done.1), custom_call_target="tpu_custom_call" | custom-call | flops 540672 | bytes 811008 | tf_op jit(solution)/shard_map/combine/pallas_call | solution.py:228
  55.6 20.0 %collective-permute-done.20.refs_2_.refs_1_.rest_1_ = bf16[1,264,512]{2,1,0:T(8,128)(2,1)S(1)} collective-permute-done((bf16[1,264,512]{2,1,0:T(8,128)(2,1)}, bf16[1,264,512]{2,1,0:T(8,128)(2,1)S(1)}, u32[]{:S(2)}, u32[]{:S(2)}) %collective-permute-start.20) | collective-permute-done | bytes 270368 | tf_op jit(solution)/shard_map/ppermute | solution.py:36
  76.4 2.0 %combine.29 = bf16[1,264,512]{2,1,0:T(8,128)(2,1)} custom-call(f32[18,8]{1,0:T(8,128)} %coefficients.1.coefs, bf16[1,264,512]{2,1,0:T(8,128)(2,1)} %get-tuple-element.27.refs_0_, bf16[1,264,512]{2,1,0:T(8,128)(2,1)} %copy-done.6, bf16[1,264,512]{2,1,0:T(8,128)(2,1)} %copy-done.7), custom_call_target="tpu_custom_call" | custom-call | flops 811008 | bytes 1081344 | tf_op jit(solution)/shard_map/combine/pallas_call | solution.py:228
  78.4 3.1 %collective-permute-done.15.refs_2_.refs_1_.rest_1_ = bf16[1,264,512]{2,1,0:T(8,128)(2,1)S(1)} collective-permute-done((bf16[1,264,512]{2,1,0:T(8,128)(2,1)}, bf16[1,264,512]{2,1,0:T(8,128)(2,1)S(1)}, u32[]{:S(2)}, u32[]{:S(2)}) %collective-permute-start.15) | collective-permute-done | bytes 270368 | tf_op jit(solution)/shard_map/ppermute | solution.py:36
  82.1 2.0 %combine.25 = bf16[1,264,512]{2,1,0:T(8,128)(2,1)} custom-call(f32[18,8]{1,0:T(8,128)} %coefficients.1.coefs, bf16[1,264,512]{2,1,0:T(8,128)(2,1)} %get-tuple-element.25.refs_0_, bf16[1,264,512]{2,1,0:T(8,128)(2,1)} %copy-done.2, bf16[1,264,512]{2,1,0:T(8,128)(2,1)} %copy-done.5), custom_call_target="tpu_custom_call" | custom-call | flops 811008 | bytes 1081344 | tf_op jit(solution)/shard_map/combine/pallas_call | solution.py:228
  84.2 3.1 %collective-permute-done.10.refs_2_.refs_1_.rest_1_ = bf16[1,264,512]{2,1,0:T(8,128)(2,1)S(1)} collective-permute-done((bf16[1,264,512]{2,1,0:T(8,128)(2,1)}, bf16[1,264,512]{2,1,0:T(8,128)(2,1)S(1)}, u32[]{:S(2)}, u32[]{:S(2)}) %collective-permute-start.10) | collective-permute-done | bytes 270368 | tf_op jit(solution)/shard_map/ppermute | solution.py:36
  87.9 2.0 %combine.21 = bf16[1,264,512]{2,1,0:T(8,128)(2,1)} custom-call(f32[18,8]{1,0:T(8,128)} %coefficients.1.coefs, bf16[1,264,512]{2,1,0:T(8,128)(2,1)} %get-tuple-element.23.refs_0_, bf16[1,264,512]{2,1,0:T(8,128)(2,1)} %copy-done, bf16[1,264,512]{2,1,0:T(8,128)(2,1)} %copy-done.4), custom_call_target="tpu_custom_call" | custom-call | flops 811008 | bytes 1081344 | tf_op jit(solution)/shard_map/combine/pallas_call | solution.py:228
  89.9 1.9 %collective-permute-done.5.refs_2_.refs_1_.rest_1_ = bf16[1,264,512]{2,1,0:T(8,128)(2,1)S(1)} collective-permute-done((bf16[1,264,512]{2,1,0:T(8,128)(2,1)}, bf16[1,264,512]{2,1,0:T(8,128)(2,1)S(1)}, u32[]{:S(2)}, u32[]{:S(2)}) %collective-permute-start.5) | collective-permute-done | bytes 270368 | tf_op jit(solution)/shard_map/ppermute | solution.py:36
  92.5 2.0 %combine.17 = bf16[1,264,512]{2,1,0:T(8,128)(2,1)} custom-call(f32[18,8]{1,0:T(8,128)} %coefficients.1.coefs, bf16[1,264,512]{2,1,0:T(8,128)(2,1)} %get-tuple-element.21.refs_0_, bf16[1,264,512]{2,1,0:T(8,128)(2,1)} %copy-done.1, bf16[1,264,512]{2,1,0:T(8,128)(2,1)} %copy-done.3), custom_call_target="tpu_custom_call" | custom-call | flops 811008 | bytes 1081344 | tf_op jit(solution)/shard_map/combine/pallas_call | solution.py:228
  95.3 2.2 %combine.30 = bf16[1,264,512]{2,1,0:T(8,128)(2,1)} custom-call(f32[18,8]{1,0:T(8,128)} %coefficients.1.coefs, bf16[1,264,512]{2,1,0:T(8,128)(2,1)} %get-tuple-element.27.refs_0_, bf16[1,264,512]{2,1,0:T(8,128)(2,1)} %copy-done.6, bf16[1,264,512]{2,1,0:T(8,128)(2,1)} %copy-done.7, bf16[1,264,512]{2,1,0:T(8,128)(2,1)} %copy-done.11), custom_call_target="tpu_custom_call" | custom-call | flops 1081344 | bytes 1351680 | tf_op jit(solution)/shard_map/combine/pallas_call | solution.py:228
  97.4 3.6 %collective-permute-start.22 = (bf16[1,264,512]{2,1,0:T(8,128)(2,1)}, bf16[1,264,512]{2,1,0:T(8,128)(2,1)S(1)}, u32[]{:S(2)}, u32[]{:S(2)}) collective-permute-start(bf16[1,264,512]{2,1,0:T(8,128)(2,1)} %combine.30), channel_id=1, source_target_pairs={{0,8},{4,12},{1,9},{5,13},{2,10},{6,14},{3,11},{7,15},{16,24},{20,... | collective-permute-start | bytes 811016 | tf_op jit(solution)/shard_map/ppermute | solution.py:36
  101.8 2.1 %combine.26 = bf16[1,264,512]{2,1,0:T(8,128)(2,1)} custom-call(f32[18,8]{1,0:T(8,128)} %coefficients.1.coefs, bf16[1,264,512]{2,1,0:T(8,128)(2,1)} %get-tuple-element.25.refs_0_, bf16[1,264,512]{2,1,0:T(8,128)(2,1)} %copy-done.2, bf16[1,264,512]{2,1,0:T(8,128)(2,1)} %copy-done.5, bf16[1,264,512]{2,1,0:T(8,128)(2,1)} %copy-done.10), custom_call_target="tpu_custom_call" | custom-call | flops 1081344 | bytes 1351680 | tf_op jit(solution)/shard_map/combine/pallas_call | solution.py:228
  104.0 1.3 collective-permute-start.17
  106.0 2.1 %combine.22 = bf16[1,264,512]{2,1,0:T(8,128)(2,1)} custom-call(f32[18,8]{1,0:T(8,128)} %coefficients.1.coefs, bf16[1,264,512]{2,1,0:T(8,128)(2,1)} %get-tuple-element.23.refs_0_, bf16[1,264,512]{2,1,0:T(8,128)(2,1)} %copy-done, bf16[1,264,512]{2,1,0:T(8,128)(2,1)} %copy-done.4, bf16[1,264,512]{2,1,0:T(8,128)(2,1)} %copy-done.9), custom_call_target="tpu_custom_call" | custom-call | flops 1081344 | bytes 1351680 | tf_op jit(solution)/shard_map/combine/pallas_call | solution.py:228
  108.1 1.3 collective-permute-start.12
  110.1 2.1 %combine.18 = bf16[1,264,512]{2,1,0:T(8,128)(2,1)} custom-call(f32[18,8]{1,0:T(8,128)} %coefficients.1.coefs, bf16[1,264,512]{2,1,0:T(8,128)(2,1)} %get-tuple-element.21.refs_0_, bf16[1,264,512]{2,1,0:T(8,128)(2,1)} %copy-done.1, bf16[1,264,512]{2,1,0:T(8,128)(2,1)} %copy-done.3, bf16[1,264,512]{2,1,0:T(8,128)(2,1)} %copy-done.8), custom_call_target="tpu_custom_call" | custom-call | flops 1081344 | bytes 1351680 | tf_op jit(solution)/shard_map/combine/pallas_call | solution.py:228
  112.2 1.5 collective-permute-start.7
  114.5 2.1 %combine.31 = bf16[1,264,512]{2,1,0:T(8,128)(2,1)} custom-call(f32[18,8]{1,0:T(8,128)} %coefficients.1.coefs, bf16[1,264,512]{2,1,0:T(8,128)(2,1)} %get-tuple-element.27.refs_0_, bf16[1,264,512]{2,1,0:T(8,128)(2,1)} %copy-done.7, bf16[1,264,512]{2,1,0:T(8,128)(2,1)} %copy-done.11, bf16[1,264,512]{2,1,0:T(8,128)(2,1)} %copy-done.15), custom_call_target="tpu_custom_call" | custom-call | flops 1081344 | bytes 1351680 | tf_op jit(solution)/shard_map/combine/pallas_call | solution.py:228
  117.9 2.1 %combine.27 = bf16[1,264,512]{2,1,0:T(8,128)(2,1)} custom-call(f32[18,8]{1,0:T(8,128)} %coefficients.1.coefs, bf16[1,264,512]{2,1,0:T(8,128)(2,1)} %get-tuple-element.25.refs_0_, bf16[1,264,512]{2,1,0:T(8,128)(2,1)} %copy-done.5, bf16[1,264,512]{2,1,0:T(8,128)(2,1)} %copy-done.10, bf16[1,264,512]{2,1,0:T(8,128)(2,1)} %copy-done.14), custom_call_target="tpu_custom_call" | custom-call | flops 1081344 | bytes 1351680 | tf_op jit(solution)/shard_map/combine/pallas_call | solution.py:228
  120.1 1.4 collective-permute-start.18
  122.2 2.1 %combine.23 = bf16[1,264,512]{2,1,0:T(8,128)(2,1)} custom-call(f32[18,8]{1,0:T(8,128)} %coefficients.1.coefs, bf16[1,264,512]{2,1,0:T(8,128)(2,1)} %get-tuple-element.23.refs_0_, bf16[1,264,512]{2,1,0:T(8,128)(2,1)} %copy-done.4, bf16[1,264,512]{2,1,0:T(8,128)(2,1)} %copy-done.9, bf16[1,264,512]{2,1,0:T(8,128)(2,1)} %copy-done.13), custom_call_target="tpu_custom_call" | custom-call | flops 1081344 | bytes 1351680 | tf_op jit(solution)/shard_map/combine/pallas_call | solution.py:228
  125.9 2.1 %combine.19 = bf16[1,264,512]{2,1,0:T(8,128)(2,1)} custom-call(f32[18,8]{1,0:T(8,128)} %coefficients.1.coefs, bf16[1,264,512]{2,1,0:T(8,128)(2,1)} %get-tuple-element.21.refs_0_, bf16[1,264,512]{2,1,0:T(8,128)(2,1)} %copy-done.3, bf16[1,264,512]{2,1,0:T(8,128)(2,1)} %copy-done.8, bf16[1,264,512]{2,1,0:T(8,128)(2,1)} %copy-done.12), custom_call_target="tpu_custom_call" | custom-call | flops 1081344 | bytes 1351680 | tf_op jit(solution)/shard_map/combine/pallas_call | solution.py:228
  129.9 4.0 %span_outputs.4.rest_4_ = bf16[256,4096]{1,0:T(8,128)(2,1)} custom-call(f32[18,8]{1,0:T(8,128)} %coefficients.1.coefs, f32[2,3,8]{2,1,0:T(4,128)} %copy.48.scales, s32[2,8]{1,0:T(2,128)} %tensors.15, s32[2,8]{1,0:T(2,128)} %offsets.15, s32[2,8]{1,0:T(2,128)} %fbits.15, f32[256,8]{1,0:T(8,128)} %get-tuple-element.18.run_ref, ...), custom_call_target="tpu_custom_call" | custom-call | flops 335544320 | bytes 2924544 | tf_op jit(solution)/shard_map/span_outputs/pallas_call | solution.py:293
  134.7 4.0 %span_outputs.5.rest_4_ = bf16[256,4096]{1,0:T(8,128)(2,1)} custom-call(f32[18,8]{1,0:T(8,128)} %coefficients.1.coefs, f32[2,3,8]{2,1,0:T(4,128)} %copy.48.scales, s32[2,8]{1,0:T(2,128)} %tensors.15, s32[2,8]{1,0:T(2,128)} %offsets.15, s32[2,8]{1,0:T(2,128)} %fbits.15, f32[256,8]{1,0:T(8,128)} %get-tuple-element.18.run_ref, ...), custom_call_target="tpu_custom_call", output_to_operand_aliasing={{}: (15, {})} | custom-call | flops 335544320 | bytes 2924544 | tf_op jit(solution)/shard_map/span_outputs/pallas_call | solution.py:293
  139.4 4.0 %span_outputs.6.rest_4_ = bf16[256,4096]{1,0:T(8,128)(2,1)} custom-call(f32[18,8]{1,0:T(8,128)} %coefficients.1.coefs, f32[2,3,8]{2,1,0:T(4,128)} %copy.48.scales, s32[2,8]{1,0:T(2,128)} %tensors.15, s32[2,8]{1,0:T(2,128)} %offsets.15, s32[2,8]{1,0:T(2,128)} %fbits.15, f32[256,8]{1,0:T(8,128)} %get-tuple-element.18.run_ref, ...), custom_call_target="tpu_custom_call", output_to_operand_aliasing={{}: (15, {})} | custom-call | flops 335544320 | bytes 2924544 | tf_op jit(solution)/shard_map/span_outputs/pallas_call | solution.py:293
  144.2 4.0 %span_outputs.7 = bf16[256,4096]{1,0:T(8,128)(2,1)} custom-call(f32[18,8]{1,0:T(8,128)} %coefficients.1.coefs, f32[2,3,8]{2,1,0:T(4,128)} %copy.48.scales, s32[2,8]{1,0:T(2,128)} %tensors.15, s32[2,8]{1,0:T(2,128)} %offsets.15, s32[2,8]{1,0:T(2,128)} %fbits.15, f32[256,8]{1,0:T(8,128)} %get-tuple-element.18.run_ref, ...), custom_call_target="tpu_custom_call", output_to_operand_aliasing={{}: (15, {})} | custom-call | flops 335544320 | bytes 2924544 | tf_op jit(solution)/shard_map/span_outputs/pallas_call | solution.py:293
  (75 shorter events, 18.1 us)
Async XLA Ops:
  4.9 17.4 %collective-permute-start = (f32[2,8]{1,0:T(2,128)}, f32[2,8]{1,0:T(2,128)S(1)}, u32[]{:S(2)}, u32[]{:S(2)}) collective-permute-start(f32[2,8]{1,0:T(2,128)} %get-tuple-element.17), channel_id=1, source_target_pairs={{0,1},{1,0},{2,3},{3,2},{4,5},{5,4},{6,7},{7,6},{8,9},{9,8},{10,11... | collective-permute-start | bytes 200 | tf_op jit(solution)/shard_map/ppermute | solution.py:36
  12.0 27.0 %collective-permute-start.19 = (bf16[1,264,512]{2,1,0:T(8,128)(2,1)}, bf16[1,264,512]{2,1,0:T(8,128)(2,1)S(1)}, u32[]{:S(2)}, u32[]{:S(2)}) collective-permute-start(bf16[1,264,512]{2,1,0:T(8,128)(2,1)} %get-tuple-element.28), channel_id=1, source_target_pairs={{0,1},{1,0},{2,3},{3,2},{4,5},{5,4},{6,7},{7,6},{8,9},{9,8},{10,11... | collective-permute-start | bytes 811016 | tf_op jit(solution)/shard_map/ppermute | solution.py:36
  14.7 30.2 %collective-permute-start.14 = (bf16[1,264,512]{2,1,0:T(8,128)(2,1)}, bf16[1,264,512]{2,1,0:T(8,128)(2,1)S(1)}, u32[]{:S(2)}, u32[]{:S(2)}) collective-permute-start(bf16[1,264,512]{2,1,0:T(8,128)(2,1)} %get-tuple-element.26), channel_id=1, source_target_pairs={{0,1},{1,0},{2,3},{3,2},{4,5},{5,4},{6,7},{7,6},{8,9},{9,8},{10,11... | collective-permute-start | bytes 811016 | tf_op jit(solution)/shard_map/ppermute | solution.py:36
  19.5 2.8 %copy-start.20 = (f32[2,8]{1,0:T(2,128)S(1)}, f32[2,8]{1,0:T(2,128)}, u32[]{:S(2)}) copy-start(f32[2,8]{1,0:T(2,128)} %get-tuple-element.17) | copy-start | bytes 196
  19.5 28.0 %collective-permute-start.9 = (bf16[1,264,512]{2,1,0:T(8,128)(2,1)}, bf16[1,264,512]{2,1,0:T(8,128)(2,1)S(1)}, u32[]{:S(2)}, u32[]{:S(2)}) collective-permute-start(bf16[1,264,512]{2,1,0:T(8,128)(2,1)} %get-tuple-element.24), channel_id=1, source_target_pairs={{0,1},{1,0},{2,3},{3,2},{4,5},{5,4},{6,7},{7,6},{8,9},{9,8},{10,11... | collective-permute-start | bytes 811016 | tf_op jit(solution)/shard_map/ppermute | solution.py:36
  22.3 8.4 %collective-permute-start.1 = (f32[4,8]{1,0:T(4,128)S(1)}, f32[4,8]{1,0:T(4,128)S(1)}, u32[]{:S(2)}, u32[]{:S(2)}) collective-permute-start(f32[4,8]{1,0:T(4,128)S(1)} %pad_maximum_fusion.2), channel_id=1, source_target_pairs={{0,2},{1,3},{2,0},{3,1},{4,6},{5,7},{6,4},{7,5},{8,10},{9,11},{10,... | collective-permute-start | bytes 392 | tf_op jit(solution)/shard_map/ppermute | solution.py:36
  25.4 27.6 %collective-permute-start.4 = (bf16[1,264,512]{2,1,0:T(8,128)(2,1)}, bf16[1,264,512]{2,1,0:T(8,128)(2,1)S(1)}, u32[]{:S(2)}, u32[]{:S(2)}) collective-permute-start(bf16[1,264,512]{2,1,0:T(8,128)(2,1)} %get-tuple-element.22), channel_id=1, source_target_pairs={{0,1},{1,0},{2,3},{3,2},{4,5},{5,4},{6,7},{7,6},{8,9},{9,8},{10,11... | collective-permute-start | bytes 811016 | tf_op jit(solution)/shard_map/ppermute | solution.py:36
  30.8 1.2 collective-permute-start.2
  32.0 3.7 %collective-permute-start.3 = (f32[16,8]{1,0:T(8,128)S(1)}, f32[16,8]{1,0:T(8,128)S(1)}, u32[]{:S(2)}, u32[]{:S(2)}) collective-permute-start(f32[16,8]{1,0:T(8,128)S(1)} %pad_maximum_fusion), channel_id=1, source_target_pairs={{0,8},{4,12},{8,0},{12,4},{1,9},{5,13},{9,1},{13,5},{2,10},{6,14},... | collective-permute-start | bytes 1544 | tf_op jit(solution)/shard_map/ppermute | solution.py:36
  39.0 0.7 copy-start.6
  41.6 34.0 %collective-permute-start.20 = (bf16[1,264,512]{2,1,0:T(8,128)(2,1)}, bf16[1,264,512]{2,1,0:T(8,128)(2,1)S(1)}, u32[]{:S(2)}, u32[]{:S(2)}) collective-permute-start(bf16[1,264,512]{2,1,0:T(8,128)(2,1)} %combine.28), channel_id=1, source_target_pairs={{0,2},{1,3},{2,0},{3,1},{4,6},{5,7},{6,4},{7,5},{8,10},{9,11},{10,... | collective-permute-start | bytes 811016 | tf_op jit(solution)/shard_map/ppermute | solution.py:36
  44.9 0.7 copy-start.2
  47.5 33.9 %collective-permute-start.15 = (bf16[1,264,512]{2,1,0:T(8,128)(2,1)}, bf16[1,264,512]{2,1,0:T(8,128)(2,1)S(1)}, u32[]{:S(2)}, u32[]{:S(2)}) collective-permute-start(bf16[1,264,512]{2,1,0:T(8,128)(2,1)} %combine.24), channel_id=1, source_target_pairs={{0,2},{1,3},{2,0},{3,1},{4,6},{5,7},{6,4},{7,5},{8,10},{9,11},{10,... | collective-permute-start | bytes 811016 | tf_op jit(solution)/shard_map/ppermute | solution.py:36
  47.5 0.7 copy-start
  50.1 37.1 %collective-permute-start.10 = (bf16[1,264,512]{2,1,0:T(8,128)(2,1)}, bf16[1,264,512]{2,1,0:T(8,128)(2,1)S(1)}, u32[]{:S(2)}, u32[]{:S(2)}) collective-permute-start(bf16[1,264,512]{2,1,0:T(8,128)(2,1)} %combine.20), channel_id=1, source_target_pairs={{0,2},{1,3},{2,0},{3,1},{4,6},{5,7},{6,4},{7,5},{8,10},{9,11},{10,... | collective-permute-start | bytes 811016 | tf_op jit(solution)/shard_map/ppermute | solution.py:36
  53.0 0.7 copy-start.1
  55.6 36.2 %collective-permute-start.5 = (bf16[1,264,512]{2,1,0:T(8,128)(2,1)}, bf16[1,264,512]{2,1,0:T(8,128)(2,1)S(1)}, u32[]{:S(2)}, u32[]{:S(2)}) collective-permute-start(bf16[1,264,512]{2,1,0:T(8,128)(2,1)} %combine.16), channel_id=1, source_target_pairs={{0,2},{1,3},{2,0},{3,1},{4,6},{5,7},{6,4},{7,5},{8,10},{9,11},{10,... | collective-permute-start | bytes 811016 | tf_op jit(solution)/shard_map/ppermute | solution.py:36
  75.6 0.7 copy-start.7
  78.4 16.2 %collective-permute-start.21 = (bf16[1,264,512]{2,1,0:T(8,128)(2,1)}, bf16[1,264,512]{2,1,0:T(8,128)(2,1)S(1)}, u32[]{:S(2)}, u32[]{:S(2)}) collective-permute-start(bf16[1,264,512]{2,1,0:T(8,128)(2,1)} %combine.29), channel_id=1, source_target_pairs={{0,4},{4,0},{8,12},{12,8},{1,5},{5,1},{9,13},{13,9},{2,6},{6,2},{1... | collective-permute-start | bytes 811016 | tf_op jit(solution)/shard_map/ppermute | solution.py:36
  81.4 0.7 copy-start.5
  84.2 16.9 %collective-permute-start.16 = (bf16[1,264,512]{2,1,0:T(8,128)(2,1)}, bf16[1,264,512]{2,1,0:T(8,128)(2,1)S(1)}, u32[]{:S(2)}, u32[]{:S(2)}) collective-permute-start(bf16[1,264,512]{2,1,0:T(8,128)(2,1)} %combine.25), channel_id=1, source_target_pairs={{0,4},{4,0},{8,12},{12,8},{1,5},{5,1},{9,13},{13,9},{2,6},{6,2},{1... | collective-permute-start | bytes 811016 | tf_op jit(solution)/shard_map/ppermute | solution.py:36
  87.2 0.7 copy-start.4
  89.9 15.3 %collective-permute-start.11 = (bf16[1,264,512]{2,1,0:T(8,128)(2,1)}, bf16[1,264,512]{2,1,0:T(8,128)(2,1)S(1)}, u32[]{:S(2)}, u32[]{:S(2)}) collective-permute-start(bf16[1,264,512]{2,1,0:T(8,128)(2,1)} %combine.21), channel_id=1, source_target_pairs={{0,4},{4,0},{8,12},{12,8},{1,5},{5,1},{9,13},{13,9},{2,6},{6,2},{1... | collective-permute-start | bytes 811016 | tf_op jit(solution)/shard_map/ppermute | solution.py:36
  91.8 0.7 copy-start.3
  94.5 14.9 %collective-permute-start.6 = (bf16[1,264,512]{2,1,0:T(8,128)(2,1)}, bf16[1,264,512]{2,1,0:T(8,128)(2,1)S(1)}, u32[]{:S(2)}, u32[]{:S(2)}) collective-permute-start(bf16[1,264,512]{2,1,0:T(8,128)(2,1)} %combine.17), channel_id=1, source_target_pairs={{0,4},{4,0},{8,12},{12,8},{1,5},{5,1},{9,13},{13,9},{2,6},{6,2},{1... | collective-permute-start | bytes 811016 | tf_op jit(solution)/shard_map/ppermute | solution.py:36
  94.5 0.7 copy-start.11
  97.4 16.3 %collective-permute-start.22 = (bf16[1,264,512]{2,1,0:T(8,128)(2,1)}, bf16[1,264,512]{2,1,0:T(8,128)(2,1)S(1)}, u32[]{:S(2)}, u32[]{:S(2)}) collective-permute-start(bf16[1,264,512]{2,1,0:T(8,128)(2,1)} %combine.30), channel_id=1, source_target_pairs={{0,8},{4,12},{1,9},{5,13},{2,10},{6,14},{3,11},{7,15},{16,24},{20,... | collective-permute-start | bytes 811016 | tf_op jit(solution)/shard_map/ppermute | solution.py:36
  101.1 0.7 copy-start.10
  104.0 13.3 %collective-permute-start.17 = (bf16[1,264,512]{2,1,0:T(8,128)(2,1)}, bf16[1,264,512]{2,1,0:T(8,128)(2,1)S(1)}, u32[]{:S(2)}, u32[]{:S(2)}) collective-permute-start(bf16[1,264,512]{2,1,0:T(8,128)(2,1)} %combine.26), channel_id=1, source_target_pairs={{0,8},{4,12},{1,9},{5,13},{2,10},{6,14},{3,11},{7,15},{16,24},{20,... | collective-permute-start | bytes 811016 | tf_op jit(solution)/shard_map/ppermute | solution.py:36
  105.3 0.7 copy-start.9
  108.1 13.4 %collective-permute-start.12 = (bf16[1,264,512]{2,1,0:T(8,128)(2,1)}, bf16[1,264,512]{2,1,0:T(8,128)(2,1)S(1)}, u32[]{:S(2)}, u32[]{:S(2)}) collective-permute-start(bf16[1,264,512]{2,1,0:T(8,128)(2,1)} %combine.22), channel_id=1, source_target_pairs={{0,8},{4,12},{1,9},{5,13},{2,10},{6,14},{3,11},{7,15},{16,24},{20,... | collective-permute-start | bytes 811016 | tf_op jit(solution)/shard_map/ppermute | solution.py:36
  109.4 0.7 copy-start.8
  112.2 12.9 %collective-permute-start.7 = (bf16[1,264,512]{2,1,0:T(8,128)(2,1)}, bf16[1,264,512]{2,1,0:T(8,128)(2,1)S(1)}, u32[]{:S(2)}, u32[]{:S(2)}) collective-permute-start(bf16[1,264,512]{2,1,0:T(8,128)(2,1)} %combine.18), channel_id=1, source_target_pairs={{0,8},{4,12},{1,9},{5,13},{2,10},{6,14},{3,11},{7,15},{16,24},{20,... | collective-permute-start | bytes 811016 | tf_op jit(solution)/shard_map/ppermute | solution.py:36
  113.7 0.7 copy-start.15
  116.6 12.6 %collective-permute-start.23 = (bf16[1,264,512]{2,1,0:T(8,128)(2,1)}, bf16[1,264,512]{2,1,0:T(8,128)(2,1)S(1)}, u32[]{:S(2)}, u32[]{:S(2)}) collective-permute-start(bf16[1,264,512]{2,1,0:T(8,128)(2,1)} %combine.31), channel_id=1, source_target_pairs={{0,1},{1,0},{2,3},{3,2},{4,5},{5,4},{6,7},{7,6},{8,9},{9,8},{10,11... | collective-permute-start | bytes 811016 | tf_op jit(solution)/shard_map/ppermute | solution.py:36
  117.2 0.7 copy-start.14
  120.1 13.9 %collective-permute-start.18 = (bf16[1,264,512]{2,1,0:T(8,128)(2,1)}, bf16[1,264,512]{2,1,0:T(8,128)(2,1)S(1)}, u32[]{:S(2)}, u32[]{:S(2)}) collective-permute-start(bf16[1,264,512]{2,1,0:T(8,128)(2,1)} %combine.27), channel_id=1, source_target_pairs={{0,1},{1,0},{2,3},{3,2},{4,5},{5,4},{6,7},{7,6},{8,9},{9,8},{10,11... | collective-permute-start | bytes 811016 | tf_op jit(solution)/shard_map/ppermute | solution.py:36
  121.5 0.7 copy-start.13
  124.3 14.4 %collective-permute-start.13 = (bf16[1,264,512]{2,1,0:T(8,128)(2,1)}, bf16[1,264,512]{2,1,0:T(8,128)(2,1)S(1)}, u32[]{:S(2)}, u32[]{:S(2)}) collective-permute-start(bf16[1,264,512]{2,1,0:T(8,128)(2,1)} %combine.23), channel_id=1, source_target_pairs={{0,1},{1,0},{2,3},{3,2},{4,5},{5,4},{6,7},{7,6},{8,9},{9,8},{10,11... | collective-permute-start | bytes 811016 | tf_op jit(solution)/shard_map/ppermute | solution.py:36
  125.2 0.7 copy-start.12
  128.0 15.5 %collective-permute-start.8 = (bf16[1,264,512]{2,1,0:T(8,128)(2,1)}, bf16[1,264,512]{2,1,0:T(8,128)(2,1)S(1)}, u32[]{:S(2)}, u32[]{:S(2)}) collective-permute-start(bf16[1,264,512]{2,1,0:T(8,128)(2,1)} %combine.19), channel_id=1, source_target_pairs={{0,1},{1,0},{2,3},{3,2},{4,5},{5,4},{6,7},{7,6},{8,9},{9,8},{10,11... | collective-permute-start | bytes 811016 | tf_op jit(solution)/shard_map/ppermute | solution.py:36
  129.2 0.7 copy-start.19
  134.0 0.7 copy-start.18
  138.7 0.7 copy-start.17
  143.5 0.7 copy-start.16

commit v2 on v1

v2 whole, which is shorter than its diff:
```python
import functools
import math

import jax
import jax.numpy as jnp
from jax import lax
from jax.experimental import pallas as pl
from jax.experimental.pallas import tpu as pltpu
from jax.sharding import PartitionSpec as P

DK = 256
DV = 512
CH = 256
BLK = 128
NEG_FILL = -1e30
TAIL = 8
ROWS = DK + TAIL
CHUNKS = (1, 1, 1, 1)

F32 = jnp.float32
BF16 = jnp.bfloat16


def sizes(mesh):
    ctx, head = mesh.shape["ctx"], mesh.shape["head"]
    head_bits, ctx_bits = head.bit_length() - 1, ctx.bit_length() - 1
    assert head == 1 << head_bits and ctx == 1 << ctx_bits and head_bits >= 1
    return head_bits, ctx_bits


def flip(x, bit, head_bits, ctx_bits, last):
    axis, size, b = (
        ("head", 1 << head_bits, bit) if bit < head_bits else ("ctx", 1 << ctx_bits, bit - head_bits)
    )
    pairs = [(i, i ^ (1 << b)) for i in range(size) if not (last and i & (1 << b))]
    return lax.ppermute(x, axis, pairs)


def gate_kernel(i_ref, f_ref, run_ref, weight_ref, shift_ref, mf_ref):
    gate, x = i_ref[...], f_ref[...].astype(F32)
    log_forget = jnp.minimum(x, 0.0) - jnp.log1p(jnp.exp(-jnp.abs(x)))
    size = x.shape[1]
    row = lax.broadcasted_iota(jnp.int32, (size, size), 0)
    col = lax.broadcasted_iota(jnp.int32, (size, size), 1)
    before = jnp.where(row >= col, 1.0, 0.0).astype(F32)
    same = jnp.where(row == col, 1.0, 0.0).astype(BF16)
    exact = dict(precision=lax.Precision.HIGHEST, preferred_element_type=F32)
    across = (((1,), (1,)), ((), ()))
    running_row = lax.dot_general(log_forget, before, across, **exact)
    running = lax.dot_general(before, log_forget, across, **exact)
    gate_col = lax.dot_general(same, gate, across, preferred_element_type=F32)
    total = running[size - 1 : size, :]
    exponent = total - running + gate_col
    peak = jnp.max(exponent, axis=0, keepdims=True)
    run_ref[...] = running
    weight_ref[...] = jnp.exp(exponent - peak)
    shift_ref[...] = gate.astype(F32) - running_row
    mf_ref[...] = jnp.concatenate([peak, total], axis=0)


def gates(input_gate, forget_gate):
    heads, size = input_gate.shape
    col = jax.ShapeDtypeStruct((size, heads), F32)
    row = jax.ShapeDtypeStruct((heads, size), F32)
    return pl.pallas_call(
        gate_kernel,
        out_shape=(col, col, row, jax.ShapeDtypeStruct((2, heads), F32)),
        compiler_params=pltpu.CompilerParams(vmem_limit_bytes=4 << 20),
        cost_estimate=pl.CostEstimate(flops=1 << 20, bytes_accessed=1 << 20, transcendentals=0),
        name="gates",
    )(input_gate, forget_gate)


def pick(ref, h):
    x = ref[...]
    lane = lax.broadcasted_iota(jnp.int32, x.shape, 1)
    return jnp.sum(jnp.where(lane == h, x, 0.0), axis=1, keepdims=True)


def dequant(ref, at, width, tensor_id, h, scales, tensors, offsets, bits):
    rows = ref.shape[0]
    row = lax.broadcasted_iota(jnp.int32, (BLK, 1), 0)
    col = lax.broadcasted_iota(jnp.int32, (1, width), 1)
    out = []
    for b in range(rows // BLK):
        x = ref[b * BLK : (b + 1) * BLK, pl.ds(at, width)].astype(F32)
        offset, scale = offsets[b, h], scales[tensor_id, b, h]
        hit_row = jnp.where(tensors[b, h] == tensor_id, offset // DV, -1)
        hit_col = (offset % DV) % width
        flipped = -(lax.shift_left(jnp.int32(1), bits[b, h]).astype(F32)) * scale
        out.append((x * jnp.where((row == hit_row) & (col == hit_col), flipped, scale)).astype(BF16))
    return jnp.concatenate(out, axis=0)


def split(x):
    high = x.astype(BF16).astype(F32)
    middle = (x - high).astype(BF16).astype(F32)
    return high, middle, x - high - middle


def pack_tail(normer, peak, total):
    high, middle, least = split(normer)
    rows = [jnp.concatenate([high, middle], axis=1), jnp.concatenate([least, jnp.zeros_like(least)], axis=1)]
    rows += [*split(peak), *split(total)]
    at = lax.broadcasted_iota(jnp.int32, (TAIL, DV), 0)
    out = jnp.zeros((TAIL, DV), F32)
    for r, value in enumerate(rows):
        out = jnp.where(at == r, value, out)
    return out.astype(BF16)


class State:
    def __init__(self, ref, i):
        self.ref, self.i = ref, i
        t = ref[i, DK:ROWS, :].astype(F32)
        self.normer = t[0:1, :DK] + t[0:1, DK : 2 * DK] + t[1:2, :DK]
        self.peak = t[2:3] + t[3:4] + t[4:5]
        self.total = t[5:6] + t[6:7] + t[7:8]

    def matrix(self):
        return self.ref[self.i, :DK, :]


def joined(early, late):
    peak = jnp.maximum(early[0] + late[1], late[0])
    return peak, early[1] + late[1], jnp.exp(early[0] + late[1] - peak), jnp.exp(late[0] - peak)


def group_weights(bit, own, got):
    peak, total, weights = own.peak, own.total, [jnp.ones_like(own.peak)]
    for b, peer in enumerate(got):
        low = joined((peak, total), (peer.peak, peer.total))
        high = joined((peer.peak, peer.total), (peak, total))
        peak, total = jnp.where(bit[b], high[0], low[0]), low[1]
        here, there = jnp.where(bit[b], high[3], low[2]), jnp.where(bit[b], high[2], low[3])
        weights = [w * here for w in weights] + [there]
    return weights, peak, total


def start_weights(bit, include, own, got):
    peak, total, weights = None, None, []
    one = jnp.ones_like(got[-1].peak)
    peak, total = one * NEG_FILL, one * 0.0
    if own is not None:
        peak, total = jnp.where(include, own.peak, peak), jnp.where(include, own.total, total)
        weights = [jnp.where(include, one, 0.0)]
    for b, peer in zip(range(len(bit) - len(got), len(bit)), got):
        new = joined((peer.peak, peer.total), (peak, total))
        weights = [w * jnp.where(bit[b], new[3], 1.0) for w in weights] + [jnp.where(bit[b], new[2], 0.0)]
        peak, total = jnp.where(bit[b], new[0], peak), jnp.where(bit[b], new[1], total)
    return weights, peak, total


def weighted_sum(weights, states):
    matrix, normer = None, None
    for w, state in zip(weights, states):
        term, tail = state.matrix().astype(F32) * w, state.normer * w[:, :DK]
        matrix = term if matrix is None else matrix + term
        normer = tail if normer is None else normer + tail
    return matrix, normer


def device_bits(head_bits, bits):
    me = lax.axis_index("ctx") * (1 << head_bits) + lax.axis_index("head")
    return [((me >> b) & 1) == 1 for b in range(bits)]


SMEM = pl.BlockSpec(memory_space=pltpu.SMEM)
VMEM = pl.BlockSpec(memory_space=pltpu.VMEM)


def state_kernel(first, scales, tensors, offsets, fbits, mf, weight_ref, k_ref, v_ref, keep_ref, send_ref):
    own = lax.axis_index("head") & 1
    i = pl.program_id(0)
    for out_ref, side in ((send_ref, 1 - own), (keep_ref, own)):
        h = 2 * (first + i) + side
        info = (h, scales, tensors, offsets, fbits)
        k = dequant(k_ref, pl.multiple_of(side * DK, DK), DK, 1, *info)
        v = dequant(v_ref, pl.multiple_of(side * DV, DV), DV, 2, *info)
        weighted = (k.astype(F32) * pick(weight_ref, h)).astype(BF16)
        matrix = lax.dot_general(weighted, v, (((0,), (0,)), ((), ())), preferred_element_type=F32)
        out_ref[0, :DK, :] = matrix.astype(BF16)
        normer = jnp.sum(weighted.astype(F32), axis=0, keepdims=True)
        out_ref[0, DK:ROWS, :] = pack_tail(normer, jnp.full((1, DV), mf[0, h], F32), jnp.full((1, DV), mf[1, h], F32))


def whole(shape):
    return pl.BlockSpec(shape, lambda i: (0,) * len(shape))


STATE = pl.BlockSpec((1, ROWS, DV), lambda i: (i, 0, 0))


def span_states(first, count, small, mf, weight, key_codes, value_codes):
    rows = key_codes.shape[0]
    out = jax.ShapeDtypeStruct((count, ROWS, DV), BF16)
    return pl.pallas_call(
        functools.partial(state_kernel, first),
        grid=(count,),
        in_specs=[SMEM] * 5
        + [
            whole(weight.shape),
            pl.BlockSpec((rows, 2 * DK), lambda i: (0, first + i)),
            pl.BlockSpec((rows, 2 * DV), lambda i: (0, first + i)),
        ],
        out_specs=(STATE, STATE),
        out_shape=(out, out),
        compiler_params=pltpu.CompilerParams(vmem_limit_bytes=12 << 20),
        cost_estimate=pl.CostEstimate(
            flops=count * 4 * rows * DK * DV, bytes_accessed=count * rows * 2 * (2 * DK + 4 * DV), transcendentals=0
        ),
        name="span_states",
    )(*small, mf, weight, key_codes, value_codes)


def combine_kernel(head_bits, bits, last, *refs):
    parts, out_ref = refs[:-1], refs[-1]
    bit = device_bits(head_bits, bits)
    for i in range(out_ref.shape[0]):
        states = [State(ref, i) for ref in parts]
        if last:
            weights, peak, total = start_weights(bit, jnp.logical_not(bit[0]), states[0], states[1:])
        else:
            weights, peak, total = group_weights(bit, states[0], states[1:])
        matrix, normer = weighted_sum(weights, states)
        out_ref[i, :DK, :] = matrix.astype(BF16)
        out_ref[i, DK:ROWS, :] = pack_tail(normer, peak, total)


def combine(head_bits, bits, last, parts):
    count = parts[0].shape[0]
    return pl.pallas_call(
        functools.partial(combine_kernel, head_bits, bits, last),
        in_specs=[VMEM] * len(parts),
        out_specs=VMEM,
        out_shape=jax.ShapeDtypeStruct((count, ROWS, DV), BF16),
        compiler_params=pltpu.CompilerParams(vmem_limit_bytes=8 << 20),
        cost_estimate=pl.CostEstimate(
            flops=count * ROWS * DV * 2 * len(parts), bytes_accessed=count * ROWS * DV * 2 * (len(parts) + 1), transcendentals=0
        ),
        name="combine",
    )(*parts)


def output_kernel(
    head_bits, bits, first, scales, tensors, offsets, fbits, run_ref, shift_ref, q_ref, k_ref, v_ref, back_ref, *rest
):
    parts, out_ref = rest[:bits], rest[-1]
    bit = device_bits(head_bits, bits)
    own = lax.axis_index("head") & 1
    i = pl.program_id(0)
    factor = 1.0 / math.sqrt(DK)
    size = q_ref.shape[0]
    row = lax.broadcasted_iota(jnp.int32, (size, size), 0)
    col = lax.broadcasted_iota(jnp.int32, (size, size), 1)
    for side, mine in ((own, True), (1 - own, False)):
        h = 2 * (first + i) + side
        info = (h, scales, tensors, offsets, fbits)
        if mine:
            states = [State(ref, 0) for ref in parts]
            weights, peak, _ = start_weights(bit, None, None, states)
            start, normer = weighted_sum(weights, states)
            start = start.astype(BF16)
        else:
            back = State(back_ref, 0)
            start, normer, peak = back.matrix(), back.normer, back.peak
        narrow, wide = pl.multiple_of(side * DK, DK), pl.multiple_of(side * DV, DV)
        q = dequant(q_ref, narrow, DK, 0, *info)
        k = dequant(k_ref, narrow, DK, 1, *info)
        v = dequant(v_ref, wide, DV, 2, *info)
        run = pick(run_ref, h)
        exponent = jnp.where(row >= col, run + shift_ref[pl.ds(h, 1), :], NEG_FILL)
        inter = run + peak[:, :1]
        row_peak = jnp.maximum(jnp.max(exponent, axis=1, keepdims=True), inter)
        decay = jnp.exp(exponent - row_peak)
        scores = lax.dot_general(q, k, (((1,), (1,)), ((), ())), preferred_element_type=F32) * factor
        product = decay * scores
        lifted = (q.astype(F32) * (factor * jnp.exp(inter - row_peak))).astype(BF16)
        numerator = jnp.dot(product.astype(BF16), v, preferred_element_type=F32)
        numerator = numerator + jnp.dot(lifted, start, preferred_element_type=F32)
        denominator = jnp.sum(product, axis=1, keepdims=True) + jnp.sum(
            lifted.astype(F32) * normer, axis=1, keepdims=True
        )
        out_ref[:, pl.ds(wide, DV)] = (numerator / jnp.maximum(jnp.abs(denominator), 1.0)).astype(BF16)


def span_outputs(head_bits, bits, first, small, run, shift, codes, back, parts, before):
    q, k, v = codes
    count, rows = back.shape[0], q.shape[0]
    narrow = pl.BlockSpec((rows, 2 * DK), lambda i: (0, first + i))
    wide = pl.BlockSpec((rows, 2 * DV), lambda i: (0, first + i))
    operands = [*small, run, shift, q, k, v, back, *parts]
    in_specs = [SMEM] * 4 + [whole(run.shape), whole(shift.shape)] + [narrow, narrow, wide, STATE] + [STATE] * len(parts)
    aliases = {}
    if before is not None:
        aliases = {len(operands): 0}
        operands.append(before)
        in_specs.append(pl.BlockSpec(memory_space=pl.ANY))
    return pl.pallas_call(
        functools.partial(output_kernel, head_bits, bits, first),
        grid=(count,),
        in_specs=in_specs,
        out_specs=wide,
        out_shape=jax.ShapeDtypeStruct(v.shape, BF16),
        input_output_aliases=aliases,
        compiler_params=pltpu.CompilerParams(vmem_limit_bytes=16 << 20),
        cost_estimate=pl.CostEstimate(
            flops=count * 4 * rows * (rows * DK + rows * DV + DK * DV),
            bytes_accessed=count * (rows * 2 * (4 * DK + 4 * DV) + ROWS * DV * 2 * (1 + len(parts))),
            transcendentals=count * 2 * rows * rows,
        ),
        name="span_outputs",
    )(*operands)


def body(
    head_bits,
    ctx_bits,
    query_codes,
    key_codes,
    value_codes,
    block_scales,
    fault_tensor,
    fault_offset,
    fault_bit,
    input_gate,
    forget_gate,
):
    bits = head_bits + ctx_bits
    assert query_codes.shape[0] == CH
    small = (block_scales.transpose(1, 0, 2), fault_tensor, fault_offset, fault_bit)
    codes = (query_codes, key_codes, value_codes)
    exchange = functools.partial(flip, head_bits=head_bits, ctx_bits=ctx_bits)
    run, weight, shift, mf = gates(input_gate.T, forget_gate.T)

    starts = [sum(CHUNKS[:c]) for c in range(len(CHUNKS))]
    assert 2 * sum(CHUNKS) == input_gate.shape[1]
    out = None
    for first, count in zip(starts, CHUNKS):
        keep, send = span_states(first, count, small, mf, weight, key_codes, value_codes)
        got = [exchange(send, 0, last=False)]
        for b in range(1, bits):
            group = combine(head_bits, bits, False, [keep, *got])
            got.append(exchange(group, b, last=b == bits - 1))
        back = exchange(combine(head_bits, bits, True, [keep, *got[1:]]), 0, last=False)
        out = span_outputs(head_bits, bits, first, small, run, shift, codes, back, got, out)
    return out


def solution(mesh):
    rows = P(("grp", "ctx", "head"), None)
    placed = (rows, rows, rows, P(("grp", "ctx", "head"), None, None)) + (rows,) * 5
    return jax.shard_map(
        functools.partial(body, *sizes(mesh)), mesh=mesh, in_specs=placed, out_specs=rows, check_vma=False
    )
```

time: 149 us -> 113 us (0.76)
  Pallas kernels: 63.4 us -> 19.4 us
  waiting for transfers between devices: 35 us -> 64.7 us
  local copies, waits for them, and re-layouts: 20.1 us -> 6.94 us
  starting transfers between devices: 29.6 us -> 21.3 us
    pallas_call x22 -> x21, Pallas kernels: 52.3 us -> 14.5 us  [the longest x4 10.4 us: span_outputs(): pl.pallas_call(functools.partial(output_kernel, head_bits, bits, first),...]
    ppermute x24 -> x20, waiting for transfers between devices: 35 us -> 64.7 us  [flip(): return lax.ppermute(x, axis, pairs)]
    unnamed x45 -> x30, local copies, waits for them, and re-layouts: 18.3 us -> 6.94 us
    ppermute x24 -> x20, starting transfers between devices: 29.6 us -> 21.3 us  [flip(): return lax.ppermute(x, axis, pairs)]
    pallas_call x4, Pallas kernels: 11 us -> 4.9 us  [span_states(): pl.pallas_call(functools.partial(state_kernel, first), grid=(count,), in_...]
    concatenate x1 -> x0, local copies, waits for them, and re-layouts: 1.8 us -> none  [body(): table = jnp.concatenate([table, exchange(table, b, last=False)], axis=0)]
  transfers between devices with their start and end apart: 24 -> 20, of which waited for: 8 -> 11; matrix products, arithmetic and copies ran while one was open for 2% -> 0% of each run, Pallas kernels for 39% -> 13%
where the time goes in v2:
time: 113 us
  waiting for transfers between devices  64.7 us (57%)
  starting transfers between devices  21.3 us (19%)
  Pallas kernels  19.4 us (17%)
  local copies, waits for them, and re-layouts  6.94 us (6%)
    ppermute x20, waiting for transfers between devices, flip(): return lax.ppermute(x, axis, pairs)  64.7 us
    ppermute x20, starting transfers between devices, flip(): return lax.ppermute(x, axis, pairs)  21.3 us
    pallas_call x4, Pallas kernels, span_outputs(): pl.pallas_call(functools.partial(output_kernel, head_bits, bits, first),...  10.4 us
    unnamed x30, local copies, waits for them, and re-layouts  6.94 us
    pallas_call x4, Pallas kernels, span_states(): pl.pallas_call(functools.partial(state_kernel, first), grid=(count,), in_...  4.9 us
    pallas_call x16, Pallas kernels, combine(): pl.pallas_call(functools.partial(combine_kernel, head_bits, bits, last),...  3.53 us
  transfers between devices with their start and end apart: 20, of which 11 were waited for; matrix products, arithmetic and copies ran while one was open for 0% of the time, Pallas kernels for 13%

profile of v2, /device:TPU:0, one launch (start us, length us, event | category | flops | bytes accessed | tf_op | source)
XLA Modules:
  0.0 112.7 jit_solution(11482061898291607808)
XLA Ops:
  0.0 0.7 copy-done.13
  0.7 0.7 copy-done.14
  1.4 0.6 gates.1
  2.0 1.6 %copy-done = bf16[256,4096]{1,0:T(8,128)(2,1)S(1)} copy-done((bf16[256,4096]{1,0:T(8,128)(2,1)S(1)}, bf16[256,4096]{1,0:T(8,128)(2,1)}, u32[]{:S(2)}) %copy-start) | copy-done | bytes 2097176
  3.6 1.2 %copy-done.2 = bf16[256,2048]{1,0:T(8,128)(2,1)S(1)} copy-done((bf16[256,2048]{1,0:T(8,128)(2,1)S(1)}, bf16[256,2048]{1,0:T(8,128)(2,1)}, u32[]{:S(2)}) %copy-start.2) | copy-done | bytes 1048600
  4.8 0.7 copy-done.5
  5.5 0.7 copy-done.7
  6.2 0.7 copy-done.9
  6.9 0.7 copy-done.11
  7.5 1.2 %span_states.7 = (bf16[1,264,512]{2,1,0:T(8,128)(2,1)S(1)}, bf16[1,264,512]{2,1,0:T(8,128)(2,1)S(1)}) custom-call(f32[3,2,8]{2,1,0:T(2,128)S(1)} %bitcast.3, s32[2,8]{1,0:T(2,128)S(1)} %copy-done.7, s32[2,8]{1,0:T(2,128)S(1)} %copy-done.9, s32[2,8]{1,0:T(2,128)S(1)} %copy-done.11, f32[2,8]{1,0:T(2,128)S(1)} %get-tuple-element.19.mf, ...), custom_call_target="tpu_custom_call" | custom-call | flops 134217728 | bytes 1310720 | tf_op jit(solution)/shard_map/span_states/pallas_call | solution.py:197
  8.8 3.1 %collective-permute-start.15 = (bf16[1,264,512]{2,1,0:T(8,128)(2,1)S(1)}, bf16[1,264,512]{2,1,0:T(8,128)(2,1)S(1)}, u32[]{:S(2)}, u32[]{:S(2)}) collective-permute-start(bf16[1,264,512]{2,1,0:T(8,128)(2,1)S(1)} %get-tuple-element.28), channel_id=1, source_target_pairs={{0,1},{1,0},{2,3},{3,2},{4,5},{5,4},{6,7},{7,6},{8,9},{9,8},{10,11... | collective-permute-start | bytes 811016 | tf_op jit(solution)/shard_map/ppermute | solution.py:36
  11.9 1.2 %span_states.6 = (bf16[1,264,512]{2,1,0:T(8,128)(2,1)S(1)}, bf16[1,264,512]{2,1,0:T(8,128)(2,1)S(1)}) custom-call(f32[3,2,8]{2,1,0:T(2,128)S(1)} %bitcast.4, s32[2,8]{1,0:T(2,128)S(1)} %copy-done.7, s32[2,8]{1,0:T(2,128)S(1)} %copy-done.9, s32[2,8]{1,0:T(2,128)S(1)} %copy-done.11, f32[2,8]{1,0:T(2,128)S(1)} %get-tuple-element.19.mf, ...), custom_call_target="tpu_custom_call" | custom-call | flops 134217728 | bytes 1310720 | tf_op jit(solution)/shard_map/span_states/pallas_call | solution.py:197
  13.2 1.2 %span_states.5 = (bf16[1,264,512]{2,1,0:T(8,128)(2,1)S(1)}, bf16[1,264,512]{2,1,0:T(8,128)(2,1)S(1)}) custom-call(f32[3,2,8]{2,1,0:T(2,128)S(1)} %bitcast.5, s32[2,8]{1,0:T(2,128)S(1)} %copy-done.7, s32[2,8]{1,0:T(2,128)S(1)} %copy-done.9, s32[2,8]{1,0:T(2,128)S(1)} %copy-done.11, f32[2,8]{1,0:T(2,128)S(1)} %get-tuple-element.19.mf, ...), custom_call_target="tpu_custom_call" | custom-call | flops 134217728 | bytes 1310720 | tf_op jit(solution)/shard_map/span_states/pallas_call | solution.py:197
  14.4 2.1 %collective-permute-start.5 = (bf16[1,264,512]{2,1,0:T(8,128)(2,1)S(1)}, bf16[1,264,512]{2,1,0:T(8,128)(2,1)S(1)}, u32[]{:S(2)}, u32[]{:S(2)}) collective-permute-start(bf16[1,264,512]{2,1,0:T(8,128)(2,1)S(1)} %get-tuple-element.24), channel_id=1, source_target_pairs={{0,1},{1,0},{2,3},{3,2},{4,5},{5,4},{6,7},{7,6},{8,9},{9,8},{10,11... | collective-permute-start | bytes 811016 | tf_op jit(solution)/shard_map/ppermute | solution.py:36
  16.5 1.2 %span_states.4 = (bf16[1,264,512]{2,1,0:T(8,128)(2,1)S(1)}, bf16[1,264,512]{2,1,0:T(8,128)(2,1)S(1)}) custom-call(f32[3,2,8]{2,1,0:T(2,128)S(1)} %bitcast.6, s32[2,8]{1,0:T(2,128)S(1)} %copy-done.7, s32[2,8]{1,0:T(2,128)S(1)} %copy-done.9, s32[2,8]{1,0:T(2,128)S(1)} %copy-done.11, f32[2,8]{1,0:T(2,128)S(1)} %get-tuple-element.19.mf, ...), custom_call_target="tpu_custom_call" | custom-call | flops 134217728 | bytes 1310720 | tf_op jit(solution)/shard_map/span_states/pallas_call | solution.py:197
  17.8 1.4 %collective-permute-done.15.refs_1_.rest_0_ = bf16[1,264,512]{2,1,0:T(8,128)(2,1)S(1)} collective-permute-done((bf16[1,264,512]{2,1,0:T(8,128)(2,1)S(1)}, bf16[1,264,512]{2,1,0:T(8,128)(2,1)S(1)}, u32[]{:S(2)}, u32[]{:S(2)}) %collective-permute-start.15) | collective-permute-done | bytes 270368 | tf_op jit(solution)/shard_map/ppermute | solution.py:36
  19.4 3.1 %collective-permute-start.16 = (bf16[1,264,512]{2,1,0:T(8,128)(2,1)S(1)}, bf16[1,264,512]{2,1,0:T(8,128)(2,1)S(1)}, u32[]{:S(2)}, u32[]{:S(2)}) collective-permute-start(bf16[1,264,512]{2,1,0:T(8,128)(2,1)S(1)} %combine.28), channel_id=1, source_target_pairs={{0,2},{1,3},{2,0},{3,1},{4,6},{5,7},{6,4},{7,5},{8,10},{9,11},{10,... | collective-permute-start | bytes 811016 | tf_op jit(solution)/shard_map/ppermute | solution.py:36
  22.5 8.4 %collective-permute-done.10.refs_1_.rest_0_ = bf16[1,264,512]{2,1,0:T(8,128)(2,1)S(1)} collective-permute-done((bf16[1,264,512]{2,1,0:T(8,128)(2,1)S(1)}, bf16[1,264,512]{2,1,0:T(8,128)(2,1)S(1)}, u32[]{:S(2)}, u32[]{:S(2)}) %collective-permute-start.10) | collective-permute-done | bytes 270368 | tf_op jit(solution)/shard_map/ppermute | solution.py:36
  31.0 2.2 %collective-permute-start.11 = (bf16[1,264,512]{2,1,0:T(8,128)(2,1)S(1)}, bf16[1,264,512]{2,1,0:T(8,128)(2,1)S(1)}, u32[]{:S(2)}, u32[]{:S(2)}) collective-permute-start(bf16[1,264,512]{2,1,0:T(8,128)(2,1)S(1)} %combine.24), channel_id=1, source_target_pairs={{0,2},{1,3},{2,0},{3,1},{4,6},{5,7},{6,4},{7,5},{8,10},{9,11},{10,... | collective-permute-start | bytes 811016 | tf_op jit(solution)/shard_map/ppermute | solution.py:36
  33.1 8.5 %collective-permute-done.5.refs_1_.rest_0_ = bf16[1,264,512]{2,1,0:T(8,128)(2,1)S(1)} collective-permute-done((bf16[1,264,512]{2,1,0:T(8,128)(2,1)S(1)}, bf16[1,264,512]{2,1,0:T(8,128)(2,1)S(1)}, u32[]{:S(2)}, u32[]{:S(2)}) %collective-permute-start.5) | collective-permute-done | bytes 270368 | tf_op jit(solution)/shard_map/ppermute | solution.py:36
  41.9 4.7 %collective-permute-done.refs_1_.rest_0_ = bf16[1,264,512]{2,1,0:T(8,128)(2,1)S(1)} collective-permute-done((bf16[1,264,512]{2,1,0:T(8,128)(2,1)S(1)}, bf16[1,264,512]{2,1,0:T(8,128)(2,1)S(1)}, u32[]{:S(2)}, u32[]{:S(2)}) %collective-permute-start) | collective-permute-done | bytes 270368 | tf_op jit(solution)/shard_map/ppermute | solution.py:36
  47.2 15.5 %collective-permute-done.11.refs_2_.refs_1_.rest_1_ = bf16[1,264,512]{2,1,0:T(8,128)(2,1)S(1)} collective-permute-done((bf16[1,264,512]{2,1,0:T(8,128)(2,1)S(1)}, bf16[1,264,512]{2,1,0:T(8,128)(2,1)S(1)}, u32[]{:S(2)}, u32[]{:S(2)}) %collective-permute-start.11) | collective-permute-done | bytes 270368 | tf_op jit(solution)/shard_map/ppermute | solution.py:36
  62.9 5.5 %collective-permute-done.6.refs_2_.refs_1_.rest_1_ = bf16[1,264,512]{2,1,0:T(8,128)(2,1)S(1)} collective-permute-done((bf16[1,264,512]{2,1,0:T(8,128)(2,1)S(1)}, bf16[1,264,512]{2,1,0:T(8,128)(2,1)S(1)}, u32[]{:S(2)}, u32[]{:S(2)}) %collective-permute-start.6) | collective-permute-done | bytes 270368 | tf_op jit(solution)/shard_map/ppermute | solution.py:36
  68.7 4.8 %collective-permute-done.1.refs_2_.refs_1_.rest_1_ = bf16[1,264,512]{2,1,0:T(8,128)(2,1)S(1)} collective-permute-done((bf16[1,264,512]{2,1,0:T(8,128)(2,1)S(1)}, bf16[1,264,512]{2,1,0:T(8,128)(2,1)S(1)}, u32[]{:S(2)}, u32[]{:S(2)}) %collective-permute-start.1) | collective-permute-done | bytes 270368 | tf_op jit(solution)/shard_map/ppermute | solution.py:36
  73.8 0.3 combine.30
  74.1 3.5 %collective-permute-start.18 = (bf16[1,264,512]{2,1,0:T(8,128)(2,1)S(1)}, bf16[1,264,512]{2,1,0:T(8,128)(2,1)S(1)}, u32[]{:S(2)}, u32[]{:S(2)}) collective-permute-start(bf16[1,264,512]{2,1,0:T(8,128)(2,1)S(1)} %combine.30), channel_id=1, source_target_pairs={{0,8},{4,12},{1,9},{5,13},{2,10},{6,14},{3,11},{7,15},{16,24},{20,... | collective-permute-start | bytes 811016 | tf_op jit(solution)/shard_map/ppermute | solution.py:36
  77.6 0.3 combine.26
  77.9 1.3 %collective-permute-start.13 = (bf16[1,264,512]{2,1,0:T(8,128)(2,1)S(1)}, bf16[1,264,512]{2,1,0:T(8,128)(2,1)S(1)}, u32[]{:S(2)}, u32[]{:S(2)}) collective-permute-start(bf16[1,264,512]{2,1,0:T(8,128)(2,1)S(1)} %combine.26), channel_id=1, source_target_pairs={{0,8},{4,12},{1,9},{5,13},{2,10},{6,14},{3,11},{7,15},{16,24},{20,... | collective-permute-start | bytes 811016 | tf_op jit(solution)/shard_map/ppermute | solution.py:36
  79.2 0.3 combine.22
  79.5 1.3 %collective-permute-start.8 = (bf16[1,264,512]{2,1,0:T(8,128)(2,1)S(1)}, bf16[1,264,512]{2,1,0:T(8,128)(2,1)S(1)}, u32[]{:S(2)}, u32[]{:S(2)}) collective-permute-start(bf16[1,264,512]{2,1,0:T(8,128)(2,1)S(1)} %combine.22), channel_id=1, source_target_pairs={{0,8},{4,12},{1,9},{5,13},{2,10},{6,14},{3,11},{7,15},{16,24},{20,... | collective-permute-start | bytes 811016 | tf_op jit(solution)/shard_map/ppermute | solution.py:36
  80.8 0.3 combine.18
  81.1 1.5 %collective-permute-start.3 = (bf16[1,264,512]{2,1,0:T(8,128)(2,1)S(1)}, bf16[1,264,512]{2,1,0:T(8,128)(2,1)S(1)}, u32[]{:S(2)}, u32[]{:S(2)}) collective-permute-start(bf16[1,264,512]{2,1,0:T(8,128)(2,1)S(1)} %combine.18), channel_id=1, source_target_pairs={{0,8},{4,12},{1,9},{5,13},{2,10},{6,14},{3,11},{7,15},{16,24},{20,... | collective-permute-start | bytes 811016 | tf_op jit(solution)/shard_map/ppermute | solution.py:36
  82.6 1.8 %collective-permute-done.18.refs_3_.rest_3_ = bf16[1,264,512]{2,1,0:T(8,128)(2,1)S(1)} collective-permute-done((bf16[1,264,512]{2,1,0:T(8,128)(2,1)S(1)}, bf16[1,264,512]{2,1,0:T(8,128)(2,1)S(1)}, u32[]{:S(2)}, u32[]{:S(2)}) %collective-permute-start.18) | collective-permute-done | bytes 270368 | tf_op jit(solution)/shard_map/ppermute | solution.py:36
  84.4 0.3 combine.31
  84.8 0.7 collective-permute-start.19
  85.4 4.8 %collective-permute-done.13.refs_3_.rest_3_ = bf16[1,264,512]{2,1,0:T(8,128)(2,1)S(1)} collective-permute-done((bf16[1,264,512]{2,1,0:T(8,128)(2,1)S(1)}, bf16[1,264,512]{2,1,0:T(8,128)(2,1)S(1)}, u32[]{:S(2)}, u32[]{:S(2)}) %collective-permute-start.13) | collective-permute-done | bytes 270368 | tf_op jit(solution)/shard_map/ppermute | solution.py:36
  90.2 0.3 combine.27
  90.5 0.7 collective-permute-start.14
  91.1 4.9 %collective-permute-done.8.refs_3_.rest_3_ = bf16[1,264,512]{2,1,0:T(8,128)(2,1)S(1)} collective-permute-done((bf16[1,264,512]{2,1,0:T(8,128)(2,1)S(1)}, bf16[1,264,512]{2,1,0:T(8,128)(2,1)S(1)}, u32[]{:S(2)}, u32[]{:S(2)}) %collective-permute-start.8) | collective-permute-done | bytes 270368 | tf_op jit(solution)/shard_map/ppermute | solution.py:36
  96.0 0.3 combine.23
  96.3 0.7 collective-permute-start.9
  96.9 4.4 %collective-permute-done.3.refs_3_.rest_3_ = bf16[1,264,512]{2,1,0:T(8,128)(2,1)S(1)} collective-permute-done((bf16[1,264,512]{2,1,0:T(8,128)(2,1)S(1)}, bf16[1,264,512]{2,1,0:T(8,128)(2,1)S(1)}, u32[]{:S(2)}, u32[]{:S(2)}) %collective-permute-start.3) | collective-permute-done | bytes 270368 | tf_op jit(solution)/shard_map/ppermute | solution.py:36
  101.3 0.3 combine.19
  101.6 0.7 collective-permute-start.4
  102.3 2.6 %span_outputs.4.rest_4_ = bf16[256,4096]{1,0:T(8,128)(2,1)} custom-call(f32[3,2,8]{2,1,0:T(2,128)S(1)} %bitcast.7, s32[2,8]{1,0:T(2,128)S(1)} %copy-done.8, s32[2,8]{1,0:T(2,128)S(1)} %copy-done.10, s32[2,8]{1,0:T(2,128)S(1)} %copy-done.12, f32[256,8]{1,0:T(8,128)S(1)} %get-tuple-element.17.run_ref, f32[8,256]{1,0:T(8,128)S(1)} %get-tuple-element.18.shift_ref, ...), custom_call_target="tpu_custom_call" | custom-call | flops 335544320 | bytes 2924544 | tf_op jit(solution)/shard_map/span_outputs/pallas_call | solution.py:299
  104.9 2.6 %span_outputs.5.rest_4_ = bf16[256,4096]{1,0:T(8,128)(2,1)} custom-call(f32[3,2,8]{2,1,0:T(2,128)S(1)} %bitcast.8, s32[2,8]{1,0:T(2,128)S(1)} %copy-done.8, s32[2,8]{1,0:T(2,128)S(1)} %copy-done.10, s32[2,8]{1,0:T(2,128)S(1)} %copy-done.12, f32[256,8]{1,0:T(8,128)S(1)} %get-tuple-element.17.run_ref, ...), custom_call_target="tpu_custom_call", output_to_operand_aliasing={{}: (14, {})} | custom-call | flops 335544320 | bytes 2924544 | tf_op jit(solution)/shard_map/span_outputs/pallas_call | solution.py:299
  107.5 2.6 %span_outputs.6.rest_4_ = bf16[256,4096]{1,0:T(8,128)(2,1)} custom-call(f32[3,2,8]{2,1,0:T(2,128)S(1)} %bitcast.9, s32[2,8]{1,0:T(2,128)S(1)} %copy-done.8, s32[2,8]{1,0:T(2,128)S(1)} %copy-done.10, s32[2,8]{1,0:T(2,128)S(1)} %copy-done.12, f32[256,8]{1,0:T(8,128)S(1)} %get-tuple-element.17.run_ref, ...), custom_call_target="tpu_custom_call", output_to_operand_aliasing={{}: (14, {})} | custom-call | flops 335544320 | bytes 2924544 | tf_op jit(solution)/shard_map/span_outputs/pallas_call | solution.py:299
  110.1 2.6 %span_outputs.7 = bf16[256,4096]{1,0:T(8,128)(2,1)} custom-call(f32[3,2,8]{2,1,0:T(2,128)S(1)} %bitcast.10, s32[2,8]{1,0:T(2,128)S(1)} %copy-done.8, s32[2,8]{1,0:T(2,128)S(1)} %copy-done.10, s32[2,8]{1,0:T(2,128)S(1)} %copy-done.12, f32[256,8]{1,0:T(8,128)S(1)} %get-tuple-element.17.run_ref, ...), custom_call_target="tpu_custom_call", output_to_operand_aliasing={{}: (14, {})} | custom-call | flops 335544320 | bytes 2924544 | tf_op jit(solution)/shard_map/span_outputs/pallas_call | solution.py:299
  (47 shorter events, 2.0 us)
Async XLA Ops:
  0.0 0.7 copy-start.13
  0.7 0.7 copy-start.14
  2.0 1.6 %copy-start = (bf16[256,4096]{1,0:T(8,128)(2,1)S(1)}, bf16[256,4096]{1,0:T(8,128)(2,1)}, u32[]{:S(2)}) copy-start(bf16[256,4096]{1,0:T(8,128)(2,1)} %v_ref.15) | copy-start | bytes 6291460
  3.6 1.2 %copy-start.2 = (bf16[256,2048]{1,0:T(8,128)(2,1)S(1)}, bf16[256,2048]{1,0:T(8,128)(2,1)}, u32[]{:S(2)}) copy-start(bf16[256,2048]{1,0:T(8,128)(2,1)} %k_ref.15) | copy-start | bytes 3145732
  4.8 0.7 copy-start.5
  5.5 0.7 copy-start.7
  6.2 0.7 copy-start.9
  6.9 0.7 copy-start.11
  8.8 10.5 %collective-permute-start.15 = (bf16[1,264,512]{2,1,0:T(8,128)(2,1)S(1)}, bf16[1,264,512]{2,1,0:T(8,128)(2,1)S(1)}, u32[]{:S(2)}, u32[]{:S(2)}) collective-permute-start(bf16[1,264,512]{2,1,0:T(8,128)(2,1)S(1)} %get-tuple-element.28), channel_id=1, source_target_pairs={{0,1},{1,0},{2,3},{3,2},{4,5},{5,4},{6,7},{7,6},{8,9},{9,8},{10,11... | collective-permute-start | bytes 811016 | tf_op jit(solution)/shard_map/ppermute | solution.py:36
  13.1 17.7 %collective-permute-start.10 = (bf16[1,264,512]{2,1,0:T(8,128)(2,1)S(1)}, bf16[1,264,512]{2,1,0:T(8,128)(2,1)S(1)}, u32[]{:S(2)}, u32[]{:S(2)}) collective-permute-start(bf16[1,264,512]{2,1,0:T(8,128)(2,1)S(1)} %get-tuple-element.26), channel_id=1, source_target_pairs={{0,1},{1,0},{2,3},{3,2},{4,5},{5,4},{6,7},{7,6},{8,9},{9,8},{10,11... | collective-permute-start | bytes 811016 | tf_op jit(solution)/shard_map/ppermute | solution.py:36
  14.4 27.3 %collective-permute-start.5 = (bf16[1,264,512]{2,1,0:T(8,128)(2,1)S(1)}, bf16[1,264,512]{2,1,0:T(8,128)(2,1)S(1)}, u32[]{:S(2)}, u32[]{:S(2)}) collective-permute-start(bf16[1,264,512]{2,1,0:T(8,128)(2,1)S(1)} %get-tuple-element.24), channel_id=1, source_target_pairs={{0,1},{1,0},{2,3},{3,2},{4,5},{5,4},{6,7},{7,6},{8,9},{9,8},{10,11... | collective-permute-start | bytes 811016 | tf_op jit(solution)/shard_map/ppermute | solution.py:36
  17.8 28.9 %collective-permute-start = (bf16[1,264,512]{2,1,0:T(8,128)(2,1)S(1)}, bf16[1,264,512]{2,1,0:T(8,128)(2,1)S(1)}, u32[]{:S(2)}, u32[]{:S(2)}) collective-permute-start(bf16[1,264,512]{2,1,0:T(8,128)(2,1)S(1)} %get-tuple-element.22), channel_id=1, source_target_pairs={{0,1},{1,0},{2,3},{3,2},{4,5},{5,4},{6,7},{7,6},{8,9},{9,8},{10,11... | collective-permute-start | bytes 811016 | tf_op jit(solution)/shard_map/ppermute | solution.py:36
  19.4 27.5 %collective-permute-start.16 = (bf16[1,264,512]{2,1,0:T(8,128)(2,1)S(1)}, bf16[1,264,512]{2,1,0:T(8,128)(2,1)S(1)}, u32[]{:S(2)}, u32[]{:S(2)}) collective-permute-start(bf16[1,264,512]{2,1,0:T(8,128)(2,1)S(1)} %combine.28), channel_id=1, source_target_pairs={{0,2},{1,3},{2,0},{3,1},{4,6},{5,7},{6,4},{7,5},{8,10},{9,11},{10,... | collective-permute-start | bytes 811016 | tf_op jit(solution)/shard_map/ppermute | solution.py:36
  31.0 31.7 %collective-permute-start.11 = (bf16[1,264,512]{2,1,0:T(8,128)(2,1)S(1)}, bf16[1,264,512]{2,1,0:T(8,128)(2,1)S(1)}, u32[]{:S(2)}, u32[]{:S(2)}) collective-permute-start(bf16[1,264,512]{2,1,0:T(8,128)(2,1)S(1)} %combine.24), channel_id=1, source_target_pairs={{0,2},{1,3},{2,0},{3,1},{4,6},{5,7},{6,4},{7,5},{8,10},{9,11},{10,... | collective-permute-start | bytes 811016 | tf_op jit(solution)/shard_map/ppermute | solution.py:36
  41.8 26.6 %collective-permute-start.6 = (bf16[1,264,512]{2,1,0:T(8,128)(2,1)S(1)}, bf16[1,264,512]{2,1,0:T(8,128)(2,1)S(1)}, u32[]{:S(2)}, u32[]{:S(2)}) collective-permute-start(bf16[1,264,512]{2,1,0:T(8,128)(2,1)S(1)} %combine.20), channel_id=1, source_target_pairs={{0,2},{1,3},{2,0},{3,1},{4,6},{5,7},{6,4},{7,5},{8,10},{9,11},{10,... | collective-permute-start | bytes 811016 | tf_op jit(solution)/shard_map/ppermute | solution.py:36
  46.8 26.7 %collective-permute-start.1 = (bf16[1,264,512]{2,1,0:T(8,128)(2,1)S(1)}, bf16[1,264,512]{2,1,0:T(8,128)(2,1)S(1)}, u32[]{:S(2)}, u32[]{:S(2)}) collective-permute-start(bf16[1,264,512]{2,1,0:T(8,128)(2,1)S(1)} %combine.16), channel_id=1, source_target_pairs={{0,2},{1,3},{2,0},{3,1},{4,6},{5,7},{6,4},{7,5},{8,10},{9,11},{10,... | collective-permute-start | bytes 811016 | tf_op jit(solution)/shard_map/ppermute | solution.py:36
  47.1 26.7 %collective-permute-start.17 = (bf16[1,264,512]{2,1,0:T(8,128)(2,1)S(1)}, bf16[1,264,512]{2,1,0:T(8,128)(2,1)S(1)}, u32[]{:S(2)}, u32[]{:S(2)}) collective-permute-start(bf16[1,264,512]{2,1,0:T(8,128)(2,1)S(1)} %combine.29), channel_id=1, source_target_pairs={{0,4},{4,0},{8,12},{12,8},{1,5},{5,1},{9,13},{13,9},{2,6},{6,2},{1... | collective-permute-start | bytes 811016 | tf_op jit(solution)/shard_map/ppermute | solution.py:36
  62.8 14.7 %collective-permute-start.12 = (bf16[1,264,512]{2,1,0:T(8,128)(2,1)S(1)}, bf16[1,264,512]{2,1,0:T(8,128)(2,1)S(1)}, u32[]{:S(2)}, u32[]{:S(2)}) collective-permute-start(bf16[1,264,512]{2,1,0:T(8,128)(2,1)S(1)} %combine.25), channel_id=1, source_target_pairs={{0,4},{4,0},{8,12},{12,8},{1,5},{5,1},{9,13},{13,9},{2,6},{6,2},{1... | collective-permute-start | bytes 811016 | tf_op jit(solution)/shard_map/ppermute | solution.py:36
  68.6 10.6 %collective-permute-start.7 = (bf16[1,264,512]{2,1,0:T(8,128)(2,1)S(1)}, bf16[1,264,512]{2,1,0:T(8,128)(2,1)S(1)}, u32[]{:S(2)}, u32[]{:S(2)}) collective-permute-start(bf16[1,264,512]{2,1,0:T(8,128)(2,1)S(1)} %combine.21), channel_id=1, source_target_pairs={{0,4},{4,0},{8,12},{12,8},{1,5},{5,1},{9,13},{13,9},{2,6},{6,2},{1... | collective-permute-start | bytes 811016 | tf_op jit(solution)/shard_map/ppermute | solution.py:36
  73.7 7.1 %collective-permute-start.2 = (bf16[1,264,512]{2,1,0:T(8,128)(2,1)S(1)}, bf16[1,264,512]{2,1,0:T(8,128)(2,1)S(1)}, u32[]{:S(2)}, u32[]{:S(2)}) collective-permute-start(bf16[1,264,512]{2,1,0:T(8,128)(2,1)S(1)} %combine.17), channel_id=1, source_target_pairs={{0,4},{4,0},{8,12},{12,8},{1,5},{5,1},{9,13},{13,9},{2,6},{6,2},{1... | collective-permute-start | bytes 811016 | tf_op jit(solution)/shard_map/ppermute | solution.py:36
  74.1 10.3 %collective-permute-start.18 = (bf16[1,264,512]{2,1,0:T(8,128)(2,1)S(1)}, bf16[1,264,512]{2,1,0:T(8,128)(2,1)S(1)}, u32[]{:S(2)}, u32[]{:S(2)}) collective-permute-start(bf16[1,264,512]{2,1,0:T(8,128)(2,1)S(1)} %combine.30), channel_id=1, source_target_pairs={{0,8},{4,12},{1,9},{5,13},{2,10},{6,14},{3,11},{7,15},{16,24},{20,... | collective-permute-start | bytes 811016 | tf_op jit(solution)/shard_map/ppermute | solution.py:36
  77.9 12.3 %collective-permute-start.13 = (bf16[1,264,512]{2,1,0:T(8,128)(2,1)S(1)}, bf16[1,264,512]{2,1,0:T(8,128)(2,1)S(1)}, u32[]{:S(2)}, u32[]{:S(2)}) collective-permute-start(bf16[1,264,512]{2,1,0:T(8,128)(2,1)S(1)} %combine.26), channel_id=1, source_target_pairs={{0,8},{4,12},{1,9},{5,13},{2,10},{6,14},{3,11},{7,15},{16,24},{20,... | collective-permute-start | bytes 811016 | tf_op jit(solution)/shard_map/ppermute | solution.py:36
  79.5 16.5 %collective-permute-start.8 = (bf16[1,264,512]{2,1,0:T(8,128)(2,1)S(1)}, bf16[1,264,512]{2,1,0:T(8,128)(2,1)S(1)}, u32[]{:S(2)}, u32[]{:S(2)}) collective-permute-start(bf16[1,264,512]{2,1,0:T(8,128)(2,1)S(1)} %combine.22), channel_id=1, source_target_pairs={{0,8},{4,12},{1,9},{5,13},{2,10},{6,14},{3,11},{7,15},{16,24},{20,... | collective-permute-start | bytes 811016 | tf_op jit(solution)/shard_map/ppermute | solution.py:36
  81.1 20.2 %collective-permute-start.3 = (bf16[1,264,512]{2,1,0:T(8,128)(2,1)S(1)}, bf16[1,264,512]{2,1,0:T(8,128)(2,1)S(1)}, u32[]{:S(2)}, u32[]{:S(2)}) collective-permute-start(bf16[1,264,512]{2,1,0:T(8,128)(2,1)S(1)} %combine.18), channel_id=1, source_target_pairs={{0,8},{4,12},{1,9},{5,13},{2,10},{6,14},{3,11},{7,15},{16,24},{20,... | collective-permute-start | bytes 811016 | tf_op jit(solution)/shard_map/ppermute | solution.py:36
  84.4 17.8 %copy-start.4 = (bf16[256,2048]{1,0:T(8,128)(2,1)S(1)}, bf16[256,2048]{1,0:T(8,128)(2,1)}, u32[]{:S(2)}) copy-start(bf16[256,2048]{1,0:T(8,128)(2,1)} %q_ref.7) | copy-start | bytes 3145732
  84.7 17.6 %copy-start.1 = (bf16[256,4096]{1,0:T(8,128)(2,1)S(1)}, bf16[256,4096]{1,0:T(8,128)(2,1)}, u32[]{:S(2)}) copy-start(bf16[256,4096]{1,0:T(8,128)(2,1)} %v_ref.15) | copy-start | bytes 6291460
  84.7 17.6 %copy-start.3 = (bf16[256,2048]{1,0:T(8,128)(2,1)S(1)}, bf16[256,2048]{1,0:T(8,128)(2,1)}, u32[]{:S(2)}) copy-start(bf16[256,2048]{1,0:T(8,128)(2,1)} %k_ref.15) | copy-start | bytes 3145732
  84.7 17.6 %copy-start.6 = (f32[2,3,8]{2,0,1:T(2,128)S(1)}, f32[2,3,8]{2,0,1:T(2,128)}, u32[]{:S(2)}) copy-start(f32[2,3,8]{2,0,1:T(2,128)} %param.12) | copy-start | bytes 580
  84.7 17.6 %copy-start.8 = (s32[2,8]{1,0:T(2,128)S(1)}, s32[2,8]{1,0:T(2,128)}, u32[]{:S(2)}) copy-start(s32[2,8]{1,0:T(2,128)} %tensors.15) | copy-start | bytes 196
  84.7 17.6 %copy-start.10 = (s32[2,8]{1,0:T(2,128)S(1)}, s32[2,8]{1,0:T(2,128)}, u32[]{:S(2)}) copy-start(s32[2,8]{1,0:T(2,128)} %offsets.15) | copy-start | bytes 196
  84.7 17.6 %copy-start.12 = (s32[2,8]{1,0:T(2,128)S(1)}, s32[2,8]{1,0:T(2,128)}, u32[]{:S(2)}) copy-start(s32[2,8]{1,0:T(2,128)} %fbits.15) | copy-start | bytes 196
  84.8 17.5 %collective-permute-start.19 = (bf16[1,264,512]{2,1,0:T(8,128)(2,1)S(1)}, bf16[1,264,512]{2,1,0:T(8,128)(2,1)S(1)}, u32[]{:S(2)}, u32[]{:S(2)}) collective-permute-start(bf16[1,264,512]{2,1,0:T(8,128)(2,1)S(1)} %combine.31), channel_id=1, source_target_pairs={{0,1},{1,0},{2,3},{3,2},{4,5},{5,4},{6,7},{7,6},{8,9},{9,8},{10,11... | collective-permute-start | bytes 811016 | tf_op jit(solution)/shard_map/ppermute | solution.py:36
  90.5 14.4 %collective-permute-start.14 = (bf16[1,264,512]{2,1,0:T(8,128)(2,1)S(1)}, bf16[1,264,512]{2,1,0:T(8,128)(2,1)S(1)}, u32[]{:S(2)}, u32[]{:S(2)}) collective-permute-start(bf16[1,264,512]{2,1,0:T(8,128)(2,1)S(1)} %combine.27), channel_id=1, source_target_pairs={{0,1},{1,0},{2,3},{3,2},{4,5},{5,4},{6,7},{7,6},{8,9},{9,8},{10,11... | collective-permute-start | bytes 811016 | tf_op jit(solution)/shard_map/ppermute | solution.py:36
  96.3 11.2 %collective-permute-start.9 = (bf16[1,264,512]{2,1,0:T(8,128)(2,1)S(1)}, bf16[1,264,512]{2,1,0:T(8,128)(2,1)S(1)}, u32[]{:S(2)}, u32[]{:S(2)}) collective-permute-start(bf16[1,264,512]{2,1,0:T(8,128)(2,1)S(1)} %combine.23), channel_id=1, source_target_pairs={{0,1},{1,0},{2,3},{3,2},{4,5},{5,4},{6,7},{7,6},{8,9},{9,8},{10,11... | collective-permute-start | bytes 811016 | tf_op jit(solution)/shard_map/ppermute | solution.py:36
  101.6 8.5 %collective-permute-start.4 = (bf16[1,264,512]{2,1,0:T(8,128)(2,1)S(1)}, bf16[1,264,512]{2,1,0:T(8,128)(2,1)S(1)}, u32[]{:S(2)}, u32[]{:S(2)}) collective-permute-start(bf16[1,264,512]{2,1,0:T(8,128)(2,1)S(1)} %combine.19), channel_id=1, source_target_pairs={{0,1},{1,0},{2,3},{3,2},{4,5},{5,4},{6,7},{7,6},{8,9},{9,8},{10,11... | collective-permute-start | bytes 811016 | tf_op jit(solution)/shard_map/ppermute | solution.py:36

commit v3 on v2

--- a/solution.py
+++ b/solution.py
@@ -16,6 +16,7 @@
 TAIL = 8
 ROWS = DK + TAIL
 CHUNKS = (1, 1, 1, 1)
+AHEAD, DUE, GAP = 2, (8.0, 24.0, 26.5, 34.0, 42.0), 12.0
 
 F32 = jnp.float32
 BF16 = jnp.bfloat16
@@ -165,6 +166,21 @@
     return [((me >> b) & 1) == 1 for b in range(bits)]
 
 
+def ordered(kernel, operands, after):
+    if after is None:
+        return kernel, [], []
+    at = operands
+
+    def run(*refs):
+        kernel(*refs[:at], *refs[at + 1 :])
+
+    return run, [after], [pl.BlockSpec(memory_space=pl.ANY)]
+
+
+def in_hbm(x):
+    return pltpu.with_memory_space_constraint(x, pltpu.HBM)
+
+
 SMEM = pl.BlockSpec(memory_space=pltpu.SMEM)
 VMEM = pl.BlockSpec(memory_space=pltpu.VMEM)
 
@@ -191,18 +207,20 @@
 STATE = pl.BlockSpec((1, ROWS, DV), lambda i: (i, 0, 0))
 
 
-def span_states(first, count, small, mf, weight, key_codes, value_codes):
+def span_states(first, count, small, mf, weight, key_codes, value_codes, after):
     rows = key_codes.shape[0]
     out = jax.ShapeDtypeStruct((count, ROWS, DV), BF16)
+    kernel, extra, extra_specs = ordered(functools.partial(state_kernel, first), 8, after)
     return pl.pallas_call(
-        functools.partial(state_kernel, first),
+        kernel,
         grid=(count,),
         in_specs=[SMEM] * 5
         + [
             whole(weight.shape),
             pl.BlockSpec((rows, 2 * DK), lambda i: (0, first + i)),
             pl.BlockSpec((rows, 2 * DV), lambda i: (0, first + i)),
-        ],
+        ]
+        + extra_specs,
         out_specs=(STATE, STATE),
         out_shape=(out, out),
         compiler_params=pltpu.CompilerParams(vmem_limit_bytes=12 << 20),
@@ -210,7 +228,7 @@
             flops=count * 4 * rows * DK * DV, bytes_accessed=count * rows * 2 * (2 * DK + 4 * DV), transcendentals=0
         ),
         name="span_states",
-    )(*small, mf, weight, key_codes, value_codes)
+    )(*small, mf, weight, key_codes, value_codes, *extra)
 
 
 def combine_kernel(head_bits, bits, last, *refs):
@@ -227,11 +245,12 @@
         out_ref[i, DK:ROWS, :] = pack_tail(normer, peak, total)
 
 
-def combine(head_bits, bits, last, parts):
+def combine(head_bits, bits, last, parts, after):
     count = parts[0].shape[0]
+    kernel, extra, extra_specs = ordered(functools.partial(combine_kernel, head_bits, bits, last), len(parts), after)
     return pl.pallas_call(
-        functools.partial(combine_kernel, head_bits, bits, last),
-        in_specs=[VMEM] * len(parts),
+        kernel,
+        in_specs=[VMEM] * len(parts) + extra_specs,
         out_specs=VMEM,
         out_shape=jax.ShapeDtypeStruct((count, ROWS, DV), BF16),
         compiler_params=pltpu.CompilerParams(vmem_limit_bytes=8 << 20),
@@ -239,7 +258,7 @@
             flops=count * ROWS * DV * 2 * len(parts), bytes_accessed=count * ROWS * DV * 2 * (len(parts) + 1), transcendentals=0
         ),
         name="combine",
-    )(*parts)
+    )(*parts, *extra)
 
 
 def output_kernel(
@@ -284,7 +303,7 @@
         out_ref[:, pl.ds(wide, DV)] = (numerator / jnp.maximum(jnp.abs(denominator), 1.0)).astype(BF16)
 
 
-def span_outputs(head_bits, bits, first, small, run, shift, codes, back, parts, before):
+def span_outputs(head_bits, bits, first, small, run, shift, codes, back, parts, before, after):
     q, k, v = codes
     count, rows = back.shape[0], q.shape[0]
     narrow = pl.BlockSpec((rows, 2 * DK), lambda i: (0, first + i))
@@ -296,10 +315,11 @@
         aliases = {len(operands): 0}
         operands.append(before)
         in_specs.append(pl.BlockSpec(memory_space=pl.ANY))
+    kernel, extra, extra_specs = ordered(functools.partial(output_kernel, head_bits, bits, first), len(operands), after)
     return pl.pallas_call(
-        functools.partial(output_kernel, head_bits, bits, first),
+        kernel,
         grid=(count,),
-        in_specs=in_specs,
+        in_specs=in_specs + extra_specs,
         out_specs=wide,
         out_shape=jax.ShapeDtypeStruct(v.shape, BF16),
         input_output_aliases=aliases,
@@ -310,7 +330,7 @@
             transcendentals=count * 2 * rows * rows,
         ),
         name="span_outputs",
-    )(*operands)
+    )(*operands, *extra)
 
 
 def body(
@@ -328,23 +348,43 @@
 ):
     bits = head_bits + ctx_bits
     assert query_codes.shape[0] == CH
-    small = (block_scales.transpose(1, 0, 2), fault_tensor, fault_offset, fault_bit)
+    small = tuple(in_hbm(x) for x in (block_scales.transpose(1, 0, 2), fault_tensor, fault_offset, fault_bit))
     codes = (query_codes, key_codes, value_codes)
     exchange = functools.partial(flip, head_bits=head_bits, ctx_bits=ctx_bits)
-    run, weight, shift, mf = gates(input_gate.T, forget_gate.T)
+    run, weight, shift, mf = gates(in_hbm(input_gate.T), in_hbm(forget_gate.T))
 
     starts = [sum(CHUNKS[:c]) for c in range(len(CHUNKS))]
     assert 2 * sum(CHUNKS) == input_gate.shape[1]
-    out = None
-    for first, count in zip(starts, CHUNKS):
-        keep, send = span_states(first, count, small, mf, weight, key_codes, value_codes)
-        got = [exchange(send, 0, last=False)]
-        for b in range(1, bits):
-            group = combine(head_bits, bits, False, [keep, *got])
-            got.append(exchange(group, b, last=b == bits - 1))
-        back = exchange(combine(head_bits, bits, True, [keep, *got[1:]]), 0, last=False)
-        out = span_outputs(head_bits, bits, first, small, run, shift, codes, back, got, out)
+    keys, values = in_hbm(key_codes), in_hbm(value_codes)
+    keep, got, back = {}, {}, {}
+    out = token = None
+    for stage, c in order(len(CHUNKS), bits):
+        first, count = starts[c], CHUNKS[c]
+        if stage == 0:
+            keep[c], token = span_states(first, count, small, mf, weight, keys, values, token)
+        elif stage < bits:
+            token = combine(head_bits, bits, False, [keep[c], *got[c]], token)
+        elif stage == bits:
+            token = combine(head_bits, bits, True, [keep[c], *got[c][1:]], token)
+        else:
+            out = span_outputs(head_bits, bits, first, small, run, shift, codes, back[c], got[c], out, token)
+        if stage < bits:
+            got.setdefault(c, []).append(exchange(token, stage, last=stage == bits - 1))
+        elif stage == bits:
+            back[c] = exchange(token, 0, last=False)
     return out
+
+
+def order(chunks, bits):
+    def due(step):
+        stage, c = step
+        if stage == 0:
+            return 0.1 * c if c < AHEAD else DUE[0] + GAP * (c - AHEAD) + 0.5
+        late = bits + 1 - stage
+        at = DUE[stage - 1] if stage <= 2 else DUE[4] if late == 0 else DUE[3] if late == 1 else DUE[2] + 0.01 * stage
+        return at + GAP * c
+
+    return sorted([(stage, c) for c in range(chunks) for stage in range(bits + 2)], key=due)
 
 
 def solution(mesh):

time: 113 us -> 118 us (1.044)
  local copies, waits for them, and re-layouts: 6.94 us -> 0.02 us
  waiting for transfers between devices: 64.7 us -> 71 us
  Pallas kernels: 19.4 us -> 22.7 us
  starting transfers between devices: 21.3 us -> 23.7 us
    unnamed x30 -> x6, local copies, waits for them, and re-layouts: 6.94 us -> 0.02 us
    ppermute x20, waiting for transfers between devices: 64.7 us -> 71 us  [flip(): return lax.ppermute(x, axis, pairs)]
    pallas_call x24, Pallas kernels: 18.8 us -> 21.3 us  [the longest x4 10.9 us: span_outputs(): pl.pallas_call(kernel, grid=(count,), in_specs=in_specs + extra_specs, ou...]
    ppermute x20, starting transfers between devices: 21.3 us -> 23.7 us  [flip(): return lax.ppermute(x, axis, pairs)]
  transfers between devices with their start and end apart: 20 -> 20, of which waited for: 11 -> 19; matrix products, arithmetic and copies ran while one was open for 0% -> 0% of each run, Pallas kernels for 13% -> 13%
where the time goes in v3:
time: 118 us
  waiting for transfers between devices  71 us (60%)
  starting transfers between devices  23.7 us (20%)
  Pallas kernels  22.7 us (19%)
    ppermute x20, waiting for transfers between devices, flip(): return lax.ppermute(x, axis, pairs)  71 us
    ppermute x20, starting transfers between devices, flip(): return lax.ppermute(x, axis, pairs)  23.7 us
    pallas_call x4, Pallas kernels, span_outputs(): pl.pallas_call(kernel, grid=(count,), in_specs=in_specs + extra_specs, ou...  10.9 us
    pallas_call x4, Pallas kernels, span_states(): pl.pallas_call(kernel, grid=(count,), in_specs=[SMEM] * 5 + [whole(weight...  6.89 us
    pallas_call x16, Pallas kernels, combine(): pl.pallas_call(kernel, in_specs=[VMEM] * len(parts) + extra_specs, out_sp...  3.54 us
  transfers between devices with their start and end apart: 20, of which 19 were waited for; matrix products, arithmetic and copies ran while one was open for 0% of the time, Pallas kernels for 13%

profile of v3, /device:TPU:0, one launch (start us, length us, event | category | flops | bytes accessed | tf_op | source)
XLA Modules:
  0.0 117.6 jit_solution(11036463007158303976)
XLA Ops:
  0.0 1.3 %gates.1 = (f32[256,8]{1,0:T(8,128)S(1)}, f32[256,8]{1,0:T(8,128)S(1)}, f32[8,256]{1,0:T(8,128)S(1)}, f32[2,8]{1,0:T(2,128)S(1)}) custom-call(bf16[8,256]{1,0:T(8,128)(2,1)} %bitcast.11, bf16[8,256]{1,0:T(8,128)(2,1)} %bitcast.12), custom_call_target="tpu_custom_call" | custom-call | flops 1048576 | bytes 1048576 | tf_op jit(solution)/shard_map/gates/pallas_call | solution.py:66
  1.3 1.7 %span_states.4 = (bf16[1,264,512]{2,1,0:T(8,128)(2,1)S(1)}, bf16[1,264,512]{2,1,0:T(8,128)(2,1)S(1)}) custom-call(f32[3,2,8]{2,1,0:T(2,128)} %bitcast.3, s32[2,8]{1,0:T(2,128)} %refs_1_.13, s32[2,8]{1,0:T(2,128)} %refs_2_.13, s32[2,8]{1,0:T(2,128)} %refs_3_.13, f32[2,8]{1,0:T(2,128)S(1)} %get-tuple-element.19.mf.refs_4_, ...), custom_call_target="tpu_custom_call" | custom-call | flops 134217728 | bytes 1310720 | tf_op jit(solution)/shard_map/span_states/pallas_call | solution.py:214
  3.1 3.1 %collective-permute-start.1 = (bf16[1,264,512]{2,1,0:T(8,128)(2,1)S(1)}, bf16[1,264,512]{2,1,0:T(8,128)(2,1)S(1)}, u32[]{:S(2)}, u32[]{:S(2)}) collective-permute-start(bf16[1,264,512]{2,1,0:T(8,128)(2,1)S(1)} %get-tuple-element.21.refs_8_), channel_id=1, source_target_pairs={{0,1},{1,0},{2,3},{3,2},{4,5},{5,4},{6,7},{7,6},{8,9},{9,8},{10,11... | collective-permute-start | bytes 811016 | tf_op jit(solution)/shard_map/ppermute | solution.py:37
  6.2 1.7 %span_states.5 = (bf16[1,264,512]{2,1,0:T(8,128)(2,1)S(1)}, bf16[1,264,512]{2,1,0:T(8,128)(2,1)S(1)}) custom-call(f32[3,2,8]{2,1,0:T(2,128)} %bitcast.4, s32[2,8]{1,0:T(2,128)} %refs_1_.13, s32[2,8]{1,0:T(2,128)} %refs_2_.13, s32[2,8]{1,0:T(2,128)} %refs_3_.13, f32[2,8]{1,0:T(2,128)S(1)} %get-tuple-element.19.mf.refs_4_, ...), custom_call_target="tpu_custom_call" | custom-call | flops 134217728 | bytes 1310720 | tf_op jit(solution)/shard_map/span_states/pallas_call | solution.py:214
  8.0 5.5 %collective-permute-done.1.refs_1_.refs_10_ = bf16[1,264,512]{2,1,0:T(8,128)(2,1)S(1)} collective-permute-done((bf16[1,264,512]{2,1,0:T(8,128)(2,1)S(1)}, bf16[1,264,512]{2,1,0:T(8,128)(2,1)S(1)}, u32[]{:S(2)}, u32[]{:S(2)}) %collective-permute-start.1) | collective-permute-done | bytes 270368 | tf_op jit(solution)/shard_map/ppermute | solution.py:37
  13.7 3.1 %collective-permute-start.4 = (bf16[1,264,512]{2,1,0:T(8,128)(2,1)S(1)}, bf16[1,264,512]{2,1,0:T(8,128)(2,1)S(1)}, u32[]{:S(2)}, u32[]{:S(2)}) collective-permute-start(bf16[1,264,512]{2,1,0:T(8,128)(2,1)S(1)} %combine.16.refs_8_), channel_id=1, source_target_pairs={{0,2},{1,3},{2,0},{3,1},{4,6},{5,7},{6,4},{7,5},{8,10},{9,11},{10,... | collective-permute-start | bytes 811016 | tf_op jit(solution)/shard_map/ppermute | solution.py:37
  16.8 1.7 %span_states.6 = (bf16[1,264,512]{2,1,0:T(8,128)(2,1)S(1)}, bf16[1,264,512]{2,1,0:T(8,128)(2,1)S(1)}) custom-call(f32[3,2,8]{2,1,0:T(2,128)} %bitcast.5, s32[2,8]{1,0:T(2,128)} %refs_1_.13, s32[2,8]{1,0:T(2,128)} %refs_2_.13, s32[2,8]{1,0:T(2,128)} %refs_3_.13, f32[2,8]{1,0:T(2,128)S(1)} %get-tuple-element.19.mf.refs_4_, ...), custom_call_target="tpu_custom_call" | custom-call | flops 134217728 | bytes 1310720 | tf_op jit(solution)/shard_map/span_states/pallas_call | solution.py:214
  18.5 5.1 %collective-permute-done.refs_1_.refs_10_ = bf16[1,264,512]{2,1,0:T(8,128)(2,1)S(1)} collective-permute-done((bf16[1,264,512]{2,1,0:T(8,128)(2,1)S(1)}, bf16[1,264,512]{2,1,0:T(8,128)(2,1)S(1)}, u32[]{:S(2)}, u32[]{:S(2)}) %collective-permute-start) | collective-permute-done | bytes 270368 | tf_op jit(solution)/shard_map/ppermute | solution.py:37
  23.7 1.7 %span_states.7 = (bf16[1,264,512]{2,1,0:T(8,128)(2,1)S(1)}, bf16[1,264,512]{2,1,0:T(8,128)(2,1)S(1)}) custom-call(f32[3,2,8]{2,1,0:T(2,128)} %bitcast.6, s32[2,8]{1,0:T(2,128)} %refs_1_.13, s32[2,8]{1,0:T(2,128)} %refs_2_.13, s32[2,8]{1,0:T(2,128)} %refs_3_.13, f32[2,8]{1,0:T(2,128)S(1)} %get-tuple-element.19.mf.refs_4_, ...), custom_call_target="tpu_custom_call" | custom-call | flops 134217728 | bytes 1310720 | tf_op jit(solution)/shard_map/span_states/pallas_call | solution.py:214
  25.4 1.8 %collective-permute-done.4.refs_2_.refs_1_.refs_11_ = bf16[1,264,512]{2,1,0:T(8,128)(2,1)S(1)} collective-permute-done((bf16[1,264,512]{2,1,0:T(8,128)(2,1)S(1)}, bf16[1,264,512]{2,1,0:T(8,128)(2,1)S(1)}, u32[]{:S(2)}, u32[]{:S(2)}) %collective-permute-start.4) | collective-permute-done | bytes 270368 | tf_op jit(solution)/shard_map/ppermute | solution.py:37
  27.5 0.7 collective-permute-start.7
  28.3 0.8 collective-permute-done.5.refs_3_.refs_2_.refs_12_
  29.1 0.3 combine.19.refs_2_
  29.4 3.5 %collective-permute-start.6 = (bf16[1,264,512]{2,1,0:T(8,128)(2,1)S(1)}, bf16[1,264,512]{2,1,0:T(8,128)(2,1)S(1)}, u32[]{:S(2)}, u32[]{:S(2)}) collective-permute-start(bf16[1,264,512]{2,1,0:T(8,128)(2,1)S(1)} %combine.19.refs_2_), channel_id=1, source_target_pairs={{0,8},{4,12},{1,9},{5,13},{2,10},{6,14},{3,11},{7,15},{16,24},{20,... | collective-permute-start | bytes 811016 | tf_op jit(solution)/shard_map/ppermute | solution.py:37
  32.8 2.6 %collective-permute-start.3 = (bf16[1,264,512]{2,1,0:T(8,128)(2,1)S(1)}, bf16[1,264,512]{2,1,0:T(8,128)(2,1)S(1)}, u32[]{:S(2)}, u32[]{:S(2)}) collective-permute-start(bf16[1,264,512]{2,1,0:T(8,128)(2,1)S(1)} %combine.17.refs_8_), channel_id=1, source_target_pairs={{0,2},{1,3},{2,0},{3,1},{4,6},{5,7},{6,4},{7,5},{8,10},{9,11},{10,... | collective-permute-start | bytes 811016 | tf_op jit(solution)/shard_map/ppermute | solution.py:37
  35.4 2.8 %collective-permute-done.7.refs_1_.refs_10_ = bf16[1,264,512]{2,1,0:T(8,128)(2,1)S(1)} collective-permute-done((bf16[1,264,512]{2,1,0:T(8,128)(2,1)S(1)}, bf16[1,264,512]{2,1,0:T(8,128)(2,1)S(1)}, u32[]{:S(2)}, u32[]{:S(2)}) %collective-permute-start.7) | collective-permute-done | bytes 270368 | tf_op jit(solution)/shard_map/ppermute | solution.py:37
  38.3 0.5 collective-permute-done.6.refs_3_.refs_13_
  38.8 0.3 combine.21.refs_3_
  39.1 8.8 %collective-permute-done.3.refs_2_.refs_1_.refs_11_ = bf16[1,264,512]{2,1,0:T(8,128)(2,1)S(1)} collective-permute-done((bf16[1,264,512]{2,1,0:T(8,128)(2,1)S(1)}, bf16[1,264,512]{2,1,0:T(8,128)(2,1)S(1)}, u32[]{:S(2)}, u32[]{:S(2)}) %collective-permute-start.3) | collective-permute-done | bytes 270368 | tf_op jit(solution)/shard_map/ppermute | solution.py:37
  48.2 0.6 collective-permute-start.2
  48.8 0.9 collective-permute-done.8.refs_3_.refs_2_.refs_12_
  49.7 0.3 combine.23.refs_2_.refs_14_
  50.0 1.6 %collective-permute-start.11 = (bf16[1,264,512]{2,1,0:T(8,128)(2,1)S(1)}, bf16[1,264,512]{2,1,0:T(8,128)(2,1)S(1)}, u32[]{:S(2)}, u32[]{:S(2)}) collective-permute-start(bf16[1,264,512]{2,1,0:T(8,128)(2,1)S(1)} %combine.23.refs_2_.refs_14_), channel_id=1, source_target_pairs={{0,8},{4,12},{1,9},{5,13},{2,10},{6,14},{3,11},{7,15},{16,24},{20,... | collective-permute-start | bytes 811016 | tf_op jit(solution)/shard_map/ppermute | solution.py:37
  51.6 2.5 %collective-permute-start.10 = (bf16[1,264,512]{2,1,0:T(8,128)(2,1)S(1)}, bf16[1,264,512]{2,1,0:T(8,128)(2,1)S(1)}, u32[]{:S(2)}, u32[]{:S(2)}) collective-permute-start(bf16[1,264,512]{2,1,0:T(8,128)(2,1)S(1)} %combine.20.refs_4_), channel_id=1, source_target_pairs={{0,2},{1,3},{2,0},{3,1},{4,6},{5,7},{6,4},{7,5},{8,10},{9,11},{10,... | collective-permute-start | bytes 811016 | tf_op jit(solution)/shard_map/ppermute | solution.py:37
  54.1 6.7 %collective-permute-done.2.refs_1_.refs_10_ = bf16[1,264,512]{2,1,0:T(8,128)(2,1)S(1)} collective-permute-done((bf16[1,264,512]{2,1,0:T(8,128)(2,1)S(1)}, bf16[1,264,512]{2,1,0:T(8,128)(2,1)S(1)}, u32[]{:S(2)}, u32[]{:S(2)}) %collective-permute-start.2) | collective-permute-done | bytes 270368 | tf_op jit(solution)/shard_map/ppermute | solution.py:37
  61.0 0.3 combine.25.refs_3_
  61.2 5.4 %collective-permute-done.10.refs_2_.refs_1_.refs_11_ = bf16[1,264,512]{2,1,0:T(8,128)(2,1)S(1)} collective-permute-done((bf16[1,264,512]{2,1,0:T(8,128)(2,1)S(1)}, bf16[1,264,512]{2,1,0:T(8,128)(2,1)S(1)}, u32[]{:S(2)}, u32[]{:S(2)}) %collective-permute-start.10) | collective-permute-done | bytes 270368 | tf_op jit(solution)/shard_map/ppermute | solution.py:37
  66.9 1.5 %collective-permute-done.12.refs_3_.refs_2_.refs_12_ = bf16[1,264,512]{2,1,0:T(8,128)(2,1)S(1)} collective-permute-done((bf16[1,264,512]{2,1,0:T(8,128)(2,1)S(1)}, bf16[1,264,512]{2,1,0:T(8,128)(2,1)S(1)}, u32[]{:S(2)}, u32[]{:S(2)}) %collective-permute-start.12) | collective-permute-done | bytes 270368 | tf_op jit(solution)/shard_map/ppermute | solution.py:37
  68.4 0.3 combine.27.refs_4_.refs_15_
  68.7 1.6 %collective-permute-start.13 = (bf16[1,264,512]{2,1,0:T(8,128)(2,1)S(1)}, bf16[1,264,512]{2,1,0:T(8,128)(2,1)S(1)}, u32[]{:S(2)}, u32[]{:S(2)}) collective-permute-start(bf16[1,264,512]{2,1,0:T(8,128)(2,1)S(1)} %combine.27.refs_4_.refs_15_), channel_id=1, source_target_pairs={{0,8},{4,12},{1,9},{5,13},{2,10},{6,14},{3,11},{7,15},{16,24},{20,... | collective-permute-start | bytes 811016 | tf_op jit(solution)/shard_map/ppermute | solution.py:37
  70.4 6.0 %collective-permute-done.13.refs_3_.refs_13_ = bf16[1,264,512]{2,1,0:T(8,128)(2,1)S(1)} collective-permute-done((bf16[1,264,512]{2,1,0:T(8,128)(2,1)S(1)}, bf16[1,264,512]{2,1,0:T(8,128)(2,1)S(1)}, u32[]{:S(2)}, u32[]{:S(2)}) %collective-permute-start.13) | collective-permute-done | bytes 270368 | tf_op jit(solution)/shard_map/ppermute | solution.py:37
  76.3 0.3 combine.28.refs_3_
  76.6 8.7 %collective-permute-done.9.refs_2_.refs_1_.refs_11_ = bf16[1,264,512]{2,1,0:T(8,128)(2,1)S(1)} collective-permute-done((bf16[1,264,512]{2,1,0:T(8,128)(2,1)S(1)}, bf16[1,264,512]{2,1,0:T(8,128)(2,1)S(1)}, u32[]{:S(2)}, u32[]{:S(2)}) %collective-permute-start.9) | collective-permute-done | bytes 270368 | tf_op jit(solution)/shard_map/ppermute | solution.py:37
  85.3 0.2 combine.29.refs_4_
  85.6 1.5 %collective-permute-done.14.refs_3_.refs_2_.refs_12_ = bf16[1,264,512]{2,1,0:T(8,128)(2,1)S(1)} collective-permute-done((bf16[1,264,512]{2,1,0:T(8,128)(2,1)S(1)}, bf16[1,264,512]{2,1,0:T(8,128)(2,1)S(1)}, u32[]{:S(2)}, u32[]{:S(2)}) %collective-permute-start.14) | collective-permute-done | bytes 270368 | tf_op jit(solution)/shard_map/ppermute | solution.py:37
  87.2 0.3 combine.30.refs_4_.refs_15_
  87.4 1.7 %collective-permute-start.15 = (bf16[1,264,512]{2,1,0:T(8,128)(2,1)S(1)}, bf16[1,264,512]{2,1,0:T(8,128)(2,1)S(1)}, u32[]{:S(2)}, u32[]{:S(2)}) collective-permute-start(bf16[1,264,512]{2,1,0:T(8,128)(2,1)S(1)} %combine.30.refs_4_.refs_15_), channel_id=1, source_target_pairs={{0,8},{4,12},{1,9},{5,13},{2,10},{6,14},{3,11},{7,15},{16,24},{20,... | collective-permute-start | bytes 811016 | tf_op jit(solution)/shard_map/ppermute | solution.py:37
  89.2 2.0 %collective-permute-start.18 = (bf16[1,264,512]{2,1,0:T(8,128)(2,1)S(1)}, bf16[1,264,512]{2,1,0:T(8,128)(2,1)S(1)}, u32[]{:S(2)}, u32[]{:S(2)}) collective-permute-start(bf16[1,264,512]{2,1,0:T(8,128)(2,1)S(1)} %combine.25.refs_3_), channel_id=1, source_target_pairs={{0,1},{1,0},{2,3},{3,2},{4,5},{5,4},{6,7},{7,6},{8,9},{9,8},{10,11... | collective-permute-start | bytes 811016 | tf_op jit(solution)/shard_map/ppermute | solution.py:37
  91.3 3.7 %collective-permute-done.15.refs_3_.refs_13_ = bf16[1,264,512]{2,1,0:T(8,128)(2,1)S(1)} collective-permute-done((bf16[1,264,512]{2,1,0:T(8,128)(2,1)S(1)}, bf16[1,264,512]{2,1,0:T(8,128)(2,1)S(1)}, u32[]{:S(2)}, u32[]{:S(2)}) %collective-permute-start.15) | collective-permute-done | bytes 270368 | tf_op jit(solution)/shard_map/ppermute | solution.py:37
  95.0 0.3 combine.31.refs_15_
  95.4 3.2 %collective-permute-done.19.refs_9_ = bf16[1,264,512]{2,1,0:T(8,128)(2,1)S(1)} collective-permute-done((bf16[1,264,512]{2,1,0:T(8,128)(2,1)S(1)}, bf16[1,264,512]{2,1,0:T(8,128)(2,1)S(1)}, u32[]{:S(2)}, u32[]{:S(2)}) %collective-permute-start.19) | collective-permute-done | bytes 270368 | tf_op jit(solution)/shard_map/ppermute | solution.py:37
  98.6 2.7 %span_outputs.4.refs_14_ = bf16[256,4096]{1,0:T(8,128)(2,1)} custom-call(f32[3,2,8]{2,1,0:T(2,128)} %bitcast.7, s32[2,8]{1,0:T(2,128)} %refs_1_.13, s32[2,8]{1,0:T(2,128)} %refs_2_.13, s32[2,8]{1,0:T(2,128)} %refs_3_.13, f32[256,8]{1,0:T(8,128)S(1)} %get-tuple-element.17.refs_4_, f32[8,256]{1,0:T(8,128)S(1)} %get-tuple-element.18.refs_5_, ...), custom_call_target="tpu_custom_call" | custom-call | flops 335544320 | bytes 2924544 | tf_op jit(solution)/shard_map/span_outputs/pallas_call | solution.py:319
  101.4 3.0 %collective-permute-done.18.refs_9_ = bf16[1,264,512]{2,1,0:T(8,128)(2,1)S(1)} collective-permute-done((bf16[1,264,512]{2,1,0:T(8,128)(2,1)S(1)}, bf16[1,264,512]{2,1,0:T(8,128)(2,1)S(1)}, u32[]{:S(2)}, u32[]{:S(2)}) %collective-permute-start.18) | collective-permute-done | bytes 270368 | tf_op jit(solution)/shard_map/ppermute | solution.py:37
  104.4 2.7 %span_outputs.5.refs_14_ = bf16[256,4096]{1,0:T(8,128)(2,1)} custom-call(f32[3,2,8]{2,1,0:T(2,128)} %bitcast.8, s32[2,8]{1,0:T(2,128)} %refs_1_.13, s32[2,8]{1,0:T(2,128)} %refs_2_.13, s32[2,8]{1,0:T(2,128)} %refs_3_.13, f32[256,8]{1,0:T(8,128)S(1)} %get-tuple-element.17.refs_4_, ...), custom_call_target="tpu_custom_call", output_to_operand_aliasing={{}: (14, {})} | custom-call | flops 335544320 | bytes 2924544 | tf_op jit(solution)/shard_map/span_outputs/pallas_call | solution.py:319
  107.1 3.1 %collective-permute-done.17.refs_9_ = bf16[1,264,512]{2,1,0:T(8,128)(2,1)S(1)} collective-permute-done((bf16[1,264,512]{2,1,0:T(8,128)(2,1)S(1)}, bf16[1,264,512]{2,1,0:T(8,128)(2,1)S(1)}, u32[]{:S(2)}, u32[]{:S(2)}) %collective-permute-start.17) | collective-permute-done | bytes 270368 | tf_op jit(solution)/shard_map/ppermute | solution.py:37
  110.2 2.7 %span_outputs.6.refs_14_ = bf16[256,4096]{1,0:T(8,128)(2,1)} custom-call(f32[3,2,8]{2,1,0:T(2,128)} %bitcast.9, s32[2,8]{1,0:T(2,128)} %refs_1_.13, s32[2,8]{1,0:T(2,128)} %refs_2_.13, s32[2,8]{1,0:T(2,128)} %refs_3_.13, f32[256,8]{1,0:T(8,128)S(1)} %get-tuple-element.17.refs_4_, ...), custom_call_target="tpu_custom_call", output_to_operand_aliasing={{}: (14, {})} | custom-call | flops 335544320 | bytes 2924544 | tf_op jit(solution)/shard_map/span_outputs/pallas_call | solution.py:319
  112.9 2.0 %collective-permute-done.16.refs_9_ = bf16[1,264,512]{2,1,0:T(8,128)(2,1)S(1)} collective-permute-done((bf16[1,264,512]{2,1,0:T(8,128)(2,1)S(1)}, bf16[1,264,512]{2,1,0:T(8,128)(2,1)S(1)}, u32[]{:S(2)}, u32[]{:S(2)}) %collective-permute-start.16) | collective-permute-done | bytes 270368 | tf_op jit(solution)/shard_map/ppermute | solution.py:37
  114.9 2.7 %span_outputs.7 = bf16[256,4096]{1,0:T(8,128)(2,1)} custom-call(f32[3,2,8]{2,1,0:T(2,128)} %bitcast.10, s32[2,8]{1,0:T(2,128)} %refs_1_.13, s32[2,8]{1,0:T(2,128)} %refs_2_.13, s32[2,8]{1,0:T(2,128)} %refs_3_.13, f32[256,8]{1,0:T(8,128)S(1)} %get-tuple-element.17.refs_4_, f32[8,256]{1,0:T(8,128)S(1)} %get-tuple-element.18.refs_5_, ...), custom_call_target="tpu_custom_call", output_to_operand_aliasing={{}: (14, {})} | custom-call | flops 335544320 | bytes 2924544 | tf_op jit(solution)/shard_map/span_outputs/pallas_call | solution.py:319
  (23 shorter events, 1.9 us)
Async XLA Ops:
  3.1 10.4 %collective-permute-start.1 = (bf16[1,264,512]{2,1,0:T(8,128)(2,1)S(1)}, bf16[1,264,512]{2,1,0:T(8,128)(2,1)S(1)}, u32[]{:S(2)}, u32[]{:S(2)}) collective-permute-start(bf16[1,264,512]{2,1,0:T(8,128)(2,1)S(1)} %get-tuple-element.21.refs_8_), channel_id=1, source_target_pairs={{0,1},{1,0},{2,3},{3,2},{4,5},{5,4},{6,7},{7,6},{8,9},{9,8},{10,11... | collective-permute-start | bytes 811016 | tf_op jit(solution)/shard_map/ppermute | solution.py:37
  7.9 15.6 %collective-permute-start = (bf16[1,264,512]{2,1,0:T(8,128)(2,1)S(1)}, bf16[1,264,512]{2,1,0:T(8,128)(2,1)S(1)}, u32[]{:S(2)}, u32[]{:S(2)}) collective-permute-start(bf16[1,264,512]{2,1,0:T(8,128)(2,1)S(1)} %get-tuple-element.23.refs_2_), channel_id=1, source_target_pairs={{0,1},{1,0},{2,3},{3,2},{4,5},{5,4},{6,7},{7,6},{8,9},{9,8},{10,11... | collective-permute-start | bytes 811016 | tf_op jit(solution)/shard_map/ppermute | solution.py:37
  13.7 13.6 %collective-permute-start.4 = (bf16[1,264,512]{2,1,0:T(8,128)(2,1)S(1)}, bf16[1,264,512]{2,1,0:T(8,128)(2,1)S(1)}, u32[]{:S(2)}, u32[]{:S(2)}) collective-permute-start(bf16[1,264,512]{2,1,0:T(8,128)(2,1)S(1)} %combine.16.refs_8_), channel_id=1, source_target_pairs={{0,2},{1,3},{2,0},{3,1},{4,6},{5,7},{6,4},{7,5},{8,10},{9,11},{10,... | collective-permute-start | bytes 811016 | tf_op jit(solution)/shard_map/ppermute | solution.py:37
  27.5 1.6 %collective-permute-start.5 = (bf16[1,264,512]{2,1,0:T(8,128)(2,1)S(1)}, bf16[1,264,512]{2,1,0:T(8,128)(2,1)S(1)}, u32[]{:S(2)}, u32[]{:S(2)}) collective-permute-start(bf16[1,264,512]{2,1,0:T(8,128)(2,1)S(1)} %combine.18.refs_4_), channel_id=1, source_target_pairs={{0,4},{4,0},{8,12},{12,8},{1,5},{5,1},{9,13},{13,9},{2,6},{6,2},{1... | collective-permute-start | bytes 811016 | tf_op jit(solution)/shard_map/ppermute | solution.py:37
  27.5 10.6 %collective-permute-start.7 = (bf16[1,264,512]{2,1,0:T(8,128)(2,1)S(1)}, bf16[1,264,512]{2,1,0:T(8,128)(2,1)S(1)}, u32[]{:S(2)}, u32[]{:S(2)}) collective-permute-start(bf16[1,264,512]{2,1,0:T(8,128)(2,1)S(1)} %get-tuple-element.25.refs_2_), channel_id=1, source_target_pairs={{0,1},{1,0},{2,3},{3,2},{4,5},{5,4},{6,7},{7,6},{8,9},{9,8},{10,11... | collective-permute-start | bytes 811016 | tf_op jit(solution)/shard_map/ppermute | solution.py:37
  29.4 9.5 %collective-permute-start.6 = (bf16[1,264,512]{2,1,0:T(8,128)(2,1)S(1)}, bf16[1,264,512]{2,1,0:T(8,128)(2,1)S(1)}, u32[]{:S(2)}, u32[]{:S(2)}) collective-permute-start(bf16[1,264,512]{2,1,0:T(8,128)(2,1)S(1)} %combine.19.refs_2_), channel_id=1, source_target_pairs={{0,8},{4,12},{1,9},{5,13},{2,10},{6,14},{3,11},{7,15},{16,24},{20,... | collective-permute-start | bytes 811016 | tf_op jit(solution)/shard_map/ppermute | solution.py:37
  32.8 15.0 %collective-permute-start.3 = (bf16[1,264,512]{2,1,0:T(8,128)(2,1)S(1)}, bf16[1,264,512]{2,1,0:T(8,128)(2,1)S(1)}, u32[]{:S(2)}, u32[]{:S(2)}) collective-permute-start(bf16[1,264,512]{2,1,0:T(8,128)(2,1)S(1)} %combine.17.refs_8_), channel_id=1, source_target_pairs={{0,2},{1,3},{2,0},{3,1},{4,6},{5,7},{6,4},{7,5},{8,10},{9,11},{10,... | collective-permute-start | bytes 811016 | tf_op jit(solution)/shard_map/ppermute | solution.py:37
  48.1 1.6 %collective-permute-start.8 = (bf16[1,264,512]{2,1,0:T(8,128)(2,1)S(1)}, bf16[1,264,512]{2,1,0:T(8,128)(2,1)S(1)}, u32[]{:S(2)}, u32[]{:S(2)}) collective-permute-start(bf16[1,264,512]{2,1,0:T(8,128)(2,1)S(1)} %combine.22.refs_4_), channel_id=1, source_target_pairs={{0,4},{4,0},{8,12},{12,8},{1,5},{5,1},{9,13},{13,9},{2,6},{6,2},{1... | collective-permute-start | bytes 811016 | tf_op jit(solution)/shard_map/ppermute | solution.py:37
  48.2 12.6 %collective-permute-start.2 = (bf16[1,264,512]{2,1,0:T(8,128)(2,1)S(1)}, bf16[1,264,512]{2,1,0:T(8,128)(2,1)S(1)}, u32[]{:S(2)}, u32[]{:S(2)}) collective-permute-start(bf16[1,264,512]{2,1,0:T(8,128)(2,1)S(1)} %get-tuple-element.27.refs_3_), channel_id=1, source_target_pairs={{0,1},{1,0},{2,3},{3,2},{4,5},{5,4},{6,7},{7,6},{8,9},{9,8},{10,11... | collective-permute-start | bytes 811016 | tf_op jit(solution)/shard_map/ppermute | solution.py:37
  50.0 11.0 %collective-permute-start.11 = (bf16[1,264,512]{2,1,0:T(8,128)(2,1)S(1)}, bf16[1,264,512]{2,1,0:T(8,128)(2,1)S(1)}, u32[]{:S(2)}, u32[]{:S(2)}) collective-permute-start(bf16[1,264,512]{2,1,0:T(8,128)(2,1)S(1)} %combine.23.refs_2_.refs_14_), channel_id=1, source_target_pairs={{0,8},{4,12},{1,9},{5,13},{2,10},{6,14},{3,11},{7,15},{16,24},{20,... | collective-permute-start | bytes 811016 | tf_op jit(solution)/shard_map/ppermute | solution.py:37
  51.6 15.1 %collective-permute-start.10 = (bf16[1,264,512]{2,1,0:T(8,128)(2,1)S(1)}, bf16[1,264,512]{2,1,0:T(8,128)(2,1)S(1)}, u32[]{:S(2)}, u32[]{:S(2)}) collective-permute-start(bf16[1,264,512]{2,1,0:T(8,128)(2,1)S(1)} %combine.20.refs_4_), channel_id=1, source_target_pairs={{0,2},{1,3},{2,0},{3,1},{4,6},{5,7},{6,4},{7,5},{8,10},{9,11},{10,... | collective-permute-start | bytes 811016 | tf_op jit(solution)/shard_map/ppermute | solution.py:37
  66.8 1.6 %collective-permute-start.12 = (bf16[1,264,512]{2,1,0:T(8,128)(2,1)S(1)}, bf16[1,264,512]{2,1,0:T(8,128)(2,1)S(1)}, u32[]{:S(2)}, u32[]{:S(2)}) collective-permute-start(bf16[1,264,512]{2,1,0:T(8,128)(2,1)S(1)} %combine.26.refs_4_), channel_id=1, source_target_pairs={{0,4},{4,0},{8,12},{12,8},{1,5},{5,1},{9,13},{13,9},{2,6},{6,2},{1... | collective-permute-start | bytes 811016 | tf_op jit(solution)/shard_map/ppermute | solution.py:37
  68.7 7.6 %collective-permute-start.13 = (bf16[1,264,512]{2,1,0:T(8,128)(2,1)S(1)}, bf16[1,264,512]{2,1,0:T(8,128)(2,1)S(1)}, u32[]{:S(2)}, u32[]{:S(2)}) collective-permute-start(bf16[1,264,512]{2,1,0:T(8,128)(2,1)S(1)} %combine.27.refs_4_.refs_15_), channel_id=1, source_target_pairs={{0,8},{4,12},{1,9},{5,13},{2,10},{6,14},{3,11},{7,15},{16,24},{20,... | collective-permute-start | bytes 811016 | tf_op jit(solution)/shard_map/ppermute | solution.py:37
  70.3 15.0 %collective-permute-start.9 = (bf16[1,264,512]{2,1,0:T(8,128)(2,1)S(1)}, bf16[1,264,512]{2,1,0:T(8,128)(2,1)S(1)}, u32[]{:S(2)}, u32[]{:S(2)}) collective-permute-start(bf16[1,264,512]{2,1,0:T(8,128)(2,1)S(1)} %combine.24.refs_4_), channel_id=1, source_target_pairs={{0,2},{1,3},{2,0},{3,1},{4,6},{5,7},{6,4},{7,5},{8,10},{9,11},{10,... | collective-permute-start | bytes 811016 | tf_op jit(solution)/shard_map/ppermute | solution.py:37
  76.6 22.0 %copy-start = (bf16[256,4096]{1,0:T(8,128)(2,1)S(1)}, bf16[256,4096]{1,0:T(8,128)(2,1)}, u32[]{:S(2)}) copy-start(bf16[256,4096]{1,0:T(8,128)(2,1)} %refs_8_.7) | copy-start | bytes 6291460
  76.6 22.0 %copy-start.1 = (bf16[256,2048]{1,0:T(8,128)(2,1)S(1)}, bf16[256,2048]{1,0:T(8,128)(2,1)}, u32[]{:S(2)}) copy-start(bf16[256,2048]{1,0:T(8,128)(2,1)} %refs_7_.13) | copy-start | bytes 3145732
  76.6 22.0 %copy-start.2 = (bf16[256,2048]{1,0:T(8,128)(2,1)S(1)}, bf16[256,2048]{1,0:T(8,128)(2,1)}, u32[]{:S(2)}) copy-start(bf16[256,2048]{1,0:T(8,128)(2,1)} %refs_6_.13) | copy-start | bytes 3145732
  85.5 1.6 %collective-permute-start.14 = (bf16[1,264,512]{2,1,0:T(8,128)(2,1)S(1)}, bf16[1,264,512]{2,1,0:T(8,128)(2,1)S(1)}, u32[]{:S(2)}, u32[]{:S(2)}) collective-permute-start(bf16[1,264,512]{2,1,0:T(8,128)(2,1)S(1)} %combine.29.refs_4_), channel_id=1, source_target_pairs={{0,4},{4,0},{8,12},{12,8},{1,5},{5,1},{9,13},{13,9},{2,6},{6,2},{1... | collective-permute-start | bytes 811016 | tf_op jit(solution)/shard_map/ppermute | solution.py:37
  87.4 7.6 %collective-permute-start.15 = (bf16[1,264,512]{2,1,0:T(8,128)(2,1)S(1)}, bf16[1,264,512]{2,1,0:T(8,128)(2,1)S(1)}, u32[]{:S(2)}, u32[]{:S(2)}) collective-permute-start(bf16[1,264,512]{2,1,0:T(8,128)(2,1)S(1)} %combine.30.refs_4_.refs_15_), channel_id=1, source_target_pairs={{0,8},{4,12},{1,9},{5,13},{2,10},{6,14},{3,11},{7,15},{16,24},{20,... | collective-permute-start | bytes 811016 | tf_op jit(solution)/shard_map/ppermute | solution.py:37
  89.2 9.4 %collective-permute-start.19 = (bf16[1,264,512]{2,1,0:T(8,128)(2,1)S(1)}, bf16[1,264,512]{2,1,0:T(8,128)(2,1)S(1)}, u32[]{:S(2)}, u32[]{:S(2)}) collective-permute-start(bf16[1,264,512]{2,1,0:T(8,128)(2,1)S(1)} %combine.21.refs_3_), channel_id=1, source_target_pairs={{0,1},{1,0},{2,3},{3,2},{4,5},{5,4},{6,7},{7,6},{8,9},{9,8},{10,11... | collective-permute-start | bytes 811016 | tf_op jit(solution)/shard_map/ppermute | solution.py:37
  89.2 15.1 %collective-permute-start.18 = (bf16[1,264,512]{2,1,0:T(8,128)(2,1)S(1)}, bf16[1,264,512]{2,1,0:T(8,128)(2,1)S(1)}, u32[]{:S(2)}, u32[]{:S(2)}) collective-permute-start(bf16[1,264,512]{2,1,0:T(8,128)(2,1)S(1)} %combine.25.refs_3_), channel_id=1, source_target_pairs={{0,1},{1,0},{2,3},{3,2},{4,5},{5,4},{6,7},{7,6},{8,9},{9,8},{10,11... | collective-permute-start | bytes 811016 | tf_op jit(solution)/shard_map/ppermute | solution.py:37
  91.3 18.9 %collective-permute-start.17 = (bf16[1,264,512]{2,1,0:T(8,128)(2,1)S(1)}, bf16[1,264,512]{2,1,0:T(8,128)(2,1)S(1)}, u32[]{:S(2)}, u32[]{:S(2)}) collective-permute-start(bf16[1,264,512]{2,1,0:T(8,128)(2,1)S(1)} %combine.28.refs_3_), channel_id=1, source_target_pairs={{0,1},{1,0},{2,3},{3,2},{4,5},{5,4},{6,7},{7,6},{8,9},{9,8},{10,11... | collective-permute-start | bytes 811016 | tf_op jit(solution)/shard_map/ppermute | solution.py:37
  95.3 19.6 %collective-permute-start.16 = (bf16[1,264,512]{2,1,0:T(8,128)(2,1)S(1)}, bf16[1,264,512]{2,1,0:T(8,128)(2,1)S(1)}, u32[]{:S(2)}, u32[]{:S(2)}) collective-permute-start(bf16[1,264,512]{2,1,0:T(8,128)(2,1)S(1)} %combine.31.refs_15_), channel_id=1, source_target_pairs={{0,1},{1,0},{2,3},{3,2},{4,5},{5,4},{6,7},{7,6},{8,9},{9,8},{10,11... | collective-permute-start | bytes 811016 | tf_op jit(solution)/shard_map/ppermute | solution.py:37

commit v4 on v3

--- a/solution.py
+++ b/solution.py
@@ -15,8 +15,11 @@
 NEG_FILL = -1e30
 TAIL = 8
 ROWS = DK + TAIL
-CHUNKS = (1, 1, 1, 1)
-AHEAD, DUE, GAP = 2, (8.0, 24.0, 26.5, 34.0, 42.0), 12.0
+CHUNKS = ((0, 0, DV), (1, 0, DV), (2, 0, DV), (3, 0, DV))
+ORDER = (
+    (0, 0), (0, 1), (1, 0), (0, 2), (1, 1), (0, 3), (2, 0), (1, 2), (2, 1), (3, 0), (1, 3), (4, 0),
+    (3, 1), (2, 2), (3, 2), (4, 1), (2, 3), (3, 3), (4, 2), (5, 0), (4, 3), (5, 1), (5, 2), (5, 3),
+)
 
 F32 = jnp.float32
 BF16 = jnp.bfloat16
@@ -78,16 +81,16 @@
     return jnp.sum(jnp.where(lane == h, x, 0.0), axis=1, keepdims=True)
 
 
-def dequant(ref, at, width, tensor_id, h, scales, tensors, offsets, bits):
+def dequant(ref, at, lo, width, full, tensor_id, h, scales, tensors, offsets, bits):
     rows = ref.shape[0]
     row = lax.broadcasted_iota(jnp.int32, (BLK, 1), 0)
-    col = lax.broadcasted_iota(jnp.int32, (1, width), 1)
+    col = lax.broadcasted_iota(jnp.int32, (1, width), 1) + lo
     out = []
     for b in range(rows // BLK):
-        x = ref[b * BLK : (b + 1) * BLK, pl.ds(at, width)].astype(F32)
+        x = ref[b * BLK : (b + 1) * BLK, pl.ds(pl.multiple_of(at + lo, 128), width)].astype(F32)
         offset, scale = offsets[b, h], scales[tensor_id, b, h]
         hit_row = jnp.where(tensors[b, h] == tensor_id, offset // DV, -1)
-        hit_col = (offset % DV) % width
+        hit_col = (offset % DV) % full
         flipped = -(lax.shift_left(jnp.int32(1), bits[b, h]).astype(F32)) * scale
         out.append((x * jnp.where((row == hit_row) & (col == hit_col), flipped, scale)).astype(BF16))
     return jnp.concatenate(out, axis=0)
@@ -100,26 +103,27 @@
 
 
 def pack_tail(normer, peak, total):
-    high, middle, least = split(normer)
-    rows = [jnp.concatenate([high, middle], axis=1), jnp.concatenate([least, jnp.zeros_like(least)], axis=1)]
+    width = peak.shape[1]
+    blank = jnp.zeros((1, width - DK), F32)
+    rows = [jnp.concatenate([x, blank], axis=1) if width > DK else x for x in split(normer)[:2]]
     rows += [*split(peak), *split(total)]
-    at = lax.broadcasted_iota(jnp.int32, (TAIL, DV), 0)
-    out = jnp.zeros((TAIL, DV), F32)
+    at = lax.broadcasted_iota(jnp.int32, (TAIL, width), 0)
+    out = jnp.zeros((TAIL, width), F32)
     for r, value in enumerate(rows):
         out = jnp.where(at == r, value, out)
     return out.astype(BF16)
 
 
 class State:
-    def __init__(self, ref, i):
-        self.ref, self.i = ref, i
-        t = ref[i, DK:ROWS, :].astype(F32)
-        self.normer = t[0:1, :DK] + t[0:1, DK : 2 * DK] + t[1:2, :DK]
+    def __init__(self, ref):
+        self.ref = ref
+        t = ref[DK:ROWS, :].astype(F32)
+        self.normer = t[0:1, :DK] + t[1:2, :DK]
         self.peak = t[2:3] + t[3:4] + t[4:5]
         self.total = t[5:6] + t[6:7] + t[7:8]
 
     def matrix(self):
-        return self.ref[self.i, :DK, :]
+        return self.ref[:DK, :]
 
 
 def joined(early, late):
@@ -185,47 +189,46 @@
 VMEM = pl.BlockSpec(memory_space=pltpu.VMEM)
 
 
-def state_kernel(first, scales, tensors, offsets, fbits, mf, weight_ref, k_ref, v_ref, keep_ref, send_ref):
+def state_kernel(pair, lo, scales, tensors, offsets, fbits, mf, weight_ref, k_ref, v_ref, keep_ref, send_ref):
     own = lax.axis_index("head") & 1
-    i = pl.program_id(0)
+    width = keep_ref.shape[1]
     for out_ref, side in ((send_ref, 1 - own), (keep_ref, own)):
-        h = 2 * (first + i) + side
+        h = 2 * pair + side
         info = (h, scales, tensors, offsets, fbits)
-        k = dequant(k_ref, pl.multiple_of(side * DK, DK), DK, 1, *info)
-        v = dequant(v_ref, pl.multiple_of(side * DV, DV), DV, 2, *info)
+        k = dequant(k_ref, pl.multiple_of(side * DK, DK), 0, DK, DK, 1, *info)
+        v = dequant(v_ref, pl.multiple_of(side * DV, DV), lo, width, DV, 2, *info)
         weighted = (k.astype(F32) * pick(weight_ref, h)).astype(BF16)
         matrix = lax.dot_general(weighted, v, (((0,), (0,)), ((), ())), preferred_element_type=F32)
-        out_ref[0, :DK, :] = matrix.astype(BF16)
+        out_ref[:DK, :] = matrix.astype(BF16)
         normer = jnp.sum(weighted.astype(F32), axis=0, keepdims=True)
-        out_ref[0, DK:ROWS, :] = pack_tail(normer, jnp.full((1, DV), mf[0, h], F32), jnp.full((1, DV), mf[1, h], F32))
+        peak, total = jnp.full((1, width), mf[0, h], F32), jnp.full((1, width), mf[1, h], F32)
+        out_ref[DK:ROWS, :] = pack_tail(normer, peak, total)
 
 
 def whole(shape):
     return pl.BlockSpec(shape, lambda i: (0,) * len(shape))
 
 
-STATE = pl.BlockSpec((1, ROWS, DV), lambda i: (i, 0, 0))
-
-
-def span_states(first, count, small, mf, weight, key_codes, value_codes, after):
+def span_states(chunk, small, mf, weight, key_codes, value_codes, after):
+    pair, lo, width = chunk
     rows = key_codes.shape[0]
-    out = jax.ShapeDtypeStruct((count, ROWS, DV), BF16)
-    kernel, extra, extra_specs = ordered(functools.partial(state_kernel, first), 8, after)
+    out = jax.ShapeDtypeStruct((ROWS, width), BF16)
+    kernel, extra, extra_specs = ordered(functools.partial(state_kernel, pair, lo), 8, after)
     return pl.pallas_call(
         kernel,
-        grid=(count,),
+        grid=(1,),
         in_specs=[SMEM] * 5
         + [
             whole(weight.shape),
-            pl.BlockSpec((rows, 2 * DK), lambda i: (0, first + i)),
-            pl.BlockSpec((rows, 2 * DV), lambda i: (0, first + i)),
+            pl.BlockSpec((rows, 2 * DK), lambda i: (0, pair)),
+            pl.BlockSpec((rows, 2 * DV), lambda i: (0, pair)),
         ]
         + extra_specs,
-        out_specs=(STATE, STATE),
+        out_specs=(whole(out.shape),) * 2,
         out_shape=(out, out),
         compiler_params=pltpu.CompilerParams(vmem_limit_bytes=12 << 20),
         cost_estimate=pl.CostEstimate(
-            flops=count * 4 * rows * DK * DV, bytes_accessed=count * rows * 2 * (2 * DK + 4 * DV), transcendentals=0
+            flops=4 * rows * DK * width, bytes_accessed=rows * 2 * (2 * DK + 4 * DV), transcendentals=0
         ),
         name="span_states",
     )(*small, mf, weight, key_codes, value_codes, *extra)
@@ -234,59 +237,63 @@
 def combine_kernel(head_bits, bits, last, *refs):
     parts, out_ref = refs[:-1], refs[-1]
     bit = device_bits(head_bits, bits)
-    for i in range(out_ref.shape[0]):
-        states = [State(ref, i) for ref in parts]
-        if last:
-            weights, peak, total = start_weights(bit, jnp.logical_not(bit[0]), states[0], states[1:])
-        else:
-            weights, peak, total = group_weights(bit, states[0], states[1:])
-        matrix, normer = weighted_sum(weights, states)
-        out_ref[i, :DK, :] = matrix.astype(BF16)
-        out_ref[i, DK:ROWS, :] = pack_tail(normer, peak, total)
+    states = [State(ref) for ref in parts]
+    if last:
+        weights, peak, total = start_weights(bit, jnp.logical_not(bit[0]), states[0], states[1:])
+    else:
+        weights, peak, total = group_weights(bit, states[0], states[1:])
+    matrix, normer = weighted_sum(weights, states)
+    out_ref[:DK, :] = matrix.astype(BF16)
+    out_ref[DK:ROWS, :] = pack_tail(normer, peak, total)
 
 
 def combine(head_bits, bits, last, parts, after):
-    count = parts[0].shape[0]
+    size = parts[0].size
     kernel, extra, extra_specs = ordered(functools.partial(combine_kernel, head_bits, bits, last), len(parts), after)
     return pl.pallas_call(
         kernel,
         in_specs=[VMEM] * len(parts) + extra_specs,
         out_specs=VMEM,
-        out_shape=jax.ShapeDtypeStruct((count, ROWS, DV), BF16),
+        out_shape=jax.ShapeDtypeStruct(parts[0].shape, BF16),
         compiler_params=pltpu.CompilerParams(vmem_limit_bytes=8 << 20),
         cost_estimate=pl.CostEstimate(
-            flops=count * ROWS * DV * 2 * len(parts), bytes_accessed=count * ROWS * DV * 2 * (len(parts) + 1), transcendentals=0
+            flops=size * 2 * len(parts), bytes_accessed=size * 2 * (len(parts) + 1), transcendentals=0
         ),
         name="combine",
     )(*parts, *extra)
 
 
 def output_kernel(
-    head_bits, bits, first, scales, tensors, offsets, fbits, run_ref, shift_ref, q_ref, k_ref, v_ref, back_ref, *rest
+    head_bits, bits, pair, pieces, scales, tensors, offsets, fbits, run_ref, shift_ref, q_ref, k_ref, v_ref, *rest
 ):
-    parts, out_ref = rest[:bits], rest[-1]
+    groups = [rest[p * (bits + 1) : (p + 1) * (bits + 1)] for p in range(pieces)]
+    out_ref, token_ref = rest[-2:]
+    token_ref[...] = jnp.zeros_like(token_ref)
     bit = device_bits(head_bits, bits)
     own = lax.axis_index("head") & 1
-    i = pl.program_id(0)
     factor = 1.0 / math.sqrt(DK)
     size = q_ref.shape[0]
     row = lax.broadcasted_iota(jnp.int32, (size, size), 0)
     col = lax.broadcasted_iota(jnp.int32, (size, size), 1)
     for side, mine in ((own, True), (1 - own, False)):
-        h = 2 * (first + i) + side
+        h = 2 * pair + side
         info = (h, scales, tensors, offsets, fbits)
-        if mine:
-            states = [State(ref, 0) for ref in parts]
-            weights, peak, _ = start_weights(bit, None, None, states)
-            start, normer = weighted_sum(weights, states)
-            start = start.astype(BF16)
-        else:
-            back = State(back_ref, 0)
-            start, normer, peak = back.matrix(), back.normer, back.peak
+        starts = []
+        for back_ref, *parts in groups:
+            if mine:
+                states = [State(ref) for ref in parts]
+                weights, peak, _ = start_weights(bit, None, None, states)
+                start, normer = weighted_sum(weights, states)
+                starts.append(start.astype(BF16))
+            else:
+                back = State(back_ref)
+                normer, peak = back.normer, back.peak
+                starts.append(back.matrix())
+        start = jnp.concatenate(starts, axis=1) if pieces > 1 else starts[0]
         narrow, wide = pl.multiple_of(side * DK, DK), pl.multiple_of(side * DV, DV)
-        q = dequant(q_ref, narrow, DK, 0, *info)
-        k = dequant(k_ref, narrow, DK, 1, *info)
-        v = dequant(v_ref, wide, DV, 2, *info)
+        q = dequant(q_ref, narrow, 0, DK, DK, 0, *info)
+        k = dequant(k_ref, narrow, 0, DK, DK, 1, *info)
+        v = dequant(v_ref, wide, 0, DV, DV, 2, *info)
         run = pick(run_ref, h)
         exponent = jnp.where(row >= col, run + shift_ref[pl.ds(h, 1), :], NEG_FILL)
         inter = run + peak[:, :1]
@@ -303,31 +310,35 @@
         out_ref[:, pl.ds(wide, DV)] = (numerator / jnp.maximum(jnp.abs(denominator), 1.0)).astype(BF16)
 
 
-def span_outputs(head_bits, bits, first, small, run, shift, codes, back, parts, before, after):
+def span_outputs(head_bits, bits, pair, small, run, shift, codes, groups, before, after):
     q, k, v = codes
-    count, rows = back.shape[0], q.shape[0]
-    narrow = pl.BlockSpec((rows, 2 * DK), lambda i: (0, first + i))
-    wide = pl.BlockSpec((rows, 2 * DV), lambda i: (0, first + i))
-    operands = [*small, run, shift, q, k, v, back, *parts]
-    in_specs = [SMEM] * 4 + [whole(run.shape), whole(shift.shape)] + [narrow, narrow, wide, STATE] + [STATE] * len(parts)
+    rows = q.shape[0]
+    narrow = pl.BlockSpec((rows, 2 * DK), lambda i: (0, pair))
+    wide = pl.BlockSpec((rows, 2 * DV), lambda i: (0, pair))
+    states = [x for group in groups for x in group]
+    operands = [*small, run, shift, q, k, v, *states]
+    in_specs = [SMEM] * 4 + [whole(run.shape), whole(shift.shape), narrow, narrow, wide]
+    in_specs += [whole(x.shape) for x in states]
     aliases = {}
     if before is not None:
         aliases = {len(operands): 0}
         operands.append(before)
         in_specs.append(pl.BlockSpec(memory_space=pl.ANY))
-    kernel, extra, extra_specs = ordered(functools.partial(output_kernel, head_bits, bits, first), len(operands), after)
+    kernel, extra, extra_specs = ordered(
+        functools.partial(output_kernel, head_bits, bits, pair, len(groups)), len(operands), after
+    )
     return pl.pallas_call(
         kernel,
-        grid=(count,),
+        grid=(1,),
         in_specs=in_specs + extra_specs,
-        out_specs=wide,
-        out_shape=jax.ShapeDtypeStruct(v.shape, BF16),
+        out_specs=(wide, whole((8, 128))),
+        out_shape=(jax.ShapeDtypeStruct(v.shape, BF16), jax.ShapeDtypeStruct((8, 128), F32)),
         input_output_aliases=aliases,
         compiler_params=pltpu.CompilerParams(vmem_limit_bytes=16 << 20),
         cost_estimate=pl.CostEstimate(
-            flops=count * 4 * rows * (rows * DK + rows * DV + DK * DV),
-            bytes_accessed=count * (rows * 2 * (4 * DK + 4 * DV) + ROWS * DV * 2 * (1 + len(parts))),
-            transcendentals=count * 2 * rows * rows,
+            flops=4 * rows * (rows * DK + rows * DV + DK * DV),
+            bytes_accessed=rows * 2 * (4 * DK + 4 * DV) + sum(x.size for x in states) * 2,
+            transcendentals=2 * rows * rows,
         ),
         name="span_outputs",
     )(*operands, *extra)
@@ -348,26 +359,24 @@
 ):
     bits = head_bits + ctx_bits
     assert query_codes.shape[0] == CH
+    assert sum(width for _, _, width in CHUNKS) * 2 == value_codes.shape[1]
     small = tuple(in_hbm(x) for x in (block_scales.transpose(1, 0, 2), fault_tensor, fault_offset, fault_bit))
     codes = (query_codes, key_codes, value_codes)
     exchange = functools.partial(flip, head_bits=head_bits, ctx_bits=ctx_bits)
     run, weight, shift, mf = gates(in_hbm(input_gate.T), in_hbm(forget_gate.T))
-
-    starts = [sum(CHUNKS[:c]) for c in range(len(CHUNKS))]
-    assert 2 * sum(CHUNKS) == input_gate.shape[1]
     keys, values = in_hbm(key_codes), in_hbm(value_codes)
     keep, got, back = {}, {}, {}
     out = token = None
-    for stage, c in order(len(CHUNKS), bits):
-        first, count = starts[c], CHUNKS[c]
+    for stage, c in order(bits):
         if stage == 0:
-            keep[c], token = span_states(first, count, small, mf, weight, keys, values, token)
+            keep[c], token = span_states(CHUNKS[c], small, mf, weight, keys, values, token)
         elif stage < bits:
             token = combine(head_bits, bits, False, [keep[c], *got[c]], token)
         elif stage == bits:
             token = combine(head_bits, bits, True, [keep[c], *got[c][1:]], token)
         else:
-            out = span_outputs(head_bits, bits, first, small, run, shift, codes, back[c], got[c], out, token)
+            groups = [[back[d], *got[d]] for d in of_pair(c)]
+            out, token = span_outputs(head_bits, bits, c, small, run, shift, codes, groups, out, token)
         if stage < bits:
             got.setdefault(c, []).append(exchange(token, stage, last=stage == bits - 1))
         elif stage == bits:
@@ -375,16 +384,13 @@
     return out
 
 
-def order(chunks, bits):
-    def due(step):
-        stage, c = step
-        if stage == 0:
-            return 0.1 * c if c < AHEAD else DUE[0] + GAP * (c - AHEAD) + 0.5
-        late = bits + 1 - stage
-        at = DUE[stage - 1] if stage <= 2 else DUE[4] if late == 0 else DUE[3] if late == 1 else DUE[2] + 0.01 * stage
-        return at + GAP * c
-
-    return sorted([(stage, c) for c in range(chunks) for stage in range(bits + 2)], key=due)
+def of_pair(pair):
+    return [c for c, chunk in enumerate(CHUNKS) if chunk[0] == pair]
+
+
+def order(bits):
+    stages = {0: [0], 1: [1], 2: range(2, bits - 1), 3: [bits - 1], 4: [bits], 5: [bits + 1]}
+    return [(stage, c) for place, c in ORDER for stage in stages[place]]
 
 
 def solution(mesh):

time: 118 us -> 106 us (0.90)
  waiting for transfers between devices: 71 us -> 60 us
    ppermute x20, waiting for transfers between devices: 71 us -> 60 us  [flip(): return lax.ppermute(x, axis, pairs)]
  transfers between devices with their start and end apart: 20 -> 20, of which waited for: 19 -> 17; matrix products, arithmetic and copies ran while one was open for 0% -> 0% of each run, Pallas kernels for 13% -> 16%
where the time goes in v4:
time: 106 us; the launch traced here: 105 us
  waiting for transfers between devices  60 us (57%)
  starting transfers between devices  22.6 us (21%)
  Pallas kernels  22.5 us (21%)
    ppermute x20, waiting for transfers between devices, flip(): return lax.ppermute(x, axis, pairs)  60 us
    ppermute x20, starting transfers between devices, flip(): return lax.ppermute(x, axis, pairs)  22.6 us
    pallas_call x4, Pallas kernels, span_outputs(): pl.pallas_call(kernel, grid=(1,), in_specs=in_specs + extra_specs, out_sp...  10.8 us
    pallas_call x4, Pallas kernels, span_states(): pl.pallas_call(kernel, grid=(1,), in_specs=[SMEM] * 5 + [whole(weight.sha...  6.86 us
    pallas_call x16, Pallas kernels, combine(): pl.pallas_call(kernel, in_specs=[VMEM] * len(parts) + extra_specs, out_sp...  3.48 us
  transfers between devices with their start and end apart: 20, of which 17 were waited for; matrix products, arithmetic and copies ran while one was open for 0% of the time, Pallas kernels for 16%

profile of v4, /device:TPU:0, one launch (start us, length us, event | category | flops | bytes accessed | tf_op | source)
XLA Modules:
  0.0 105.4 jit_solution(18004072101212047785)
XLA Ops:
  0.0 1.3 %gates.1 = (f32[256,8]{1,0:T(8,128)S(1)}, f32[256,8]{1,0:T(8,128)S(1)}, f32[8,256]{1,0:T(8,128)S(1)}, f32[2,8]{1,0:T(2,128)S(1)}) custom-call(bf16[8,256]{1,0:T(8,128)(2,1)} %bitcast.11, bf16[8,256]{1,0:T(8,128)(2,1)} %bitcast.12), custom_call_target="tpu_custom_call" | custom-call | flops 1048576 | bytes 1048576 | tf_op jit(solution)/shard_map/gates/pallas_call | solution.py:69
  1.3 1.7 %span_states.4 = (bf16[264,512]{1,0:T(8,128)(2,1)S(1)}, bf16[264,512]{1,0:T(8,128)(2,1)S(1)}) custom-call(f32[3,2,8]{2,1,0:T(2,128)} %bitcast.3, s32[2,8]{1,0:T(2,128)} %refs_1_.13, s32[2,8]{1,0:T(2,128)} %refs_2_.13, s32[2,8]{1,0:T(2,128)} %refs_3_.13, f32[2,8]{1,0:T(2,128)S(1)} %get-tuple-element.26.mf.refs_4_, ...), custom_call_target="tpu_custom_call" | custom-call | flops 134217728 | bytes 1310720 | tf_op jit(solution)/shard_map/span_states/pallas_call | solution.py:217
  3.1 3.1 %collective-permute-start.1 = (bf16[264,512]{1,0:T(8,128)(2,1)S(1)}, bf16[264,512]{1,0:T(8,128)(2,1)S(1)}, u32[]{:S(2)}, u32[]{:S(2)}) collective-permute-start(bf16[264,512]{1,0:T(8,128)(2,1)S(1)} %get-tuple-element.28.refs_8_), channel_id=1, source_target_pairs={{0,1},{1,0},{2,3},{3,2},{4,5},{5,4},{6,7},{7,6},{8,9},{9,8},{10,11... | collective-permute-start | bytes 811016 | tf_op jit(solution)/shard_map/ppermute | solution.py:40
  6.2 1.7 %span_states.5 = (bf16[264,512]{1,0:T(8,128)(2,1)S(1)}, bf16[264,512]{1,0:T(8,128)(2,1)S(1)}) custom-call(f32[3,2,8]{2,1,0:T(2,128)} %bitcast.4, s32[2,8]{1,0:T(2,128)} %refs_1_.13, s32[2,8]{1,0:T(2,128)} %refs_2_.13, s32[2,8]{1,0:T(2,128)} %refs_3_.13, f32[2,8]{1,0:T(2,128)S(1)} %get-tuple-element.26.mf.refs_4_, ...), custom_call_target="tpu_custom_call" | custom-call | flops 134217728 | bytes 1310720 | tf_op jit(solution)/shard_map/span_states/pallas_call | solution.py:217
  8.0 5.5 %collective-permute-done.1.refs_1_.refs_10_ = bf16[264,512]{1,0:T(8,128)(2,1)S(1)} collective-permute-done((bf16[264,512]{1,0:T(8,128)(2,1)S(1)}, bf16[264,512]{1,0:T(8,128)(2,1)S(1)}, u32[]{:S(2)}, u32[]{:S(2)}) %collective-permute-start.1) | collective-permute-done | bytes 270368 | tf_op jit(solution)/shard_map/ppermute | solution.py:40
  13.7 3.1 %collective-permute-start.3 = (bf16[264,512]{1,0:T(8,128)(2,1)S(1)}, bf16[264,512]{1,0:T(8,128)(2,1)S(1)}, u32[]{:S(2)}, u32[]{:S(2)}) collective-permute-start(bf16[264,512]{1,0:T(8,128)(2,1)S(1)} %combine.16.refs_8_), channel_id=1, source_target_pairs={{0,2},{1,3},{2,0},{3,1},{4,6},{5,7},{6,4},{7,5},{8,10},{9,11},{10,... | collective-permute-start | bytes 811016 | tf_op jit(solution)/shard_map/ppermute | solution.py:40
  16.7 1.7 %span_states.6 = (bf16[264,512]{1,0:T(8,128)(2,1)S(1)}, bf16[264,512]{1,0:T(8,128)(2,1)S(1)}) custom-call(f32[3,2,8]{2,1,0:T(2,128)} %bitcast.5, s32[2,8]{1,0:T(2,128)} %refs_1_.13, s32[2,8]{1,0:T(2,128)} %refs_2_.13, s32[2,8]{1,0:T(2,128)} %refs_3_.13, f32[2,8]{1,0:T(2,128)S(1)} %get-tuple-element.26.mf.refs_4_, ...), custom_call_target="tpu_custom_call" | custom-call | flops 134217728 | bytes 1310720 | tf_op jit(solution)/shard_map/span_states/pallas_call | solution.py:217
  18.5 1.6 %collective-permute-start.6 = (bf16[264,512]{1,0:T(8,128)(2,1)S(1)}, bf16[264,512]{1,0:T(8,128)(2,1)S(1)}, u32[]{:S(2)}, u32[]{:S(2)}) collective-permute-start(bf16[264,512]{1,0:T(8,128)(2,1)S(1)} %get-tuple-element.32.refs_2_), channel_id=1, source_target_pairs={{0,1},{1,0},{2,3},{3,2},{4,5},{5,4},{6,7},{7,6},{8,9},{9,8},{10,11... | collective-permute-start | bytes 811016 | tf_op jit(solution)/shard_map/ppermute | solution.py:40
  20.1 4.3 %collective-permute-done.refs_1_.refs_10_ = bf16[264,512]{1,0:T(8,128)(2,1)S(1)} collective-permute-done((bf16[264,512]{1,0:T(8,128)(2,1)S(1)}, bf16[264,512]{1,0:T(8,128)(2,1)S(1)}, u32[]{:S(2)}, u32[]{:S(2)}) %collective-permute-start) | collective-permute-done | bytes 270368 | tf_op jit(solution)/shard_map/ppermute | solution.py:40
  24.6 1.7 %span_states.7 = (bf16[264,512]{1,0:T(8,128)(2,1)S(1)}, bf16[264,512]{1,0:T(8,128)(2,1)S(1)}) custom-call(f32[3,2,8]{2,1,0:T(2,128)} %bitcast.6, s32[2,8]{1,0:T(2,128)} %refs_1_.13, s32[2,8]{1,0:T(2,128)} %refs_2_.13, s32[2,8]{1,0:T(2,128)} %refs_3_.13, f32[2,8]{1,0:T(2,128)S(1)} %get-tuple-element.26.mf.refs_4_, ...), custom_call_target="tpu_custom_call" | custom-call | flops 134217728 | bytes 1310720 | tf_op jit(solution)/shard_map/span_states/pallas_call | solution.py:217
  26.3 0.9 collective-permute-done.3.refs_2_.refs_1_.refs_11_
  27.2 0.2 combine.18.refs_2_
  27.5 3.2 %collective-permute-start.2 = (bf16[264,512]{1,0:T(8,128)(2,1)S(1)}, bf16[264,512]{1,0:T(8,128)(2,1)S(1)}, u32[]{:S(2)}, u32[]{:S(2)}) collective-permute-start(bf16[264,512]{1,0:T(8,128)(2,1)S(1)} %get-tuple-element.34.refs_3_), channel_id=1, source_target_pairs={{0,1},{1,0},{2,3},{3,2},{4,5},{5,4},{6,7},{7,6},{8,9},{9,8},{10,11... | collective-permute-start | bytes 811016 | tf_op jit(solution)/shard_map/ppermute | solution.py:40
  30.7 5.3 %collective-permute-done.6.refs_1_.refs_10_ = bf16[264,512]{1,0:T(8,128)(2,1)S(1)} collective-permute-done((bf16[264,512]{1,0:T(8,128)(2,1)S(1)}, bf16[264,512]{1,0:T(8,128)(2,1)S(1)}, u32[]{:S(2)}, u32[]{:S(2)}) %collective-permute-start.6) | collective-permute-done | bytes 270368 | tf_op jit(solution)/shard_map/ppermute | solution.py:40
  36.1 2.4 %collective-permute-done.5.refs_2_.refs_1_.refs_11_ = bf16[264,512]{1,0:T(8,128)(2,1)S(1)} collective-permute-done((bf16[264,512]{1,0:T(8,128)(2,1)S(1)}, bf16[264,512]{1,0:T(8,128)(2,1)S(1)}, u32[]{:S(2)}, u32[]{:S(2)}) %collective-permute-start.5) | collective-permute-done | bytes 270368 | tf_op jit(solution)/shard_map/ppermute | solution.py:40
  38.5 0.2 combine.20.refs_4_
  38.7 0.3 combine.21.refs_2_
  39.0 3.5 %collective-permute-start.9 = (bf16[264,512]{1,0:T(8,128)(2,1)S(1)}, bf16[264,512]{1,0:T(8,128)(2,1)S(1)}, u32[]{:S(2)}, u32[]{:S(2)}) collective-permute-start(bf16[264,512]{1,0:T(8,128)(2,1)S(1)} %combine.21.refs_2_), channel_id=1, source_target_pairs={{0,8},{4,12},{1,9},{5,13},{2,10},{6,14},{3,11},{7,15},{16,24},{20,... | collective-permute-start | bytes 811016 | tf_op jit(solution)/shard_map/ppermute | solution.py:40
  42.6 1.1 %collective-permute-start.11 = (bf16[264,512]{1,0:T(8,128)(2,1)S(1)}, bf16[264,512]{1,0:T(8,128)(2,1)S(1)}, u32[]{:S(2)}, u32[]{:S(2)}) collective-permute-start(bf16[264,512]{1,0:T(8,128)(2,1)S(1)} %combine.19.refs_3_), channel_id=1, source_target_pairs={{0,2},{1,3},{2,0},{3,1},{4,6},{5,7},{6,4},{7,5},{8,10},{9,11},{10,... | collective-permute-start | bytes 811016 | tf_op jit(solution)/shard_map/ppermute | solution.py:40
  43.9 2.6 %collective-permute-done.9.refs_3_.refs_13_ = bf16[264,512]{1,0:T(8,128)(2,1)S(1)} collective-permute-done((bf16[264,512]{1,0:T(8,128)(2,1)S(1)}, bf16[264,512]{1,0:T(8,128)(2,1)S(1)}, u32[]{:S(2)}, u32[]{:S(2)}) %collective-permute-start.9) | collective-permute-done | bytes 270368 | tf_op jit(solution)/shard_map/ppermute | solution.py:40
  46.5 0.3 combine.23.refs_4_
  46.8 0.3 combine.24.refs_3_
  47.0 11.2 %collective-permute-done.11.refs_2_.refs_1_.refs_11_ = bf16[264,512]{1,0:T(8,128)(2,1)S(1)} collective-permute-done((bf16[264,512]{1,0:T(8,128)(2,1)S(1)}, bf16[264,512]{1,0:T(8,128)(2,1)S(1)}, u32[]{:S(2)}, u32[]{:S(2)}) %collective-permute-start.11) | collective-permute-done | bytes 270368 | tf_op jit(solution)/shard_map/ppermute | solution.py:40
  58.2 0.2 combine.25.refs_4_
  58.5 1.3 %collective-permute-start.10 = (bf16[264,512]{1,0:T(8,128)(2,1)S(1)}, bf16[264,512]{1,0:T(8,128)(2,1)S(1)}, u32[]{:S(2)}, u32[]{:S(2)}) collective-permute-start(bf16[264,512]{1,0:T(8,128)(2,1)S(1)} %combine.24.refs_3_), channel_id=1, source_target_pairs={{0,8},{4,12},{1,9},{5,13},{2,10},{6,14},{3,11},{7,15},{16,24},{20,... | collective-permute-start | bytes 811016 | tf_op jit(solution)/shard_map/ppermute | solution.py:40
  59.9 0.1 collective-permute-done.12.refs_3_.refs_2_.refs_12_
  60.0 0.3 combine.26.refs_4_
  60.3 6.1 %collective-permute-done.10.refs_3_.refs_13_ = bf16[264,512]{1,0:T(8,128)(2,1)S(1)} collective-permute-done((bf16[264,512]{1,0:T(8,128)(2,1)S(1)}, bf16[264,512]{1,0:T(8,128)(2,1)S(1)}, u32[]{:S(2)}, u32[]{:S(2)}) %collective-permute-start.10) | collective-permute-done | bytes 270368 | tf_op jit(solution)/shard_map/ppermute | solution.py:40
  66.4 0.3 combine.27.refs_3_
  66.7 8.0 %collective-permute-done.7.refs_2_.refs_1_.refs_11_ = bf16[264,512]{1,0:T(8,128)(2,1)S(1)} collective-permute-done((bf16[264,512]{1,0:T(8,128)(2,1)S(1)}, bf16[264,512]{1,0:T(8,128)(2,1)S(1)}, u32[]{:S(2)}, u32[]{:S(2)}) %collective-permute-start.7) | collective-permute-done | bytes 270368 | tf_op jit(solution)/shard_map/ppermute | solution.py:40
  74.7 0.2 combine.28.refs_4_
  74.9 0.1 collective-permute-start.13
  75.1 1.3 %collective-permute-start.16 = (bf16[264,512]{1,0:T(8,128)(2,1)S(1)}, bf16[264,512]{1,0:T(8,128)(2,1)S(1)}, u32[]{:S(2)}, u32[]{:S(2)}) collective-permute-start(bf16[264,512]{1,0:T(8,128)(2,1)S(1)} %combine.26.refs_4_), channel_id=1, source_target_pairs={{0,8},{4,12},{1,9},{5,13},{2,10},{6,14},{3,11},{7,15},{16,24},{20,... | collective-permute-start | bytes 811016 | tf_op jit(solution)/shard_map/ppermute | solution.py:40
  76.6 0.3 combine.29.refs_4_
  76.8 1.5 %collective-permute-start.14 = (bf16[264,512]{1,0:T(8,128)(2,1)S(1)}, bf16[264,512]{1,0:T(8,128)(2,1)S(1)}, u32[]{:S(2)}, u32[]{:S(2)}) collective-permute-start(bf16[264,512]{1,0:T(8,128)(2,1)S(1)} %combine.29.refs_4_), channel_id=1, source_target_pairs={{0,8},{4,12},{1,9},{5,13},{2,10},{6,14},{3,11},{7,15},{16,24},{20,... | collective-permute-start | bytes 811016 | tf_op jit(solution)/shard_map/ppermute | solution.py:40
  78.3 2.0 %collective-permute-start.19 = (bf16[264,512]{1,0:T(8,128)(2,1)S(1)}, bf16[264,512]{1,0:T(8,128)(2,1)S(1)}, u32[]{:S(2)}, u32[]{:S(2)}) collective-permute-start(bf16[264,512]{1,0:T(8,128)(2,1)S(1)} %combine.27.refs_3_), channel_id=1, source_target_pairs={{0,1},{1,0},{2,3},{3,2},{4,5},{5,4},{6,7},{7,6},{8,9},{9,8},{10,11... | collective-permute-start | bytes 811016 | tf_op jit(solution)/shard_map/ppermute | solution.py:40
  80.3 2.9 %collective-permute-done.16.refs_3_.refs_13_ = bf16[264,512]{1,0:T(8,128)(2,1)S(1)} collective-permute-done((bf16[264,512]{1,0:T(8,128)(2,1)S(1)}, bf16[264,512]{1,0:T(8,128)(2,1)S(1)}, u32[]{:S(2)}, u32[]{:S(2)}) %collective-permute-start.16) | collective-permute-done | bytes 270368 | tf_op jit(solution)/shard_map/ppermute | solution.py:40
  83.2 0.3 combine.30.refs_14_
  83.6 2.2 %collective-permute-done.15.refs_9_ = bf16[264,512]{1,0:T(8,128)(2,1)S(1)} collective-permute-done((bf16[264,512]{1,0:T(8,128)(2,1)S(1)}, bf16[264,512]{1,0:T(8,128)(2,1)S(1)}, u32[]{:S(2)}, u32[]{:S(2)}) %collective-permute-start.15) | collective-permute-done | bytes 270368 | tf_op jit(solution)/shard_map/ppermute | solution.py:40
  85.8 2.7 %span_outputs.4 = (bf16[256,4096]{1,0:T(8,128)(2,1)}, f32[8,128]{1,0:T(8,128)S(1)}) custom-call(f32[3,2,8]{2,1,0:T(2,128)} %bitcast.7, s32[2,8]{1,0:T(2,128)} %refs_1_.13, s32[2,8]{1,0:T(2,128)} %refs_2_.13, s32[2,8]{1,0:T(2,128)} %refs_3_.13, f32[256,8]{1,0:T(8,128)S(1)} %get-tuple-element.24.refs_4_, f32[8,256]{1,0:T(8,128)S(1)} %get-tuple-element.25.refs_5_, ...), custom_call_target="tpu_custom_call" | custom-call | flops 335544320 | bytes 2924544 | tf_op jit(solution)/shard_map/span_outputs/pallas_call | solution.py:330
  88.6 0.2 collective-permute-done.14.refs_3_.refs_13_
  88.8 0.3 combine.31.refs_15_
  89.1 2.5 %collective-permute-done.19.refs_9_ = bf16[264,512]{1,0:T(8,128)(2,1)S(1)} collective-permute-done((bf16[264,512]{1,0:T(8,128)(2,1)S(1)}, bf16[264,512]{1,0:T(8,128)(2,1)S(1)}, u32[]{:S(2)}, u32[]{:S(2)}) %collective-permute-start.19) | collective-permute-done | bytes 270368 | tf_op jit(solution)/shard_map/ppermute | solution.py:40
  91.6 2.7 %span_outputs.5 = (bf16[256,4096]{1,0:T(8,128)(2,1)}, f32[8,128]{1,0:T(8,128)S(1)}) custom-call(f32[3,2,8]{2,1,0:T(2,128)} %bitcast.8, s32[2,8]{1,0:T(2,128)} %refs_1_.13, s32[2,8]{1,0:T(2,128)} %refs_2_.13, s32[2,8]{1,0:T(2,128)} %refs_3_.13, f32[256,8]{1,0:T(8,128)S(1)} %get-tuple-element.24.refs_4_, ...), custom_call_target="tpu_custom_call", output_to_operand_aliasing={{0}: (14, {})} | custom-call | flops 335544320 | bytes 2924544 | tf_op jit(solution)/shard_map/span_outputs/pallas_call | solution.py:330
  94.3 3.1 %collective-permute-done.18.refs_9_ = bf16[264,512]{1,0:T(8,128)(2,1)S(1)} collective-permute-done((bf16[264,512]{1,0:T(8,128)(2,1)S(1)}, bf16[264,512]{1,0:T(8,128)(2,1)S(1)}, u32[]{:S(2)}, u32[]{:S(2)}) %collective-permute-start.18) | collective-permute-done | bytes 270368 | tf_op jit(solution)/shard_map/ppermute | solution.py:40
  97.4 2.7 %span_outputs.6 = (bf16[256,4096]{1,0:T(8,128)(2,1)}, f32[8,128]{1,0:T(8,128)S(1)}) custom-call(f32[3,2,8]{2,1,0:T(2,128)} %bitcast.9, s32[2,8]{1,0:T(2,128)} %refs_1_.13, s32[2,8]{1,0:T(2,128)} %refs_2_.13, s32[2,8]{1,0:T(2,128)} %refs_3_.13, f32[256,8]{1,0:T(8,128)S(1)} %get-tuple-element.24.refs_4_, ...), custom_call_target="tpu_custom_call", output_to_operand_aliasing={{0}: (14, {})} | custom-call | flops 335544320 | bytes 2924544 | tf_op jit(solution)/shard_map/span_outputs/pallas_call | solution.py:330
  100.1 2.6 %collective-permute-done.17.refs_9_ = bf16[264,512]{1,0:T(8,128)(2,1)S(1)} collective-permute-done((bf16[264,512]{1,0:T(8,128)(2,1)S(1)}, bf16[264,512]{1,0:T(8,128)(2,1)S(1)}, u32[]{:S(2)}, u32[]{:S(2)}) %collective-permute-start.17) | collective-permute-done | bytes 270368 | tf_op jit(solution)/shard_map/ppermute | solution.py:40
  102.7 2.7 %span_outputs.7 = (bf16[256,4096]{1,0:T(8,128)(2,1)}, f32[8,128]{1,0:T(8,128)}) custom-call(f32[3,2,8]{2,1,0:T(2,128)} %bitcast.10, s32[2,8]{1,0:T(2,128)} %refs_1_.13, s32[2,8]{1,0:T(2,128)} %refs_2_.13, s32[2,8]{1,0:T(2,128)} %refs_3_.13, f32[256,8]{1,0:T(8,128)S(1)} %get-tuple-element.24.refs_4_, ...), custom_call_target="tpu_custom_call", output_to_operand_aliasing={{0}: (14, {})} | custom-call | flops 335544320 | bytes 2924544 | tf_op jit(solution)/shard_map/span_outputs/pallas_call | solution.py:330
  (23 shorter events, 1.3 us)
Async XLA Ops:
  3.1 10.5 %collective-permute-start.1 = (bf16[264,512]{1,0:T(8,128)(2,1)S(1)}, bf16[264,512]{1,0:T(8,128)(2,1)S(1)}, u32[]{:S(2)}, u32[]{:S(2)}) collective-permute-start(bf16[264,512]{1,0:T(8,128)(2,1)S(1)} %get-tuple-element.28.refs_8_), channel_id=1, source_target_pairs={{0,1},{1,0},{2,3},{3,2},{4,5},{5,4},{6,7},{7,6},{8,9},{9,8},{10,11... | collective-permute-start | bytes 811016 | tf_op jit(solution)/shard_map/ppermute | solution.py:40
  7.9 16.5 %collective-permute-start = (bf16[264,512]{1,0:T(8,128)(2,1)S(1)}, bf16[264,512]{1,0:T(8,128)(2,1)S(1)}, u32[]{:S(2)}, u32[]{:S(2)}) collective-permute-start(bf16[264,512]{1,0:T(8,128)(2,1)S(1)} %get-tuple-element.30.refs_2_), channel_id=1, source_target_pairs={{0,1},{1,0},{2,3},{3,2},{4,5},{5,4},{6,7},{7,6},{8,9},{9,8},{10,11... | collective-permute-start | bytes 811016 | tf_op jit(solution)/shard_map/ppermute | solution.py:40
  13.7 13.6 %collective-permute-start.3 = (bf16[264,512]{1,0:T(8,128)(2,1)S(1)}, bf16[264,512]{1,0:T(8,128)(2,1)S(1)}, u32[]{:S(2)}, u32[]{:S(2)}) collective-permute-start(bf16[264,512]{1,0:T(8,128)(2,1)S(1)} %combine.16.refs_8_), channel_id=1, source_target_pairs={{0,2},{1,3},{2,0},{3,1},{4,6},{5,7},{6,4},{7,5},{8,10},{9,11},{10,... | collective-permute-start | bytes 811016 | tf_op jit(solution)/shard_map/ppermute | solution.py:40
  18.5 17.5 %collective-permute-start.6 = (bf16[264,512]{1,0:T(8,128)(2,1)S(1)}, bf16[264,512]{1,0:T(8,128)(2,1)S(1)}, u32[]{:S(2)}, u32[]{:S(2)}) collective-permute-start(bf16[264,512]{1,0:T(8,128)(2,1)S(1)} %get-tuple-element.32.refs_2_), channel_id=1, source_target_pairs={{0,1},{1,0},{2,3},{3,2},{4,5},{5,4},{6,7},{7,6},{8,9},{9,8},{10,11... | collective-permute-start | bytes 811016 | tf_op jit(solution)/shard_map/ppermute | solution.py:40
  24.5 14.0 %collective-permute-start.5 = (bf16[264,512]{1,0:T(8,128)(2,1)S(1)}, bf16[264,512]{1,0:T(8,128)(2,1)S(1)}, u32[]{:S(2)}, u32[]{:S(2)}) collective-permute-start(bf16[264,512]{1,0:T(8,128)(2,1)S(1)} %combine.17.refs_8_), channel_id=1, source_target_pairs={{0,2},{1,3},{2,0},{3,1},{4,6},{5,7},{6,4},{7,5},{8,10},{9,11},{10,... | collective-permute-start | bytes 811016 | tf_op jit(solution)/shard_map/ppermute | solution.py:40
  27.5 11.2 %collective-permute-start.4 = (bf16[264,512]{1,0:T(8,128)(2,1)S(1)}, bf16[264,512]{1,0:T(8,128)(2,1)S(1)}, u32[]{:S(2)}, u32[]{:S(2)}) collective-permute-start(bf16[264,512]{1,0:T(8,128)(2,1)S(1)} %combine.18.refs_2_), channel_id=1, source_target_pairs={{0,4},{4,0},{8,12},{12,8},{1,5},{5,1},{9,13},{13,9},{2,6},{6,2},{1... | collective-permute-start | bytes 811016 | tf_op jit(solution)/shard_map/ppermute | solution.py:40
  27.5 16.2 %collective-permute-start.2 = (bf16[264,512]{1,0:T(8,128)(2,1)S(1)}, bf16[264,512]{1,0:T(8,128)(2,1)S(1)}, u32[]{:S(2)}, u32[]{:S(2)}) collective-permute-start(bf16[264,512]{1,0:T(8,128)(2,1)S(1)} %get-tuple-element.34.refs_3_), channel_id=1, source_target_pairs={{0,1},{1,0},{2,3},{3,2},{4,5},{5,4},{6,7},{7,6},{8,9},{9,8},{10,11... | collective-permute-start | bytes 811016 | tf_op jit(solution)/shard_map/ppermute | solution.py:40
  39.0 7.5 %collective-permute-start.9 = (bf16[264,512]{1,0:T(8,128)(2,1)S(1)}, bf16[264,512]{1,0:T(8,128)(2,1)S(1)}, u32[]{:S(2)}, u32[]{:S(2)}) collective-permute-start(bf16[264,512]{1,0:T(8,128)(2,1)S(1)} %combine.21.refs_2_), channel_id=1, source_target_pairs={{0,8},{4,12},{1,9},{5,13},{2,10},{6,14},{3,11},{7,15},{16,24},{20,... | collective-permute-start | bytes 811016 | tf_op jit(solution)/shard_map/ppermute | solution.py:40
  42.5 4.2 %collective-permute-start.8 = (bf16[264,512]{1,0:T(8,128)(2,1)S(1)}, bf16[264,512]{1,0:T(8,128)(2,1)S(1)}, u32[]{:S(2)}, u32[]{:S(2)}) collective-permute-start(bf16[264,512]{1,0:T(8,128)(2,1)S(1)} %combine.20.refs_4_), channel_id=1, source_target_pairs={{0,4},{4,0},{8,12},{12,8},{1,5},{5,1},{9,13},{13,9},{2,6},{6,2},{1... | collective-permute-start | bytes 811016 | tf_op jit(solution)/shard_map/ppermute | solution.py:40
  42.6 15.6 %collective-permute-start.11 = (bf16[264,512]{1,0:T(8,128)(2,1)S(1)}, bf16[264,512]{1,0:T(8,128)(2,1)S(1)}, u32[]{:S(2)}, u32[]{:S(2)}) collective-permute-start(bf16[264,512]{1,0:T(8,128)(2,1)S(1)} %combine.19.refs_3_), channel_id=1, source_target_pairs={{0,2},{1,3},{2,0},{3,1},{4,6},{5,7},{6,4},{7,5},{8,10},{9,11},{10,... | collective-permute-start | bytes 811016 | tf_op jit(solution)/shard_map/ppermute | solution.py:40
  58.4 1.6 %collective-permute-start.12 = (bf16[264,512]{1,0:T(8,128)(2,1)S(1)}, bf16[264,512]{1,0:T(8,128)(2,1)S(1)}, u32[]{:S(2)}, u32[]{:S(2)}) collective-permute-start(bf16[264,512]{1,0:T(8,128)(2,1)S(1)} %combine.25.refs_4_), channel_id=1, source_target_pairs={{0,4},{4,0},{8,12},{12,8},{1,5},{5,1},{9,13},{13,9},{2,6},{6,2},{1... | collective-permute-start | bytes 811016 | tf_op jit(solution)/shard_map/ppermute | solution.py:40
  58.5 8.0 %collective-permute-start.10 = (bf16[264,512]{1,0:T(8,128)(2,1)S(1)}, bf16[264,512]{1,0:T(8,128)(2,1)S(1)}, u32[]{:S(2)}, u32[]{:S(2)}) collective-permute-start(bf16[264,512]{1,0:T(8,128)(2,1)S(1)} %combine.24.refs_3_), channel_id=1, source_target_pairs={{0,8},{4,12},{1,9},{5,13},{2,10},{6,14},{3,11},{7,15},{16,24},{20,... | collective-permute-start | bytes 811016 | tf_op jit(solution)/shard_map/ppermute | solution.py:40
  59.8 15.0 %collective-permute-start.7 = (bf16[264,512]{1,0:T(8,128)(2,1)S(1)}, bf16[264,512]{1,0:T(8,128)(2,1)S(1)}, u32[]{:S(2)}, u32[]{:S(2)}) collective-permute-start(bf16[264,512]{1,0:T(8,128)(2,1)S(1)} %combine.22.refs_4_), channel_id=1, source_target_pairs={{0,2},{1,3},{2,0},{3,1},{4,6},{5,7},{6,4},{7,5},{8,10},{9,11},{10,... | collective-permute-start | bytes 811016 | tf_op jit(solution)/shard_map/ppermute | solution.py:40
  66.7 19.1 %copy-start = (bf16[256,4096]{1,0:T(8,128)(2,1)S(1)}, bf16[256,4096]{1,0:T(8,128)(2,1)}, u32[]{:S(2)}) copy-start(bf16[256,4096]{1,0:T(8,128)(2,1)} %refs_8_.7) | copy-start | bytes 6291460
  66.7 19.1 %copy-start.1 = (bf16[256,2048]{1,0:T(8,128)(2,1)S(1)}, bf16[256,2048]{1,0:T(8,128)(2,1)}, u32[]{:S(2)}) copy-start(bf16[256,2048]{1,0:T(8,128)(2,1)} %refs_7_.13) | copy-start | bytes 3145732
  66.7 19.1 %copy-start.2 = (bf16[256,2048]{1,0:T(8,128)(2,1)S(1)}, bf16[256,2048]{1,0:T(8,128)(2,1)}, u32[]{:S(2)}) copy-start(bf16[256,2048]{1,0:T(8,128)(2,1)} %refs_6_.13) | copy-start | bytes 3145732
  74.9 1.6 %collective-permute-start.13 = (bf16[264,512]{1,0:T(8,128)(2,1)S(1)}, bf16[264,512]{1,0:T(8,128)(2,1)S(1)}, u32[]{:S(2)}, u32[]{:S(2)}) collective-permute-start(bf16[264,512]{1,0:T(8,128)(2,1)S(1)} %combine.28.refs_4_), channel_id=1, source_target_pairs={{0,4},{4,0},{8,12},{12,8},{1,5},{5,1},{9,13},{13,9},{2,6},{6,2},{1... | collective-permute-start | bytes 811016 | tf_op jit(solution)/shard_map/ppermute | solution.py:40
  75.1 8.1 %collective-permute-start.16 = (bf16[264,512]{1,0:T(8,128)(2,1)S(1)}, bf16[264,512]{1,0:T(8,128)(2,1)S(1)}, u32[]{:S(2)}, u32[]{:S(2)}) collective-permute-start(bf16[264,512]{1,0:T(8,128)(2,1)S(1)} %combine.26.refs_4_), channel_id=1, source_target_pairs={{0,8},{4,12},{1,9},{5,13},{2,10},{6,14},{3,11},{7,15},{16,24},{20,... | collective-permute-start | bytes 811016 | tf_op jit(solution)/shard_map/ppermute | solution.py:40
  76.4 9.4 %collective-permute-start.15 = (bf16[264,512]{1,0:T(8,128)(2,1)S(1)}, bf16[264,512]{1,0:T(8,128)(2,1)S(1)}, u32[]{:S(2)}, u32[]{:S(2)}) collective-permute-start(bf16[264,512]{1,0:T(8,128)(2,1)S(1)} %combine.23.refs_4_), channel_id=1, source_target_pairs={{0,1},{1,0},{2,3},{3,2},{4,5},{5,4},{6,7},{7,6},{8,9},{9,8},{10,11... | collective-permute-start | bytes 811016 | tf_op jit(solution)/shard_map/ppermute | solution.py:40
  76.8 11.9 %collective-permute-start.14 = (bf16[264,512]{1,0:T(8,128)(2,1)S(1)}, bf16[264,512]{1,0:T(8,128)(2,1)S(1)}, u32[]{:S(2)}, u32[]{:S(2)}) collective-permute-start(bf16[264,512]{1,0:T(8,128)(2,1)S(1)} %combine.29.refs_4_), channel_id=1, source_target_pairs={{0,8},{4,12},{1,9},{5,13},{2,10},{6,14},{3,11},{7,15},{16,24},{20,... | collective-permute-start | bytes 811016 | tf_op jit(solution)/shard_map/ppermute | solution.py:40
  78.3 13.3 %collective-permute-start.19 = (bf16[264,512]{1,0:T(8,128)(2,1)S(1)}, bf16[264,512]{1,0:T(8,128)(2,1)S(1)}, u32[]{:S(2)}, u32[]{:S(2)}) collective-permute-start(bf16[264,512]{1,0:T(8,128)(2,1)S(1)} %combine.27.refs_3_), channel_id=1, source_target_pairs={{0,1},{1,0},{2,3},{3,2},{4,5},{5,4},{6,7},{7,6},{8,9},{9,8},{10,11... | collective-permute-start | bytes 811016 | tf_op jit(solution)/shard_map/ppermute | solution.py:40
  83.5 13.9 %collective-permute-start.18 = (bf16[264,512]{1,0:T(8,128)(2,1)S(1)}, bf16[264,512]{1,0:T(8,128)(2,1)S(1)}, u32[]{:S(2)}, u32[]{:S(2)}) collective-permute-start(bf16[264,512]{1,0:T(8,128)(2,1)S(1)} %combine.30.refs_14_), channel_id=1, source_target_pairs={{0,1},{1,0},{2,3},{3,2},{4,5},{5,4},{6,7},{7,6},{8,9},{9,8},{10,11... | collective-permute-start | bytes 811016 | tf_op jit(solution)/shard_map/ppermute | solution.py:40
  89.0 13.6 %collective-permute-start.17 = (bf16[264,512]{1,0:T(8,128)(2,1)S(1)}, bf16[264,512]{1,0:T(8,128)(2,1)S(1)}, u32[]{:S(2)}, u32[]{:S(2)}) collective-permute-start(bf16[264,512]{1,0:T(8,128)(2,1)S(1)} %combine.31.refs_15_), channel_id=1, source_target_pairs={{0,1},{1,0},{2,3},{3,2},{4,5},{5,4},{6,7},{7,6},{8,9},{9,8},{10,11... | collective-permute-start | bytes 811016 | tf_op jit(solution)/shard_map/ppermute | solution.py:40

commit v5 on v4

--- a/solution.py
+++ b/solution.py
@@ -15,10 +15,11 @@
 NEG_FILL = -1e30
 TAIL = 8
 ROWS = DK + TAIL
-CHUNKS = ((0, 0, DV), (1, 0, DV), (2, 0, DV), (3, 0, DV))
+CHUNKS = ((0, 0, DV // 2), (0, DV // 2, DV // 2), (1, 0, DV), (2, 0, DV), (3, 0, DV))
 ORDER = (
-    (0, 0), (0, 1), (1, 0), (0, 2), (1, 1), (0, 3), (2, 0), (1, 2), (2, 1), (3, 0), (1, 3), (4, 0),
-    (3, 1), (2, 2), (3, 2), (4, 1), (2, 3), (3, 3), (4, 2), (5, 0), (4, 3), (5, 1), (5, 2), (5, 3),
+    (0, 0), (0, 1), (0, 2), (1, 0), (1, 1), (0, 3), (1, 2), (2, 1), (0, 4), (1, 3), (2, 0), (3, 0), (3, 1), (2, 2),
+    (4, 0), (1, 4), (3, 2), (4, 1), (5, 0), (2, 3), (3, 3), (5, 1), (4, 2), (2, 4), (3, 4), (4, 3), (6, 0), (6, 1),
+    (4, 4), (5, 3), (6, 2), (5, 2), (6, 3),
 )
 
 F32 = jnp.float32
@@ -264,84 +265,86 @@
 
 
 def output_kernel(
-    head_bits, bits, pair, pieces, scales, tensors, offsets, fbits, run_ref, shift_ref, q_ref, k_ref, v_ref, *rest
+    head_bits, bits, pair, mine, pieces, scales, tensors, offsets, fbits, run_ref, shift_ref, q_ref, k_ref, v_ref, *rest
 ):
-    groups = [rest[p * (bits + 1) : (p + 1) * (bits + 1)] for p in range(pieces)]
+    count = len(rest[:-2]) // pieces
+    groups = [rest[p * count : (p + 1) * count] for p in range(pieces)]
     out_ref, token_ref = rest[-2:]
     token_ref[...] = jnp.zeros_like(token_ref)
     bit = device_bits(head_bits, bits)
-    own = lax.axis_index("head") & 1
+    h = 2 * pair + head_side(mine)
     factor = 1.0 / math.sqrt(DK)
     size = q_ref.shape[0]
     row = lax.broadcasted_iota(jnp.int32, (size, size), 0)
     col = lax.broadcasted_iota(jnp.int32, (size, size), 1)
-    for side, mine in ((own, True), (1 - own, False)):
-        h = 2 * pair + side
-        info = (h, scales, tensors, offsets, fbits)
-        starts = []
-        for back_ref, *parts in groups:
-            if mine:
-                states = [State(ref) for ref in parts]
-                weights, peak, _ = start_weights(bit, None, None, states)
-                start, normer = weighted_sum(weights, states)
-                starts.append(start.astype(BF16))
-            else:
-                back = State(back_ref)
-                normer, peak = back.normer, back.peak
-                starts.append(back.matrix())
-        start = jnp.concatenate(starts, axis=1) if pieces > 1 else starts[0]
-        narrow, wide = pl.multiple_of(side * DK, DK), pl.multiple_of(side * DV, DV)
-        q = dequant(q_ref, narrow, 0, DK, DK, 0, *info)
-        k = dequant(k_ref, narrow, 0, DK, DK, 1, *info)
-        v = dequant(v_ref, wide, 0, DV, DV, 2, *info)
-        run = pick(run_ref, h)
-        exponent = jnp.where(row >= col, run + shift_ref[pl.ds(h, 1), :], NEG_FILL)
-        inter = run + peak[:, :1]
-        row_peak = jnp.maximum(jnp.max(exponent, axis=1, keepdims=True), inter)
-        decay = jnp.exp(exponent - row_peak)
-        scores = lax.dot_general(q, k, (((1,), (1,)), ((), ())), preferred_element_type=F32) * factor
-        product = decay * scores
-        lifted = (q.astype(F32) * (factor * jnp.exp(inter - row_peak))).astype(BF16)
-        numerator = jnp.dot(product.astype(BF16), v, preferred_element_type=F32)
-        numerator = numerator + jnp.dot(lifted, start, preferred_element_type=F32)
-        denominator = jnp.sum(product, axis=1, keepdims=True) + jnp.sum(
-            lifted.astype(F32) * normer, axis=1, keepdims=True
-        )
-        out_ref[:, pl.ds(wide, DV)] = (numerator / jnp.maximum(jnp.abs(denominator), 1.0)).astype(BF16)
-
-
-def span_outputs(head_bits, bits, pair, small, run, shift, codes, groups, before, after):
+    info = (h, scales, tensors, offsets, fbits)
+    starts = []
+    for group in groups:
+        states = [State(ref) for ref in group]
+        if mine:
+            weights, peak, _ = start_weights(bit, None, None, states)
+            start, normer = weighted_sum(weights, states)
+            starts.append(start.astype(BF16))
+        else:
+            normer, peak = states[0].normer, states[0].peak
+            starts.append(states[0].matrix())
+    start = jnp.concatenate(starts, axis=1) if pieces > 1 else starts[0]
+    q = dequant(q_ref, 0, 0, DK, DK, 0, *info)
+    k = dequant(k_ref, 0, 0, DK, DK, 1, *info)
+    v = dequant(v_ref, 0, 0, DV, DV, 2, *info)
+    run = pick(run_ref, h)
+    exponent = jnp.where(row >= col, run + shift_ref[pl.ds(h, 1), :], NEG_FILL)
+    inter = run + peak[:, :1]
+    row_peak = jnp.maximum(jnp.max(exponent, axis=1, keepdims=True), inter)
+    decay = jnp.exp(exponent - row_peak)
+    scores = lax.dot_general(q, k, (((1,), (1,)), ((), ())), preferred_element_type=F32) * factor
+    product = decay * scores
+    lifted = (q.astype(F32) * (factor * jnp.exp(inter - row_peak))).astype(BF16)
+    numerator = jnp.dot(product.astype(BF16), v, preferred_element_type=F32)
+    numerator = numerator + jnp.dot(lifted, start, preferred_element_type=F32)
+    denominator = jnp.sum(product, axis=1, keepdims=True) + jnp.sum(lifted.astype(F32) * normer, axis=1, keepdims=True)
+    out_ref[...] = (numerator / jnp.maximum(jnp.abs(denominator), 1.0)).astype(BF16)
+
+
+def head_side(mine):
+    own = lax.axis_index("head") & 1
+    return own if mine else 1 - own
+
+
+def span_outputs(head_bits, bits, pair, mine, small, run, shift, codes, groups, before, after):
     q, k, v = codes
     rows = q.shape[0]
-    narrow = pl.BlockSpec((rows, 2 * DK), lambda i: (0, pair))
-    wide = pl.BlockSpec((rows, 2 * DV), lambda i: (0, pair))
+    narrow = pl.BlockSpec((rows, DK), lambda i: (0, 2 * pair + head_side(mine)))
+    wide = pl.BlockSpec((rows, DV), lambda i: (0, 2 * pair + head_side(mine)))
     states = [x for group in groups for x in group]
     operands = [*small, run, shift, q, k, v, *states]
     in_specs = [SMEM] * 4 + [whole(run.shape), whole(shift.shape), narrow, narrow, wide]
     in_specs += [whole(x.shape) for x in states]
+    kernel = functools.partial(output_kernel, head_bits, bits, pair, mine, len(groups))
+    kernel, extra, extra_specs = ordered(kernel, len(operands), after)
+    operands += extra
+    in_specs += extra_specs
     aliases = {}
     if before is not None:
+        kernel, extra, extra_specs = ordered(kernel, len(operands), before)
         aliases = {len(operands): 0}
-        operands.append(before)
-        in_specs.append(pl.BlockSpec(memory_space=pl.ANY))
-    kernel, extra, extra_specs = ordered(
-        functools.partial(output_kernel, head_bits, bits, pair, len(groups)), len(operands), after
-    )
+        operands += extra
+        in_specs += extra_specs
     return pl.pallas_call(
         kernel,
         grid=(1,),
-        in_specs=in_specs + extra_specs,
+        in_specs=in_specs,
         out_specs=(wide, whole((8, 128))),
         out_shape=(jax.ShapeDtypeStruct(v.shape, BF16), jax.ShapeDtypeStruct((8, 128), F32)),
         input_output_aliases=aliases,
         compiler_params=pltpu.CompilerParams(vmem_limit_bytes=16 << 20),
         cost_estimate=pl.CostEstimate(
-            flops=4 * rows * (rows * DK + rows * DV + DK * DV),
-            bytes_accessed=rows * 2 * (4 * DK + 4 * DV) + sum(x.size for x in states) * 2,
-            transcendentals=2 * rows * rows,
+            flops=2 * rows * (rows * DK + rows * DV + DK * DV),
+            bytes_accessed=rows * 2 * (2 * DK + 2 * DV) + sum(x.size for x in states) * 2,
+            transcendentals=rows * rows,
         ),
         name="span_outputs",
-    )(*operands, *extra)
+    )(*operands)
 
 
 def body(
@@ -375,8 +378,11 @@
         elif stage == bits:
             token = combine(head_bits, bits, True, [keep[c], *got[c][1:]], token)
         else:
-            groups = [[back[d], *got[d]] for d in of_pair(c)]
-            out, token = span_outputs(head_bits, bits, c, small, run, shift, codes, groups, out, token)
+            mine = stage == bits + 1
+            groups = [got[d] if mine else [back[d]] for d in of_pair(c)]
+            out, token = span_outputs(
+                head_bits, bits, c, mine, small, run, shift, codes, groups, out, token
+            )
         if stage < bits:
             got.setdefault(c, []).append(exchange(token, stage, last=stage == bits - 1))
         elif stage == bits:
@@ -389,7 +395,7 @@
 
 
 def order(bits):
-    stages = {0: [0], 1: [1], 2: range(2, bits - 1), 3: [bits - 1], 4: [bits], 5: [bits + 1]}
+    stages = {0: [0], 1: [1], 2: range(2, bits - 1), 3: [bits - 1], 4: [bits], 5: [bits + 1], 6: [bits + 2]}
     return [(stage, c) for place, c in ORDER for stage in stages[place]]
 
 

time: 106 us -> 109 us (1.028)
  waiting for transfers between devices: 60 us -> 51.3 us
  Pallas kernels: 22.5 us -> 31 us
  starting transfers between devices: 22.6 us -> 25.4 us
    ppermute x20 -> x25, waiting for transfers between devices: 60 us -> 51.3 us  [flip(): return lax.ppermute(x, axis, pairs)]
    pallas_call x4 -> x8, Pallas kernels: 10.8 us -> 17.6 us  [span_outputs(): pl.pallas_call(kernel, grid=(1,), in_specs=in_specs, out_specs=(wide, who...]
    ppermute x20 -> x25, starting transfers between devices: 22.6 us -> 25.4 us  [flip(): return lax.ppermute(x, axis, pairs)]
    pallas_call x4 -> x5, Pallas kernels: 6.86 us -> 8.4 us  [span_states(): pl.pallas_call(kernel, grid=(1,), in_specs=[SMEM] * 5 + [whole(weight.sha...]
    pallas_call x16 -> x20, Pallas kernels: 3.48 us -> 3.61 us  [combine(): pl.pallas_call(kernel, in_specs=[VMEM] * len(parts) + extra_specs, out_sp...]
  transfers between devices with their start and end apart: 20 -> 25, of which waited for: 17 -> 16; matrix products, arithmetic and copies ran while one was open for 0% -> 0% of each run, Pallas kernels for 16% -> 24%
where the time goes in v5:
time: 109 us; the launch traced here: 108 us
  waiting for transfers between devices  51.3 us (47%)
  Pallas kernels  31 us (28%)
  starting transfers between devices  25.4 us (23%)
    ppermute x25, waiting for transfers between devices, flip(): return lax.ppermute(x, axis, pairs)  51.3 us
    ppermute x25, starting transfers between devices, flip(): return lax.ppermute(x, axis, pairs)  25.4 us
    pallas_call x8, Pallas kernels, span_outputs(): pl.pallas_call(kernel, grid=(1,), in_specs=in_specs, out_specs=(wide, who...  17.6 us
    pallas_call x5, Pallas kernels, span_states(): pl.pallas_call(kernel, grid=(1,), in_specs=[SMEM] * 5 + [whole(weight.sha...  8.4 us
    pallas_call x20, Pallas kernels, combine(): pl.pallas_call(kernel, in_specs=[VMEM] * len(parts) + extra_specs, out_sp...  3.61 us
  transfers between devices with their start and end apart: 25, of which 16 were waited for; matrix products, arithmetic and copies ran while one was open for 0% of the time, Pallas kernels for 24%

profile of v5, /device:TPU:0, one launch (start us, length us, event | category | flops | bytes accessed | tf_op | source)
XLA Modules:
  0.0 108.0 jit_solution(14171250653393926065)
XLA Ops:
  0.0 1.3 %gates.1 = (f32[256,8]{1,0:T(8,128)S(1)}, f32[256,8]{1,0:T(8,128)S(1)}, f32[8,256]{1,0:T(8,128)S(1)}, f32[2,8]{1,0:T(2,128)S(1)}) custom-call(bf16[8,256]{1,0:T(8,128)(2,1)} %bitcast.16, bf16[8,256]{1,0:T(8,128)(2,1)} %bitcast.17), custom_call_target="tpu_custom_call" | custom-call | flops 1048576 | bytes 1048576 | tf_op jit(solution)/shard_map/gates/pallas_call | solution.py:70
  1.3 1.6 %span_states.5 = (bf16[264,256]{1,0:T(8,128)(2,1)S(1)}, bf16[264,256]{1,0:T(8,128)(2,1)S(1)}) custom-call(f32[3,2,8]{2,1,0:T(2,128)} %bitcast.3, s32[2,8]{1,0:T(2,128)} %refs_1_.23, s32[2,8]{1,0:T(2,128)} %refs_2_.23, s32[2,8]{1,0:T(2,128)} %refs_3_.23, f32[2,8]{1,0:T(2,128)S(1)} %get-tuple-element.36.mf.refs_4_, ...), custom_call_target="tpu_custom_call" | custom-call | flops 67108864 | bytes 1310720 | tf_op jit(solution)/shard_map/span_states/pallas_call | solution.py:218
  3.0 3.1 %collective-permute-start.1 = (bf16[264,256]{1,0:T(8,128)(2,1)S(1)}, bf16[264,256]{1,0:T(8,128)(2,1)S(1)}, u32[]{:S(2)}, u32[]{:S(2)}) collective-permute-start(bf16[264,256]{1,0:T(8,128)(2,1)S(1)} %get-tuple-element.38.refs_8_), channel_id=1, source_target_pairs={{0,1},{1,0},{2,3},{3,2},{4,5},{5,4},{6,7},{7,6},{8,9},{9,8},{10,11... | collective-permute-start | bytes 405512 | tf_op jit(solution)/shard_map/ppermute | solution.py:41
  6.1 1.6 %span_states.6 = (bf16[264,256]{1,0:T(8,128)(2,1)S(1)}, bf16[264,256]{1,0:T(8,128)(2,1)S(1)}) custom-call(f32[3,2,8]{2,1,0:T(2,128)} %bitcast.4, s32[2,8]{1,0:T(2,128)} %refs_1_.23, s32[2,8]{1,0:T(2,128)} %refs_2_.23, s32[2,8]{1,0:T(2,128)} %refs_3_.23, f32[2,8]{1,0:T(2,128)S(1)} %get-tuple-element.36.mf.refs_4_, ...), custom_call_target="tpu_custom_call" | custom-call | flops 67108864 | bytes 1310720 | tf_op jit(solution)/shard_map/span_states/pallas_call | solution.py:218
  7.8 1.7 %span_states.7 = (bf16[264,512]{1,0:T(8,128)(2,1)S(1)}, bf16[264,512]{1,0:T(8,128)(2,1)S(1)}) custom-call(f32[3,2,8]{2,1,0:T(2,128)} %bitcast.5, s32[2,8]{1,0:T(2,128)} %refs_1_.23, s32[2,8]{1,0:T(2,128)} %refs_2_.23, s32[2,8]{1,0:T(2,128)} %refs_3_.23, f32[2,8]{1,0:T(2,128)S(1)} %get-tuple-element.36.mf.refs_4_, ...), custom_call_target="tpu_custom_call" | custom-call | flops 134217728 | bytes 1310720 | tf_op jit(solution)/shard_map/span_states/pallas_call | solution.py:218
  9.5 2.1 %collective-permute-start.3 = (bf16[264,512]{1,0:T(8,128)(2,1)S(1)}, bf16[264,512]{1,0:T(8,128)(2,1)S(1)}, u32[]{:S(2)}, u32[]{:S(2)}) collective-permute-start(bf16[264,512]{1,0:T(8,128)(2,1)S(1)} %get-tuple-element.42.refs_2_), channel_id=1, source_target_pairs={{0,1},{1,0},{2,3},{3,2},{4,5},{5,4},{6,7},{7,6},{8,9},{9,8},{10,11... | collective-permute-start | bytes 811016 | tf_op jit(solution)/shard_map/ppermute | solution.py:41
  11.7 2.2 %collective-permute-done.refs_1_.refs_13_ = bf16[264,256]{1,0:T(8,128)(2,1)S(1)} collective-permute-done((bf16[264,256]{1,0:T(8,128)(2,1)S(1)}, bf16[264,256]{1,0:T(8,128)(2,1)S(1)}, u32[]{:S(2)}, u32[]{:S(2)}) %collective-permute-start) | collective-permute-done | bytes 135200 | tf_op jit(solution)/shard_map/ppermute | solution.py:41
  14.0 1.7 %span_states.8 = (bf16[264,512]{1,0:T(8,128)(2,1)S(1)}, bf16[264,512]{1,0:T(8,128)(2,1)S(1)}) custom-call(f32[3,2,8]{2,1,0:T(2,128)} %bitcast.6, s32[2,8]{1,0:T(2,128)} %refs_1_.23, s32[2,8]{1,0:T(2,128)} %refs_2_.23, s32[2,8]{1,0:T(2,128)} %refs_3_.23, f32[2,8]{1,0:T(2,128)S(1)} %get-tuple-element.36.mf.refs_4_, ...), custom_call_target="tpu_custom_call" | custom-call | flops 134217728 | bytes 1310720 | tf_op jit(solution)/shard_map/span_states/pallas_call | solution.py:218
  15.7 1.3 %collective-permute-start.6 = (bf16[264,512]{1,0:T(8,128)(2,1)S(1)}, bf16[264,512]{1,0:T(8,128)(2,1)S(1)}, u32[]{:S(2)}, u32[]{:S(2)}) collective-permute-start(bf16[264,512]{1,0:T(8,128)(2,1)S(1)} %get-tuple-element.44.refs_2_), channel_id=1, source_target_pairs={{0,1},{1,0},{2,3},{3,2},{4,5},{5,4},{6,7},{7,6},{8,9},{9,8},{10,11... | collective-permute-start | bytes 811016 | tf_op jit(solution)/shard_map/ppermute | solution.py:41
  17.0 2.6 %collective-permute-start.2 = (bf16[264,256]{1,0:T(8,128)(2,1)S(1)}, bf16[264,256]{1,0:T(8,128)(2,1)S(1)}, u32[]{:S(2)}, u32[]{:S(2)}) collective-permute-start(bf16[264,256]{1,0:T(8,128)(2,1)S(1)} %combine.21.refs_8_), channel_id=1, source_target_pairs={{0,2},{1,3},{2,0},{3,1},{4,6},{5,7},{6,4},{7,5},{8,10},{9,11},{10,... | collective-permute-start | bytes 405512 | tf_op jit(solution)/shard_map/ppermute | solution.py:41
  19.6 0.3 collective-permute-start.5
  20.0 6.2 %collective-permute-done.3.refs_1_.refs_9_ = bf16[264,512]{1,0:T(8,128)(2,1)S(1)} collective-permute-done((bf16[264,512]{1,0:T(8,128)(2,1)S(1)}, bf16[264,512]{1,0:T(8,128)(2,1)S(1)}, u32[]{:S(2)}, u32[]{:S(2)}) %collective-permute-start.3) | collective-permute-done | bytes 270368 | tf_op jit(solution)/shard_map/ppermute | solution.py:41
  26.3 0.8 collective-permute-start.9
  27.3 1.7 %span_states.9 = (bf16[264,512]{1,0:T(8,128)(2,1)S(1)}, bf16[264,512]{1,0:T(8,128)(2,1)S(1)}) custom-call(f32[3,2,8]{2,1,0:T(2,128)} %bitcast.7, s32[2,8]{1,0:T(2,128)} %refs_1_.23, s32[2,8]{1,0:T(2,128)} %refs_2_.23, s32[2,8]{1,0:T(2,128)} %refs_3_.23, f32[2,8]{1,0:T(2,128)S(1)} %get-tuple-element.36.mf.refs_4_, ...), custom_call_target="tpu_custom_call" | custom-call | flops 134217728 | bytes 1310720 | tf_op jit(solution)/shard_map/span_states/pallas_call | solution.py:218
  29.0 2.6 %collective-permute-done.6.refs_1_.refs_9_ = bf16[264,512]{1,0:T(8,128)(2,1)S(1)} collective-permute-done((bf16[264,512]{1,0:T(8,128)(2,1)S(1)}, bf16[264,512]{1,0:T(8,128)(2,1)S(1)}, u32[]{:S(2)}, u32[]{:S(2)}) %collective-permute-start.6) | collective-permute-done | bytes 270368 | tf_op jit(solution)/shard_map/ppermute | solution.py:41
  31.7 7.2 %collective-permute-done.5.refs_2_.refs_1_.refs_10_ = bf16[264,256]{1,0:T(8,128)(2,1)S(1)} collective-permute-done((bf16[264,256]{1,0:T(8,128)(2,1)S(1)}, bf16[264,256]{1,0:T(8,128)(2,1)S(1)}, u32[]{:S(2)}, u32[]{:S(2)}) %collective-permute-start.5) | collective-permute-done | bytes 135200 | tf_op jit(solution)/shard_map/ppermute | solution.py:41
  39.1 0.5 collective-permute-start.10
  39.6 0.8 collective-permute-done.7.refs_3_.refs_2_.refs_11_
  40.8 1.8 %collective-permute-done.9.refs_2_.refs_10_.refs_1_ = bf16[264,512]{1,0:T(8,128)(2,1)S(1)} collective-permute-done((bf16[264,512]{1,0:T(8,128)(2,1)S(1)}, bf16[264,512]{1,0:T(8,128)(2,1)S(1)}, u32[]{:S(2)}, u32[]{:S(2)}) %collective-permute-start.9) | collective-permute-done | bytes 270368 | tf_op jit(solution)/shard_map/ppermute | solution.py:41
  43.0 3.7 %collective-permute-start.8 = (bf16[264,256]{1,0:T(8,128)(2,1)S(1)}, bf16[264,256]{1,0:T(8,128)(2,1)S(1)}, u32[]{:S(2)}, u32[]{:S(2)}) collective-permute-start(bf16[264,256]{1,0:T(8,128)(2,1)S(1)} %combine.26.refs_4_), channel_id=1, source_target_pairs={{0,8},{4,12},{1,9},{5,13},{2,10},{6,14},{3,11},{7,15},{16,24},{20,... | collective-permute-start | bytes 405512 | tf_op jit(solution)/shard_map/ppermute | solution.py:41
  46.6 1.3 %collective-permute-start.15 = (bf16[264,256]{1,0:T(8,128)(2,1)S(1)}, bf16[264,256]{1,0:T(8,128)(2,1)S(1)}, u32[]{:S(2)}, u32[]{:S(2)}) collective-permute-start(bf16[264,256]{1,0:T(8,128)(2,1)S(1)} %combine.27.refs_3_), channel_id=1, source_target_pairs={{0,8},{4,12},{1,9},{5,13},{2,10},{6,14},{3,11},{7,15},{16,24},{20,... | collective-permute-start | bytes 405512 | tf_op jit(solution)/shard_map/ppermute | solution.py:41
  47.9 2.6 %collective-permute-done.8.refs_3_.refs_12_ = bf16[264,256]{1,0:T(8,128)(2,1)S(1)} collective-permute-done((bf16[264,256]{1,0:T(8,128)(2,1)S(1)}, bf16[264,256]{1,0:T(8,128)(2,1)S(1)}, u32[]{:S(2)}, u32[]{:S(2)}) %collective-permute-start.8) | collective-permute-done | bytes 135200 | tf_op jit(solution)/shard_map/ppermute | solution.py:41
  50.9 0.3 combine.31.refs_4_
  51.2 1.5 %collective-permute-done.15.refs_3_.refs_16_ = bf16[264,256]{1,0:T(8,128)(2,1)S(1)} collective-permute-done((bf16[264,256]{1,0:T(8,128)(2,1)S(1)}, bf16[264,256]{1,0:T(8,128)(2,1)S(1)}, u32[]{:S(2)}, u32[]{:S(2)}) %collective-permute-start.15) | collective-permute-done | bytes 135200 | tf_op jit(solution)/shard_map/ppermute | solution.py:41
  52.8 2.3 %span_outputs.8 = (bf16[256,4096]{1,0:T(8,128)(2,1)}, f32[8,128]{1,0:T(8,128)S(1)}) custom-call(f32[3,2,8]{2,1,0:T(2,128)} %bitcast.8, s32[2,8]{1,0:T(2,128)} %refs_1_.23, s32[2,8]{1,0:T(2,128)} %refs_2_.23, s32[2,8]{1,0:T(2,128)} %refs_3_.23, f32[256,8]{1,0:T(8,128)S(1)} %get-tuple-element.34.refs_4_, f32[8,256]{1,0:T(8,128)S(1)} %get-tuple-element.35.refs_5_, ...), custom_call_target="tpu_custom_call" | custom-call | flops 167772160 | bytes 1867776 | tf_op jit(solution)/shard_map/span_outputs/pallas_call | solution.py:333
  55.1 3.3 %collective-permute-done.14.refs_2_.refs_1_.refs_10_ = bf16[264,512]{1,0:T(8,128)(2,1)S(1)} collective-permute-done((bf16[264,512]{1,0:T(8,128)(2,1)S(1)}, bf16[264,512]{1,0:T(8,128)(2,1)S(1)}, u32[]{:S(2)}, u32[]{:S(2)}) %collective-permute-start.14) | collective-permute-done | bytes 270368 | tf_op jit(solution)/shard_map/ppermute | solution.py:41
  58.7 3.3 %collective-permute-start.13 = (bf16[264,512]{1,0:T(8,128)(2,1)S(1)}, bf16[264,512]{1,0:T(8,128)(2,1)S(1)}, u32[]{:S(2)}, u32[]{:S(2)}) collective-permute-start(bf16[264,512]{1,0:T(8,128)(2,1)S(1)} %combine.31.refs_4_), channel_id=1, source_target_pairs={{0,8},{4,12},{1,9},{5,13},{2,10},{6,14},{3,11},{7,15},{16,24},{20,... | collective-permute-start | bytes 811016 | tf_op jit(solution)/shard_map/ppermute | solution.py:41
  62.0 0.6 collective-permute-start.11
  62.6 0.3 combine.34.refs_13_
  62.9 5.5 %collective-permute-done.13.refs_12_.refs_3_ = bf16[264,512]{1,0:T(8,128)(2,1)S(1)} collective-permute-done((bf16[264,512]{1,0:T(8,128)(2,1)S(1)}, bf16[264,512]{1,0:T(8,128)(2,1)S(1)}, u32[]{:S(2)}, u32[]{:S(2)}) %collective-permute-start.13) | collective-permute-done | bytes 270368 | tf_op jit(solution)/shard_map/ppermute | solution.py:41
  68.4 2.3 %span_outputs.9 = (bf16[256,4096]{1,0:T(8,128)(2,1)}, f32[8,128]{1,0:T(8,128)S(1)}) custom-call(f32[3,2,8]{2,1,0:T(2,128)} %bitcast.9, s32[2,8]{1,0:T(2,128)} %refs_1_.23, s32[2,8]{1,0:T(2,128)} %refs_2_.23, s32[2,8]{1,0:T(2,128)} %refs_3_.23, f32[256,8]{1,0:T(8,128)S(1)} %get-tuple-element.34.refs_4_, ...), custom_call_target="tpu_custom_call", output_to_operand_aliasing={{0}: (14, {})} | custom-call | flops 167772160 | bytes 1867776 | tf_op jit(solution)/shard_map/span_outputs/pallas_call | solution.py:333
  70.6 0.3 combine.35.refs_3_
  70.9 6.3 %collective-permute-done.11.refs_2_.refs_1_.refs_10_ = bf16[264,512]{1,0:T(8,128)(2,1)S(1)} collective-permute-done((bf16[264,512]{1,0:T(8,128)(2,1)S(1)}, bf16[264,512]{1,0:T(8,128)(2,1)S(1)}, u32[]{:S(2)}, u32[]{:S(2)}) %collective-permute-start.11) | collective-permute-done | bytes 270368 | tf_op jit(solution)/shard_map/ppermute | solution.py:41
  77.6 1.6 %collective-permute-start.22 = (bf16[264,512]{1,0:T(8,128)(2,1)S(1)}, bf16[264,512]{1,0:T(8,128)(2,1)S(1)}, u32[]{:S(2)}, u32[]{:S(2)}) collective-permute-start(bf16[264,512]{1,0:T(8,128)(2,1)S(1)} %combine.34.refs_13_), channel_id=1, source_target_pairs={{0,8},{4,12},{1,9},{5,13},{2,10},{6,14},{3,11},{7,15},{16,24},{20,... | collective-permute-start | bytes 811016 | tf_op jit(solution)/shard_map/ppermute | solution.py:41
  79.2 0.3 combine.37.refs_4_
  79.5 1.6 %collective-permute-start.18 = (bf16[264,512]{1,0:T(8,128)(2,1)S(1)}, bf16[264,512]{1,0:T(8,128)(2,1)S(1)}, u32[]{:S(2)}, u32[]{:S(2)}) collective-permute-start(bf16[264,512]{1,0:T(8,128)(2,1)S(1)} %combine.37.refs_4_), channel_id=1, source_target_pairs={{0,8},{4,12},{1,9},{5,13},{2,10},{6,14},{3,11},{7,15},{16,24},{20,... | collective-permute-start | bytes 811016 | tf_op jit(solution)/shard_map/ppermute | solution.py:41
  81.1 2.0 %collective-permute-start.20 = (bf16[264,256]{1,0:T(8,128)(2,1)S(1)}, bf16[264,256]{1,0:T(8,128)(2,1)S(1)}, u32[]{:S(2)}, u32[]{:S(2)}) collective-permute-start(bf16[264,256]{1,0:T(8,128)(2,1)S(1)} %combine.29.refs_2_), channel_id=1, source_target_pairs={{0,1},{1,0},{2,3},{3,2},{4,5},{5,4},{6,7},{7,6},{8,9},{9,8},{10,11... | collective-permute-start | bytes 405512 | tf_op jit(solution)/shard_map/ppermute | solution.py:41
  83.2 2.8 %collective-permute-done.22.refs_3_.refs_12_ = bf16[264,512]{1,0:T(8,128)(2,1)S(1)} collective-permute-done((bf16[264,512]{1,0:T(8,128)(2,1)S(1)}, bf16[264,512]{1,0:T(8,128)(2,1)S(1)}, u32[]{:S(2)}, u32[]{:S(2)}) %collective-permute-start.22) | collective-permute-done | bytes 270368 | tf_op jit(solution)/shard_map/ppermute | solution.py:41
  86.0 0.3 combine.38.refs_11_
  86.3 5.1 %collective-permute-done.20.refs_9_ = bf16[264,256]{1,0:T(8,128)(2,1)S(1)} collective-permute-done((bf16[264,256]{1,0:T(8,128)(2,1)S(1)}, bf16[264,256]{1,0:T(8,128)(2,1)S(1)}, u32[]{:S(2)}, u32[]{:S(2)}) %collective-permute-start.20) | collective-permute-done | bytes 135200 | tf_op jit(solution)/shard_map/ppermute | solution.py:41
  91.5 2.9 %collective-permute-done.21.refs_10_ = bf16[264,256]{1,0:T(8,128)(2,1)S(1)} collective-permute-done((bf16[264,256]{1,0:T(8,128)(2,1)S(1)}, bf16[264,256]{1,0:T(8,128)(2,1)S(1)}, u32[]{:S(2)}, u32[]{:S(2)}) %collective-permute-start.21) | collective-permute-done | bytes 135200 | tf_op jit(solution)/shard_map/ppermute | solution.py:41
  94.4 2.1 %span_outputs.10 = (bf16[256,4096]{1,0:T(8,128)(2,1)}, f32[8,128]{1,0:T(8,128)S(1)}) custom-call(f32[3,2,8]{2,1,0:T(2,128)} %bitcast.10, s32[2,8]{1,0:T(2,128)} %refs_1_.23, s32[2,8]{1,0:T(2,128)} %refs_2_.23, s32[2,8]{1,0:T(2,128)} %refs_3_.23, f32[256,8]{1,0:T(8,128)S(1)} %get-tuple-element.34.refs_4_, ...), custom_call_target="tpu_custom_call", output_to_operand_aliasing={{0}: (12, {})} | custom-call | flops 167772160 | bytes 1056768 | tf_op jit(solution)/shard_map/span_outputs/pallas_call | solution.py:333
  96.5 2.1 %span_outputs.11 = (bf16[256,4096]{1,0:T(8,128)(2,1)}, f32[8,128]{1,0:T(8,128)S(1)}) custom-call(f32[3,2,8]{2,1,0:T(2,128)} %bitcast.11, s32[2,8]{1,0:T(2,128)} %refs_1_.23, s32[2,8]{1,0:T(2,128)} %refs_2_.23, s32[2,8]{1,0:T(2,128)} %refs_3_.23, f32[256,8]{1,0:T(8,128)S(1)} %get-tuple-element.34.refs_4_, ...), custom_call_target="tpu_custom_call", output_to_operand_aliasing={{0}: (11, {})} | custom-call | flops 167772160 | bytes 1056768 | tf_op jit(solution)/shard_map/span_outputs/pallas_call | solution.py:333
  98.6 0.3 combine.39.refs_13_
  99.0 2.3 %span_outputs.12 = (bf16[256,4096]{1,0:T(8,128)(2,1)}, f32[8,128]{1,0:T(8,128)S(1)}) custom-call(f32[3,2,8]{2,1,0:T(2,128)} %bitcast.12, s32[2,8]{1,0:T(2,128)} %refs_1_.23, s32[2,8]{1,0:T(2,128)} %refs_2_.23, s32[2,8]{1,0:T(2,128)} %refs_3_.23, f32[256,8]{1,0:T(8,128)S(1)} %get-tuple-element.34.refs_4_, ...), custom_call_target="tpu_custom_call", output_to_operand_aliasing={{0}: (14, {})} | custom-call | flops 167772160 | bytes 1867776 | tf_op jit(solution)/shard_map/span_outputs/pallas_call | solution.py:333
  101.3 2.1 %span_outputs.13 = (bf16[256,4096]{1,0:T(8,128)(2,1)}, f32[8,128]{1,0:T(8,128)S(1)}) custom-call(f32[3,2,8]{2,1,0:T(2,128)} %bitcast.13, s32[2,8]{1,0:T(2,128)} %refs_1_.23, s32[2,8]{1,0:T(2,128)} %refs_2_.23, s32[2,8]{1,0:T(2,128)} %refs_3_.23, f32[256,8]{1,0:T(8,128)S(1)} %get-tuple-element.34.refs_4_, ...), custom_call_target="tpu_custom_call", output_to_operand_aliasing={{0}: (11, {})} | custom-call | flops 167772160 | bytes 1056768 | tf_op jit(solution)/shard_map/span_outputs/pallas_call | solution.py:333
  103.4 2.3 %span_outputs.14 = (bf16[256,4096]{1,0:T(8,128)(2,1)}, f32[8,128]{1,0:T(8,128)S(1)}) custom-call(f32[3,2,8]{2,1,0:T(2,128)} %bitcast.14, s32[2,8]{1,0:T(2,128)} %refs_1_.23, s32[2,8]{1,0:T(2,128)} %refs_2_.23, s32[2,8]{1,0:T(2,128)} %refs_3_.23, f32[256,8]{1,0:T(8,128)S(1)} %get-tuple-element.34.refs_4_, ...), custom_call_target="tpu_custom_call", output_to_operand_aliasing={{0}: (14, {})} | custom-call | flops 167772160 | bytes 1867776 | tf_op jit(solution)/shard_map/span_outputs/pallas_call | solution.py:333
  105.9 2.1 %span_outputs.15 = (bf16[256,4096]{1,0:T(8,128)(2,1)}, f32[8,128]{1,0:T(8,128)}) custom-call(f32[3,2,8]{2,1,0:T(2,128)} %bitcast.15, s32[2,8]{1,0:T(2,128)} %refs_1_.23, s32[2,8]{1,0:T(2,128)} %refs_2_.23, s32[2,8]{1,0:T(2,128)} %refs_3_.23, f32[256,8]{1,0:T(8,128)S(1)} %get-tuple-element.34.refs_4_, ...), custom_call_target="tpu_custom_call", output_to_operand_aliasing={{0}: (11, {})} | custom-call | flops 167772160 | bytes 1056768 | tf_op jit(solution)/shard_map/span_outputs/pallas_call | solution.py:333
  (42 shorter events, 3.2 us)
Async XLA Ops:
  3.0 8.6 %collective-permute-start.1 = (bf16[264,256]{1,0:T(8,128)(2,1)S(1)}, bf16[264,256]{1,0:T(8,128)(2,1)S(1)}, u32[]{:S(2)}, u32[]{:S(2)}) collective-permute-start(bf16[264,256]{1,0:T(8,128)(2,1)S(1)} %get-tuple-element.38.refs_8_), channel_id=1, source_target_pairs={{0,1},{1,0},{2,3},{3,2},{4,5},{5,4},{6,7},{7,6},{8,9},{9,8},{10,11... | collective-permute-start | bytes 405512 | tf_op jit(solution)/shard_map/ppermute | solution.py:41
  7.7 6.2 %collective-permute-start = (bf16[264,256]{1,0:T(8,128)(2,1)S(1)}, bf16[264,256]{1,0:T(8,128)(2,1)S(1)}, u32[]{:S(2)}, u32[]{:S(2)}) collective-permute-start(bf16[264,256]{1,0:T(8,128)(2,1)S(1)} %get-tuple-element.40.refs_8_), channel_id=1, source_target_pairs={{0,1},{1,0},{2,3},{3,2},{4,5},{5,4},{6,7},{7,6},{8,9},{9,8},{10,11... | collective-permute-start | bytes 405512 | tf_op jit(solution)/shard_map/ppermute | solution.py:41
  9.5 16.6 %collective-permute-start.3 = (bf16[264,512]{1,0:T(8,128)(2,1)S(1)}, bf16[264,512]{1,0:T(8,128)(2,1)S(1)}, u32[]{:S(2)}, u32[]{:S(2)}) collective-permute-start(bf16[264,512]{1,0:T(8,128)(2,1)S(1)} %get-tuple-element.42.refs_2_), channel_id=1, source_target_pairs={{0,1},{1,0},{2,3},{3,2},{4,5},{5,4},{6,7},{7,6},{8,9},{9,8},{10,11... | collective-permute-start | bytes 811016 | tf_op jit(solution)/shard_map/ppermute | solution.py:41
  15.7 15.8 %collective-permute-start.6 = (bf16[264,512]{1,0:T(8,128)(2,1)S(1)}, bf16[264,512]{1,0:T(8,128)(2,1)S(1)}, u32[]{:S(2)}, u32[]{:S(2)}) collective-permute-start(bf16[264,512]{1,0:T(8,128)(2,1)S(1)} %get-tuple-element.44.refs_2_), channel_id=1, source_target_pairs={{0,1},{1,0},{2,3},{3,2},{4,5},{5,4},{6,7},{7,6},{8,9},{9,8},{10,11... | collective-permute-start | bytes 811016 | tf_op jit(solution)/shard_map/ppermute | solution.py:41
  17.0 10.1 %collective-permute-start.2 = (bf16[264,256]{1,0:T(8,128)(2,1)S(1)}, bf16[264,256]{1,0:T(8,128)(2,1)S(1)}, u32[]{:S(2)}, u32[]{:S(2)}) collective-permute-start(bf16[264,256]{1,0:T(8,128)(2,1)S(1)} %combine.21.refs_8_), channel_id=1, source_target_pairs={{0,2},{1,3},{2,0},{3,1},{4,6},{5,7},{6,4},{7,5},{8,10},{9,11},{10,... | collective-permute-start | bytes 405512 | tf_op jit(solution)/shard_map/ppermute | solution.py:41
  19.6 19.3 %collective-permute-start.5 = (bf16[264,256]{1,0:T(8,128)(2,1)S(1)}, bf16[264,256]{1,0:T(8,128)(2,1)S(1)}, u32[]{:S(2)}, u32[]{:S(2)}) collective-permute-start(bf16[264,256]{1,0:T(8,128)(2,1)S(1)} %combine.20.refs_2_), channel_id=1, source_target_pairs={{0,2},{1,3},{2,0},{3,1},{4,6},{5,7},{6,4},{7,5},{8,10},{9,11},{10,... | collective-permute-start | bytes 405512 | tf_op jit(solution)/shard_map/ppermute | solution.py:41
  26.3 16.3 %collective-permute-start.9 = (bf16[264,512]{1,0:T(8,128)(2,1)S(1)}, bf16[264,512]{1,0:T(8,128)(2,1)S(1)}, u32[]{:S(2)}, u32[]{:S(2)}) collective-permute-start(bf16[264,512]{1,0:T(8,128)(2,1)S(1)} %combine.22.refs_3_), channel_id=1, source_target_pairs={{0,2},{1,3},{2,0},{3,1},{4,6},{5,7},{6,4},{7,5},{8,10},{9,11},{10,... | collective-permute-start | bytes 811016 | tf_op jit(solution)/shard_map/ppermute | solution.py:41
  39.0 1.4 %collective-permute-start.7 = (bf16[264,256]{1,0:T(8,128)(2,1)S(1)}, bf16[264,256]{1,0:T(8,128)(2,1)S(1)}, u32[]{:S(2)}, u32[]{:S(2)}) collective-permute-start(bf16[264,256]{1,0:T(8,128)(2,1)S(1)} %combine.25.refs_4_), channel_id=1, source_target_pairs={{0,4},{4,0},{8,12},{12,8},{1,5},{5,1},{9,13},{13,9},{2,6},{6,2},{1... | collective-permute-start | bytes 405512 | tf_op jit(solution)/shard_map/ppermute | solution.py:41
  39.1 1.5 %collective-permute-start.10 = (bf16[264,256]{1,0:T(8,128)(2,1)S(1)}, bf16[264,256]{1,0:T(8,128)(2,1)S(1)}, u32[]{:S(2)}, u32[]{:S(2)}) collective-permute-start(bf16[264,256]{1,0:T(8,128)(2,1)S(1)} %combine.23.refs_8_), channel_id=1, source_target_pairs={{0,4},{4,0},{8,12},{12,8},{1,5},{5,1},{9,13},{13,9},{2,6},{6,2},{1... | collective-permute-start | bytes 405512 | tf_op jit(solution)/shard_map/ppermute | solution.py:41
  39.6 11.1 %collective-permute-start.4 = (bf16[264,512]{1,0:T(8,128)(2,1)S(1)}, bf16[264,512]{1,0:T(8,128)(2,1)S(1)}, u32[]{:S(2)}, u32[]{:S(2)}) collective-permute-start(bf16[264,512]{1,0:T(8,128)(2,1)S(1)} %get-tuple-element.46.refs_2_), channel_id=1, source_target_pairs={{0,1},{1,0},{2,3},{3,2},{4,5},{5,4},{6,7},{7,6},{8,9},{9,8},{10,11... | collective-permute-start | bytes 811016 | tf_op jit(solution)/shard_map/ppermute | solution.py:41
  42.8 10.0 %copy-start = (bf16[256,4096]{1,0:T(8,128)(2,1)S(1)}, bf16[256,4096]{1,0:T(8,128)(2,1)}, u32[]{:S(2)}) copy-start(bf16[256,4096]{1,0:T(8,128)(2,1)} %refs_8_.15) | copy-start | bytes 6291460
  42.8 10.0 %copy-start.1 = (bf16[256,2048]{1,0:T(8,128)(2,1)S(1)}, bf16[256,2048]{1,0:T(8,128)(2,1)}, u32[]{:S(2)}) copy-start(bf16[256,2048]{1,0:T(8,128)(2,1)} %refs_7_.23) | copy-start | bytes 3145732
  42.8 10.0 %copy-start.2 = (bf16[256,2048]{1,0:T(8,128)(2,1)S(1)}, bf16[256,2048]{1,0:T(8,128)(2,1)}, u32[]{:S(2)}) copy-start(bf16[256,2048]{1,0:T(8,128)(2,1)} %refs_6_.23) | copy-start | bytes 3145732
  42.8 8.1 %collective-permute-start.12 = (bf16[264,512]{1,0:T(8,128)(2,1)S(1)}, bf16[264,512]{1,0:T(8,128)(2,1)S(1)}, u32[]{:S(2)}, u32[]{:S(2)}) collective-permute-start(bf16[264,512]{1,0:T(8,128)(2,1)S(1)} %combine.28.refs_4_), channel_id=1, source_target_pairs={{0,4},{4,0},{8,12},{12,8},{1,5},{5,1},{9,13},{13,9},{2,6},{6,2},{1... | collective-permute-start | bytes 811016 | tf_op jit(solution)/shard_map/ppermute | solution.py:41
  42.9 15.6 %collective-permute-start.14 = (bf16[264,512]{1,0:T(8,128)(2,1)S(1)}, bf16[264,512]{1,0:T(8,128)(2,1)S(1)}, u32[]{:S(2)}, u32[]{:S(2)}) collective-permute-start(bf16[264,512]{1,0:T(8,128)(2,1)S(1)} %combine.24.refs_3_), channel_id=1, source_target_pairs={{0,2},{1,3},{2,0},{3,1},{4,6},{5,7},{6,4},{7,5},{8,10},{9,11},{10,... | collective-permute-start | bytes 811016 | tf_op jit(solution)/shard_map/ppermute | solution.py:41
  43.0 7.6 %collective-permute-start.8 = (bf16[264,256]{1,0:T(8,128)(2,1)S(1)}, bf16[264,256]{1,0:T(8,128)(2,1)S(1)}, u32[]{:S(2)}, u32[]{:S(2)}) collective-permute-start(bf16[264,256]{1,0:T(8,128)(2,1)S(1)} %combine.26.refs_4_), channel_id=1, source_target_pairs={{0,8},{4,12},{1,9},{5,13},{2,10},{6,14},{3,11},{7,15},{16,24},{20,... | collective-permute-start | bytes 405512 | tf_op jit(solution)/shard_map/ppermute | solution.py:41
  46.6 6.0 %collective-permute-start.15 = (bf16[264,256]{1,0:T(8,128)(2,1)S(1)}, bf16[264,256]{1,0:T(8,128)(2,1)S(1)}, u32[]{:S(2)}, u32[]{:S(2)}) collective-permute-start(bf16[264,256]{1,0:T(8,128)(2,1)S(1)} %combine.27.refs_3_), channel_id=1, source_target_pairs={{0,8},{4,12},{1,9},{5,13},{2,10},{6,14},{3,11},{7,15},{16,24},{20,... | collective-permute-start | bytes 405512 | tf_op jit(solution)/shard_map/ppermute | solution.py:41
  58.7 3.9 %collective-permute-start.16 = (bf16[264,512]{1,0:T(8,128)(2,1)S(1)}, bf16[264,512]{1,0:T(8,128)(2,1)S(1)}, u32[]{:S(2)}, u32[]{:S(2)}) collective-permute-start(bf16[264,512]{1,0:T(8,128)(2,1)S(1)} %combine.33.refs_4_), channel_id=1, source_target_pairs={{0,4},{4,0},{8,12},{12,8},{1,5},{5,1},{9,13},{13,9},{2,6},{6,2},{1... | collective-permute-start | bytes 811016 | tf_op jit(solution)/shard_map/ppermute | solution.py:41
  58.7 9.6 %collective-permute-start.13 = (bf16[264,512]{1,0:T(8,128)(2,1)S(1)}, bf16[264,512]{1,0:T(8,128)(2,1)S(1)}, u32[]{:S(2)}, u32[]{:S(2)}) collective-permute-start(bf16[264,512]{1,0:T(8,128)(2,1)S(1)} %combine.31.refs_4_), channel_id=1, source_target_pairs={{0,8},{4,12},{1,9},{5,13},{2,10},{6,14},{3,11},{7,15},{16,24},{20,... | collective-permute-start | bytes 811016 | tf_op jit(solution)/shard_map/ppermute | solution.py:41
  62.0 15.2 %collective-permute-start.11 = (bf16[264,512]{1,0:T(8,128)(2,1)S(1)}, bf16[264,512]{1,0:T(8,128)(2,1)S(1)}, u32[]{:S(2)}, u32[]{:S(2)}) collective-permute-start(bf16[264,512]{1,0:T(8,128)(2,1)S(1)} %combine.30.refs_4_), channel_id=1, source_target_pairs={{0,2},{1,3},{2,0},{3,1},{4,6},{5,7},{6,4},{7,5},{8,10},{9,11},{10,... | collective-permute-start | bytes 811016 | tf_op jit(solution)/shard_map/ppermute | solution.py:41
  77.5 1.8 %collective-permute-start.17 = (bf16[264,512]{1,0:T(8,128)(2,1)S(1)}, bf16[264,512]{1,0:T(8,128)(2,1)S(1)}, u32[]{:S(2)}, u32[]{:S(2)}) collective-permute-start(bf16[264,512]{1,0:T(8,128)(2,1)S(1)} %combine.36.refs_4_), channel_id=1, source_target_pairs={{0,4},{4,0},{8,12},{12,8},{1,5},{5,1},{9,13},{13,9},{2,6},{6,2},{1... | collective-permute-start | bytes 811016 | tf_op jit(solution)/shard_map/ppermute | solution.py:41
  77.6 8.4 %collective-permute-start.22 = (bf16[264,512]{1,0:T(8,128)(2,1)S(1)}, bf16[264,512]{1,0:T(8,128)(2,1)S(1)}, u32[]{:S(2)}, u32[]{:S(2)}) collective-permute-start(bf16[264,512]{1,0:T(8,128)(2,1)S(1)} %combine.34.refs_13_), channel_id=1, source_target_pairs={{0,8},{4,12},{1,9},{5,13},{2,10},{6,14},{3,11},{7,15},{16,24},{20,... | collective-permute-start | bytes 811016 | tf_op jit(solution)/shard_map/ppermute | solution.py:41
  79.2 17.3 %collective-permute-start.19 = (bf16[264,512]{1,0:T(8,128)(2,1)S(1)}, bf16[264,512]{1,0:T(8,128)(2,1)S(1)}, u32[]{:S(2)}, u32[]{:S(2)}) collective-permute-start(bf16[264,512]{1,0:T(8,128)(2,1)S(1)} %combine.35.refs_3_), channel_id=1, source_target_pairs={{0,1},{1,0},{2,3},{3,2},{4,5},{5,4},{6,7},{7,6},{8,9},{9,8},{10,11... | collective-permute-start | bytes 811016 | tf_op jit(solution)/shard_map/ppermute | solution.py:41
  79.5 19.1 %collective-permute-start.18 = (bf16[264,512]{1,0:T(8,128)(2,1)S(1)}, bf16[264,512]{1,0:T(8,128)(2,1)S(1)}, u32[]{:S(2)}, u32[]{:S(2)}) collective-permute-start(bf16[264,512]{1,0:T(8,128)(2,1)S(1)} %combine.37.refs_4_), channel_id=1, source_target_pairs={{0,8},{4,12},{1,9},{5,13},{2,10},{6,14},{3,11},{7,15},{16,24},{20,... | collective-permute-start | bytes 811016 | tf_op jit(solution)/shard_map/ppermute | solution.py:41
  81.1 10.4 %collective-permute-start.20 = (bf16[264,256]{1,0:T(8,128)(2,1)S(1)}, bf16[264,256]{1,0:T(8,128)(2,1)S(1)}, u32[]{:S(2)}, u32[]{:S(2)}) collective-permute-start(bf16[264,256]{1,0:T(8,128)(2,1)S(1)} %combine.29.refs_2_), channel_id=1, source_target_pairs={{0,1},{1,0},{2,3},{3,2},{4,5},{5,4},{6,7},{7,6},{8,9},{9,8},{10,11... | collective-permute-start | bytes 405512 | tf_op jit(solution)/shard_map/ppermute | solution.py:41
  83.1 11.3 %collective-permute-start.21 = (bf16[264,256]{1,0:T(8,128)(2,1)S(1)}, bf16[264,256]{1,0:T(8,128)(2,1)S(1)}, u32[]{:S(2)}, u32[]{:S(2)}) collective-permute-start(bf16[264,256]{1,0:T(8,128)(2,1)S(1)} %combine.32.refs_17_), channel_id=1, source_target_pairs={{0,1},{1,0},{2,3},{3,2},{4,5},{5,4},{6,7},{7,6},{8,9},{9,8},{10,11... | collective-permute-start | bytes 405512 | tf_op jit(solution)/shard_map/ppermute | solution.py:41
  86.3 15.0 %collective-permute-start.24 = (bf16[264,512]{1,0:T(8,128)(2,1)S(1)}, bf16[264,512]{1,0:T(8,128)(2,1)S(1)}, u32[]{:S(2)}, u32[]{:S(2)}) collective-permute-start(bf16[264,512]{1,0:T(8,128)(2,1)S(1)} %combine.38.refs_11_), channel_id=1, source_target_pairs={{0,1},{1,0},{2,3},{3,2},{4,5},{5,4},{6,7},{7,6},{8,9},{9,8},{10,11... | collective-permute-start | bytes 811016 | tf_op jit(solution)/shard_map/ppermute | solution.py:41
  98.9 7.0 %collective-permute-start.23 = (bf16[264,512]{1,0:T(8,128)(2,1)S(1)}, bf16[264,512]{1,0:T(8,128)(2,1)S(1)}, u32[]{:S(2)}, u32[]{:S(2)}) collective-permute-start(bf16[264,512]{1,0:T(8,128)(2,1)S(1)} %combine.39.refs_13_), channel_id=1, source_target_pairs={{0,1},{1,0},{2,3},{3,2},{4,5},{5,4},{6,7},{7,6},{8,9},{9,8},{10,11... | collective-permute-start | bytes 811016 | tf_op jit(solution)/shard_map/ppermute | solution.py:41

commit v6 on v5

--- a/solution.py
+++ b/solution.py
@@ -41,7 +41,12 @@
     return lax.ppermute(x, axis, pairs)
 
 
-def gate_kernel(i_ref, f_ref, run_ref, weight_ref, shift_ref, mf_ref):
+def table_rows(blocks):
+    at = {"scale": 0, "row": 3 * blocks, DK: 6 * blocks, DV: 7 * blocks, "factor": 8 * blocks, "peak": 9 * blocks}
+    return at, 9 * blocks + 2
+
+
+def gate_kernel(i_ref, f_ref, scales, tensors, offsets, fbits, run_ref, weight_ref, shift_ref, table_ref):
     gate, x = i_ref[...], f_ref[...].astype(F32)
     log_forget = jnp.minimum(x, 0.0) - jnp.log1p(jnp.exp(-jnp.abs(x)))
     size = x.shape[1]
@@ -60,20 +65,30 @@
     run_ref[...] = running
     weight_ref[...] = jnp.exp(exponent - peak)
     shift_ref[...] = gate.astype(F32) - running_row
-    mf_ref[...] = jnp.concatenate([peak, total], axis=0)
-
-
-def gates(input_gate, forget_gate):
+    blocks = tensors.shape[0]
+    at, _ = table_rows(blocks)
+    offset = offsets[...]
+    for e in range(3):
+        table_ref[at["scale"] + e * blocks : at["scale"] + (e + 1) * blocks, :] = scales[e]
+        struck = jnp.where(tensors[...] == e, lax.shift_right_logical(offset, DV.bit_length() - 1), -1)
+        table_ref[at["row"] + e * blocks : at["row"] + (e + 1) * blocks, :] = struck.astype(F32)
+    for width in (DK, DV):
+        table_ref[at[width] : at[width] + blocks, :] = (offset & (width - 1)).astype(F32)
+    table_ref[at["factor"] : at["factor"] + blocks, :] = -(lax.shift_left(jnp.ones_like(offset), fbits[...]).astype(F32))
+    table_ref[at["peak"] :, :] = jnp.concatenate([peak, total], axis=0)
+
+
+def gates(input_gate, forget_gate, small):
     heads, size = input_gate.shape
     col = jax.ShapeDtypeStruct((size, heads), F32)
     row = jax.ShapeDtypeStruct((heads, size), F32)
     return pl.pallas_call(
         gate_kernel,
-        out_shape=(col, col, row, jax.ShapeDtypeStruct((2, heads), F32)),
+        out_shape=(col, col, row, jax.ShapeDtypeStruct((table_rows(small[1].shape[0])[1], heads), F32)),
         compiler_params=pltpu.CompilerParams(vmem_limit_bytes=4 << 20),
         cost_estimate=pl.CostEstimate(flops=1 << 20, bytes_accessed=1 << 20, transcendentals=0),
         name="gates",
-    )(input_gate, forget_gate)
+    )(input_gate, forget_gate, *small)
 
 
 def pick(ref, h):
@@ -82,18 +97,17 @@
     return jnp.sum(jnp.where(lane == h, x, 0.0), axis=1, keepdims=True)
 
 
-def dequant(ref, at, lo, width, full, tensor_id, h, scales, tensors, offsets, bits):
-    rows = ref.shape[0]
-    row = lax.broadcasted_iota(jnp.int32, (BLK, 1), 0)
-    col = lax.broadcasted_iota(jnp.int32, (1, width), 1) + lo
+def dequant(ref, at, lo, width, full, tensor_id, h, table):
+    blocks = ref.shape[0] // BLK
+    rows, _ = table_rows(blocks)
+    row = lax.broadcasted_iota(jnp.int32, (BLK, 1), 0).astype(F32)
+    col = (lax.broadcasted_iota(jnp.int32, (1, width), 1) + lo).astype(F32)
     out = []
-    for b in range(rows // BLK):
+    for b in range(blocks):
         x = ref[b * BLK : (b + 1) * BLK, pl.ds(pl.multiple_of(at + lo, 128), width)].astype(F32)
-        offset, scale = offsets[b, h], scales[tensor_id, b, h]
-        hit_row = jnp.where(tensors[b, h] == tensor_id, offset // DV, -1)
-        hit_col = (offset % DV) % full
-        flipped = -(lax.shift_left(jnp.int32(1), bits[b, h]).astype(F32)) * scale
-        out.append((x * jnp.where((row == hit_row) & (col == hit_col), flipped, scale)).astype(BF16))
+        scale = table[rows["scale"] + tensor_id * blocks + b, h]
+        hit = (row == table[rows["row"] + tensor_id * blocks + b, h]) & (col == table[rows[full] + b, h])
+        out.append((x * jnp.where(hit, table[rows["factor"] + b, h] * scale, scale)).astype(BF16))
     return jnp.concatenate(out, axis=0)
 
 
@@ -190,49 +204,51 @@
 VMEM = pl.BlockSpec(memory_space=pltpu.VMEM)
 
 
-def state_kernel(pair, lo, scales, tensors, offsets, fbits, mf, weight_ref, k_ref, v_ref, keep_ref, send_ref):
+def state_kernel(pair, lo, at, table, weight_ref, k_ref, v_ref, keep_ref, send_ref):
     own = lax.axis_index("head") & 1
     width = keep_ref.shape[1]
+    peak_row = table_rows(k_ref.shape[0] // BLK)[0]["peak"]
     for out_ref, side in ((send_ref, 1 - own), (keep_ref, own)):
         h = 2 * pair + side
-        info = (h, scales, tensors, offsets, fbits)
-        k = dequant(k_ref, pl.multiple_of(side * DK, DK), 0, DK, DK, 1, *info)
-        v = dequant(v_ref, pl.multiple_of(side * DV, DV), lo, width, DV, 2, *info)
+        k = dequant(k_ref, pl.multiple_of((at + side) * DK, DK), 0, DK, DK, 1, h, table)
+        v = dequant(v_ref, pl.multiple_of((at + side) * DV, DV), lo, width, DV, 2, h, table)
         weighted = (k.astype(F32) * pick(weight_ref, h)).astype(BF16)
         matrix = lax.dot_general(weighted, v, (((0,), (0,)), ((), ())), preferred_element_type=F32)
         out_ref[:DK, :] = matrix.astype(BF16)
         normer = jnp.sum(weighted.astype(F32), axis=0, keepdims=True)
-        peak, total = jnp.full((1, width), mf[0, h], F32), jnp.full((1, width), mf[1, h], F32)
+        peak = jnp.full((1, width), table[peak_row, h], F32)
+        total = jnp.full((1, width), table[peak_row + 1, h], F32)
         out_ref[DK:ROWS, :] = pack_tail(normer, peak, total)
 
 
-def whole(shape):
-    return pl.BlockSpec(shape, lambda i: (0,) * len(shape))
-
-
-def span_states(chunk, small, mf, weight, key_codes, value_codes, after):
+def span_states(chunk, table, weight, key_codes, value_codes, after):
     pair, lo, width = chunk
     rows = key_codes.shape[0]
     out = jax.ShapeDtypeStruct((ROWS, width), BF16)
-    kernel, extra, extra_specs = ordered(functools.partial(state_kernel, pair, lo), 8, after)
+    if after is None:
+        at = 0
+        spec = dict(
+            grid=(1,),
+            in_specs=[SMEM, VMEM]
+            + [pl.BlockSpec((rows, 2 * DK), lambda i: (0, pair)), pl.BlockSpec((rows, 2 * DV), lambda i: (0, pair))],
+        )
+        key_codes, value_codes = in_hbm(key_codes), in_hbm(value_codes)
+    else:
+        at = 2 * pair
+        spec = dict(in_specs=[SMEM, VMEM, VMEM, VMEM])
+    kernel, extra, extra_specs = ordered(functools.partial(state_kernel, pair, lo, at), 4, after)
+    spec["in_specs"] += extra_specs
     return pl.pallas_call(
         kernel,
-        grid=(1,),
-        in_specs=[SMEM] * 5
-        + [
-            whole(weight.shape),
-            pl.BlockSpec((rows, 2 * DK), lambda i: (0, pair)),
-            pl.BlockSpec((rows, 2 * DV), lambda i: (0, pair)),
-        ]
-        + extra_specs,
-        out_specs=(whole(out.shape),) * 2,
+        **spec,
+        out_specs=(VMEM,) * 2,
         out_shape=(out, out),
         compiler_params=pltpu.CompilerParams(vmem_limit_bytes=12 << 20),
         cost_estimate=pl.CostEstimate(
             flops=4 * rows * DK * width, bytes_accessed=rows * 2 * (2 * DK + 4 * DV), transcendentals=0
         ),
         name="span_states",
-    )(*small, mf, weight, key_codes, value_codes, *extra)
+    )(table, weight, key_codes, value_codes, *extra)
 
 
 def combine_kernel(head_bits, bits, last, *refs):
@@ -264,20 +280,19 @@
     )(*parts, *extra)
 
 
-def output_kernel(
-    head_bits, bits, pair, mine, pieces, scales, tensors, offsets, fbits, run_ref, shift_ref, q_ref, k_ref, v_ref, *rest
-):
-    count = len(rest[:-2]) // pieces
+def output_kernel(head_bits, bits, pair, mine, pieces, table, run_ref, shift_ref, q_ref, k_ref, v_ref, *rest):
+    count = len(rest[:-4]) // pieces
     groups = [rest[p * count : (p + 1) * count] for p in range(pieces)]
-    out_ref, token_ref = rest[-2:]
+    out_ref, token_ref, result_ref, sem = rest[-4:]
     token_ref[...] = jnp.zeros_like(token_ref)
     bit = device_bits(head_bits, bits)
-    h = 2 * pair + head_side(mine)
+    own = lax.axis_index("head") & 1
+    h = 2 * pair + (own if mine else 1 - own)
+    narrow, wide = pl.multiple_of(h * DK, DK), pl.multiple_of(h * DV, DV)
     factor = 1.0 / math.sqrt(DK)
     size = q_ref.shape[0]
     row = lax.broadcasted_iota(jnp.int32, (size, size), 0)
     col = lax.broadcasted_iota(jnp.int32, (size, size), 1)
-    info = (h, scales, tensors, offsets, fbits)
     starts = []
     for group in groups:
         states = [State(ref) for ref in group]
@@ -289,9 +304,9 @@
             normer, peak = states[0].normer, states[0].peak
             starts.append(states[0].matrix())
     start = jnp.concatenate(starts, axis=1) if pieces > 1 else starts[0]
-    q = dequant(q_ref, 0, 0, DK, DK, 0, *info)
-    k = dequant(k_ref, 0, 0, DK, DK, 1, *info)
-    v = dequant(v_ref, 0, 0, DV, DV, 2, *info)
+    q = dequant(q_ref, narrow, 0, DK, DK, 0, h, table)
+    k = dequant(k_ref, narrow, 0, DK, DK, 1, h, table)
+    v = dequant(v_ref, wide, 0, DV, DV, 2, h, table)
     run = pick(run_ref, h)
     exponent = jnp.where(row >= col, run + shift_ref[pl.ds(h, 1), :], NEG_FILL)
     inter = run + peak[:, :1]
@@ -303,23 +318,17 @@
     numerator = jnp.dot(product.astype(BF16), v, preferred_element_type=F32)
     numerator = numerator + jnp.dot(lifted, start, preferred_element_type=F32)
     denominator = jnp.sum(product, axis=1, keepdims=True) + jnp.sum(lifted.astype(F32) * normer, axis=1, keepdims=True)
-    out_ref[...] = (numerator / jnp.maximum(jnp.abs(denominator), 1.0)).astype(BF16)
-
-
-def head_side(mine):
-    own = lax.axis_index("head") & 1
-    return own if mine else 1 - own
-
-
-def span_outputs(head_bits, bits, pair, mine, small, run, shift, codes, groups, before, after):
-    q, k, v = codes
-    rows = q.shape[0]
-    narrow = pl.BlockSpec((rows, DK), lambda i: (0, 2 * pair + head_side(mine)))
-    wide = pl.BlockSpec((rows, DV), lambda i: (0, 2 * pair + head_side(mine)))
+    result_ref[...] = (numerator / jnp.maximum(jnp.abs(denominator), 1.0)).astype(BF16)
+    write = pltpu.make_async_copy(result_ref, out_ref.at[:, pl.ds(wide, DV)], sem)
+    write.start()
+    write.wait()
+
+
+def span_outputs(head_bits, bits, pair, mine, table, run, shift, codes, groups, before, after):
+    rows, width = codes[2].shape
     states = [x for group in groups for x in group]
-    operands = [*small, run, shift, q, k, v, *states]
-    in_specs = [SMEM] * 4 + [whole(run.shape), whole(shift.shape), narrow, narrow, wide]
-    in_specs += [whole(x.shape) for x in states]
+    operands = [table, run, shift, *codes, *states]
+    in_specs = [SMEM] + [VMEM] * (len(operands) - 1)
     kernel = functools.partial(output_kernel, head_bits, bits, pair, mine, len(groups))
     kernel, extra, extra_specs = ordered(kernel, len(operands), after)
     operands += extra
@@ -332,12 +341,12 @@
         in_specs += extra_specs
     return pl.pallas_call(
         kernel,
-        grid=(1,),
         in_specs=in_specs,
-        out_specs=(wide, whole((8, 128))),
-        out_shape=(jax.ShapeDtypeStruct(v.shape, BF16), jax.ShapeDtypeStruct((8, 128), F32)),
+        out_specs=(pl.BlockSpec(memory_space=pl.ANY), VMEM),
+        out_shape=(jax.ShapeDtypeStruct((rows, width), BF16), jax.ShapeDtypeStruct((8, 128), F32)),
+        scratch_shapes=[pltpu.VMEM((rows, DV), BF16), pltpu.SemaphoreType.DMA],
         input_output_aliases=aliases,
-        compiler_params=pltpu.CompilerParams(vmem_limit_bytes=16 << 20),
+        compiler_params=pltpu.CompilerParams(vmem_limit_bytes=12 << 20),
         cost_estimate=pl.CostEstimate(
             flops=2 * rows * (rows * DK + rows * DV + DK * DV),
             bytes_accessed=rows * 2 * (2 * DK + 2 * DV) + sum(x.size for x in states) * 2,
@@ -366,13 +375,12 @@
     small = tuple(in_hbm(x) for x in (block_scales.transpose(1, 0, 2), fault_tensor, fault_offset, fault_bit))
     codes = (query_codes, key_codes, value_codes)
     exchange = functools.partial(flip, head_bits=head_bits, ctx_bits=ctx_bits)
-    run, weight, shift, mf = gates(in_hbm(input_gate.T), in_hbm(forget_gate.T))
-    keys, values = in_hbm(key_codes), in_hbm(value_codes)
+    run, weight, shift, table = gates(in_hbm(input_gate.T), in_hbm(forget_gate.T), small)
     keep, got, back = {}, {}, {}
     out = token = None
     for stage, c in order(bits):
         if stage == 0:
-            keep[c], token = span_states(CHUNKS[c], small, mf, weight, keys, values, token)
+            keep[c], token = span_states(CHUNKS[c], table, weight, key_codes, value_codes, token)
         elif stage < bits:
             token = combine(head_bits, bits, False, [keep[c], *got[c]], token)
         elif stage == bits:
@@ -381,7 +389,7 @@
             mine = stage == bits + 1
             groups = [got[d] if mine else [back[d]] for d in of_pair(c)]
             out, token = span_outputs(
-                head_bits, bits, c, mine, small, run, shift, codes, groups, out, token
+                head_bits, bits, c, mine, table, run, shift, codes, groups, out, token
             )
         if stage < bits:
             got.setdefault(c, []).append(exchange(token, stage, last=stage == bits - 1))

time: 109 us -> 109 us (level)
  waiting for transfers between devices: 51.3 us -> 53.1 us
  Pallas kernels: 31 us -> 29.8 us
    ppermute x25, waiting for transfers between devices: 51.3 us -> 53.1 us  [flip(): return lax.ppermute(x, axis, pairs)]
    pallas_call x13, Pallas kernels: 26 us -> 24.6 us  [the longest x8 17.9 us: span_outputs(): pl.pallas_call(kernel, in_specs=in_specs, out_specs=(pl.BlockSpec(memory_...]
  transfers between devices with their start and end apart: 25 -> 25, of which waited for: 16 -> 16; matrix products, arithmetic and copies ran while one was open for 0% -> 0% of each run, Pallas kernels for 24% -> 22%
where the time goes in v6:
time: 109 us
  waiting for transfers between devices  53.1 us (49%)
  Pallas kernels  29.8 us (27%)
  starting transfers between devices  25.2 us (23%)
    ppermute x25, waiting for transfers between devices, flip(): return lax.ppermute(x, axis, pairs)  53.1 us
    ppermute x25, starting transfers between devices, flip(): return lax.ppermute(x, axis, pairs)  25.2 us
    pallas_call x8, Pallas kernels, span_outputs(): pl.pallas_call(kernel, in_specs=in_specs, out_specs=(pl.BlockSpec(memory_...  17.9 us
    pallas_call x5, Pallas kernels, span_states(): pl.pallas_call(kernel, **spec, out_specs=(VMEM,) * 2, out_shape=(out, out...  6.71 us
    pallas_call x20, Pallas kernels, combine(): pl.pallas_call(kernel, in_specs=[VMEM] * len(parts) + extra_specs, out_sp...  3.61 us
  transfers between devices with their start and end apart: 25, of which 16 were waited for; matrix products, arithmetic and copies ran while one was open for 0% of the time, Pallas kernels for 22%

profile of v6, /device:TPU:0, one launch (start us, length us, event | category | flops | bytes accessed | tf_op | source)
XLA Modules:
  0.0 108.6 jit_solution(1802444952844366297)
XLA Ops:
  0.0 1.5 %gates.1 = (f32[256,8]{1,0:T(8,128)S(1)}, f32[256,8]{1,0:T(8,128)S(1)}, f32[8,256]{1,0:T(8,128)S(1)}, f32[20,8]{1,0:T(8,128)S(1)}) custom-call(bf16[8,256]{1,0:T(8,128)(2,1)} %bitcast.3, bf16[8,256]{1,0:T(8,128)(2,1)} %bitcast.4, f32[3,2,8]{2,1,0:T(2,128)} %bitcast.5, s32[2,8]{1,0:T(2,128)} %tensors.1, s32[2,8]{1,0:T(2,128)} %offsets.1, s32[2,8]{1,0:T(2,128)} %fbits.1), custom_call_target="tpu_custom_call" | custom-call | flops 1048576 | bytes 1048576 | tf_op jit(solution)/shard_map/gates/pallas_call | solution.py:85
  1.5 1.6 %span_states.5 = (bf16[264,256]{1,0:T(8,128)(2,1)S(1)}, bf16[264,256]{1,0:T(8,128)(2,1)S(1)}) custom-call(f32[20,8]{1,0:T(8,128)S(1)} %get-tuple-element.34.table.refs_0_, f32[256,8]{1,0:T(8,128)S(1)} %get-tuple-element.37.weight_ref.refs_1_, bf16[256,2048]{1,0:T(8,128)(2,1)} %refs_4_.15, bf16[256,4096]{1,0:T(8,128)(2,1)} %refs_5_.15), custom_call_target="tpu_custom_call" | custom-call | flops 67108864 | bytes 1310720 | tf_op jit(solution)/shard_map/span_states/pallas_call | solution.py:241
  3.2 3.1 %collective-permute-start.1 = (bf16[264,256]{1,0:T(8,128)(2,1)S(1)}, bf16[264,256]{1,0:T(8,128)(2,1)S(1)}, u32[]{:S(2)}, u32[]{:S(2)}) collective-permute-start(bf16[264,256]{1,0:T(8,128)(2,1)S(1)} %get-tuple-element.38.refs_4_), channel_id=1, source_target_pairs={{0,1},{1,0},{2,3},{3,2},{4,5},{5,4},{6,7},{7,6},{8,9},{9,8},{10,11... | collective-permute-start | bytes 405512 | tf_op jit(solution)/shard_map/ppermute | solution.py:41
  6.3 1.2 %span_states.6 = (bf16[264,256]{1,0:T(8,128)(2,1)S(1)}, bf16[264,256]{1,0:T(8,128)(2,1)S(1)}) custom-call(f32[20,8]{1,0:T(8,128)S(1)} %get-tuple-element.34.table.refs_0_, f32[256,8]{1,0:T(8,128)S(1)} %get-tuple-element.37.weight_ref.refs_1_, bf16[256,2048]{1,0:T(8,128)(2,1)S(1)} %copy-done.1, bf16[256,4096]{1,0:T(8,128)(2,1)S(1)} %copy-done, ...), custom_call_target="tpu_custom_call" | custom-call | flops 67108864 | bytes 1310720 | tf_op jit(solution)/shard_map/span_states/pallas_call | solution.py:241
  7.6 1.3 %span_states.7 = (bf16[264,512]{1,0:T(8,128)(2,1)S(1)}, bf16[264,512]{1,0:T(8,128)(2,1)S(1)}) custom-call(f32[20,8]{1,0:T(8,128)S(1)} %get-tuple-element.34.table.refs_0_, f32[256,8]{1,0:T(8,128)S(1)} %get-tuple-element.37.weight_ref.refs_1_, bf16[256,2048]{1,0:T(8,128)(2,1)S(1)} %copy-done.1, bf16[256,4096]{1,0:T(8,128)(2,1)S(1)} %copy-done, ...), custom_call_target="tpu_custom_call" | custom-call | flops 134217728 | bytes 1310720 | tf_op jit(solution)/shard_map/span_states/pallas_call | solution.py:241
  8.9 2.1 %collective-permute-start.3 = (bf16[264,512]{1,0:T(8,128)(2,1)S(1)}, bf16[264,512]{1,0:T(8,128)(2,1)S(1)}, u32[]{:S(2)}, u32[]{:S(2)}) collective-permute-start(bf16[264,512]{1,0:T(8,128)(2,1)S(1)} %get-tuple-element.42.refs_2_), channel_id=1, source_target_pairs={{0,1},{1,0},{2,3},{3,2},{4,5},{5,4},{6,7},{7,6},{8,9},{9,8},{10,11... | collective-permute-start | bytes 811016 | tf_op jit(solution)/shard_map/ppermute | solution.py:41
  11.0 3.0 %collective-permute-done.refs_1_.refs_10_ = bf16[264,256]{1,0:T(8,128)(2,1)S(1)} collective-permute-done((bf16[264,256]{1,0:T(8,128)(2,1)S(1)}, bf16[264,256]{1,0:T(8,128)(2,1)S(1)}, u32[]{:S(2)}, u32[]{:S(2)}) %collective-permute-start) | collective-permute-done | bytes 135200 | tf_op jit(solution)/shard_map/ppermute | solution.py:41
  14.1 1.3 %span_states.8 = (bf16[264,512]{1,0:T(8,128)(2,1)S(1)}, bf16[264,512]{1,0:T(8,128)(2,1)S(1)}) custom-call(f32[20,8]{1,0:T(8,128)S(1)} %get-tuple-element.34.table.refs_0_, f32[256,8]{1,0:T(8,128)S(1)} %get-tuple-element.37.weight_ref.refs_1_, bf16[256,2048]{1,0:T(8,128)(2,1)S(1)} %copy-done.1, bf16[256,4096]{1,0:T(8,128)(2,1)S(1)} %copy-done, ...), custom_call_target="tpu_custom_call" | custom-call | flops 134217728 | bytes 1310720 | tf_op jit(solution)/shard_map/span_states/pallas_call | solution.py:241
  15.4 1.7 %collective-permute-start.6 = (bf16[264,512]{1,0:T(8,128)(2,1)S(1)}, bf16[264,512]{1,0:T(8,128)(2,1)S(1)}, u32[]{:S(2)}, u32[]{:S(2)}) collective-permute-start(bf16[264,512]{1,0:T(8,128)(2,1)S(1)} %get-tuple-element.44.refs_2_), channel_id=1, source_target_pairs={{0,1},{1,0},{2,3},{3,2},{4,5},{5,4},{6,7},{7,6},{8,9},{9,8},{10,11... | collective-permute-start | bytes 811016 | tf_op jit(solution)/shard_map/ppermute | solution.py:41
  17.1 2.6 %collective-permute-start.2 = (bf16[264,256]{1,0:T(8,128)(2,1)S(1)}, bf16[264,256]{1,0:T(8,128)(2,1)S(1)}, u32[]{:S(2)}, u32[]{:S(2)}) collective-permute-start(bf16[264,256]{1,0:T(8,128)(2,1)S(1)} %combine.21.refs_4_), channel_id=1, source_target_pairs={{0,2},{1,3},{2,0},{3,1},{4,6},{5,7},{6,4},{7,5},{8,10},{9,11},{10,... | collective-permute-start | bytes 405512 | tf_op jit(solution)/shard_map/ppermute | solution.py:41
  19.7 0.3 collective-permute-start.5
  20.0 6.9 %collective-permute-done.3.refs_1_.refs_6_ = bf16[264,512]{1,0:T(8,128)(2,1)S(1)} collective-permute-done((bf16[264,512]{1,0:T(8,128)(2,1)S(1)}, bf16[264,512]{1,0:T(8,128)(2,1)S(1)}, u32[]{:S(2)}, u32[]{:S(2)}) %collective-permute-start.3) | collective-permute-done | bytes 270368 | tf_op jit(solution)/shard_map/ppermute | solution.py:41
  27.1 0.4 collective-permute-start.9
  27.7 1.3 %span_states.9 = (bf16[264,512]{1,0:T(8,128)(2,1)S(1)}, bf16[264,512]{1,0:T(8,128)(2,1)S(1)}) custom-call(f32[20,8]{1,0:T(8,128)S(1)} %get-tuple-element.34.table.refs_0_, f32[256,8]{1,0:T(8,128)S(1)} %get-tuple-element.37.weight_ref.refs_1_, bf16[256,2048]{1,0:T(8,128)(2,1)S(1)} %copy-done.1, bf16[256,4096]{1,0:T(8,128)(2,1)S(1)} %copy-done, ...), custom_call_target="tpu_custom_call" | custom-call | flops 134217728 | bytes 1310720 | tf_op jit(solution)/shard_map/span_states/pallas_call | solution.py:241
  29.1 2.9 %collective-permute-done.6.refs_1_.refs_6_ = bf16[264,512]{1,0:T(8,128)(2,1)S(1)} collective-permute-done((bf16[264,512]{1,0:T(8,128)(2,1)S(1)}, bf16[264,512]{1,0:T(8,128)(2,1)S(1)}, u32[]{:S(2)}, u32[]{:S(2)}) %collective-permute-start.6) | collective-permute-done | bytes 270368 | tf_op jit(solution)/shard_map/ppermute | solution.py:41
  32.1 6.6 %collective-permute-done.5.refs_2_.refs_1_.refs_7_ = bf16[264,256]{1,0:T(8,128)(2,1)S(1)} collective-permute-done((bf16[264,256]{1,0:T(8,128)(2,1)S(1)}, bf16[264,256]{1,0:T(8,128)(2,1)S(1)}, u32[]{:S(2)}, u32[]{:S(2)}) %collective-permute-start.5) | collective-permute-done | bytes 135200 | tf_op jit(solution)/shard_map/ppermute | solution.py:41
  38.8 0.5 collective-permute-start.10
  39.3 0.8 collective-permute-done.7.refs_3_.refs_2_.refs_8_
  40.5 1.7 %collective-permute-done.9.refs_2_.refs_7_.refs_1_ = bf16[264,512]{1,0:T(8,128)(2,1)S(1)} collective-permute-done((bf16[264,512]{1,0:T(8,128)(2,1)S(1)}, bf16[264,512]{1,0:T(8,128)(2,1)S(1)}, u32[]{:S(2)}, u32[]{:S(2)}) %collective-permute-start.9) | collective-permute-done | bytes 270368 | tf_op jit(solution)/shard_map/ppermute | solution.py:41
  42.6 3.5 %collective-permute-start.8 = (bf16[264,256]{1,0:T(8,128)(2,1)S(1)}, bf16[264,256]{1,0:T(8,128)(2,1)S(1)}, u32[]{:S(2)}, u32[]{:S(2)}) collective-permute-start(bf16[264,256]{1,0:T(8,128)(2,1)S(1)} %combine.26.refs_4_), channel_id=1, source_target_pairs={{0,8},{4,12},{1,9},{5,13},{2,10},{6,14},{3,11},{7,15},{16,24},{20,... | collective-permute-start | bytes 405512 | tf_op jit(solution)/shard_map/ppermute | solution.py:41
  46.2 1.3 %collective-permute-start.15 = (bf16[264,256]{1,0:T(8,128)(2,1)S(1)}, bf16[264,256]{1,0:T(8,128)(2,1)S(1)}, u32[]{:S(2)}, u32[]{:S(2)}) collective-permute-start(bf16[264,256]{1,0:T(8,128)(2,1)S(1)} %combine.27.refs_3_), channel_id=1, source_target_pairs={{0,8},{4,12},{1,9},{5,13},{2,10},{6,14},{3,11},{7,15},{16,24},{20,... | collective-permute-start | bytes 405512 | tf_op jit(solution)/shard_map/ppermute | solution.py:41
  47.5 2.6 %collective-permute-done.8.refs_3_.refs_9_ = bf16[264,256]{1,0:T(8,128)(2,1)S(1)} collective-permute-done((bf16[264,256]{1,0:T(8,128)(2,1)S(1)}, bf16[264,256]{1,0:T(8,128)(2,1)S(1)}, u32[]{:S(2)}, u32[]{:S(2)}) %collective-permute-start.8) | collective-permute-done | bytes 135200 | tf_op jit(solution)/shard_map/ppermute | solution.py:41
  50.4 0.3 combine.31.refs_4_
  50.7 1.6 %collective-permute-done.15.refs_3_.refs_13_ = bf16[264,256]{1,0:T(8,128)(2,1)S(1)} collective-permute-done((bf16[264,256]{1,0:T(8,128)(2,1)S(1)}, bf16[264,256]{1,0:T(8,128)(2,1)S(1)}, u32[]{:S(2)}, u32[]{:S(2)}) %collective-permute-start.15) | collective-permute-done | bytes 135200 | tf_op jit(solution)/shard_map/ppermute | solution.py:41
  52.5 2.3 %span_outputs.8 = (bf16[256,4096]{1,0:T(8,128)(2,1)}, f32[8,128]{1,0:T(8,128)S(1)}) custom-call(f32[20,8]{1,0:T(8,128)S(1)} %get-tuple-element.34.table.refs_0_, f32[256,8]{1,0:T(8,128)S(1)} %get-tuple-element.35.refs_1_, f32[8,256]{1,0:T(8,128)S(1)} %get-tuple-element.36.refs_2_, bf16[256,2048]{1,0:T(8,128)(2,1)S(1)} %copy-done.2, ...), custom_call_target="tpu_custom_call" | custom-call | flops 167772160 | bytes 1867776 | tf_op jit(solution)/shard_map/span_outputs/pallas_call | solution.py:342
  54.7 3.4 %collective-permute-done.14.refs_2_.refs_1_.refs_7_ = bf16[264,512]{1,0:T(8,128)(2,1)S(1)} collective-permute-done((bf16[264,512]{1,0:T(8,128)(2,1)S(1)}, bf16[264,512]{1,0:T(8,128)(2,1)S(1)}, u32[]{:S(2)}, u32[]{:S(2)}) %collective-permute-start.14) | collective-permute-done | bytes 270368 | tf_op jit(solution)/shard_map/ppermute | solution.py:41
  58.4 3.4 %collective-permute-start.13 = (bf16[264,512]{1,0:T(8,128)(2,1)S(1)}, bf16[264,512]{1,0:T(8,128)(2,1)S(1)}, u32[]{:S(2)}, u32[]{:S(2)}) collective-permute-start(bf16[264,512]{1,0:T(8,128)(2,1)S(1)} %combine.31.refs_4_), channel_id=1, source_target_pairs={{0,8},{4,12},{1,9},{5,13},{2,10},{6,14},{3,11},{7,15},{16,24},{20,... | collective-permute-start | bytes 811016 | tf_op jit(solution)/shard_map/ppermute | solution.py:41
  61.8 0.3 collective-permute-start.11
  62.2 0.3 combine.34.refs_10_
  62.4 5.7 %collective-permute-done.13.refs_9_.refs_3_ = bf16[264,512]{1,0:T(8,128)(2,1)S(1)} collective-permute-done((bf16[264,512]{1,0:T(8,128)(2,1)S(1)}, bf16[264,512]{1,0:T(8,128)(2,1)S(1)}, u32[]{:S(2)}, u32[]{:S(2)}) %collective-permute-start.13) | collective-permute-done | bytes 270368 | tf_op jit(solution)/shard_map/ppermute | solution.py:41
  68.2 2.2 %span_outputs.9 = (bf16[256,4096]{1,0:T(8,128)(2,1)}, f32[8,128]{1,0:T(8,128)S(1)}) custom-call(f32[20,8]{1,0:T(8,128)S(1)} %get-tuple-element.34.table.refs_0_, f32[256,8]{1,0:T(8,128)S(1)} %get-tuple-element.35.refs_1_, f32[8,256]{1,0:T(8,128)S(1)} %get-tuple-element.36.refs_2_, bf16[256,2048]{1,0:T(8,128)(2,1)S(1)} %copy-done.2, ...), custom_call_target="tpu_custom_call", output_to_operand_aliasing={{0}: (11, {})} | custom-call | flops 167772160 | bytes 1867776 | tf_op jit(solution)/shard_map/span_outputs/pallas_call | solution.py:342
  70.4 0.3 combine.35.refs_3_
  70.7 6.5 %collective-permute-done.11.refs_2_.refs_1_.refs_7_ = bf16[264,512]{1,0:T(8,128)(2,1)S(1)} collective-permute-done((bf16[264,512]{1,0:T(8,128)(2,1)S(1)}, bf16[264,512]{1,0:T(8,128)(2,1)S(1)}, u32[]{:S(2)}, u32[]{:S(2)}) %collective-permute-start.11) | collective-permute-done | bytes 270368 | tf_op jit(solution)/shard_map/ppermute | solution.py:41
  77.5 1.6 %collective-permute-start.22 = (bf16[264,512]{1,0:T(8,128)(2,1)S(1)}, bf16[264,512]{1,0:T(8,128)(2,1)S(1)}, u32[]{:S(2)}, u32[]{:S(2)}) collective-permute-start(bf16[264,512]{1,0:T(8,128)(2,1)S(1)} %combine.34.refs_10_), channel_id=1, source_target_pairs={{0,8},{4,12},{1,9},{5,13},{2,10},{6,14},{3,11},{7,15},{16,24},{20,... | collective-permute-start | bytes 811016 | tf_op jit(solution)/shard_map/ppermute | solution.py:41
  79.1 0.3 combine.37.refs_4_
  79.4 1.6 %collective-permute-start.18 = (bf16[264,512]{1,0:T(8,128)(2,1)S(1)}, bf16[264,512]{1,0:T(8,128)(2,1)S(1)}, u32[]{:S(2)}, u32[]{:S(2)}) collective-permute-start(bf16[264,512]{1,0:T(8,128)(2,1)S(1)} %combine.37.refs_4_), channel_id=1, source_target_pairs={{0,8},{4,12},{1,9},{5,13},{2,10},{6,14},{3,11},{7,15},{16,24},{20,... | collective-permute-start | bytes 811016 | tf_op jit(solution)/shard_map/ppermute | solution.py:41
  81.0 1.9 %collective-permute-start.20 = (bf16[264,256]{1,0:T(8,128)(2,1)S(1)}, bf16[264,256]{1,0:T(8,128)(2,1)S(1)}, u32[]{:S(2)}, u32[]{:S(2)}) collective-permute-start(bf16[264,256]{1,0:T(8,128)(2,1)S(1)} %combine.29.refs_2_), channel_id=1, source_target_pairs={{0,1},{1,0},{2,3},{3,2},{4,5},{5,4},{6,7},{7,6},{8,9},{9,8},{10,11... | collective-permute-start | bytes 405512 | tf_op jit(solution)/shard_map/ppermute | solution.py:41
  83.1 2.8 %collective-permute-done.22.refs_3_.refs_9_ = bf16[264,512]{1,0:T(8,128)(2,1)S(1)} collective-permute-done((bf16[264,512]{1,0:T(8,128)(2,1)S(1)}, bf16[264,512]{1,0:T(8,128)(2,1)S(1)}, u32[]{:S(2)}, u32[]{:S(2)}) %collective-permute-start.22) | collective-permute-done | bytes 270368 | tf_op jit(solution)/shard_map/ppermute | solution.py:41
  86.2 5.1 %collective-permute-done.20.refs_6_ = bf16[264,256]{1,0:T(8,128)(2,1)S(1)} collective-permute-done((bf16[264,256]{1,0:T(8,128)(2,1)S(1)}, bf16[264,256]{1,0:T(8,128)(2,1)S(1)}, u32[]{:S(2)}, u32[]{:S(2)}) %collective-permute-start.20) | collective-permute-done | bytes 135200 | tf_op jit(solution)/shard_map/ppermute | solution.py:41
  91.3 2.9 %collective-permute-done.21.refs_7_ = bf16[264,256]{1,0:T(8,128)(2,1)S(1)} collective-permute-done((bf16[264,256]{1,0:T(8,128)(2,1)S(1)}, bf16[264,256]{1,0:T(8,128)(2,1)S(1)}, u32[]{:S(2)}, u32[]{:S(2)}) %collective-permute-start.21) | collective-permute-done | bytes 135200 | tf_op jit(solution)/shard_map/ppermute | solution.py:41
  94.2 2.1 %span_outputs.10 = (bf16[256,4096]{1,0:T(8,128)(2,1)}, f32[8,128]{1,0:T(8,128)S(1)}) custom-call(f32[20,8]{1,0:T(8,128)S(1)} %get-tuple-element.34.table.refs_0_, f32[256,8]{1,0:T(8,128)S(1)} %get-tuple-element.35.refs_1_, f32[8,256]{1,0:T(8,128)S(1)} %get-tuple-element.36.refs_2_, bf16[256,2048]{1,0:T(8,128)(2,1)S(1)} %copy-done.2, ...), custom_call_target="tpu_custom_call", output_to_operand_aliasing={{0}: (9, {})} | custom-call | flops 167772160 | bytes 1056768 | tf_op jit(solution)/shard_map/span_outputs/pallas_call | solution.py:342
  96.4 2.1 %span_outputs.11 = (bf16[256,4096]{1,0:T(8,128)(2,1)}, f32[8,128]{1,0:T(8,128)S(1)}) custom-call(f32[20,8]{1,0:T(8,128)S(1)} %get-tuple-element.34.table.refs_0_, f32[256,8]{1,0:T(8,128)S(1)} %get-tuple-element.35.refs_1_, f32[8,256]{1,0:T(8,128)S(1)} %get-tuple-element.36.refs_2_, bf16[256,2048]{1,0:T(8,128)(2,1)S(1)} %copy-done.2, ...), custom_call_target="tpu_custom_call", output_to_operand_aliasing={{0}: (8, {})} | custom-call | flops 167772160 | bytes 1056768 | tf_op jit(solution)/shard_map/span_outputs/pallas_call | solution.py:342
  98.5 0.3 combine.39.refs_10_
  98.8 2.2 %span_outputs.12 = (bf16[256,4096]{1,0:T(8,128)(2,1)}, f32[8,128]{1,0:T(8,128)S(1)}) custom-call(f32[20,8]{1,0:T(8,128)S(1)} %get-tuple-element.34.table.refs_0_, f32[256,8]{1,0:T(8,128)S(1)} %get-tuple-element.35.refs_1_, f32[8,256]{1,0:T(8,128)S(1)} %get-tuple-element.36.refs_2_, ...), custom_call_target="tpu_custom_call", output_to_operand_aliasing={{0}: (11, {})} | custom-call | flops 167772160 | bytes 1867776 | tf_op jit(solution)/shard_map/span_outputs/pallas_call | solution.py:342
  101.1 2.1 %span_outputs.13 = (bf16[256,4096]{1,0:T(8,128)(2,1)}, f32[8,128]{1,0:T(8,128)S(1)}) custom-call(f32[20,8]{1,0:T(8,128)S(1)} %get-tuple-element.34.table.refs_0_, f32[256,8]{1,0:T(8,128)S(1)} %get-tuple-element.35.refs_1_, f32[8,256]{1,0:T(8,128)S(1)} %get-tuple-element.36.refs_2_, bf16[256,2048]{1,0:T(8,128)(2,1)S(1)} %copy-done.2, ...), custom_call_target="tpu_custom_call", output_to_operand_aliasing={{0}: (8, {})} | custom-call | flops 167772160 | bytes 1056768 | tf_op jit(solution)/shard_map/span_outputs/pallas_call | solution.py:342
  103.2 2.3 %span_outputs.14 = (bf16[256,4096]{1,0:T(8,128)(2,1)}, f32[8,128]{1,0:T(8,128)S(1)}) custom-call(f32[20,8]{1,0:T(8,128)S(1)} %get-tuple-element.34.table.refs_0_, f32[256,8]{1,0:T(8,128)S(1)} %get-tuple-element.35.refs_1_, f32[8,256]{1,0:T(8,128)S(1)} %get-tuple-element.36.refs_2_, ...), custom_call_target="tpu_custom_call", output_to_operand_aliasing={{0}: (11, {})} | custom-call | flops 167772160 | bytes 1867776 | tf_op jit(solution)/shard_map/span_outputs/pallas_call | solution.py:342
  105.4 0.4 collective-permute-done.23.refs_6_
  105.8 2.7 %span_outputs.15 = (bf16[256,4096]{1,0:T(8,128)(2,1)}, f32[8,128]{1,0:T(8,128)}) custom-call(f32[20,8]{1,0:T(8,128)S(1)} %get-tuple-element.34.table.refs_0_, f32[256,8]{1,0:T(8,128)S(1)} %get-tuple-element.35.refs_1_, f32[8,256]{1,0:T(8,128)S(1)} %get-tuple-element.36.refs_2_, bf16[256,2048]{1,0:T(8,128)(2,1)S(1)} %copy-done.2, ...), custom_call_target="tpu_custom_call", output_to_operand_aliasing={{0}: (8, {})} | custom-call | flops 167772160 | bytes 1056768 | tf_op jit(solution)/shard_map/span_outputs/pallas_call | solution.py:342
  (42 shorter events, 3.3 us)
Async XLA Ops:
  0.0 6.3 %copy-start = (bf16[256,4096]{1,0:T(8,128)(2,1)S(1)}, bf16[256,4096]{1,0:T(8,128)(2,1)}, u32[]{:S(2)}) copy-start(bf16[256,4096]{1,0:T(8,128)(2,1)} %refs_5_.15) | copy-start | bytes 6291460
  0.0 6.3 %copy-start.1 = (bf16[256,2048]{1,0:T(8,128)(2,1)S(1)}, bf16[256,2048]{1,0:T(8,128)(2,1)}, u32[]{:S(2)}) copy-start(bf16[256,2048]{1,0:T(8,128)(2,1)} %refs_4_.15) | copy-start | bytes 3145732
  3.2 7.8 %collective-permute-start.1 = (bf16[264,256]{1,0:T(8,128)(2,1)S(1)}, bf16[264,256]{1,0:T(8,128)(2,1)S(1)}, u32[]{:S(2)}, u32[]{:S(2)}) collective-permute-start(bf16[264,256]{1,0:T(8,128)(2,1)S(1)} %get-tuple-element.38.refs_4_), channel_id=1, source_target_pairs={{0,1},{1,0},{2,3},{3,2},{4,5},{5,4},{6,7},{7,6},{8,9},{9,8},{10,11... | collective-permute-start | bytes 405512 | tf_op jit(solution)/shard_map/ppermute | solution.py:41
  7.5 6.5 %collective-permute-start = (bf16[264,256]{1,0:T(8,128)(2,1)S(1)}, bf16[264,256]{1,0:T(8,128)(2,1)S(1)}, u32[]{:S(2)}, u32[]{:S(2)}) collective-permute-start(bf16[264,256]{1,0:T(8,128)(2,1)S(1)} %get-tuple-element.40.refs_4_), channel_id=1, source_target_pairs={{0,1},{1,0},{2,3},{3,2},{4,5},{5,4},{6,7},{7,6},{8,9},{9,8},{10,11... | collective-permute-start | bytes 405512 | tf_op jit(solution)/shard_map/ppermute | solution.py:41
  8.9 18.1 %collective-permute-start.3 = (bf16[264,512]{1,0:T(8,128)(2,1)S(1)}, bf16[264,512]{1,0:T(8,128)(2,1)S(1)}, u32[]{:S(2)}, u32[]{:S(2)}) collective-permute-start(bf16[264,512]{1,0:T(8,128)(2,1)S(1)} %get-tuple-element.42.refs_2_), channel_id=1, source_target_pairs={{0,1},{1,0},{2,3},{3,2},{4,5},{5,4},{6,7},{7,6},{8,9},{9,8},{10,11... | collective-permute-start | bytes 811016 | tf_op jit(solution)/shard_map/ppermute | solution.py:41
  15.4 16.5 %collective-permute-start.6 = (bf16[264,512]{1,0:T(8,128)(2,1)S(1)}, bf16[264,512]{1,0:T(8,128)(2,1)S(1)}, u32[]{:S(2)}, u32[]{:S(2)}) collective-permute-start(bf16[264,512]{1,0:T(8,128)(2,1)S(1)} %get-tuple-element.44.refs_2_), channel_id=1, source_target_pairs={{0,1},{1,0},{2,3},{3,2},{4,5},{5,4},{6,7},{7,6},{8,9},{9,8},{10,11... | collective-permute-start | bytes 811016 | tf_op jit(solution)/shard_map/ppermute | solution.py:41
  17.1 10.5 %collective-permute-start.2 = (bf16[264,256]{1,0:T(8,128)(2,1)S(1)}, bf16[264,256]{1,0:T(8,128)(2,1)S(1)}, u32[]{:S(2)}, u32[]{:S(2)}) collective-permute-start(bf16[264,256]{1,0:T(8,128)(2,1)S(1)} %combine.21.refs_4_), channel_id=1, source_target_pairs={{0,2},{1,3},{2,0},{3,1},{4,6},{5,7},{6,4},{7,5},{8,10},{9,11},{10,... | collective-permute-start | bytes 405512 | tf_op jit(solution)/shard_map/ppermute | solution.py:41
  19.7 18.9 %collective-permute-start.5 = (bf16[264,256]{1,0:T(8,128)(2,1)S(1)}, bf16[264,256]{1,0:T(8,128)(2,1)S(1)}, u32[]{:S(2)}, u32[]{:S(2)}) collective-permute-start(bf16[264,256]{1,0:T(8,128)(2,1)S(1)} %combine.20.refs_2_), channel_id=1, source_target_pairs={{0,2},{1,3},{2,0},{3,1},{4,6},{5,7},{6,4},{7,5},{8,10},{9,11},{10,... | collective-permute-start | bytes 405512 | tf_op jit(solution)/shard_map/ppermute | solution.py:41
  27.1 15.2 %collective-permute-start.9 = (bf16[264,512]{1,0:T(8,128)(2,1)S(1)}, bf16[264,512]{1,0:T(8,128)(2,1)S(1)}, u32[]{:S(2)}, u32[]{:S(2)}) collective-permute-start(bf16[264,512]{1,0:T(8,128)(2,1)S(1)} %combine.22.refs_3_), channel_id=1, source_target_pairs={{0,2},{1,3},{2,0},{3,1},{4,6},{5,7},{6,4},{7,5},{8,10},{9,11},{10,... | collective-permute-start | bytes 811016 | tf_op jit(solution)/shard_map/ppermute | solution.py:41
  38.7 1.4 %collective-permute-start.7 = (bf16[264,256]{1,0:T(8,128)(2,1)S(1)}, bf16[264,256]{1,0:T(8,128)(2,1)S(1)}, u32[]{:S(2)}, u32[]{:S(2)}) collective-permute-start(bf16[264,256]{1,0:T(8,128)(2,1)S(1)} %combine.25.refs_4_), channel_id=1, source_target_pairs={{0,4},{4,0},{8,12},{12,8},{1,5},{5,1},{9,13},{13,9},{2,6},{6,2},{1... | collective-permute-start | bytes 405512 | tf_op jit(solution)/shard_map/ppermute | solution.py:41
  38.8 1.5 %collective-permute-start.10 = (bf16[264,256]{1,0:T(8,128)(2,1)S(1)}, bf16[264,256]{1,0:T(8,128)(2,1)S(1)}, u32[]{:S(2)}, u32[]{:S(2)}) collective-permute-start(bf16[264,256]{1,0:T(8,128)(2,1)S(1)} %combine.23.refs_4_), channel_id=1, source_target_pairs={{0,4},{4,0},{8,12},{12,8},{1,5},{5,1},{9,13},{13,9},{2,6},{6,2},{1... | collective-permute-start | bytes 405512 | tf_op jit(solution)/shard_map/ppermute | solution.py:41
  39.3 11.0 %collective-permute-start.4 = (bf16[264,512]{1,0:T(8,128)(2,1)S(1)}, bf16[264,512]{1,0:T(8,128)(2,1)S(1)}, u32[]{:S(2)}, u32[]{:S(2)}) collective-permute-start(bf16[264,512]{1,0:T(8,128)(2,1)S(1)} %get-tuple-element.46.refs_2_), channel_id=1, source_target_pairs={{0,1},{1,0},{2,3},{3,2},{4,5},{5,4},{6,7},{7,6},{8,9},{9,8},{10,11... | collective-permute-start | bytes 811016 | tf_op jit(solution)/shard_map/ppermute | solution.py:41
  42.4 10.0 %copy-start.2 = (bf16[256,2048]{1,0:T(8,128)(2,1)S(1)}, bf16[256,2048]{1,0:T(8,128)(2,1)}, u32[]{:S(2)}) copy-start(bf16[256,2048]{1,0:T(8,128)(2,1)} %refs_3_.23) | copy-start | bytes 3145732
  42.5 8.0 %collective-permute-start.12 = (bf16[264,512]{1,0:T(8,128)(2,1)S(1)}, bf16[264,512]{1,0:T(8,128)(2,1)S(1)}, u32[]{:S(2)}, u32[]{:S(2)}) collective-permute-start(bf16[264,512]{1,0:T(8,128)(2,1)S(1)} %combine.28.refs_4_), channel_id=1, source_target_pairs={{0,4},{4,0},{8,12},{12,8},{1,5},{5,1},{9,13},{13,9},{2,6},{6,2},{1... | collective-permute-start | bytes 811016 | tf_op jit(solution)/shard_map/ppermute | solution.py:41
  42.5 15.6 %collective-permute-start.14 = (bf16[264,512]{1,0:T(8,128)(2,1)S(1)}, bf16[264,512]{1,0:T(8,128)(2,1)S(1)}, u32[]{:S(2)}, u32[]{:S(2)}) collective-permute-start(bf16[264,512]{1,0:T(8,128)(2,1)S(1)} %combine.24.refs_3_), channel_id=1, source_target_pairs={{0,2},{1,3},{2,0},{3,1},{4,6},{5,7},{6,4},{7,5},{8,10},{9,11},{10,... | collective-permute-start | bytes 811016 | tf_op jit(solution)/shard_map/ppermute | solution.py:41
  42.6 7.5 %collective-permute-start.8 = (bf16[264,256]{1,0:T(8,128)(2,1)S(1)}, bf16[264,256]{1,0:T(8,128)(2,1)S(1)}, u32[]{:S(2)}, u32[]{:S(2)}) collective-permute-start(bf16[264,256]{1,0:T(8,128)(2,1)S(1)} %combine.26.refs_4_), channel_id=1, source_target_pairs={{0,8},{4,12},{1,9},{5,13},{2,10},{6,14},{3,11},{7,15},{16,24},{20,... | collective-permute-start | bytes 405512 | tf_op jit(solution)/shard_map/ppermute | solution.py:41
  46.2 6.2 %collective-permute-start.15 = (bf16[264,256]{1,0:T(8,128)(2,1)S(1)}, bf16[264,256]{1,0:T(8,128)(2,1)S(1)}, u32[]{:S(2)}, u32[]{:S(2)}) collective-permute-start(bf16[264,256]{1,0:T(8,128)(2,1)S(1)} %combine.27.refs_3_), channel_id=1, source_target_pairs={{0,8},{4,12},{1,9},{5,13},{2,10},{6,14},{3,11},{7,15},{16,24},{20,... | collective-permute-start | bytes 405512 | tf_op jit(solution)/shard_map/ppermute | solution.py:41
  58.3 3.8 %collective-permute-start.16 = (bf16[264,512]{1,0:T(8,128)(2,1)S(1)}, bf16[264,512]{1,0:T(8,128)(2,1)S(1)}, u32[]{:S(2)}, u32[]{:S(2)}) collective-permute-start(bf16[264,512]{1,0:T(8,128)(2,1)S(1)} %combine.33.refs_4_), channel_id=1, source_target_pairs={{0,4},{4,0},{8,12},{12,8},{1,5},{5,1},{9,13},{13,9},{2,6},{6,2},{1... | collective-permute-start | bytes 811016 | tf_op jit(solution)/shard_map/ppermute | solution.py:41
  58.4 9.8 %collective-permute-start.13 = (bf16[264,512]{1,0:T(8,128)(2,1)S(1)}, bf16[264,512]{1,0:T(8,128)(2,1)S(1)}, u32[]{:S(2)}, u32[]{:S(2)}) collective-permute-start(bf16[264,512]{1,0:T(8,128)(2,1)S(1)} %combine.31.refs_4_), channel_id=1, source_target_pairs={{0,8},{4,12},{1,9},{5,13},{2,10},{6,14},{3,11},{7,15},{16,24},{20,... | collective-permute-start | bytes 811016 | tf_op jit(solution)/shard_map/ppermute | solution.py:41
  61.8 15.3 %collective-permute-start.11 = (bf16[264,512]{1,0:T(8,128)(2,1)S(1)}, bf16[264,512]{1,0:T(8,128)(2,1)S(1)}, u32[]{:S(2)}, u32[]{:S(2)}) collective-permute-start(bf16[264,512]{1,0:T(8,128)(2,1)S(1)} %combine.30.refs_4_), channel_id=1, source_target_pairs={{0,2},{1,3},{2,0},{3,1},{4,6},{5,7},{6,4},{7,5},{8,10},{9,11},{10,... | collective-permute-start | bytes 811016 | tf_op jit(solution)/shard_map/ppermute | solution.py:41
  77.4 1.7 %collective-permute-start.17 = (bf16[264,512]{1,0:T(8,128)(2,1)S(1)}, bf16[264,512]{1,0:T(8,128)(2,1)S(1)}, u32[]{:S(2)}, u32[]{:S(2)}) collective-permute-start(bf16[264,512]{1,0:T(8,128)(2,1)S(1)} %combine.36.refs_4_), channel_id=1, source_target_pairs={{0,4},{4,0},{8,12},{12,8},{1,5},{5,1},{9,13},{13,9},{2,6},{6,2},{1... | collective-permute-start | bytes 811016 | tf_op jit(solution)/shard_map/ppermute | solution.py:41
  77.5 8.4 %collective-permute-start.22 = (bf16[264,512]{1,0:T(8,128)(2,1)S(1)}, bf16[264,512]{1,0:T(8,128)(2,1)S(1)}, u32[]{:S(2)}, u32[]{:S(2)}) collective-permute-start(bf16[264,512]{1,0:T(8,128)(2,1)S(1)} %combine.34.refs_10_), channel_id=1, source_target_pairs={{0,8},{4,12},{1,9},{5,13},{2,10},{6,14},{3,11},{7,15},{16,24},{20,... | collective-permute-start | bytes 811016 | tf_op jit(solution)/shard_map/ppermute | solution.py:41
  79.0 17.3 %collective-permute-start.19 = (bf16[264,512]{1,0:T(8,128)(2,1)S(1)}, bf16[264,512]{1,0:T(8,128)(2,1)S(1)}, u32[]{:S(2)}, u32[]{:S(2)}) collective-permute-start(bf16[264,512]{1,0:T(8,128)(2,1)S(1)} %combine.35.refs_3_), channel_id=1, source_target_pairs={{0,1},{1,0},{2,3},{3,2},{4,5},{5,4},{6,7},{7,6},{8,9},{9,8},{10,11... | collective-permute-start | bytes 811016 | tf_op jit(solution)/shard_map/ppermute | solution.py:41
  79.4 19.1 %collective-permute-start.18 = (bf16[264,512]{1,0:T(8,128)(2,1)S(1)}, bf16[264,512]{1,0:T(8,128)(2,1)S(1)}, u32[]{:S(2)}, u32[]{:S(2)}) collective-permute-start(bf16[264,512]{1,0:T(8,128)(2,1)S(1)} %combine.37.refs_4_), channel_id=1, source_target_pairs={{0,8},{4,12},{1,9},{5,13},{2,10},{6,14},{3,11},{7,15},{16,24},{20,... | collective-permute-start | bytes 811016 | tf_op jit(solution)/shard_map/ppermute | solution.py:41
  81.0 10.3 %collective-permute-start.20 = (bf16[264,256]{1,0:T(8,128)(2,1)S(1)}, bf16[264,256]{1,0:T(8,128)(2,1)S(1)}, u32[]{:S(2)}, u32[]{:S(2)}) collective-permute-start(bf16[264,256]{1,0:T(8,128)(2,1)S(1)} %combine.29.refs_2_), channel_id=1, source_target_pairs={{0,1},{1,0},{2,3},{3,2},{4,5},{5,4},{6,7},{7,6},{8,9},{9,8},{10,11... | collective-permute-start | bytes 405512 | tf_op jit(solution)/shard_map/ppermute | solution.py:41
  83.0 11.3 %collective-permute-start.21 = (bf16[264,256]{1,0:T(8,128)(2,1)S(1)}, bf16[264,256]{1,0:T(8,128)(2,1)S(1)}, u32[]{:S(2)}, u32[]{:S(2)}) collective-permute-start(bf16[264,256]{1,0:T(8,128)(2,1)S(1)} %combine.32.refs_14_), channel_id=1, source_target_pairs={{0,1},{1,0},{2,3},{3,2},{4,5},{5,4},{6,7},{7,6},{8,9},{9,8},{10,11... | collective-permute-start | bytes 405512 | tf_op jit(solution)/shard_map/ppermute | solution.py:41
  86.1 14.9 %collective-permute-start.24 = (bf16[264,512]{1,0:T(8,128)(2,1)S(1)}, bf16[264,512]{1,0:T(8,128)(2,1)S(1)}, u32[]{:S(2)}, u32[]{:S(2)}) collective-permute-start(bf16[264,512]{1,0:T(8,128)(2,1)S(1)} %combine.38.refs_8_), channel_id=1, source_target_pairs={{0,1},{1,0},{2,3},{3,2},{4,5},{5,4},{6,7},{7,6},{8,9},{9,8},{10,11... | collective-permute-start | bytes 811016 | tf_op jit(solution)/shard_map/ppermute | solution.py:41
  98.7 7.1 %collective-permute-start.23 = (bf16[264,512]{1,0:T(8,128)(2,1)S(1)}, bf16[264,512]{1,0:T(8,128)(2,1)S(1)}, u32[]{:S(2)}, u32[]{:S(2)}) collective-permute-start(bf16[264,512]{1,0:T(8,128)(2,1)S(1)} %combine.39.refs_10_), channel_id=1, source_target_pairs={{0,1},{1,0},{2,3},{3,2},{4,5},{5,4},{6,7},{7,6},{8,9},{9,8},{10,11... | collective-permute-start | bytes 811016 | tf_op jit(solution)/shard_map/ppermute | solution.py:41

commit v7 on v6

--- a/solution.py
+++ b/solution.py
@@ -46,7 +46,7 @@
     return at, 9 * blocks + 2
 
 
-def gate_kernel(i_ref, f_ref, scales, tensors, offsets, fbits, run_ref, weight_ref, shift_ref, table_ref):
+def gate_kernel(i_ref, f_ref, scales, tensors, offsets, fbits, run_ref, weight_ref, shift_ref, table_ref, rows_ref):
     gate, x = i_ref[...], f_ref[...].astype(F32)
     log_forget = jnp.minimum(x, 0.0) - jnp.log1p(jnp.exp(-jnp.abs(x)))
     size = x.shape[1]
@@ -69,22 +69,26 @@
     at, _ = table_rows(blocks)
     offset = offsets[...]
     for e in range(3):
-        table_ref[at["scale"] + e * blocks : at["scale"] + (e + 1) * blocks, :] = scales[e]
+        rows_ref[at["scale"] + e * blocks : at["scale"] + (e + 1) * blocks, :] = scales[e]
         struck = jnp.where(tensors[...] == e, lax.shift_right_logical(offset, DV.bit_length() - 1), -1)
-        table_ref[at["row"] + e * blocks : at["row"] + (e + 1) * blocks, :] = struck.astype(F32)
+        rows_ref[at["row"] + e * blocks : at["row"] + (e + 1) * blocks, :] = struck.astype(F32)
     for width in (DK, DV):
-        table_ref[at[width] : at[width] + blocks, :] = (offset & (width - 1)).astype(F32)
-    table_ref[at["factor"] : at["factor"] + blocks, :] = -(lax.shift_left(jnp.ones_like(offset), fbits[...]).astype(F32))
-    table_ref[at["peak"] :, :] = jnp.concatenate([peak, total], axis=0)
+        rows_ref[at[width] : at[width] + blocks, :] = (offset & (width - 1)).astype(F32)
+    rows_ref[at["factor"] : at["factor"] + blocks, :] = -(lax.shift_left(jnp.ones_like(offset), fbits[...]).astype(F32))
+    rows_ref[at["peak"] :, :] = jnp.concatenate([peak, total], axis=0)
+    for h in range(table_ref.shape[0]):
+        table_ref[h] = jnp.broadcast_to(rows_ref[:, h : h + 1], table_ref.shape[1:])
 
 
 def gates(input_gate, forget_gate, small):
     heads, size = input_gate.shape
     col = jax.ShapeDtypeStruct((size, heads), F32)
     row = jax.ShapeDtypeStruct((heads, size), F32)
+    rows = table_rows(small[1].shape[0])[1]
     return pl.pallas_call(
         gate_kernel,
-        out_shape=(col, col, row, jax.ShapeDtypeStruct((table_rows(small[1].shape[0])[1], heads), F32)),
+        out_shape=(col, col, row, jax.ShapeDtypeStruct((heads, rows, 128), F32)),
+        scratch_shapes=[pltpu.VMEM((rows, heads), F32)],
         compiler_params=pltpu.CompilerParams(vmem_limit_bytes=4 << 20),
         cost_estimate=pl.CostEstimate(flops=1 << 20, bytes_accessed=1 << 20, transcendentals=0),
         name="gates",
@@ -97,17 +101,28 @@
     return jnp.sum(jnp.where(lane == h, x, 0.0), axis=1, keepdims=True)
 
 
-def dequant(ref, at, lo, width, full, tensor_id, h, table):
+def across(x, width):
+    return jnp.concatenate([x] * (width // x.shape[1]), axis=1)
+
+
+def dequant(ref, at, lo, width, full, tensor_id, table):
     blocks = ref.shape[0] // BLK
     rows, _ = table_rows(blocks)
-    row = lax.broadcasted_iota(jnp.int32, (BLK, 1), 0).astype(F32)
+    row = lax.broadcasted_iota(jnp.int32, (BLK, 128), 0).astype(F32)
     col = (lax.broadcasted_iota(jnp.int32, (1, width), 1) + lo).astype(F32)
+
+    def entry(r):
+        return table[r : r + 1, :]
+
     out = []
     for b in range(blocks):
         x = ref[b * BLK : (b + 1) * BLK, pl.ds(pl.multiple_of(at + lo, 128), width)].astype(F32)
-        scale = table[rows["scale"] + tensor_id * blocks + b, h]
-        hit = (row == table[rows["row"] + tensor_id * blocks + b, h]) & (col == table[rows[full] + b, h])
-        out.append((x * jnp.where(hit, table[rows["factor"] + b, h] * scale, scale)).astype(BF16))
+        scale = entry(rows["scale"] + tensor_id * blocks + b)
+        in_row = jnp.where(row == entry(rows["row"] + tensor_id * blocks + b), 1.0, 0.0)
+        in_col = jnp.where(col == across(entry(rows[full] + b), width), 1.0, 0.0)
+        struck = across(entry(rows["factor"] + b) * scale, width)
+        factor = jnp.where(across(in_row, width) * in_col > 0.5, struck, across(scale, width))
+        out.append((x * factor).astype(BF16))
     return jnp.concatenate(out, axis=0)
 
 
@@ -204,20 +219,21 @@
 VMEM = pl.BlockSpec(memory_space=pltpu.VMEM)
 
 
-def state_kernel(pair, lo, at, table, weight_ref, k_ref, v_ref, keep_ref, send_ref):
+def state_kernel(pair, lo, at, table_ref, weight_ref, k_ref, v_ref, keep_ref, send_ref):
     own = lax.axis_index("head") & 1
     width = keep_ref.shape[1]
     peak_row = table_rows(k_ref.shape[0] // BLK)[0]["peak"]
     for out_ref, side in ((send_ref, 1 - own), (keep_ref, own)):
         h = 2 * pair + side
-        k = dequant(k_ref, pl.multiple_of((at + side) * DK, DK), 0, DK, DK, 1, h, table)
-        v = dequant(v_ref, pl.multiple_of((at + side) * DV, DV), lo, width, DV, 2, h, table)
+        table = table_ref.at[h]
+        k = dequant(k_ref, pl.multiple_of((at + side) * DK, DK), 0, DK, DK, 1, table[...])
+        v = dequant(v_ref, pl.multiple_of((at + side) * DV, DV), lo, width, DV, 2, table[...])
         weighted = (k.astype(F32) * pick(weight_ref, h)).astype(BF16)
         matrix = lax.dot_general(weighted, v, (((0,), (0,)), ((), ())), preferred_element_type=F32)
         out_ref[:DK, :] = matrix.astype(BF16)
         normer = jnp.sum(weighted.astype(F32), axis=0, keepdims=True)
-        peak = jnp.full((1, width), table[peak_row, h], F32)
-        total = jnp.full((1, width), table[peak_row + 1, h], F32)
+        peak = across(table[peak_row : peak_row + 1, :], width)
+        total = across(table[peak_row + 1 : peak_row + 2, :], width)
         out_ref[DK:ROWS, :] = pack_tail(normer, peak, total)
 
 
@@ -229,13 +245,13 @@
         at = 0
         spec = dict(
             grid=(1,),
-            in_specs=[SMEM, VMEM]
+            in_specs=[VMEM, VMEM]
             + [pl.BlockSpec((rows, 2 * DK), lambda i: (0, pair)), pl.BlockSpec((rows, 2 * DV), lambda i: (0, pair))],
         )
         key_codes, value_codes = in_hbm(key_codes), in_hbm(value_codes)
     else:
         at = 2 * pair
-        spec = dict(in_specs=[SMEM, VMEM, VMEM, VMEM])
+        spec = dict(in_specs=[VMEM] * 4)
     kernel, extra, extra_specs = ordered(functools.partial(state_kernel, pair, lo, at), 4, after)
     spec["in_specs"] += extra_specs
     return pl.pallas_call(
@@ -280,14 +296,25 @@
     )(*parts, *extra)
 
 
-def output_kernel(head_bits, bits, pair, mine, pieces, table, run_ref, shift_ref, q_ref, k_ref, v_ref, *rest):
-    count = len(rest[:-4]) // pieces
-    groups = [rest[p * count : (p + 1) * count] for p in range(pieces)]
-    out_ref, token_ref, result_ref, sem = rest[-4:]
-    token_ref[...] = jnp.zeros_like(token_ref)
+def output_kernel(head_bits, bits, pair, mine, pieces, done, table_ref, run_ref, shift_ref, q_ref, k_ref, v_ref, *rest):
+    if done is None:
+        parts, earlier, (result_ref,) = rest[:-1], (), rest[-1:]
+    else:
+        parts, earlier, (out_ref, result_ref, sems) = rest[: -3 - len(done)], rest[-3 - len(done) : -3], rest[-3:]
+    own = lax.axis_index("head") & 1
+
+    def write(ref, pair, mine, n):
+        at = pl.multiple_of((2 * pair + (own if mine else 1 - own)) * DV, DV)
+        return pltpu.make_async_copy(ref, out_ref.at[:, pl.ds(at, DV)], sems.at[n])
+
+    writes = [write(ref, *which, n) for n, (ref, which) in enumerate(zip(earlier, done or ()))]
+    for copy in writes:
+        copy.start()
+    count = len(parts) // pieces
+    groups = [parts[p * count : (p + 1) * count] for p in range(pieces)]
     bit = device_bits(head_bits, bits)
-    own = lax.axis_index("head") & 1
     h = 2 * pair + (own if mine else 1 - own)
+    table = table_ref.at[h]
     narrow, wide = pl.multiple_of(h * DK, DK), pl.multiple_of(h * DV, DV)
     factor = 1.0 / math.sqrt(DK)
     size = q_ref.shape[0]
@@ -304,9 +331,9 @@
             normer, peak = states[0].normer, states[0].peak
             starts.append(states[0].matrix())
     start = jnp.concatenate(starts, axis=1) if pieces > 1 else starts[0]
-    q = dequant(q_ref, narrow, 0, DK, DK, 0, h, table)
-    k = dequant(k_ref, narrow, 0, DK, DK, 1, h, table)
-    v = dequant(v_ref, wide, 0, DV, DV, 2, h, table)
+    q = dequant(q_ref, narrow, 0, DK, DK, 0, table[...])
+    k = dequant(k_ref, narrow, 0, DK, DK, 1, table[...])
+    v = dequant(v_ref, wide, 0, DV, DV, 2, table[...])
     run = pick(run_ref, h)
     exponent = jnp.where(row >= col, run + shift_ref[pl.ds(h, 1), :], NEG_FILL)
     inter = run + peak[:, :1]
@@ -319,41 +346,40 @@
     numerator = numerator + jnp.dot(lifted, start, preferred_element_type=F32)
     denominator = jnp.sum(product, axis=1, keepdims=True) + jnp.sum(lifted.astype(F32) * normer, axis=1, keepdims=True)
     result_ref[...] = (numerator / jnp.maximum(jnp.abs(denominator), 1.0)).astype(BF16)
-    write = pltpu.make_async_copy(result_ref, out_ref.at[:, pl.ds(wide, DV)], sem)
-    write.start()
-    write.wait()
-
-
-def span_outputs(head_bits, bits, pair, mine, table, run, shift, codes, groups, before, after):
+    if done is not None:
+        writes.append(write(result_ref, pair, mine, len(done)))
+        writes[-1].start()
+        for copy in writes:
+            copy.wait()
+
+
+def span_outputs(head_bits, bits, pair, mine, table, run, shift, codes, groups, done, earlier, after):
     rows, width = codes[2].shape
-    states = [x for group in groups for x in group]
-    operands = [table, run, shift, *codes, *states]
-    in_specs = [SMEM] + [VMEM] * (len(operands) - 1)
-    kernel = functools.partial(output_kernel, head_bits, bits, pair, mine, len(groups))
+    operands = [table, run, shift, *codes, *[x for group in groups for x in group], *earlier]
+    in_specs = [VMEM] * len(operands)
+    kernel = functools.partial(output_kernel, head_bits, bits, pair, mine, len(groups), done)
     kernel, extra, extra_specs = ordered(kernel, len(operands), after)
-    operands += extra
-    in_specs += extra_specs
-    aliases = {}
-    if before is not None:
-        kernel, extra, extra_specs = ordered(kernel, len(operands), before)
-        aliases = {len(operands): 0}
-        operands += extra
-        in_specs += extra_specs
+    result = jax.ShapeDtypeStruct((rows, DV), BF16)
+    if done is None:
+        outs = dict(out_specs=VMEM, out_shape=result)
+    else:
+        outs = dict(
+            out_specs=pl.BlockSpec(memory_space=pl.ANY),
+            out_shape=jax.ShapeDtypeStruct((rows, width), BF16),
+            scratch_shapes=[pltpu.VMEM(result.shape, BF16), pltpu.SemaphoreType.DMA((len(done) + 1,))],
+        )
     return pl.pallas_call(
         kernel,
-        in_specs=in_specs,
-        out_specs=(pl.BlockSpec(memory_space=pl.ANY), VMEM),
-        out_shape=(jax.ShapeDtypeStruct((rows, width), BF16), jax.ShapeDtypeStruct((8, 128), F32)),
-        scratch_shapes=[pltpu.VMEM((rows, DV), BF16), pltpu.SemaphoreType.DMA],
-        input_output_aliases=aliases,
+        in_specs=in_specs + extra_specs,
+        **outs,
         compiler_params=pltpu.CompilerParams(vmem_limit_bytes=12 << 20),
         cost_estimate=pl.CostEstimate(
             flops=2 * rows * (rows * DK + rows * DV + DK * DV),
-            bytes_accessed=rows * 2 * (2 * DK + 2 * DV) + sum(x.size for x in states) * 2,
+            bytes_accessed=rows * 2 * (2 * DK + 2 * DV),
             transcendentals=rows * rows,
         ),
         name="span_outputs",
-    )(*operands)
+    )(*operands, *extra)
 
 
 def body(
@@ -377,7 +403,7 @@
     exchange = functools.partial(flip, head_bits=head_bits, ctx_bits=ctx_bits)
     run, weight, shift, table = gates(in_hbm(input_gate.T), in_hbm(forget_gate.T), small)
     keep, got, back = {}, {}, {}
-    out = token = None
+    results, token = {}, None
     for stage, c in order(bits):
         if stage == 0:
             keep[c], token = span_states(CHUNKS[c], table, weight, key_codes, value_codes, token)
@@ -388,14 +414,17 @@
         else:
             mine = stage == bits + 1
             groups = [got[d] if mine else [back[d]] for d in of_pair(c)]
-            out, token = span_outputs(
-                head_bits, bits, c, mine, table, run, shift, codes, groups, out, token
+            final = len(results) == input_gate.shape[1] - 1
+            token = span_outputs(
+                head_bits, bits, c, mine, table, run, shift, codes, groups,
+                tuple(results) if final else None, results.values() if final else (), token,
             )
+            results[c, mine] = token
         if stage < bits:
             got.setdefault(c, []).append(exchange(token, stage, last=stage == bits - 1))
         elif stage == bits:
             back[c] = exchange(token, 0, last=False)
-    return out
+    return token
 
 
 def of_pair(pair):

time: 109 us -> 107 us (0.982)
  Pallas kernels: 29.8 us -> 16.8 us
  waiting for transfers between devices: 53.1 us -> 59.4 us
  starting transfers between devices: 25.2 us -> 30.2 us
    pallas_call x8, Pallas kernels: 17.9 us -> 7.25 us  [span_outputs(): pl.pallas_call(kernel, in_specs=in_specs + extra_specs, **outs, compiler_...]
    ppermute x25, waiting for transfers between devices: 53.1 us -> 59.4 us  [flip(): return lax.ppermute(x, axis, pairs)]
    ppermute x25, starting transfers between devices: 25.2 us -> 30.2 us  [flip(): return lax.ppermute(x, axis, pairs)]
    pallas_call x5, Pallas kernels: 6.71 us -> 4.28 us  [span_states(): pl.pallas_call(kernel, **spec, out_specs=(VMEM,) * 2, out_shape=(out, out...]
  transfers between devices with their start and end apart: 25 -> 25, of which waited for: 16 -> 16; matrix products, arithmetic and copies ran while one was open for 0% -> 0% of each run, Pallas kernels for 22% -> 11%
where the time goes in v7:
time: 107 us
  waiting for transfers between devices  59.4 us (56%)
  starting transfers between devices  30.2 us (28%)
  Pallas kernels  16.8 us (16%)
    ppermute x25, waiting for transfers between devices, flip(): return lax.ppermute(x, axis, pairs)  59.4 us
    ppermute x25, starting transfers between devices, flip(): return lax.ppermute(x, axis, pairs)  30.2 us
    pallas_call x8, Pallas kernels, span_outputs(): pl.pallas_call(kernel, in_specs=in_specs + extra_specs, **outs, compiler_...  7.25 us
    pallas_call x5, Pallas kernels, span_states(): pl.pallas_call(kernel, **spec, out_specs=(VMEM,) * 2, out_shape=(out, out...  4.28 us
    pallas_call x20, Pallas kernels, combine(): pl.pallas_call(kernel, in_specs=[VMEM] * len(parts) + extra_specs, out_sp...  3.62 us
  transfers between devices with their start and end apart: 25, of which 16 were waited for; matrix products, arithmetic and copies ran while one was open for 0% of the time, Pallas kernels for 11%

profile of v7, /device:TPU:0, one launch (start us, length us, event | category | flops | bytes accessed | tf_op | source)
XLA Modules:
  0.0 106.9 jit_solution(10870432888023034683)
XLA Ops:
  0.0 1.6 %gates.1 = (f32[256,8]{1,0:T(8,128)S(1)}, f32[256,8]{1,0:T(8,128)S(1)}, f32[8,256]{1,0:T(8,128)S(1)}, f32[8,20,128]{2,1,0:T(8,128)S(1)}) custom-call(bf16[8,256]{1,0:T(8,128)(2,1)} %bitcast.3, bf16[8,256]{1,0:T(8,128)(2,1)} %bitcast.4, f32[3,2,8]{2,1,0:T(2,128)} %bitcast.5, s32[2,8]{1,0:T(2,128)} %tensors.1, s32[2,8]{1,0:T(2,128)} %offsets.1, s32[2,8]{1,0:T(2,128)} %fbits.1), custom_call_target="tpu_custom_call" | custom-call | flops 1048576 | bytes 1048576 | tf_op jit(solution)/shard_map/gates/pallas_call | solution.py:88
  1.6 1.7 %span_states.5 = (bf16[264,256]{1,0:T(8,128)(2,1)S(1)}, bf16[264,256]{1,0:T(8,128)(2,1)S(1)}) custom-call(f32[8,20,128]{2,1,0:T(8,128)S(1)} %get-tuple-element.19.table_ref.refs_0_, f32[256,8]{1,0:T(8,128)S(1)} %get-tuple-element.22.weight_ref.refs_1_, bf16[256,2048]{1,0:T(8,128)(2,1)} %refs_4_.15, bf16[256,4096]{1,0:T(8,128)(2,1)} %refs_5_.15), custom_call_target="tpu_custom_call" | custom-call | flops 67108864 | bytes 1310720 | tf_op jit(solution)/shard_map/span_states/pallas_call | solution.py:257
  3.3 3.1 %collective-permute-start.1 = (bf16[264,256]{1,0:T(8,128)(2,1)S(1)}, bf16[264,256]{1,0:T(8,128)(2,1)S(1)}, u32[]{:S(2)}, u32[]{:S(2)}) collective-permute-start(bf16[264,256]{1,0:T(8,128)(2,1)S(1)} %get-tuple-element.23.refs_4_), channel_id=1, source_target_pairs={{0,1},{1,0},{2,3},{3,2},{4,5},{5,4},{6,7},{7,6},{8,9},{9,8},{10,11... | collective-permute-start | bytes 405512 | tf_op jit(solution)/shard_map/ppermute | solution.py:41
  6.4 0.6 span_states.6
  7.1 0.7 span_states.7
  7.8 2.1 %collective-permute-start.3 = (bf16[264,512]{1,0:T(8,128)(2,1)S(1)}, bf16[264,512]{1,0:T(8,128)(2,1)S(1)}, u32[]{:S(2)}, u32[]{:S(2)}) collective-permute-start(bf16[264,512]{1,0:T(8,128)(2,1)S(1)} %get-tuple-element.27.refs_2_), channel_id=1, source_target_pairs={{0,1},{1,0},{2,3},{3,2},{4,5},{5,4},{6,7},{7,6},{8,9},{9,8},{10,11... | collective-permute-start | bytes 811016 | tf_op jit(solution)/shard_map/ppermute | solution.py:41
  9.8 1.0 collective-permute-done.1.refs_1_.refs_6_
  10.9 2.8 %collective-permute-done.refs_1_.refs_10_ = bf16[264,256]{1,0:T(8,128)(2,1)S(1)} collective-permute-done((bf16[264,256]{1,0:T(8,128)(2,1)S(1)}, bf16[264,256]{1,0:T(8,128)(2,1)S(1)}, u32[]{:S(2)}, u32[]{:S(2)}) %collective-permute-start) | collective-permute-done | bytes 135200 | tf_op jit(solution)/shard_map/ppermute | solution.py:41
  13.8 0.7 span_states.8
  14.5 2.1 %collective-permute-start.6 = (bf16[264,512]{1,0:T(8,128)(2,1)S(1)}, bf16[264,512]{1,0:T(8,128)(2,1)S(1)}, u32[]{:S(2)}, u32[]{:S(2)}) collective-permute-start(bf16[264,512]{1,0:T(8,128)(2,1)S(1)} %get-tuple-element.29.refs_2_), channel_id=1, source_target_pairs={{0,1},{1,0},{2,3},{3,2},{4,5},{5,4},{6,7},{7,6},{8,9},{9,8},{10,11... | collective-permute-start | bytes 811016 | tf_op jit(solution)/shard_map/ppermute | solution.py:41
  16.6 2.6 %collective-permute-start.2 = (bf16[264,256]{1,0:T(8,128)(2,1)S(1)}, bf16[264,256]{1,0:T(8,128)(2,1)S(1)}, u32[]{:S(2)}, u32[]{:S(2)}) collective-permute-start(bf16[264,256]{1,0:T(8,128)(2,1)S(1)} %combine.21.refs_4_), channel_id=1, source_target_pairs={{0,2},{1,3},{2,0},{3,1},{4,6},{5,7},{6,4},{7,5},{8,10},{9,11},{10,... | collective-permute-start | bytes 405512 | tf_op jit(solution)/shard_map/ppermute | solution.py:41
  19.2 0.3 collective-permute-start.5
  19.5 5.7 %collective-permute-done.3.refs_1_.refs_6_ = bf16[264,512]{1,0:T(8,128)(2,1)S(1)} collective-permute-done((bf16[264,512]{1,0:T(8,128)(2,1)S(1)}, bf16[264,512]{1,0:T(8,128)(2,1)S(1)}, u32[]{:S(2)}, u32[]{:S(2)}) %collective-permute-start.3) | collective-permute-done | bytes 270368 | tf_op jit(solution)/shard_map/ppermute | solution.py:41
  25.4 2.2 %collective-permute-start.9 = (bf16[264,512]{1,0:T(8,128)(2,1)S(1)}, bf16[264,512]{1,0:T(8,128)(2,1)S(1)}, u32[]{:S(2)}, u32[]{:S(2)}) collective-permute-start(bf16[264,512]{1,0:T(8,128)(2,1)S(1)} %combine.22.refs_3_), channel_id=1, source_target_pairs={{0,2},{1,3},{2,0},{3,1},{4,6},{5,7},{6,4},{7,5},{8,10},{9,11},{10,... | collective-permute-start | bytes 811016 | tf_op jit(solution)/shard_map/ppermute | solution.py:41
  27.9 0.7 span_states.9
  28.6 2.4 %collective-permute-done.6.refs_1_.refs_6_ = bf16[264,512]{1,0:T(8,128)(2,1)S(1)} collective-permute-done((bf16[264,512]{1,0:T(8,128)(2,1)S(1)}, bf16[264,512]{1,0:T(8,128)(2,1)S(1)}, u32[]{:S(2)}, u32[]{:S(2)}) %collective-permute-start.6) | collective-permute-done | bytes 270368 | tf_op jit(solution)/shard_map/ppermute | solution.py:41
  31.4 0.5 collective-permute-start.10
  31.9 2.9 %collective-permute-start.4 = (bf16[264,512]{1,0:T(8,128)(2,1)S(1)}, bf16[264,512]{1,0:T(8,128)(2,1)S(1)}, u32[]{:S(2)}, u32[]{:S(2)}) collective-permute-start(bf16[264,512]{1,0:T(8,128)(2,1)S(1)} %get-tuple-element.31.refs_2_), channel_id=1, source_target_pairs={{0,1},{1,0},{2,3},{3,2},{4,5},{5,4},{6,7},{7,6},{8,9},{9,8},{10,11... | collective-permute-start | bytes 811016 | tf_op jit(solution)/shard_map/ppermute | solution.py:41
  35.1 8.4 %collective-permute-done.9.refs_2_.refs_7_.refs_1_ = bf16[264,512]{1,0:T(8,128)(2,1)S(1)} collective-permute-done((bf16[264,512]{1,0:T(8,128)(2,1)S(1)}, bf16[264,512]{1,0:T(8,128)(2,1)S(1)}, u32[]{:S(2)}, u32[]{:S(2)}) %collective-permute-start.9) | collective-permute-done | bytes 270368 | tf_op jit(solution)/shard_map/ppermute | solution.py:41
  43.9 3.5 %collective-permute-start.8 = (bf16[264,256]{1,0:T(8,128)(2,1)S(1)}, bf16[264,256]{1,0:T(8,128)(2,1)S(1)}, u32[]{:S(2)}, u32[]{:S(2)}) collective-permute-start(bf16[264,256]{1,0:T(8,128)(2,1)S(1)} %combine.26.refs_4_), channel_id=1, source_target_pairs={{0,8},{4,12},{1,9},{5,13},{2,10},{6,14},{3,11},{7,15},{16,24},{20,... | collective-permute-start | bytes 405512 | tf_op jit(solution)/shard_map/ppermute | solution.py:41
  47.4 1.3 %collective-permute-start.15 = (bf16[264,256]{1,0:T(8,128)(2,1)S(1)}, bf16[264,256]{1,0:T(8,128)(2,1)S(1)}, u32[]{:S(2)}, u32[]{:S(2)}) collective-permute-start(bf16[264,256]{1,0:T(8,128)(2,1)S(1)} %combine.27.refs_3_), channel_id=1, source_target_pairs={{0,8},{4,12},{1,9},{5,13},{2,10},{6,14},{3,11},{7,15},{16,24},{20,... | collective-permute-start | bytes 405512 | tf_op jit(solution)/shard_map/ppermute | solution.py:41
  48.8 2.6 %collective-permute-done.8.refs_3_.refs_9_ = bf16[264,256]{1,0:T(8,128)(2,1)S(1)} collective-permute-done((bf16[264,256]{1,0:T(8,128)(2,1)S(1)}, bf16[264,256]{1,0:T(8,128)(2,1)S(1)}, u32[]{:S(2)}, u32[]{:S(2)}) %collective-permute-start.8) | collective-permute-done | bytes 135200 | tf_op jit(solution)/shard_map/ppermute | solution.py:41
  51.7 0.3 combine.31.refs_4_
  52.0 1.6 %collective-permute-done.15.refs_3_.refs_13_ = bf16[264,256]{1,0:T(8,128)(2,1)S(1)} collective-permute-done((bf16[264,256]{1,0:T(8,128)(2,1)S(1)}, bf16[264,256]{1,0:T(8,128)(2,1)S(1)}, u32[]{:S(2)}, u32[]{:S(2)}) %collective-permute-start.15) | collective-permute-done | bytes 135200 | tf_op jit(solution)/shard_map/ppermute | solution.py:41
  53.8 0.9 span_outputs.8.refs_3_.refs_7_
  54.6 4.1 %collective-permute-done.14.refs_2_.refs_1_.refs_7_ = bf16[264,512]{1,0:T(8,128)(2,1)S(1)} collective-permute-done((bf16[264,512]{1,0:T(8,128)(2,1)S(1)}, bf16[264,512]{1,0:T(8,128)(2,1)S(1)}, u32[]{:S(2)}, u32[]{:S(2)}) %collective-permute-start.14) | collective-permute-done | bytes 270368 | tf_op jit(solution)/shard_map/ppermute | solution.py:41
  59.1 3.4 %collective-permute-start.13 = (bf16[264,512]{1,0:T(8,128)(2,1)S(1)}, bf16[264,512]{1,0:T(8,128)(2,1)S(1)}, u32[]{:S(2)}, u32[]{:S(2)}) collective-permute-start(bf16[264,512]{1,0:T(8,128)(2,1)S(1)} %combine.31.refs_4_), channel_id=1, source_target_pairs={{0,8},{4,12},{1,9},{5,13},{2,10},{6,14},{3,11},{7,15},{16,24},{20,... | collective-permute-start | bytes 811016 | tf_op jit(solution)/shard_map/ppermute | solution.py:41
  62.6 0.3 combine.34.refs_10_
  62.9 5.9 %collective-permute-done.13.refs_9_.refs_3_ = bf16[264,512]{1,0:T(8,128)(2,1)S(1)} collective-permute-done((bf16[264,512]{1,0:T(8,128)(2,1)S(1)}, bf16[264,512]{1,0:T(8,128)(2,1)S(1)}, u32[]{:S(2)}, u32[]{:S(2)}) %collective-permute-start.13) | collective-permute-done | bytes 270368 | tf_op jit(solution)/shard_map/ppermute | solution.py:41
  68.8 0.9 span_outputs.9.refs_4_.refs_8_
  69.7 0.3 combine.35.refs_3_
  69.9 7.1 %collective-permute-done.11.refs_2_.refs_1_.refs_7_ = bf16[264,512]{1,0:T(8,128)(2,1)S(1)} collective-permute-done((bf16[264,512]{1,0:T(8,128)(2,1)S(1)}, bf16[264,512]{1,0:T(8,128)(2,1)S(1)}, u32[]{:S(2)}, u32[]{:S(2)}) %collective-permute-start.11) | collective-permute-done | bytes 270368 | tf_op jit(solution)/shard_map/ppermute | solution.py:41
  77.3 1.6 %collective-permute-start.22 = (bf16[264,512]{1,0:T(8,128)(2,1)S(1)}, bf16[264,512]{1,0:T(8,128)(2,1)S(1)}, u32[]{:S(2)}, u32[]{:S(2)}) collective-permute-start(bf16[264,512]{1,0:T(8,128)(2,1)S(1)} %combine.34.refs_10_), channel_id=1, source_target_pairs={{0,8},{4,12},{1,9},{5,13},{2,10},{6,14},{3,11},{7,15},{16,24},{20,... | collective-permute-start | bytes 811016 | tf_op jit(solution)/shard_map/ppermute | solution.py:41
  79.0 0.3 combine.37.refs_4_
  79.3 1.6 %collective-permute-start.18 = (bf16[264,512]{1,0:T(8,128)(2,1)S(1)}, bf16[264,512]{1,0:T(8,128)(2,1)S(1)}, u32[]{:S(2)}, u32[]{:S(2)}) collective-permute-start(bf16[264,512]{1,0:T(8,128)(2,1)S(1)} %combine.37.refs_4_), channel_id=1, source_target_pairs={{0,8},{4,12},{1,9},{5,13},{2,10},{6,14},{3,11},{7,15},{16,24},{20,... | collective-permute-start | bytes 811016 | tf_op jit(solution)/shard_map/ppermute | solution.py:41
  80.9 2.0 %collective-permute-start.20 = (bf16[264,256]{1,0:T(8,128)(2,1)S(1)}, bf16[264,256]{1,0:T(8,128)(2,1)S(1)}, u32[]{:S(2)}, u32[]{:S(2)}) collective-permute-start(bf16[264,256]{1,0:T(8,128)(2,1)S(1)} %combine.29.refs_2_), channel_id=1, source_target_pairs={{0,1},{1,0},{2,3},{3,2},{4,5},{5,4},{6,7},{7,6},{8,9},{9,8},{10,11... | collective-permute-start | bytes 405512 | tf_op jit(solution)/shard_map/ppermute | solution.py:41
  82.9 2.8 %collective-permute-done.22.refs_3_.refs_9_ = bf16[264,512]{1,0:T(8,128)(2,1)S(1)} collective-permute-done((bf16[264,512]{1,0:T(8,128)(2,1)S(1)}, bf16[264,512]{1,0:T(8,128)(2,1)S(1)}, u32[]{:S(2)}, u32[]{:S(2)}) %collective-permute-start.22) | collective-permute-done | bytes 270368 | tf_op jit(solution)/shard_map/ppermute | solution.py:41
  86.1 5.1 %collective-permute-done.20.refs_6_ = bf16[264,256]{1,0:T(8,128)(2,1)S(1)} collective-permute-done((bf16[264,256]{1,0:T(8,128)(2,1)S(1)}, bf16[264,256]{1,0:T(8,128)(2,1)S(1)}, u32[]{:S(2)}, u32[]{:S(2)}) %collective-permute-start.20) | collective-permute-done | bytes 135200 | tf_op jit(solution)/shard_map/ppermute | solution.py:41
  91.2 2.9 %collective-permute-done.21.refs_7_ = bf16[264,256]{1,0:T(8,128)(2,1)S(1)} collective-permute-done((bf16[264,256]{1,0:T(8,128)(2,1)S(1)}, bf16[264,256]{1,0:T(8,128)(2,1)S(1)}, u32[]{:S(2)}, u32[]{:S(2)}) %collective-permute-start.21) | collective-permute-done | bytes 135200 | tf_op jit(solution)/shard_map/ppermute | solution.py:41
  94.1 0.6 span_outputs.10.refs_7_.refs_9_
  94.8 0.7 span_outputs.11.refs_4_.refs_10_
  95.5 0.3 combine.39.refs_10_
  95.8 0.9 span_outputs.12.refs_7_.refs_11_
  96.7 3.2 %collective-permute-done.24.refs_6_ = bf16[264,512]{1,0:T(8,128)(2,1)S(1)} collective-permute-done((bf16[264,512]{1,0:T(8,128)(2,1)S(1)}, bf16[264,512]{1,0:T(8,128)(2,1)S(1)}, u32[]{:S(2)}, u32[]{:S(2)}) %collective-permute-start.24) | collective-permute-done | bytes 270368 | tf_op jit(solution)/shard_map/ppermute | solution.py:41
  99.9 0.7 span_outputs.13.refs_10_.refs_12_
  100.6 0.9 span_outputs.14.refs_13_.refs_14_
  101.4 3.5 %collective-permute-done.23.refs_6_ = bf16[264,512]{1,0:T(8,128)(2,1)S(1)} collective-permute-done((bf16[264,512]{1,0:T(8,128)(2,1)S(1)}, bf16[264,512]{1,0:T(8,128)(2,1)S(1)}, u32[]{:S(2)}, u32[]{:S(2)}) %collective-permute-start.23) | collective-permute-done | bytes 270368 | tf_op jit(solution)/shard_map/ppermute | solution.py:41
  104.9 1.8 %span_outputs.15 = bf16[256,4096]{1,0:T(8,128)(2,1)} custom-call(f32[8,20,128]{2,1,0:T(8,128)S(1)} %get-tuple-element.19.table_ref.refs_0_, f32[256,8]{1,0:T(8,128)S(1)} %get-tuple-element.20.refs_1_, f32[8,256]{1,0:T(8,128)S(1)} %get-tuple-element.21.refs_2_, bf16[256,2048]{1,0:T(8,128)(2,1)S(1)} %copy-done.2, bf16[256,2048]{1,0:T(8,128)(2,1)S(1)} %copy-done.1, ...), custom_call_target="tpu_custom_call" | custom-call | flops 167772160 | bytes 786432 | tf_op jit(solution)/shard_map/span_outputs/pallas_call | solution.py:371
  (42 shorter events, 3.4 us)
Async XLA Ops:
  0.0 6.4 %copy-start.1 = (bf16[256,2048]{1,0:T(8,128)(2,1)S(1)}, bf16[256,2048]{1,0:T(8,128)(2,1)}, u32[]{:S(2)}) copy-start(bf16[256,2048]{1,0:T(8,128)(2,1)} %refs_4_.15) | copy-start | bytes 3145732
  0.0 6.4 %copy-start = (bf16[256,4096]{1,0:T(8,128)(2,1)S(1)}, bf16[256,4096]{1,0:T(8,128)(2,1)}, u32[]{:S(2)}) copy-start(bf16[256,4096]{1,0:T(8,128)(2,1)} %refs_5_.15) | copy-start | bytes 6291460
  3.3 7.5 %collective-permute-start.1 = (bf16[264,256]{1,0:T(8,128)(2,1)S(1)}, bf16[264,256]{1,0:T(8,128)(2,1)S(1)}, u32[]{:S(2)}, u32[]{:S(2)}) collective-permute-start(bf16[264,256]{1,0:T(8,128)(2,1)S(1)} %get-tuple-element.23.refs_4_), channel_id=1, source_target_pairs={{0,1},{1,0},{2,3},{3,2},{4,5},{5,4},{6,7},{7,6},{8,9},{9,8},{10,11... | collective-permute-start | bytes 405512 | tf_op jit(solution)/shard_map/ppermute | solution.py:41
  7.0 6.7 %collective-permute-start = (bf16[264,256]{1,0:T(8,128)(2,1)S(1)}, bf16[264,256]{1,0:T(8,128)(2,1)S(1)}, u32[]{:S(2)}, u32[]{:S(2)}) collective-permute-start(bf16[264,256]{1,0:T(8,128)(2,1)S(1)} %get-tuple-element.25.refs_4_), channel_id=1, source_target_pairs={{0,1},{1,0},{2,3},{3,2},{4,5},{5,4},{6,7},{7,6},{8,9},{9,8},{10,11... | collective-permute-start | bytes 405512 | tf_op jit(solution)/shard_map/ppermute | solution.py:41
  7.8 17.5 %collective-permute-start.3 = (bf16[264,512]{1,0:T(8,128)(2,1)S(1)}, bf16[264,512]{1,0:T(8,128)(2,1)S(1)}, u32[]{:S(2)}, u32[]{:S(2)}) collective-permute-start(bf16[264,512]{1,0:T(8,128)(2,1)S(1)} %get-tuple-element.27.refs_2_), channel_id=1, source_target_pairs={{0,1},{1,0},{2,3},{3,2},{4,5},{5,4},{6,7},{7,6},{8,9},{9,8},{10,11... | collective-permute-start | bytes 811016 | tf_op jit(solution)/shard_map/ppermute | solution.py:41
  14.5 16.5 %collective-permute-start.6 = (bf16[264,512]{1,0:T(8,128)(2,1)S(1)}, bf16[264,512]{1,0:T(8,128)(2,1)S(1)}, u32[]{:S(2)}, u32[]{:S(2)}) collective-permute-start(bf16[264,512]{1,0:T(8,128)(2,1)S(1)} %get-tuple-element.29.refs_2_), channel_id=1, source_target_pairs={{0,1},{1,0},{2,3},{3,2},{4,5},{5,4},{6,7},{7,6},{8,9},{9,8},{10,11... | collective-permute-start | bytes 811016 | tf_op jit(solution)/shard_map/ppermute | solution.py:41
  16.6 11.2 %collective-permute-start.2 = (bf16[264,256]{1,0:T(8,128)(2,1)S(1)}, bf16[264,256]{1,0:T(8,128)(2,1)S(1)}, u32[]{:S(2)}, u32[]{:S(2)}) collective-permute-start(bf16[264,256]{1,0:T(8,128)(2,1)S(1)} %combine.21.refs_4_), channel_id=1, source_target_pairs={{0,2},{1,3},{2,0},{3,1},{4,6},{5,7},{6,4},{7,5},{8,10},{9,11},{10,... | collective-permute-start | bytes 405512 | tf_op jit(solution)/shard_map/ppermute | solution.py:41
  19.2 12.0 %collective-permute-start.5 = (bf16[264,256]{1,0:T(8,128)(2,1)S(1)}, bf16[264,256]{1,0:T(8,128)(2,1)S(1)}, u32[]{:S(2)}, u32[]{:S(2)}) collective-permute-start(bf16[264,256]{1,0:T(8,128)(2,1)S(1)} %combine.20.refs_2_), channel_id=1, source_target_pairs={{0,2},{1,3},{2,0},{3,1},{4,6},{5,7},{6,4},{7,5},{8,10},{9,11},{10,... | collective-permute-start | bytes 405512 | tf_op jit(solution)/shard_map/ppermute | solution.py:41
  25.4 18.1 %collective-permute-start.9 = (bf16[264,512]{1,0:T(8,128)(2,1)S(1)}, bf16[264,512]{1,0:T(8,128)(2,1)S(1)}, u32[]{:S(2)}, u32[]{:S(2)}) collective-permute-start(bf16[264,512]{1,0:T(8,128)(2,1)S(1)} %combine.22.refs_3_), channel_id=1, source_target_pairs={{0,2},{1,3},{2,0},{3,1},{4,6},{5,7},{6,4},{7,5},{8,10},{9,11},{10,... | collective-permute-start | bytes 811016 | tf_op jit(solution)/shard_map/ppermute | solution.py:41
  31.3 3.5 %collective-permute-start.7 = (bf16[264,256]{1,0:T(8,128)(2,1)S(1)}, bf16[264,256]{1,0:T(8,128)(2,1)S(1)}, u32[]{:S(2)}, u32[]{:S(2)}) collective-permute-start(bf16[264,256]{1,0:T(8,128)(2,1)S(1)} %combine.25.refs_4_), channel_id=1, source_target_pairs={{0,4},{4,0},{8,12},{12,8},{1,5},{5,1},{9,13},{13,9},{2,6},{6,2},{1... | collective-permute-start | bytes 405512 | tf_op jit(solution)/shard_map/ppermute | solution.py:41
  31.4 3.6 %collective-permute-start.10 = (bf16[264,256]{1,0:T(8,128)(2,1)S(1)}, bf16[264,256]{1,0:T(8,128)(2,1)S(1)}, u32[]{:S(2)}, u32[]{:S(2)}) collective-permute-start(bf16[264,256]{1,0:T(8,128)(2,1)S(1)} %combine.23.refs_4_), channel_id=1, source_target_pairs={{0,4},{4,0},{8,12},{12,8},{1,5},{5,1},{9,13},{13,9},{2,6},{6,2},{1... | collective-permute-start | bytes 405512 | tf_op jit(solution)/shard_map/ppermute | solution.py:41
  31.9 19.7 %collective-permute-start.4 = (bf16[264,512]{1,0:T(8,128)(2,1)S(1)}, bf16[264,512]{1,0:T(8,128)(2,1)S(1)}, u32[]{:S(2)}, u32[]{:S(2)}) collective-permute-start(bf16[264,512]{1,0:T(8,128)(2,1)S(1)} %get-tuple-element.31.refs_2_), channel_id=1, source_target_pairs={{0,1},{1,0},{2,3},{3,2},{4,5},{5,4},{6,7},{7,6},{8,9},{9,8},{10,11... | collective-permute-start | bytes 811016 | tf_op jit(solution)/shard_map/ppermute | solution.py:41
  43.7 10.0 %copy-start.2 = (bf16[256,2048]{1,0:T(8,128)(2,1)S(1)}, bf16[256,2048]{1,0:T(8,128)(2,1)}, u32[]{:S(2)}) copy-start(bf16[256,2048]{1,0:T(8,128)(2,1)} %refs_3_.23) | copy-start | bytes 3145732
  43.7 8.0 %collective-permute-start.12 = (bf16[264,512]{1,0:T(8,128)(2,1)S(1)}, bf16[264,512]{1,0:T(8,128)(2,1)S(1)}, u32[]{:S(2)}, u32[]{:S(2)}) collective-permute-start(bf16[264,512]{1,0:T(8,128)(2,1)S(1)} %combine.28.refs_4_), channel_id=1, source_target_pairs={{0,4},{4,0},{8,12},{12,8},{1,5},{5,1},{9,13},{13,9},{2,6},{6,2},{1... | collective-permute-start | bytes 811016 | tf_op jit(solution)/shard_map/ppermute | solution.py:41
  43.8 14.9 %collective-permute-start.14 = (bf16[264,512]{1,0:T(8,128)(2,1)S(1)}, bf16[264,512]{1,0:T(8,128)(2,1)S(1)}, u32[]{:S(2)}, u32[]{:S(2)}) collective-permute-start(bf16[264,512]{1,0:T(8,128)(2,1)S(1)} %combine.24.refs_3_), channel_id=1, source_target_pairs={{0,2},{1,3},{2,0},{3,1},{4,6},{5,7},{6,4},{7,5},{8,10},{9,11},{10,... | collective-permute-start | bytes 811016 | tf_op jit(solution)/shard_map/ppermute | solution.py:41
  43.9 7.5 %collective-permute-start.8 = (bf16[264,256]{1,0:T(8,128)(2,1)S(1)}, bf16[264,256]{1,0:T(8,128)(2,1)S(1)}, u32[]{:S(2)}, u32[]{:S(2)}) collective-permute-start(bf16[264,256]{1,0:T(8,128)(2,1)S(1)} %combine.26.refs_4_), channel_id=1, source_target_pairs={{0,8},{4,12},{1,9},{5,13},{2,10},{6,14},{3,11},{7,15},{16,24},{20,... | collective-permute-start | bytes 405512 | tf_op jit(solution)/shard_map/ppermute | solution.py:41
  47.4 6.2 %collective-permute-start.15 = (bf16[264,256]{1,0:T(8,128)(2,1)S(1)}, bf16[264,256]{1,0:T(8,128)(2,1)S(1)}, u32[]{:S(2)}, u32[]{:S(2)}) collective-permute-start(bf16[264,256]{1,0:T(8,128)(2,1)S(1)} %combine.27.refs_3_), channel_id=1, source_target_pairs={{0,8},{4,12},{1,9},{5,13},{2,10},{6,14},{3,11},{7,15},{16,24},{20,... | collective-permute-start | bytes 405512 | tf_op jit(solution)/shard_map/ppermute | solution.py:41
  59.0 3.6 %collective-permute-start.16 = (bf16[264,512]{1,0:T(8,128)(2,1)S(1)}, bf16[264,512]{1,0:T(8,128)(2,1)S(1)}, u32[]{:S(2)}, u32[]{:S(2)}) collective-permute-start(bf16[264,512]{1,0:T(8,128)(2,1)S(1)} %combine.33.refs_4_), channel_id=1, source_target_pairs={{0,4},{4,0},{8,12},{12,8},{1,5},{5,1},{9,13},{13,9},{2,6},{6,2},{1... | collective-permute-start | bytes 811016 | tf_op jit(solution)/shard_map/ppermute | solution.py:41
  59.1 9.7 %collective-permute-start.13 = (bf16[264,512]{1,0:T(8,128)(2,1)S(1)}, bf16[264,512]{1,0:T(8,128)(2,1)S(1)}, u32[]{:S(2)}, u32[]{:S(2)}) collective-permute-start(bf16[264,512]{1,0:T(8,128)(2,1)S(1)} %combine.31.refs_4_), channel_id=1, source_target_pairs={{0,8},{4,12},{1,9},{5,13},{2,10},{6,14},{3,11},{7,15},{16,24},{20,... | collective-permute-start | bytes 811016 | tf_op jit(solution)/shard_map/ppermute | solution.py:41
  62.5 14.5 %collective-permute-start.11 = (bf16[264,512]{1,0:T(8,128)(2,1)S(1)}, bf16[264,512]{1,0:T(8,128)(2,1)S(1)}, u32[]{:S(2)}, u32[]{:S(2)}) collective-permute-start(bf16[264,512]{1,0:T(8,128)(2,1)S(1)} %combine.30.refs_4_), channel_id=1, source_target_pairs={{0,2},{1,3},{2,0},{3,1},{4,6},{5,7},{6,4},{7,5},{8,10},{9,11},{10,... | collective-permute-start | bytes 811016 | tf_op jit(solution)/shard_map/ppermute | solution.py:41
  77.2 1.8 %collective-permute-start.17 = (bf16[264,512]{1,0:T(8,128)(2,1)S(1)}, bf16[264,512]{1,0:T(8,128)(2,1)S(1)}, u32[]{:S(2)}, u32[]{:S(2)}) collective-permute-start(bf16[264,512]{1,0:T(8,128)(2,1)S(1)} %combine.36.refs_4_), channel_id=1, source_target_pairs={{0,4},{4,0},{8,12},{12,8},{1,5},{5,1},{9,13},{13,9},{2,6},{6,2},{1... | collective-permute-start | bytes 811016 | tf_op jit(solution)/shard_map/ppermute | solution.py:41
  77.3 8.4 %collective-permute-start.22 = (bf16[264,512]{1,0:T(8,128)(2,1)S(1)}, bf16[264,512]{1,0:T(8,128)(2,1)S(1)}, u32[]{:S(2)}, u32[]{:S(2)}) collective-permute-start(bf16[264,512]{1,0:T(8,128)(2,1)S(1)} %combine.34.refs_10_), channel_id=1, source_target_pairs={{0,8},{4,12},{1,9},{5,13},{2,10},{6,14},{3,11},{7,15},{16,24},{20,... | collective-permute-start | bytes 811016 | tf_op jit(solution)/shard_map/ppermute | solution.py:41
  78.9 15.9 %collective-permute-start.19 = (bf16[264,512]{1,0:T(8,128)(2,1)S(1)}, bf16[264,512]{1,0:T(8,128)(2,1)S(1)}, u32[]{:S(2)}, u32[]{:S(2)}) collective-permute-start(bf16[264,512]{1,0:T(8,128)(2,1)S(1)} %combine.35.refs_3_), channel_id=1, source_target_pairs={{0,1},{1,0},{2,3},{3,2},{4,5},{5,4},{6,7},{7,6},{8,9},{9,8},{10,11... | collective-permute-start | bytes 811016 | tf_op jit(solution)/shard_map/ppermute | solution.py:41
  79.3 16.2 %collective-permute-start.18 = (bf16[264,512]{1,0:T(8,128)(2,1)S(1)}, bf16[264,512]{1,0:T(8,128)(2,1)S(1)}, u32[]{:S(2)}, u32[]{:S(2)}) collective-permute-start(bf16[264,512]{1,0:T(8,128)(2,1)S(1)} %combine.37.refs_4_), channel_id=1, source_target_pairs={{0,8},{4,12},{1,9},{5,13},{2,10},{6,14},{3,11},{7,15},{16,24},{20,... | collective-permute-start | bytes 811016 | tf_op jit(solution)/shard_map/ppermute | solution.py:41
  80.9 10.4 %collective-permute-start.20 = (bf16[264,256]{1,0:T(8,128)(2,1)S(1)}, bf16[264,256]{1,0:T(8,128)(2,1)S(1)}, u32[]{:S(2)}, u32[]{:S(2)}) collective-permute-start(bf16[264,256]{1,0:T(8,128)(2,1)S(1)} %combine.29.refs_2_), channel_id=1, source_target_pairs={{0,1},{1,0},{2,3},{3,2},{4,5},{5,4},{6,7},{7,6},{8,9},{9,8},{10,11... | collective-permute-start | bytes 405512 | tf_op jit(solution)/shard_map/ppermute | solution.py:41
  82.8 11.3 %collective-permute-start.21 = (bf16[264,256]{1,0:T(8,128)(2,1)S(1)}, bf16[264,256]{1,0:T(8,128)(2,1)S(1)}, u32[]{:S(2)}, u32[]{:S(2)}) collective-permute-start(bf16[264,256]{1,0:T(8,128)(2,1)S(1)} %combine.32.refs_14_), channel_id=1, source_target_pairs={{0,1},{1,0},{2,3},{3,2},{4,5},{5,4},{6,7},{7,6},{8,9},{9,8},{10,11... | collective-permute-start | bytes 405512 | tf_op jit(solution)/shard_map/ppermute | solution.py:41
  86.0 13.9 %collective-permute-start.24 = (bf16[264,512]{1,0:T(8,128)(2,1)S(1)}, bf16[264,512]{1,0:T(8,128)(2,1)S(1)}, u32[]{:S(2)}, u32[]{:S(2)}) collective-permute-start(bf16[264,512]{1,0:T(8,128)(2,1)S(1)} %combine.38.refs_8_), channel_id=1, source_target_pairs={{0,1},{1,0},{2,3},{3,2},{4,5},{5,4},{6,7},{7,6},{8,9},{9,8},{10,11... | collective-permute-start | bytes 811016 | tf_op jit(solution)/shard_map/ppermute | solution.py:41
  95.7 9.2 %collective-permute-start.23 = (bf16[264,512]{1,0:T(8,128)(2,1)S(1)}, bf16[264,512]{1,0:T(8,128)(2,1)S(1)}, u32[]{:S(2)}, u32[]{:S(2)}) collective-permute-start(bf16[264,512]{1,0:T(8,128)(2,1)S(1)} %combine.39.refs_10_), channel_id=1, source_target_pairs={{0,1},{1,0},{2,3},{3,2},{4,5},{5,4},{6,7},{7,6},{8,9},{9,8},{10,11... | collective-permute-start | bytes 811016 | tf_op jit(solution)/shard_map/ppermute | solution.py:41

commit v8 on v7

--- a/solution.py
+++ b/solution.py
@@ -14,7 +14,7 @@
 BLK = 128
 NEG_FILL = -1e30
 TAIL = 8
-ROWS = DK + TAIL
+BLOCK = DK
 CHUNKS = ((0, 0, DV // 2), (0, DV // 2, DV // 2), (1, 0, DV), (2, 0, DV), (3, 0, DV))
 ORDER = (
     (0, 0), (0, 1), (0, 2), (1, 0), (1, 1), (0, 3), (1, 2), (2, 1), (0, 4), (1, 3), (2, 0), (3, 0), (3, 1), (2, 2),
@@ -46,7 +46,17 @@
     return at, 9 * blocks + 2
 
 
-def gate_kernel(i_ref, f_ref, scales, tensors, offsets, fbits, run_ref, weight_ref, shift_ref, table_ref, rows_ref):
+def gate_kernel(
+    first, i_ref, f_ref, scales, tensors, offsets, fbits, k_hbm, v_hbm,
+    run_ref, weight_ref, shift_ref, table_ref, keep_ref, send_ref, rows_ref, k_ref, v_ref, sems,
+):
+    pair, lo, _ = first
+    reads = [
+        pltpu.make_async_copy(k_hbm.at[:, pl.ds(2 * pair * DK, 2 * DK)], k_ref, sems.at[0]),
+        pltpu.make_async_copy(v_hbm.at[:, pl.ds(2 * pair * DV, 2 * DV)], v_ref, sems.at[1]),
+    ]
+    for copy in reads:
+        copy.start()
     gate, x = i_ref[...], f_ref[...].astype(F32)
     log_forget = jnp.minimum(x, 0.0) - jnp.log1p(jnp.exp(-jnp.abs(x)))
     size = x.shape[1]
@@ -78,21 +88,36 @@
     rows_ref[at["peak"] :, :] = jnp.concatenate([peak, total], axis=0)
     for h in range(table_ref.shape[0]):
         table_ref[h] = jnp.broadcast_to(rows_ref[:, h : h + 1], table_ref.shape[1:])
-
-
-def gates(input_gate, forget_gate, small):
+    for copy in reads:
+        copy.wait()
+    state_kernel(pair, lo, 2 * pair, table_ref, weight_ref, k_ref, v_ref, keep_ref, send_ref)
+
+
+def gates(input_gate, forget_gate, small, key_codes, value_codes):
     heads, size = input_gate.shape
     col = jax.ShapeDtypeStruct((size, heads), F32)
     row = jax.ShapeDtypeStruct((heads, size), F32)
     rows = table_rows(small[1].shape[0])[1]
+    state = state_shape(CHUNKS[ORDER[0][1]])
     return pl.pallas_call(
-        gate_kernel,
-        out_shape=(col, col, row, jax.ShapeDtypeStruct((heads, rows, 128), F32)),
-        scratch_shapes=[pltpu.VMEM((rows, heads), F32)],
-        compiler_params=pltpu.CompilerParams(vmem_limit_bytes=4 << 20),
-        cost_estimate=pl.CostEstimate(flops=1 << 20, bytes_accessed=1 << 20, transcendentals=0),
+        functools.partial(gate_kernel, CHUNKS[ORDER[0][1]]),
+        in_specs=[VMEM] * (2 + len(small)) + [pl.BlockSpec(memory_space=pl.ANY)] * 2,
+        out_specs=(VMEM,) * 6,
+        out_shape=(col, col, row, jax.ShapeDtypeStruct((heads, rows, 128), F32), state, state),
+        scratch_shapes=[
+            pltpu.VMEM((rows, heads), F32),
+            pltpu.VMEM((size, 2 * DK), BF16),
+            pltpu.VMEM((size, 2 * DV), BF16),
+            pltpu.SemaphoreType.DMA((2,)),
+        ],
+        compiler_params=pltpu.CompilerParams(vmem_limit_bytes=8 << 20),
+        cost_estimate=pl.CostEstimate(flops=1 << 27, bytes_accessed=1 << 20, transcendentals=0),
         name="gates",
-    )(input_gate, forget_gate, *small)
+    )(in_hbm(input_gate), in_hbm(forget_gate), *small, in_hbm(key_codes), in_hbm(value_codes))
+
+
+def state_shape(chunk):
+    return jax.ShapeDtypeStruct((chunk[2] // BLOCK * DK + TAIL, BLOCK), BF16)
 
 
 def pick(ref, h):
@@ -133,12 +158,9 @@
 
 
 def pack_tail(normer, peak, total):
-    width = peak.shape[1]
-    blank = jnp.zeros((1, width - DK), F32)
-    rows = [jnp.concatenate([x, blank], axis=1) if width > DK else x for x in split(normer)[:2]]
-    rows += [*split(peak), *split(total)]
-    at = lax.broadcasted_iota(jnp.int32, (TAIL, width), 0)
-    out = jnp.zeros((TAIL, width), F32)
+    rows = [*split(normer)[:2], *split(peak), *split(total)]
+    at = lax.broadcasted_iota(jnp.int32, (TAIL, BLOCK), 0)
+    out = jnp.zeros((TAIL, BLOCK), F32)
     for r, value in enumerate(rows):
         out = jnp.where(at == r, value, out)
     return out.astype(BF16)
@@ -147,13 +169,13 @@
 class State:
     def __init__(self, ref):
         self.ref = ref
-        t = ref[DK:ROWS, :].astype(F32)
-        self.normer = t[0:1, :DK] + t[1:2, :DK]
+        t = ref[-TAIL:, :].astype(F32)
+        self.normer = t[0:1] + t[1:2]
         self.peak = t[2:3] + t[3:4] + t[4:5]
         self.total = t[5:6] + t[6:7] + t[7:8]
 
     def matrix(self):
-        return self.ref[:DK, :]
+        return self.ref[:-TAIL, :]
 
 
 def joined(early, late):
@@ -189,7 +211,7 @@
 def weighted_sum(weights, states):
     matrix, normer = None, None
     for w, state in zip(weights, states):
-        term, tail = state.matrix().astype(F32) * w, state.normer * w[:, :DK]
+        term, tail = state.matrix().astype(F32) * w, state.normer * w
         matrix = term if matrix is None else matrix + term
         normer = tail if normer is None else normer + tail
     return matrix, normer
@@ -221,42 +243,31 @@
 
 def state_kernel(pair, lo, at, table_ref, weight_ref, k_ref, v_ref, keep_ref, send_ref):
     own = lax.axis_index("head") & 1
-    width = keep_ref.shape[1]
+    width = (keep_ref.shape[0] - TAIL) // DK * BLOCK
     peak_row = table_rows(k_ref.shape[0] // BLK)[0]["peak"]
     for out_ref, side in ((send_ref, 1 - own), (keep_ref, own)):
         h = 2 * pair + side
         table = table_ref.at[h]
-        k = dequant(k_ref, pl.multiple_of((at + side) * DK, DK), 0, DK, DK, 1, table[...])
-        v = dequant(v_ref, pl.multiple_of((at + side) * DV, DV), lo, width, DV, 2, table[...])
+        k = dequant(k_ref, pl.multiple_of((h - at) * DK, DK), 0, DK, DK, 1, table[...])
+        v = dequant(v_ref, pl.multiple_of((h - at) * DV, DV), lo, width, DV, 2, table[...])
         weighted = (k.astype(F32) * pick(weight_ref, h)).astype(BF16)
         matrix = lax.dot_general(weighted, v, (((0,), (0,)), ((), ())), preferred_element_type=F32)
-        out_ref[:DK, :] = matrix.astype(BF16)
+        for c in range(width // BLOCK):
+            out_ref[c * DK : (c + 1) * DK, :] = matrix[:, c * BLOCK : (c + 1) * BLOCK].astype(BF16)
         normer = jnp.sum(weighted.astype(F32), axis=0, keepdims=True)
-        peak = across(table[peak_row : peak_row + 1, :], width)
-        total = across(table[peak_row + 1 : peak_row + 2, :], width)
-        out_ref[DK:ROWS, :] = pack_tail(normer, peak, total)
+        peak = across(table[peak_row : peak_row + 1, :], BLOCK)
+        total = across(table[peak_row + 1 : peak_row + 2, :], BLOCK)
+        out_ref[-TAIL:, :] = pack_tail(normer, peak, total)
 
 
 def span_states(chunk, table, weight, key_codes, value_codes, after):
     pair, lo, width = chunk
     rows = key_codes.shape[0]
-    out = jax.ShapeDtypeStruct((ROWS, width), BF16)
-    if after is None:
-        at = 0
-        spec = dict(
-            grid=(1,),
-            in_specs=[VMEM, VMEM]
-            + [pl.BlockSpec((rows, 2 * DK), lambda i: (0, pair)), pl.BlockSpec((rows, 2 * DV), lambda i: (0, pair))],
-        )
-        key_codes, value_codes = in_hbm(key_codes), in_hbm(value_codes)
-    else:
-        at = 2 * pair
-        spec = dict(in_specs=[VMEM] * 4)
-    kernel, extra, extra_specs = ordered(functools.partial(state_kernel, pair, lo, at), 4, after)
-    spec["in_specs"] += extra_specs
+    out = state_shape(chunk)
+    kernel, extra, extra_specs = ordered(functools.partial(state_kernel, pair, lo, 0), 4, after)
     return pl.pallas_call(
         kernel,
-        **spec,
+        in_specs=[VMEM] * 4 + extra_specs,
         out_specs=(VMEM,) * 2,
         out_shape=(out, out),
         compiler_params=pltpu.CompilerParams(vmem_limit_bytes=12 << 20),
@@ -276,8 +287,8 @@
     else:
         weights, peak, total = group_weights(bit, states[0], states[1:])
     matrix, normer = weighted_sum(weights, states)
-    out_ref[:DK, :] = matrix.astype(BF16)
-    out_ref[DK:ROWS, :] = pack_tail(normer, peak, total)
+    out_ref[:-TAIL, :] = matrix.astype(BF16)
+    out_ref[-TAIL:, :] = pack_tail(normer, peak, total)
 
 
 def combine(head_bits, bits, last, parts, after):
@@ -326,11 +337,11 @@
         if mine:
             weights, peak, _ = start_weights(bit, None, None, states)
             start, normer = weighted_sum(weights, states)
-            starts.append(start.astype(BF16))
+            start = start.astype(BF16)
         else:
-            normer, peak = states[0].normer, states[0].peak
-            starts.append(states[0].matrix())
-    start = jnp.concatenate(starts, axis=1) if pieces > 1 else starts[0]
+            start, normer, peak = states[0].matrix(), states[0].normer, states[0].peak
+        starts += [start[c : c + DK] for c in range(0, start.shape[0], DK)]
+    start = jnp.concatenate(starts, axis=1)
     q = dequant(q_ref, narrow, 0, DK, DK, 0, table[...])
     k = dequant(k_ref, narrow, 0, DK, DK, 1, table[...])
     v = dequant(v_ref, wide, 0, DV, DV, 2, table[...])
@@ -353,12 +364,15 @@
             copy.wait()
 
 
-def span_outputs(head_bits, bits, pair, mine, table, run, shift, codes, groups, done, earlier, after):
+def span_outputs(head_bits, bits, pair, mine, table, run, shift, codes, groups, done, earlier, out, after):
     rows, width = codes[2].shape
     operands = [table, run, shift, *codes, *[x for group in groups for x in group], *earlier]
     in_specs = [VMEM] * len(operands)
     kernel = functools.partial(output_kernel, head_bits, bits, pair, mine, len(groups), done)
-    kernel, extra, extra_specs = ordered(kernel, len(operands), after)
+    for x in (after, out):
+        kernel, extra, extra_specs = ordered(kernel, len(operands), x)
+        operands += extra
+        in_specs += extra_specs
     result = jax.ShapeDtypeStruct((rows, DV), BF16)
     if done is None:
         outs = dict(out_specs=VMEM, out_shape=result)
@@ -367,10 +381,11 @@
             out_specs=pl.BlockSpec(memory_space=pl.ANY),
             out_shape=jax.ShapeDtypeStruct((rows, width), BF16),
             scratch_shapes=[pltpu.VMEM(result.shape, BF16), pltpu.SemaphoreType.DMA((len(done) + 1,))],
+            input_output_aliases={} if out is None else {len(operands) - 1: 0},
         )
     return pl.pallas_call(
         kernel,
-        in_specs=in_specs + extra_specs,
+        in_specs=in_specs,
         **outs,
         compiler_params=pltpu.CompilerParams(vmem_limit_bytes=12 << 20),
         cost_estimate=pl.CostEstimate(
@@ -379,7 +394,7 @@
             transcendentals=rows * rows,
         ),
         name="span_outputs",
-    )(*operands, *extra)
+    )(*operands)
 
 
 def body(
@@ -401,11 +416,14 @@
     small = tuple(in_hbm(x) for x in (block_scales.transpose(1, 0, 2), fault_tensor, fault_offset, fault_bit))
     codes = (query_codes, key_codes, value_codes)
     exchange = functools.partial(flip, head_bits=head_bits, ctx_bits=ctx_bits)
-    run, weight, shift, table = gates(in_hbm(input_gate.T), in_hbm(forget_gate.T), small)
     keep, got, back = {}, {}, {}
-    results, token = {}, None
+    results, out, token = {}, None, None
     for stage, c in order(bits):
-        if stage == 0:
+        if not keep:
+            run, weight, shift, table, keep[c], token = gates(
+                input_gate.T, forget_gate.T, small, key_codes, value_codes
+            )
+        elif stage == 0:
             keep[c], token = span_states(CHUNKS[c], table, weight, key_codes, value_codes, token)
         elif stage < bits:
             token = combine(head_bits, bits, False, [keep[c], *got[c]], token)
@@ -414,17 +432,17 @@
         else:
             mine = stage == bits + 1
             groups = [got[d] if mine else [back[d]] for d in of_pair(c)]
-            final = len(results) == input_gate.shape[1] - 1
-            token = span_outputs(
-                head_bits, bits, c, mine, table, run, shift, codes, groups,
-                tuple(results) if final else None, results.values() if final else (), token,
-            )
+            left = input_gate.shape[1] - len(results)
+            done = tuple(results) if left == 2 else () if left == 1 else None
+            earlier = results.values() if left == 2 else ()
+            token = span_outputs(head_bits, bits, c, mine, table, run, shift, codes, groups, done, earlier, out, token)
             results[c, mine] = token
+            out, token = (token, None) if done is not None else (None, token)
         if stage < bits:
             got.setdefault(c, []).append(exchange(token, stage, last=stage == bits - 1))
         elif stage == bits:
             back[c] = exchange(token, 0, last=False)
-    return token
+    return out
 
 
 def of_pair(pair):

time: 107 us -> 105 us (0.981)
  waiting for transfers between devices: 59.4 us -> 56.2 us
  starting transfers between devices: 30.2 us -> 31.7 us
    ppermute x25, waiting for transfers between devices: 59.4 us -> 56.2 us  [flip(): return lax.ppermute(x, axis, pairs)]
    ppermute x25, starting transfers between devices: 30.2 us -> 31.7 us  [flip(): return lax.ppermute(x, axis, pairs)]
    pallas_call x14 -> x13, Pallas kernels: 13.1 us -> 13.5 us  [the longest x8 7.73 us: span_outputs(): pl.pallas_call(kernel, in_specs=in_specs, **outs, compiler_params=pltpu.C...]
  transfers between devices with their start and end apart: 25 -> 25, of which waited for: 16 -> 15; matrix products, arithmetic and copies ran while one was open for 0% -> 0% of each run, Pallas kernels for 11% -> 11%
where the time goes in v8:
time: 105 us
  waiting for transfers between devices  56.2 us (54%)
  starting transfers between devices  31.7 us (30%)
  Pallas kernels  16.9 us (16%)
    ppermute x25, waiting for transfers between devices, flip(): return lax.ppermute(x, axis, pairs)  56.2 us
    ppermute x25, starting transfers between devices, flip(): return lax.ppermute(x, axis, pairs)  31.7 us
    pallas_call x8, Pallas kernels, span_outputs(): pl.pallas_call(kernel, in_specs=in_specs, **outs, compiler_params=pltpu.C...  7.73 us
    pallas_call x20, Pallas kernels, combine(): pl.pallas_call(kernel, in_specs=[VMEM] * len(parts) + extra_specs, out_sp...  3.43 us
    pallas_call x1, Pallas kernels, gates(): pl.pallas_call(functools.partial(gate_kernel, CHUNKS[ORDER[0][1]]), in_sp...  3.14 us
    pallas_call x4, Pallas kernels, span_states(): pl.pallas_call(kernel, in_specs=[VMEM] * 4 + extra_specs, out_specs=(VMEM...  2.59 us
  transfers between devices with their start and end apart: 25, of which 15 were waited for; matrix products, arithmetic and copies ran while one was open for 0% of the time, Pallas kernels for 11%

profile of v8, /device:TPU:0, one launch (start us, length us, event | category | flops | bytes accessed | tf_op | source)
XLA Modules:
  0.0 105.2 jit_solution(3889533390692706927)
XLA Ops:
  0.0 3.1 %gates.1 = (f32[256,8]{1,0:T(8,128)S(1)}, f32[256,8]{1,0:T(8,128)S(1)}, f32[8,256]{1,0:T(8,128)S(1)}, f32[8,20,128]{2,1,0:T(8,128)S(1)}, bf16[264,256]{1,0:T(8,128)(2,1)S(1)}, /*index=5*/bf16[264,256]{1,0:T(8,128)(2,1)S(1)}) custom-call(bf16[8,256]{1,0:T(8,128)(2,1)} %bitcast.3, bf16[8,256]{1,0:T(8,128)(2,1)} %bitcast.4, f32[3,2,8]{2,1,0:T(2,128)} %bitcast.5, ...), custom_call_target="tpu_custom_call" | custom-call | flops 134217728 | bytes 1048576 | tf_op jit(solution)/shard_map/gates/pallas_call | solution.py:102
  3.1 3.1 %collective-permute-start.1 = (bf16[264,256]{1,0:T(8,128)(2,1)S(1)}, bf16[264,256]{1,0:T(8,128)(2,1)S(1)}, u32[]{:S(2)}, u32[]{:S(2)}) collective-permute-start(bf16[264,256]{1,0:T(8,128)(2,1)S(1)} %get-tuple-element.23.refs_4_), channel_id=1, source_target_pairs={{0,1},{1,0},{2,3},{3,2},{4,5},{5,4},{6,7},{7,6},{8,9},{9,8},{10,11... | collective-permute-start | bytes 405512 | tf_op jit(solution)/shard_map/ppermute | solution.py:41
  6.3 0.6 span_states.4
  6.9 0.7 span_states.5
  7.6 2.1 %collective-permute-start.3 = (bf16[520,256]{1,0:T(8,128)(2,1)S(1)}, bf16[520,256]{1,0:T(8,128)(2,1)S(1)}, u32[]{:S(2)}, u32[]{:S(2)}) collective-permute-start(bf16[520,256]{1,0:T(8,128)(2,1)S(1)} %get-tuple-element.27.refs_2_), channel_id=1, source_target_pairs={{0,1},{1,0},{2,3},{3,2},{4,5},{5,4},{6,7},{7,6},{8,9},{9,8},{10,11... | collective-permute-start | bytes 798728 | tf_op jit(solution)/shard_map/ppermute | solution.py:41
  9.7 1.0 collective-permute-done.1.refs_1_.refs_6_
  10.7 2.8 %collective-permute-done.refs_1_.refs_10_ = bf16[264,256]{1,0:T(8,128)(2,1)S(1)} collective-permute-done((bf16[264,256]{1,0:T(8,128)(2,1)S(1)}, bf16[264,256]{1,0:T(8,128)(2,1)S(1)}, u32[]{:S(2)}, u32[]{:S(2)}) %collective-permute-start) | collective-permute-done | bytes 135200 | tf_op jit(solution)/shard_map/ppermute | solution.py:41
  13.6 0.7 span_states.6
  14.3 2.2 %collective-permute-start.6 = (bf16[520,256]{1,0:T(8,128)(2,1)S(1)}, bf16[520,256]{1,0:T(8,128)(2,1)S(1)}, u32[]{:S(2)}, u32[]{:S(2)}) collective-permute-start(bf16[520,256]{1,0:T(8,128)(2,1)S(1)} %get-tuple-element.29.refs_2_), channel_id=1, source_target_pairs={{0,1},{1,0},{2,3},{3,2},{4,5},{5,4},{6,7},{7,6},{8,9},{9,8},{10,11... | collective-permute-start | bytes 798728 | tf_op jit(solution)/shard_map/ppermute | solution.py:41
  16.5 2.6 %collective-permute-start.2 = (bf16[264,256]{1,0:T(8,128)(2,1)S(1)}, bf16[264,256]{1,0:T(8,128)(2,1)S(1)}, u32[]{:S(2)}, u32[]{:S(2)}) collective-permute-start(bf16[264,256]{1,0:T(8,128)(2,1)S(1)} %combine.21.refs_4_), channel_id=1, source_target_pairs={{0,2},{1,3},{2,0},{3,1},{4,6},{5,7},{6,4},{7,5},{8,10},{9,11},{10,... | collective-permute-start | bytes 405512 | tf_op jit(solution)/shard_map/ppermute | solution.py:41
  19.0 0.3 collective-permute-start.5
  19.4 4.2 %collective-permute-done.3.refs_1_.refs_6_ = bf16[520,256]{1,0:T(8,128)(2,1)S(1)} collective-permute-done((bf16[520,256]{1,0:T(8,128)(2,1)S(1)}, bf16[520,256]{1,0:T(8,128)(2,1)S(1)}, u32[]{:S(2)}, u32[]{:S(2)}) %collective-permute-start.3) | collective-permute-done | bytes 266272 | tf_op jit(solution)/shard_map/ppermute | solution.py:41
  23.7 3.7 %collective-permute-start.9 = (bf16[520,256]{1,0:T(8,128)(2,1)S(1)}, bf16[520,256]{1,0:T(8,128)(2,1)S(1)}, u32[]{:S(2)}, u32[]{:S(2)}) collective-permute-start(bf16[520,256]{1,0:T(8,128)(2,1)S(1)} %combine.22.refs_3_), channel_id=1, source_target_pairs={{0,2},{1,3},{2,0},{3,1},{4,6},{5,7},{6,4},{7,5},{8,10},{9,11},{10,... | collective-permute-start | bytes 798728 | tf_op jit(solution)/shard_map/ppermute | solution.py:41
  27.6 0.7 span_states.7
  28.3 2.5 %collective-permute-done.6.refs_1_.refs_6_ = bf16[520,256]{1,0:T(8,128)(2,1)S(1)} collective-permute-done((bf16[520,256]{1,0:T(8,128)(2,1)S(1)}, bf16[520,256]{1,0:T(8,128)(2,1)S(1)}, u32[]{:S(2)}, u32[]{:S(2)}) %collective-permute-start.6) | collective-permute-done | bytes 266272 | tf_op jit(solution)/shard_map/ppermute | solution.py:41
  31.1 0.5 collective-permute-start.10
  31.6 2.9 %collective-permute-start.4 = (bf16[520,256]{1,0:T(8,128)(2,1)S(1)}, bf16[520,256]{1,0:T(8,128)(2,1)S(1)}, u32[]{:S(2)}, u32[]{:S(2)}) collective-permute-start(bf16[520,256]{1,0:T(8,128)(2,1)S(1)} %get-tuple-element.31.refs_2_), channel_id=1, source_target_pairs={{0,1},{1,0},{2,3},{3,2},{4,5},{5,4},{6,7},{7,6},{8,9},{9,8},{10,11... | collective-permute-start | bytes 798728 | tf_op jit(solution)/shard_map/ppermute | solution.py:41
  34.8 8.2 %collective-permute-done.9.refs_2_.refs_7_.refs_1_ = bf16[520,256]{1,0:T(8,128)(2,1)S(1)} collective-permute-done((bf16[520,256]{1,0:T(8,128)(2,1)S(1)}, bf16[520,256]{1,0:T(8,128)(2,1)S(1)}, u32[]{:S(2)}, u32[]{:S(2)}) %collective-permute-start.9) | collective-permute-done | bytes 266272 | tf_op jit(solution)/shard_map/ppermute | solution.py:41
  43.4 3.5 %collective-permute-start.8 = (bf16[264,256]{1,0:T(8,128)(2,1)S(1)}, bf16[264,256]{1,0:T(8,128)(2,1)S(1)}, u32[]{:S(2)}, u32[]{:S(2)}) collective-permute-start(bf16[264,256]{1,0:T(8,128)(2,1)S(1)} %combine.26.refs_4_), channel_id=1, source_target_pairs={{0,8},{4,12},{1,9},{5,13},{2,10},{6,14},{3,11},{7,15},{16,24},{20,... | collective-permute-start | bytes 405512 | tf_op jit(solution)/shard_map/ppermute | solution.py:41
  46.9 1.3 %collective-permute-start.15 = (bf16[264,256]{1,0:T(8,128)(2,1)S(1)}, bf16[264,256]{1,0:T(8,128)(2,1)S(1)}, u32[]{:S(2)}, u32[]{:S(2)}) collective-permute-start(bf16[264,256]{1,0:T(8,128)(2,1)S(1)} %combine.27.refs_3_), channel_id=1, source_target_pairs={{0,8},{4,12},{1,9},{5,13},{2,10},{6,14},{3,11},{7,15},{16,24},{20,... | collective-permute-start | bytes 405512 | tf_op jit(solution)/shard_map/ppermute | solution.py:41
  48.2 2.6 %collective-permute-done.8.refs_3_.refs_9_ = bf16[264,256]{1,0:T(8,128)(2,1)S(1)} collective-permute-done((bf16[264,256]{1,0:T(8,128)(2,1)S(1)}, bf16[264,256]{1,0:T(8,128)(2,1)S(1)}, u32[]{:S(2)}, u32[]{:S(2)}) %collective-permute-start.8) | collective-permute-done | bytes 135200 | tf_op jit(solution)/shard_map/ppermute | solution.py:41
  51.2 0.2 combine.31.refs_4_
  51.4 1.6 %collective-permute-done.15.refs_3_.refs_13_ = bf16[264,256]{1,0:T(8,128)(2,1)S(1)} collective-permute-done((bf16[264,256]{1,0:T(8,128)(2,1)S(1)}, bf16[264,256]{1,0:T(8,128)(2,1)S(1)}, u32[]{:S(2)}, u32[]{:S(2)}) %collective-permute-start.15) | collective-permute-done | bytes 135200 | tf_op jit(solution)/shard_map/ppermute | solution.py:41
  53.2 0.9 span_outputs.8.refs_3_.refs_10_
  54.1 4.0 %collective-permute-done.14.refs_2_.refs_1_.refs_7_ = bf16[520,256]{1,0:T(8,128)(2,1)S(1)} collective-permute-done((bf16[520,256]{1,0:T(8,128)(2,1)S(1)}, bf16[520,256]{1,0:T(8,128)(2,1)S(1)}, u32[]{:S(2)}, u32[]{:S(2)}) %collective-permute-start.14) | collective-permute-done | bytes 266272 | tf_op jit(solution)/shard_map/ppermute | solution.py:41
  58.4 3.4 %collective-permute-start.13 = (bf16[520,256]{1,0:T(8,128)(2,1)S(1)}, bf16[520,256]{1,0:T(8,128)(2,1)S(1)}, u32[]{:S(2)}, u32[]{:S(2)}) collective-permute-start(bf16[520,256]{1,0:T(8,128)(2,1)S(1)} %combine.31.refs_4_), channel_id=1, source_target_pairs={{0,8},{4,12},{1,9},{5,13},{2,10},{6,14},{3,11},{7,15},{16,24},{20,... | collective-permute-start | bytes 798728 | tf_op jit(solution)/shard_map/ppermute | solution.py:41
  61.9 0.2 combine.34.refs_10_
  62.1 5.9 %collective-permute-done.13.refs_9_.refs_3_ = bf16[520,256]{1,0:T(8,128)(2,1)S(1)} collective-permute-done((bf16[520,256]{1,0:T(8,128)(2,1)S(1)}, bf16[520,256]{1,0:T(8,128)(2,1)S(1)}, u32[]{:S(2)}, u32[]{:S(2)}) %collective-permute-start.13) | collective-permute-done | bytes 266272 | tf_op jit(solution)/shard_map/ppermute | solution.py:41
  68.0 0.8 span_outputs.9.refs_4_.refs_11_
  68.9 0.2 combine.35.refs_3_
  69.1 7.0 %collective-permute-done.11.refs_2_.refs_1_.refs_7_ = bf16[520,256]{1,0:T(8,128)(2,1)S(1)} collective-permute-done((bf16[520,256]{1,0:T(8,128)(2,1)S(1)}, bf16[520,256]{1,0:T(8,128)(2,1)S(1)}, u32[]{:S(2)}, u32[]{:S(2)}) %collective-permute-start.11) | collective-permute-done | bytes 266272 | tf_op jit(solution)/shard_map/ppermute | solution.py:41
  76.4 1.6 %collective-permute-start.22 = (bf16[520,256]{1,0:T(8,128)(2,1)S(1)}, bf16[520,256]{1,0:T(8,128)(2,1)S(1)}, u32[]{:S(2)}, u32[]{:S(2)}) collective-permute-start(bf16[520,256]{1,0:T(8,128)(2,1)S(1)} %combine.34.refs_10_), channel_id=1, source_target_pairs={{0,8},{4,12},{1,9},{5,13},{2,10},{6,14},{3,11},{7,15},{16,24},{20,... | collective-permute-start | bytes 798728 | tf_op jit(solution)/shard_map/ppermute | solution.py:41
  78.1 0.2 combine.37.refs_4_
  78.3 1.6 %collective-permute-start.18 = (bf16[520,256]{1,0:T(8,128)(2,1)S(1)}, bf16[520,256]{1,0:T(8,128)(2,1)S(1)}, u32[]{:S(2)}, u32[]{:S(2)}) collective-permute-start(bf16[520,256]{1,0:T(8,128)(2,1)S(1)} %combine.37.refs_4_), channel_id=1, source_target_pairs={{0,8},{4,12},{1,9},{5,13},{2,10},{6,14},{3,11},{7,15},{16,24},{20,... | collective-permute-start | bytes 798728 | tf_op jit(solution)/shard_map/ppermute | solution.py:41
  79.9 2.0 %collective-permute-start.20 = (bf16[264,256]{1,0:T(8,128)(2,1)S(1)}, bf16[264,256]{1,0:T(8,128)(2,1)S(1)}, u32[]{:S(2)}, u32[]{:S(2)}) collective-permute-start(bf16[264,256]{1,0:T(8,128)(2,1)S(1)} %combine.29.refs_2_), channel_id=1, source_target_pairs={{0,1},{1,0},{2,3},{3,2},{4,5},{5,4},{6,7},{7,6},{8,9},{9,8},{10,11... | collective-permute-start | bytes 405512 | tf_op jit(solution)/shard_map/ppermute | solution.py:41
  82.0 2.7 %collective-permute-done.22.refs_3_.refs_9_ = bf16[520,256]{1,0:T(8,128)(2,1)S(1)} collective-permute-done((bf16[520,256]{1,0:T(8,128)(2,1)S(1)}, bf16[520,256]{1,0:T(8,128)(2,1)S(1)}, u32[]{:S(2)}, u32[]{:S(2)}) %collective-permute-start.22) | collective-permute-done | bytes 266272 | tf_op jit(solution)/shard_map/ppermute | solution.py:41
  84.7 0.2 combine.38.refs_8_
  85.0 5.2 %collective-permute-done.20.refs_6_ = bf16[264,256]{1,0:T(8,128)(2,1)S(1)} collective-permute-done((bf16[264,256]{1,0:T(8,128)(2,1)S(1)}, bf16[264,256]{1,0:T(8,128)(2,1)S(1)}, u32[]{:S(2)}, u32[]{:S(2)}) %collective-permute-start.20) | collective-permute-done | bytes 135200 | tf_op jit(solution)/shard_map/ppermute | solution.py:41
  90.2 2.9 %collective-permute-done.21.refs_7_ = bf16[264,256]{1,0:T(8,128)(2,1)S(1)} collective-permute-done((bf16[264,256]{1,0:T(8,128)(2,1)S(1)}, bf16[264,256]{1,0:T(8,128)(2,1)S(1)}, u32[]{:S(2)}, u32[]{:S(2)}) %collective-permute-start.21) | collective-permute-done | bytes 135200 | tf_op jit(solution)/shard_map/ppermute | solution.py:41
  93.1 0.6 span_outputs.10.refs_7_.refs_12_
  93.8 0.7 span_outputs.11.refs_4_.refs_13_
  94.4 0.3 combine.39.refs_10_
  94.8 0.8 span_outputs.12.refs_7_.refs_14_
  95.6 3.2 %collective-permute-done.24.refs_6_ = bf16[520,256]{1,0:T(8,128)(2,1)S(1)} collective-permute-done((bf16[520,256]{1,0:T(8,128)(2,1)S(1)}, bf16[520,256]{1,0:T(8,128)(2,1)S(1)}, u32[]{:S(2)}, u32[]{:S(2)}) %collective-permute-start.24) | collective-permute-done | bytes 266272 | tf_op jit(solution)/shard_map/ppermute | solution.py:41
  98.8 0.7 span_outputs.13.refs_15_.refs_16_
  99.5 1.9 %span_outputs.14.refs_7_ = bf16[256,4096]{1,0:T(8,128)(2,1)} custom-call(f32[8,20,128]{2,1,0:T(8,128)S(1)} %get-tuple-element.19.refs_0_, f32[256,8]{1,0:T(8,128)S(1)} %get-tuple-element.20.refs_1_, f32[8,256]{1,0:T(8,128)S(1)} %get-tuple-element.21.refs_2_, bf16[256,2048]{1,0:T(8,128)(2,1)S(1)} %copy-done.2, bf16[256,2048]{1,0:T(8,128)(2,1)S(1)} %copy-done.1, ...), custom_call_target="tpu_custom_call" | custom-call | flops 167772160 | bytes 786432 | tf_op jit(solution)/shard_map/span_outputs/pallas_call | solution.py:386
  101.3 2.4 %collective-permute-done.23.refs_6_ = bf16[520,256]{1,0:T(8,128)(2,1)S(1)} collective-permute-done((bf16[520,256]{1,0:T(8,128)(2,1)S(1)}, bf16[520,256]{1,0:T(8,128)(2,1)S(1)}, u32[]{:S(2)}, u32[]{:S(2)}) %collective-permute-start.23) | collective-permute-done | bytes 266272 | tf_op jit(solution)/shard_map/ppermute | solution.py:41
  103.7 1.4 %span_outputs.15 = bf16[256,4096]{1,0:T(8,128)(2,1)} custom-call(f32[8,20,128]{2,1,0:T(8,128)S(1)} %get-tuple-element.19.refs_0_, f32[256,8]{1,0:T(8,128)S(1)} %get-tuple-element.20.refs_1_, f32[8,256]{1,0:T(8,128)S(1)} %get-tuple-element.21.refs_2_, bf16[256,2048]{1,0:T(8,128)(2,1)S(1)} %copy-done.2, ...), custom_call_target="tpu_custom_call", output_to_operand_aliasing={{}: (7, {})} | custom-call | flops 167772160 | bytes 786432 | tf_op jit(solution)/shard_map/span_outputs/pallas_call | solution.py:386
  (41 shorter events, 2.9 us)
Async XLA Ops:
  0.0 6.3 %copy-start = (bf16[256,4096]{1,0:T(8,128)(2,1)S(1)}, bf16[256,4096]{1,0:T(8,128)(2,1)}, u32[]{:S(2)}) copy-start(bf16[256,4096]{1,0:T(8,128)(2,1)} %refs_5_.15) | copy-start | bytes 6291460
  0.0 6.3 %copy-start.1 = (bf16[256,2048]{1,0:T(8,128)(2,1)S(1)}, bf16[256,2048]{1,0:T(8,128)(2,1)}, u32[]{:S(2)}) copy-start(bf16[256,2048]{1,0:T(8,128)(2,1)} %refs_4_.15) | copy-start | bytes 3145732
  3.1 7.5 %collective-permute-start.1 = (bf16[264,256]{1,0:T(8,128)(2,1)S(1)}, bf16[264,256]{1,0:T(8,128)(2,1)S(1)}, u32[]{:S(2)}, u32[]{:S(2)}) collective-permute-start(bf16[264,256]{1,0:T(8,128)(2,1)S(1)} %get-tuple-element.23.refs_4_), channel_id=1, source_target_pairs={{0,1},{1,0},{2,3},{3,2},{4,5},{5,4},{6,7},{7,6},{8,9},{9,8},{10,11... | collective-permute-start | bytes 405512 | tf_op jit(solution)/shard_map/ppermute | solution.py:41
  6.8 6.7 %collective-permute-start = (bf16[264,256]{1,0:T(8,128)(2,1)S(1)}, bf16[264,256]{1,0:T(8,128)(2,1)S(1)}, u32[]{:S(2)}, u32[]{:S(2)}) collective-permute-start(bf16[264,256]{1,0:T(8,128)(2,1)S(1)} %get-tuple-element.25.refs_4_), channel_id=1, source_target_pairs={{0,1},{1,0},{2,3},{3,2},{4,5},{5,4},{6,7},{7,6},{8,9},{9,8},{10,11... | collective-permute-start | bytes 405512 | tf_op jit(solution)/shard_map/ppermute | solution.py:41
  7.6 16.0 %collective-permute-start.3 = (bf16[520,256]{1,0:T(8,128)(2,1)S(1)}, bf16[520,256]{1,0:T(8,128)(2,1)S(1)}, u32[]{:S(2)}, u32[]{:S(2)}) collective-permute-start(bf16[520,256]{1,0:T(8,128)(2,1)S(1)} %get-tuple-element.27.refs_2_), channel_id=1, source_target_pairs={{0,1},{1,0},{2,3},{3,2},{4,5},{5,4},{6,7},{7,6},{8,9},{9,8},{10,11... | collective-permute-start | bytes 798728 | tf_op jit(solution)/shard_map/ppermute | solution.py:41
  14.3 16.4 %collective-permute-start.6 = (bf16[520,256]{1,0:T(8,128)(2,1)S(1)}, bf16[520,256]{1,0:T(8,128)(2,1)S(1)}, u32[]{:S(2)}, u32[]{:S(2)}) collective-permute-start(bf16[520,256]{1,0:T(8,128)(2,1)S(1)} %get-tuple-element.29.refs_2_), channel_id=1, source_target_pairs={{0,1},{1,0},{2,3},{3,2},{4,5},{5,4},{6,7},{7,6},{8,9},{9,8},{10,11... | collective-permute-start | bytes 798728 | tf_op jit(solution)/shard_map/ppermute | solution.py:41
  16.5 11.0 %collective-permute-start.2 = (bf16[264,256]{1,0:T(8,128)(2,1)S(1)}, bf16[264,256]{1,0:T(8,128)(2,1)S(1)}, u32[]{:S(2)}, u32[]{:S(2)}) collective-permute-start(bf16[264,256]{1,0:T(8,128)(2,1)S(1)} %combine.21.refs_4_), channel_id=1, source_target_pairs={{0,2},{1,3},{2,0},{3,1},{4,6},{5,7},{6,4},{7,5},{8,10},{9,11},{10,... | collective-permute-start | bytes 405512 | tf_op jit(solution)/shard_map/ppermute | solution.py:41
  19.0 11.8 %collective-permute-start.5 = (bf16[264,256]{1,0:T(8,128)(2,1)S(1)}, bf16[264,256]{1,0:T(8,128)(2,1)S(1)}, u32[]{:S(2)}, u32[]{:S(2)}) collective-permute-start(bf16[264,256]{1,0:T(8,128)(2,1)S(1)} %combine.20.refs_2_), channel_id=1, source_target_pairs={{0,2},{1,3},{2,0},{3,1},{4,6},{5,7},{6,4},{7,5},{8,10},{9,11},{10,... | collective-permute-start | bytes 405512 | tf_op jit(solution)/shard_map/ppermute | solution.py:41
  23.7 19.2 %collective-permute-start.9 = (bf16[520,256]{1,0:T(8,128)(2,1)S(1)}, bf16[520,256]{1,0:T(8,128)(2,1)S(1)}, u32[]{:S(2)}, u32[]{:S(2)}) collective-permute-start(bf16[520,256]{1,0:T(8,128)(2,1)S(1)} %combine.22.refs_3_), channel_id=1, source_target_pairs={{0,2},{1,3},{2,0},{3,1},{4,6},{5,7},{6,4},{7,5},{8,10},{9,11},{10,... | collective-permute-start | bytes 798728 | tf_op jit(solution)/shard_map/ppermute | solution.py:41
  31.0 3.5 %collective-permute-start.7 = (bf16[264,256]{1,0:T(8,128)(2,1)S(1)}, bf16[264,256]{1,0:T(8,128)(2,1)S(1)}, u32[]{:S(2)}, u32[]{:S(2)}) collective-permute-start(bf16[264,256]{1,0:T(8,128)(2,1)S(1)} %combine.25.refs_4_), channel_id=1, source_target_pairs={{0,4},{4,0},{8,12},{12,8},{1,5},{5,1},{9,13},{13,9},{2,6},{6,2},{1... | collective-permute-start | bytes 405512 | tf_op jit(solution)/shard_map/ppermute | solution.py:41
  31.1 3.6 %collective-permute-start.10 = (bf16[264,256]{1,0:T(8,128)(2,1)S(1)}, bf16[264,256]{1,0:T(8,128)(2,1)S(1)}, u32[]{:S(2)}, u32[]{:S(2)}) collective-permute-start(bf16[264,256]{1,0:T(8,128)(2,1)S(1)} %combine.23.refs_4_), channel_id=1, source_target_pairs={{0,4},{4,0},{8,12},{12,8},{1,5},{5,1},{9,13},{13,9},{2,6},{6,2},{1... | collective-permute-start | bytes 405512 | tf_op jit(solution)/shard_map/ppermute | solution.py:41
  31.6 19.4 %collective-permute-start.4 = (bf16[520,256]{1,0:T(8,128)(2,1)S(1)}, bf16[520,256]{1,0:T(8,128)(2,1)S(1)}, u32[]{:S(2)}, u32[]{:S(2)}) collective-permute-start(bf16[520,256]{1,0:T(8,128)(2,1)S(1)} %get-tuple-element.31.refs_2_), channel_id=1, source_target_pairs={{0,1},{1,0},{2,3},{3,2},{4,5},{5,4},{6,7},{7,6},{8,9},{9,8},{10,11... | collective-permute-start | bytes 798728 | tf_op jit(solution)/shard_map/ppermute | solution.py:41
  43.2 10.0 %copy-start.2 = (bf16[256,2048]{1,0:T(8,128)(2,1)S(1)}, bf16[256,2048]{1,0:T(8,128)(2,1)}, u32[]{:S(2)}) copy-start(bf16[256,2048]{1,0:T(8,128)(2,1)} %refs_3_.23) | copy-start | bytes 3145732
  43.2 8.0 %collective-permute-start.12 = (bf16[520,256]{1,0:T(8,128)(2,1)S(1)}, bf16[520,256]{1,0:T(8,128)(2,1)S(1)}, u32[]{:S(2)}, u32[]{:S(2)}) collective-permute-start(bf16[520,256]{1,0:T(8,128)(2,1)S(1)} %combine.28.refs_4_), channel_id=1, source_target_pairs={{0,4},{4,0},{8,12},{12,8},{1,5},{5,1},{9,13},{13,9},{2,6},{6,2},{1... | collective-permute-start | bytes 798728 | tf_op jit(solution)/shard_map/ppermute | solution.py:41
  43.3 14.8 %collective-permute-start.14 = (bf16[520,256]{1,0:T(8,128)(2,1)S(1)}, bf16[520,256]{1,0:T(8,128)(2,1)S(1)}, u32[]{:S(2)}, u32[]{:S(2)}) collective-permute-start(bf16[520,256]{1,0:T(8,128)(2,1)S(1)} %combine.24.refs_3_), channel_id=1, source_target_pairs={{0,2},{1,3},{2,0},{3,1},{4,6},{5,7},{6,4},{7,5},{8,10},{9,11},{10,... | collective-permute-start | bytes 798728 | tf_op jit(solution)/shard_map/ppermute | solution.py:41
  43.4 7.5 %collective-permute-start.8 = (bf16[264,256]{1,0:T(8,128)(2,1)S(1)}, bf16[264,256]{1,0:T(8,128)(2,1)S(1)}, u32[]{:S(2)}, u32[]{:S(2)}) collective-permute-start(bf16[264,256]{1,0:T(8,128)(2,1)S(1)} %combine.26.refs_4_), channel_id=1, source_target_pairs={{0,8},{4,12},{1,9},{5,13},{2,10},{6,14},{3,11},{7,15},{16,24},{20,... | collective-permute-start | bytes 405512 | tf_op jit(solution)/shard_map/ppermute | solution.py:41
  46.9 6.2 %collective-permute-start.15 = (bf16[264,256]{1,0:T(8,128)(2,1)S(1)}, bf16[264,256]{1,0:T(8,128)(2,1)S(1)}, u32[]{:S(2)}, u32[]{:S(2)}) collective-permute-start(bf16[264,256]{1,0:T(8,128)(2,1)S(1)} %combine.27.refs_3_), channel_id=1, source_target_pairs={{0,8},{4,12},{1,9},{5,13},{2,10},{6,14},{3,11},{7,15},{16,24},{20,... | collective-permute-start | bytes 405512 | tf_op jit(solution)/shard_map/ppermute | solution.py:41
  58.2 3.6 %collective-permute-start.16 = (bf16[520,256]{1,0:T(8,128)(2,1)S(1)}, bf16[520,256]{1,0:T(8,128)(2,1)S(1)}, u32[]{:S(2)}, u32[]{:S(2)}) collective-permute-start(bf16[520,256]{1,0:T(8,128)(2,1)S(1)} %combine.33.refs_4_), channel_id=1, source_target_pairs={{0,4},{4,0},{8,12},{12,8},{1,5},{5,1},{9,13},{13,9},{2,6},{6,2},{1... | collective-permute-start | bytes 798728 | tf_op jit(solution)/shard_map/ppermute | solution.py:41
  58.4 9.6 %collective-permute-start.13 = (bf16[520,256]{1,0:T(8,128)(2,1)S(1)}, bf16[520,256]{1,0:T(8,128)(2,1)S(1)}, u32[]{:S(2)}, u32[]{:S(2)}) collective-permute-start(bf16[520,256]{1,0:T(8,128)(2,1)S(1)} %combine.31.refs_4_), channel_id=1, source_target_pairs={{0,8},{4,12},{1,9},{5,13},{2,10},{6,14},{3,11},{7,15},{16,24},{20,... | collective-permute-start | bytes 798728 | tf_op jit(solution)/shard_map/ppermute | solution.py:41
  61.8 14.3 %collective-permute-start.11 = (bf16[520,256]{1,0:T(8,128)(2,1)S(1)}, bf16[520,256]{1,0:T(8,128)(2,1)S(1)}, u32[]{:S(2)}, u32[]{:S(2)}) collective-permute-start(bf16[520,256]{1,0:T(8,128)(2,1)S(1)} %combine.30.refs_4_), channel_id=1, source_target_pairs={{0,2},{1,3},{2,0},{3,1},{4,6},{5,7},{6,4},{7,5},{8,10},{9,11},{10,... | collective-permute-start | bytes 798728 | tf_op jit(solution)/shard_map/ppermute | solution.py:41
  76.3 1.8 %collective-permute-start.17 = (bf16[520,256]{1,0:T(8,128)(2,1)S(1)}, bf16[520,256]{1,0:T(8,128)(2,1)S(1)}, u32[]{:S(2)}, u32[]{:S(2)}) collective-permute-start(bf16[520,256]{1,0:T(8,128)(2,1)S(1)} %combine.36.refs_4_), channel_id=1, source_target_pairs={{0,4},{4,0},{8,12},{12,8},{1,5},{5,1},{9,13},{13,9},{2,6},{6,2},{1... | collective-permute-start | bytes 798728 | tf_op jit(solution)/shard_map/ppermute | solution.py:41
  76.4 8.3 %collective-permute-start.22 = (bf16[520,256]{1,0:T(8,128)(2,1)S(1)}, bf16[520,256]{1,0:T(8,128)(2,1)S(1)}, u32[]{:S(2)}, u32[]{:S(2)}) collective-permute-start(bf16[520,256]{1,0:T(8,128)(2,1)S(1)} %combine.34.refs_10_), channel_id=1, source_target_pairs={{0,8},{4,12},{1,9},{5,13},{2,10},{6,14},{3,11},{7,15},{16,24},{20,... | collective-permute-start | bytes 798728 | tf_op jit(solution)/shard_map/ppermute | solution.py:41
  78.0 15.8 %collective-permute-start.19 = (bf16[520,256]{1,0:T(8,128)(2,1)S(1)}, bf16[520,256]{1,0:T(8,128)(2,1)S(1)}, u32[]{:S(2)}, u32[]{:S(2)}) collective-permute-start(bf16[520,256]{1,0:T(8,128)(2,1)S(1)} %combine.35.refs_3_), channel_id=1, source_target_pairs={{0,1},{1,0},{2,3},{3,2},{4,5},{5,4},{6,7},{7,6},{8,9},{9,8},{10,11... | collective-permute-start | bytes 798728 | tf_op jit(solution)/shard_map/ppermute | solution.py:41
  78.3 16.1 %collective-permute-start.18 = (bf16[520,256]{1,0:T(8,128)(2,1)S(1)}, bf16[520,256]{1,0:T(8,128)(2,1)S(1)}, u32[]{:S(2)}, u32[]{:S(2)}) collective-permute-start(bf16[520,256]{1,0:T(8,128)(2,1)S(1)} %combine.37.refs_4_), channel_id=1, source_target_pairs={{0,8},{4,12},{1,9},{5,13},{2,10},{6,14},{3,11},{7,15},{16,24},{20,... | collective-permute-start | bytes 798728 | tf_op jit(solution)/shard_map/ppermute | solution.py:41
  79.9 10.3 %collective-permute-start.20 = (bf16[264,256]{1,0:T(8,128)(2,1)S(1)}, bf16[264,256]{1,0:T(8,128)(2,1)S(1)}, u32[]{:S(2)}, u32[]{:S(2)}) collective-permute-start(bf16[264,256]{1,0:T(8,128)(2,1)S(1)} %combine.29.refs_2_), channel_id=1, source_target_pairs={{0,1},{1,0},{2,3},{3,2},{4,5},{5,4},{6,7},{7,6},{8,9},{9,8},{10,11... | collective-permute-start | bytes 405512 | tf_op jit(solution)/shard_map/ppermute | solution.py:41
  81.9 11.2 %collective-permute-start.21 = (bf16[264,256]{1,0:T(8,128)(2,1)S(1)}, bf16[264,256]{1,0:T(8,128)(2,1)S(1)}, u32[]{:S(2)}, u32[]{:S(2)}) collective-permute-start(bf16[264,256]{1,0:T(8,128)(2,1)S(1)} %combine.32.refs_14_), channel_id=1, source_target_pairs={{0,1},{1,0},{2,3},{3,2},{4,5},{5,4},{6,7},{7,6},{8,9},{9,8},{10,11... | collective-permute-start | bytes 405512 | tf_op jit(solution)/shard_map/ppermute | solution.py:41
  85.0 13.8 %collective-permute-start.24 = (bf16[520,256]{1,0:T(8,128)(2,1)S(1)}, bf16[520,256]{1,0:T(8,128)(2,1)S(1)}, u32[]{:S(2)}, u32[]{:S(2)}) collective-permute-start(bf16[520,256]{1,0:T(8,128)(2,1)S(1)} %combine.38.refs_8_), channel_id=1, source_target_pairs={{0,1},{1,0},{2,3},{3,2},{4,5},{5,4},{6,7},{7,6},{8,9},{9,8},{10,11... | collective-permute-start | bytes 798728 | tf_op jit(solution)/shard_map/ppermute | solution.py:41
  94.7 9.0 %collective-permute-start.23 = (bf16[520,256]{1,0:T(8,128)(2,1)S(1)}, bf16[520,256]{1,0:T(8,128)(2,1)S(1)}, u32[]{:S(2)}, u32[]{:S(2)}) collective-permute-start(bf16[520,256]{1,0:T(8,128)(2,1)S(1)} %combine.39.refs_10_), channel_id=1, source_target_pairs={{0,1},{1,0},{2,3},{3,2},{4,5},{5,4},{6,7},{7,6},{8,9},{9,8},{10,11... | collective-permute-start | bytes 798728 | tf_op jit(solution)/shard_map/ppermute | solution.py:41

commit v9 on v8

--- a/solution.py
+++ b/solution.py
@@ -33,12 +33,11 @@
     return head_bits, ctx_bits
 
 
-def flip(x, bit, head_bits, ctx_bits, last):
+def flip(x, bit, head_bits, ctx_bits):
     axis, size, b = (
         ("head", 1 << head_bits, bit) if bit < head_bits else ("ctx", 1 << ctx_bits, bit - head_bits)
     )
-    pairs = [(i, i ^ (1 << b)) for i in range(size) if not (last and i & (1 << b))]
-    return lax.ppermute(x, axis, pairs)
+    return lax.ppermute(x, axis, [(i, i ^ (1 << b)) for i in range(size)])
 
 
 def table_rows(blocks):
@@ -439,9 +438,9 @@
             results[c, mine] = token
             out, token = (token, None) if done is not None else (None, token)
         if stage < bits:
-            got.setdefault(c, []).append(exchange(token, stage, last=stage == bits - 1))
+            got.setdefault(c, []).append(exchange(token, stage))
         elif stage == bits:
-            back[c] = exchange(token, 0, last=False)
+            back[c] = exchange(token, 0)
     return out
 
 

time: 105 us -> 102 us (0.971)
  starting transfers between devices: 31.7 us -> 24.9 us
  waiting for transfers between devices: 56.2 us -> 59.7 us
    ppermute x25, starting transfers between devices: 31.7 us -> 24.9 us  [flip(): return lax.ppermute(x, axis, [(i, i ^ 1 << b) for i in range(size)])]
    ppermute x25, waiting for transfers between devices: 56.2 us -> 59.7 us  [flip(): return lax.ppermute(x, axis, [(i, i ^ 1 << b) for i in range(size)])]
  transfers between devices with their start and end apart: 25 -> 25, of which waited for: 15 -> 16; matrix products, arithmetic and copies ran while one was open for 0% -> 0% of each run, Pallas kernels for 11% -> 12%
where the time goes in v9:
time: 102 us
  waiting for transfers between devices  59.7 us (59%)
  starting transfers between devices  24.9 us (24%)
  Pallas kernels  17.1 us (17%)
    ppermute x25, waiting for transfers between devices, flip(): return lax.ppermute(x, axis, [(i, i ^ 1 << b) for i in range(size)])  59.7 us
    ppermute x25, starting transfers between devices, flip(): return lax.ppermute(x, axis, [(i, i ^ 1 << b) for i in range(size)])  24.9 us
    pallas_call x8, Pallas kernels, span_outputs(): pl.pallas_call(kernel, in_specs=in_specs, **outs, compiler_params=pltpu.C...  7.9 us
    pallas_call x20, Pallas kernels, combine(): pl.pallas_call(kernel, in_specs=[VMEM] * len(parts) + extra_specs, out_sp...  3.42 us
    pallas_call x1, Pallas kernels, gates(): pl.pallas_call(functools.partial(gate_kernel, CHUNKS[ORDER[0][1]]), in_sp...  3.14 us
    pallas_call x4, Pallas kernels, span_states(): pl.pallas_call(kernel, in_specs=[VMEM] * 4 + extra_specs, out_specs=(VMEM...  2.59 us
  transfers between devices with their start and end apart: 25, of which 16 were waited for; matrix products, arithmetic and copies ran while one was open for 0% of the time, Pallas kernels for 12%

profile of v9, /device:TPU:0, one launch (start us, length us, event | category | flops | bytes accessed | tf_op | source)
XLA Modules:
  0.0 102.2 jit_solution(9736748147355237611)
XLA Ops:
  0.0 3.1 %gates.1 = (f32[256,8]{1,0:T(8,128)S(1)}, f32[256,8]{1,0:T(8,128)S(1)}, f32[8,256]{1,0:T(8,128)S(1)}, f32[8,20,128]{2,1,0:T(8,128)S(1)}, bf16[264,256]{1,0:T(8,128)(2,1)S(1)}, /*index=5*/bf16[264,256]{1,0:T(8,128)(2,1)S(1)}) custom-call(bf16[8,256]{1,0:T(8,128)(2,1)} %bitcast.3, bf16[8,256]{1,0:T(8,128)(2,1)} %bitcast.4, f32[3,2,8]{2,1,0:T(2,128)} %bitcast.5, ...), custom_call_target="tpu_custom_call" | custom-call | flops 134217728 | bytes 1048576 | tf_op jit(solution)/shard_map/gates/pallas_call | solution.py:101
  3.1 3.1 %collective-permute-start.1 = (bf16[264,256]{1,0:T(8,128)(2,1)S(1)}, bf16[264,256]{1,0:T(8,128)(2,1)S(1)}, u32[]{:S(2)}, u32[]{:S(2)}) collective-permute-start(bf16[264,256]{1,0:T(8,128)(2,1)S(1)} %get-tuple-element.23.refs_4_), channel_id=1, source_target_pairs={{0,1},{1,0},{2,3},{3,2},{4,5},{5,4},{6,7},{7,6},{8,9},{9,8},{10,11... | collective-permute-start | bytes 405512 | tf_op jit(solution)/shard_map/ppermute | solution.py:40
  6.3 0.6 span_states.4
  6.9 0.7 span_states.5
  7.6 2.1 %collective-permute-start.3 = (bf16[520,256]{1,0:T(8,128)(2,1)S(1)}, bf16[520,256]{1,0:T(8,128)(2,1)S(1)}, u32[]{:S(2)}, u32[]{:S(2)}) collective-permute-start(bf16[520,256]{1,0:T(8,128)(2,1)S(1)} %get-tuple-element.27.refs_2_), channel_id=1, source_target_pairs={{0,1},{1,0},{2,3},{3,2},{4,5},{5,4},{6,7},{7,6},{8,9},{9,8},{10,11... | collective-permute-start | bytes 798728 | tf_op jit(solution)/shard_map/ppermute | solution.py:40
  9.7 1.0 collective-permute-done.1.refs_1_.refs_6_
  10.7 2.8 %collective-permute-done.refs_1_.refs_10_ = bf16[264,256]{1,0:T(8,128)(2,1)S(1)} collective-permute-done((bf16[264,256]{1,0:T(8,128)(2,1)S(1)}, bf16[264,256]{1,0:T(8,128)(2,1)S(1)}, u32[]{:S(2)}, u32[]{:S(2)}) %collective-permute-start) | collective-permute-done | bytes 135200 | tf_op jit(solution)/shard_map/ppermute | solution.py:40
  13.6 0.7 span_states.6
  14.3 2.2 %collective-permute-start.6 = (bf16[520,256]{1,0:T(8,128)(2,1)S(1)}, bf16[520,256]{1,0:T(8,128)(2,1)S(1)}, u32[]{:S(2)}, u32[]{:S(2)}) collective-permute-start(bf16[520,256]{1,0:T(8,128)(2,1)S(1)} %get-tuple-element.29.refs_2_), channel_id=1, source_target_pairs={{0,1},{1,0},{2,3},{3,2},{4,5},{5,4},{6,7},{7,6},{8,9},{9,8},{10,11... | collective-permute-start | bytes 798728 | tf_op jit(solution)/shard_map/ppermute | solution.py:40
  16.5 2.6 %collective-permute-start.2 = (bf16[264,256]{1,0:T(8,128)(2,1)S(1)}, bf16[264,256]{1,0:T(8,128)(2,1)S(1)}, u32[]{:S(2)}, u32[]{:S(2)}) collective-permute-start(bf16[264,256]{1,0:T(8,128)(2,1)S(1)} %combine.21.refs_4_), channel_id=1, source_target_pairs={{0,2},{1,3},{2,0},{3,1},{4,6},{5,7},{6,4},{7,5},{8,10},{9,11},{10,... | collective-permute-start | bytes 405512 | tf_op jit(solution)/shard_map/ppermute | solution.py:40
  19.0 0.3 collective-permute-start.5
  19.4 4.2 %collective-permute-done.3.refs_1_.refs_6_ = bf16[520,256]{1,0:T(8,128)(2,1)S(1)} collective-permute-done((bf16[520,256]{1,0:T(8,128)(2,1)S(1)}, bf16[520,256]{1,0:T(8,128)(2,1)S(1)}, u32[]{:S(2)}, u32[]{:S(2)}) %collective-permute-start.3) | collective-permute-done | bytes 266272 | tf_op jit(solution)/shard_map/ppermute | solution.py:40
  23.7 3.7 %collective-permute-start.9 = (bf16[520,256]{1,0:T(8,128)(2,1)S(1)}, bf16[520,256]{1,0:T(8,128)(2,1)S(1)}, u32[]{:S(2)}, u32[]{:S(2)}) collective-permute-start(bf16[520,256]{1,0:T(8,128)(2,1)S(1)} %combine.22.refs_3_), channel_id=1, source_target_pairs={{0,2},{1,3},{2,0},{3,1},{4,6},{5,7},{6,4},{7,5},{8,10},{9,11},{10,... | collective-permute-start | bytes 798728 | tf_op jit(solution)/shard_map/ppermute | solution.py:40
  27.6 0.7 span_states.7
  28.3 2.5 %collective-permute-done.6.refs_1_.refs_6_ = bf16[520,256]{1,0:T(8,128)(2,1)S(1)} collective-permute-done((bf16[520,256]{1,0:T(8,128)(2,1)S(1)}, bf16[520,256]{1,0:T(8,128)(2,1)S(1)}, u32[]{:S(2)}, u32[]{:S(2)}) %collective-permute-start.6) | collective-permute-done | bytes 266272 | tf_op jit(solution)/shard_map/ppermute | solution.py:40
  31.1 0.5 collective-permute-start.10
  31.6 2.9 %collective-permute-start.4 = (bf16[520,256]{1,0:T(8,128)(2,1)S(1)}, bf16[520,256]{1,0:T(8,128)(2,1)S(1)}, u32[]{:S(2)}, u32[]{:S(2)}) collective-permute-start(bf16[520,256]{1,0:T(8,128)(2,1)S(1)} %get-tuple-element.31.refs_2_), channel_id=1, source_target_pairs={{0,1},{1,0},{2,3},{3,2},{4,5},{5,4},{6,7},{7,6},{8,9},{9,8},{10,11... | collective-permute-start | bytes 798728 | tf_op jit(solution)/shard_map/ppermute | solution.py:40
  34.8 8.2 %collective-permute-done.9.refs_2_.refs_7_.refs_1_ = bf16[520,256]{1,0:T(8,128)(2,1)S(1)} collective-permute-done((bf16[520,256]{1,0:T(8,128)(2,1)S(1)}, bf16[520,256]{1,0:T(8,128)(2,1)S(1)}, u32[]{:S(2)}, u32[]{:S(2)}) %collective-permute-start.9) | collective-permute-done | bytes 266272 | tf_op jit(solution)/shard_map/ppermute | solution.py:40
  43.4 1.5 %collective-permute-start.8 = (bf16[264,256]{1,0:T(8,128)(2,1)S(1)}, bf16[264,256]{1,0:T(8,128)(2,1)S(1)}, u32[]{:S(2)}, u32[]{:S(2)}) collective-permute-start(bf16[264,256]{1,0:T(8,128)(2,1)S(1)} %combine.26.refs_4_), channel_id=1, source_target_pairs={{0,8},{4,12},{8,0},{12,4},{1,9},{5,13},{9,1},{13,5},{2,10},{6,14},... | collective-permute-start | bytes 405512 | tf_op jit(solution)/shard_map/ppermute | solution.py:40
  44.9 0.5 collective-permute-start.15
  45.5 4.4 %collective-permute-done.8.refs_3_.refs_9_ = bf16[264,256]{1,0:T(8,128)(2,1)S(1)} collective-permute-done((bf16[264,256]{1,0:T(8,128)(2,1)S(1)}, bf16[264,256]{1,0:T(8,128)(2,1)S(1)}, u32[]{:S(2)}, u32[]{:S(2)}) %collective-permute-start.8) | collective-permute-done | bytes 135200 | tf_op jit(solution)/shard_map/ppermute | solution.py:40
  50.2 0.2 combine.31.refs_4_
  50.4 1.7 %collective-permute-done.15.refs_3_.refs_13_ = bf16[264,256]{1,0:T(8,128)(2,1)S(1)} collective-permute-done((bf16[264,256]{1,0:T(8,128)(2,1)S(1)}, bf16[264,256]{1,0:T(8,128)(2,1)S(1)}, u32[]{:S(2)}, u32[]{:S(2)}) %collective-permute-start.15) | collective-permute-done | bytes 135200 | tf_op jit(solution)/shard_map/ppermute | solution.py:40
  52.3 0.9 span_outputs.8.refs_3_.refs_10_
  53.2 4.9 %collective-permute-done.14.refs_2_.refs_1_.refs_7_ = bf16[520,256]{1,0:T(8,128)(2,1)S(1)} collective-permute-done((bf16[520,256]{1,0:T(8,128)(2,1)S(1)}, bf16[520,256]{1,0:T(8,128)(2,1)S(1)}, u32[]{:S(2)}, u32[]{:S(2)}) %collective-permute-start.14) | collective-permute-done | bytes 266272 | tf_op jit(solution)/shard_map/ppermute | solution.py:40
  58.4 1.5 %collective-permute-start.13 = (bf16[520,256]{1,0:T(8,128)(2,1)S(1)}, bf16[520,256]{1,0:T(8,128)(2,1)S(1)}, u32[]{:S(2)}, u32[]{:S(2)}) collective-permute-start(bf16[520,256]{1,0:T(8,128)(2,1)S(1)} %combine.31.refs_4_), channel_id=1, source_target_pairs={{0,8},{4,12},{8,0},{12,4},{1,9},{5,13},{9,1},{13,5},{2,10},{6,14},... | collective-permute-start | bytes 798728 | tf_op jit(solution)/shard_map/ppermute | solution.py:40
  59.9 0.2 combine.34.refs_10_
  60.1 7.0 %collective-permute-done.13.refs_9_.refs_3_ = bf16[520,256]{1,0:T(8,128)(2,1)S(1)} collective-permute-done((bf16[520,256]{1,0:T(8,128)(2,1)S(1)}, bf16[520,256]{1,0:T(8,128)(2,1)S(1)}, u32[]{:S(2)}, u32[]{:S(2)}) %collective-permute-start.13) | collective-permute-done | bytes 266272 | tf_op jit(solution)/shard_map/ppermute | solution.py:40
  67.1 0.8 span_outputs.9.refs_4_.refs_11_
  68.0 0.2 combine.35.refs_3_
  68.2 5.9 %collective-permute-done.11.refs_2_.refs_1_.refs_7_ = bf16[520,256]{1,0:T(8,128)(2,1)S(1)} collective-permute-done((bf16[520,256]{1,0:T(8,128)(2,1)S(1)}, bf16[520,256]{1,0:T(8,128)(2,1)S(1)}, u32[]{:S(2)}, u32[]{:S(2)}) %collective-permute-start.11) | collective-permute-done | bytes 266272 | tf_op jit(solution)/shard_map/ppermute | solution.py:40
  74.4 0.6 collective-permute-start.22
  75.0 0.9 collective-permute-done.17.refs_3_.refs_2_.refs_8_
  75.9 0.2 combine.37.refs_4_
  76.1 0.6 collective-permute-start.18
  76.8 2.0 %collective-permute-start.20 = (bf16[264,256]{1,0:T(8,128)(2,1)S(1)}, bf16[264,256]{1,0:T(8,128)(2,1)S(1)}, u32[]{:S(2)}, u32[]{:S(2)}) collective-permute-start(bf16[264,256]{1,0:T(8,128)(2,1)S(1)} %combine.29.refs_2_), channel_id=1, source_target_pairs={{0,1},{1,0},{2,3},{3,2},{4,5},{5,4},{6,7},{7,6},{8,9},{9,8},{10,11... | collective-permute-start | bytes 405512 | tf_op jit(solution)/shard_map/ppermute | solution.py:40
  78.8 4.9 %collective-permute-done.22.refs_3_.refs_9_ = bf16[520,256]{1,0:T(8,128)(2,1)S(1)} collective-permute-done((bf16[520,256]{1,0:T(8,128)(2,1)S(1)}, bf16[520,256]{1,0:T(8,128)(2,1)S(1)}, u32[]{:S(2)}, u32[]{:S(2)}) %collective-permute-start.22) | collective-permute-done | bytes 266272 | tf_op jit(solution)/shard_map/ppermute | solution.py:40
  84.0 3.1 %collective-permute-done.20.refs_6_ = bf16[264,256]{1,0:T(8,128)(2,1)S(1)} collective-permute-done((bf16[264,256]{1,0:T(8,128)(2,1)S(1)}, bf16[264,256]{1,0:T(8,128)(2,1)S(1)}, u32[]{:S(2)}, u32[]{:S(2)}) %collective-permute-start.20) | collective-permute-done | bytes 135200 | tf_op jit(solution)/shard_map/ppermute | solution.py:40
  87.1 2.9 %collective-permute-done.21.refs_7_ = bf16[264,256]{1,0:T(8,128)(2,1)S(1)} collective-permute-done((bf16[264,256]{1,0:T(8,128)(2,1)S(1)}, bf16[264,256]{1,0:T(8,128)(2,1)S(1)}, u32[]{:S(2)}, u32[]{:S(2)}) %collective-permute-start.21) | collective-permute-done | bytes 135200 | tf_op jit(solution)/shard_map/ppermute | solution.py:40
  90.0 0.6 span_outputs.10.refs_7_.refs_12_
  90.7 0.7 span_outputs.11.refs_4_.refs_13_
  91.4 0.3 combine.39.refs_10_
  91.7 1.0 span_outputs.12.refs_7_.refs_14_
  92.7 3.0 %collective-permute-done.24.refs_6_ = bf16[520,256]{1,0:T(8,128)(2,1)S(1)} collective-permute-done((bf16[520,256]{1,0:T(8,128)(2,1)S(1)}, bf16[520,256]{1,0:T(8,128)(2,1)S(1)}, u32[]{:S(2)}, u32[]{:S(2)}) %collective-permute-start.24) | collective-permute-done | bytes 266272 | tf_op jit(solution)/shard_map/ppermute | solution.py:40
  95.7 0.7 span_outputs.13.refs_15_.refs_16_
  96.4 1.9 %span_outputs.14.refs_7_ = bf16[256,4096]{1,0:T(8,128)(2,1)} custom-call(f32[8,20,128]{2,1,0:T(8,128)S(1)} %get-tuple-element.19.refs_0_, f32[256,8]{1,0:T(8,128)S(1)} %get-tuple-element.20.refs_1_, f32[8,256]{1,0:T(8,128)S(1)} %get-tuple-element.21.refs_2_, bf16[256,2048]{1,0:T(8,128)(2,1)S(1)} %copy-done.2, bf16[256,2048]{1,0:T(8,128)(2,1)S(1)} %copy-done.1, ...), custom_call_target="tpu_custom_call" | custom-call | flops 167772160 | bytes 786432 | tf_op jit(solution)/shard_map/span_outputs/pallas_call | solution.py:385
  98.3 2.4 %collective-permute-done.23.refs_6_ = bf16[520,256]{1,0:T(8,128)(2,1)S(1)} collective-permute-done((bf16[520,256]{1,0:T(8,128)(2,1)S(1)}, bf16[520,256]{1,0:T(8,128)(2,1)S(1)}, u32[]{:S(2)}, u32[]{:S(2)}) %collective-permute-start.23) | collective-permute-done | bytes 266272 | tf_op jit(solution)/shard_map/ppermute | solution.py:40
  100.6 1.4 %span_outputs.15 = bf16[256,4096]{1,0:T(8,128)(2,1)} custom-call(f32[8,20,128]{2,1,0:T(8,128)S(1)} %get-tuple-element.19.refs_0_, f32[256,8]{1,0:T(8,128)S(1)} %get-tuple-element.20.refs_1_, f32[8,256]{1,0:T(8,128)S(1)} %get-tuple-element.21.refs_2_, bf16[256,2048]{1,0:T(8,128)(2,1)S(1)} %copy-done.2, ...), custom_call_target="tpu_custom_call", output_to_operand_aliasing={{}: (7, {})} | custom-call | flops 167772160 | bytes 786432 | tf_op jit(solution)/shard_map/span_outputs/pallas_call | solution.py:385
  (41 shorter events, 3.0 us)
Async XLA Ops:
  0.0 6.3 %copy-start = (bf16[256,4096]{1,0:T(8,128)(2,1)S(1)}, bf16[256,4096]{1,0:T(8,128)(2,1)}, u32[]{:S(2)}) copy-start(bf16[256,4096]{1,0:T(8,128)(2,1)} %refs_5_.15) | copy-start | bytes 6291460
  0.0 6.3 %copy-start.1 = (bf16[256,2048]{1,0:T(8,128)(2,1)S(1)}, bf16[256,2048]{1,0:T(8,128)(2,1)}, u32[]{:S(2)}) copy-start(bf16[256,2048]{1,0:T(8,128)(2,1)} %refs_4_.15) | copy-start | bytes 3145732
  3.1 7.5 %collective-permute-start.1 = (bf16[264,256]{1,0:T(8,128)(2,1)S(1)}, bf16[264,256]{1,0:T(8,128)(2,1)S(1)}, u32[]{:S(2)}, u32[]{:S(2)}) collective-permute-start(bf16[264,256]{1,0:T(8,128)(2,1)S(1)} %get-tuple-element.23.refs_4_), channel_id=1, source_target_pairs={{0,1},{1,0},{2,3},{3,2},{4,5},{5,4},{6,7},{7,6},{8,9},{9,8},{10,11... | collective-permute-start | bytes 405512 | tf_op jit(solution)/shard_map/ppermute | solution.py:40
  6.8 6.7 %collective-permute-start = (bf16[264,256]{1,0:T(8,128)(2,1)S(1)}, bf16[264,256]{1,0:T(8,128)(2,1)S(1)}, u32[]{:S(2)}, u32[]{:S(2)}) collective-permute-start(bf16[264,256]{1,0:T(8,128)(2,1)S(1)} %get-tuple-element.25.refs_4_), channel_id=1, source_target_pairs={{0,1},{1,0},{2,3},{3,2},{4,5},{5,4},{6,7},{7,6},{8,9},{9,8},{10,11... | collective-permute-start | bytes 405512 | tf_op jit(solution)/shard_map/ppermute | solution.py:40
  7.6 16.0 %collective-permute-start.3 = (bf16[520,256]{1,0:T(8,128)(2,1)S(1)}, bf16[520,256]{1,0:T(8,128)(2,1)S(1)}, u32[]{:S(2)}, u32[]{:S(2)}) collective-permute-start(bf16[520,256]{1,0:T(8,128)(2,1)S(1)} %get-tuple-element.27.refs_2_), channel_id=1, source_target_pairs={{0,1},{1,0},{2,3},{3,2},{4,5},{5,4},{6,7},{7,6},{8,9},{9,8},{10,11... | collective-permute-start | bytes 798728 | tf_op jit(solution)/shard_map/ppermute | solution.py:40
  14.3 16.4 %collective-permute-start.6 = (bf16[520,256]{1,0:T(8,128)(2,1)S(1)}, bf16[520,256]{1,0:T(8,128)(2,1)S(1)}, u32[]{:S(2)}, u32[]{:S(2)}) collective-permute-start(bf16[520,256]{1,0:T(8,128)(2,1)S(1)} %get-tuple-element.29.refs_2_), channel_id=1, source_target_pairs={{0,1},{1,0},{2,3},{3,2},{4,5},{5,4},{6,7},{7,6},{8,9},{9,8},{10,11... | collective-permute-start | bytes 798728 | tf_op jit(solution)/shard_map/ppermute | solution.py:40
  16.5 11.0 %collective-permute-start.2 = (bf16[264,256]{1,0:T(8,128)(2,1)S(1)}, bf16[264,256]{1,0:T(8,128)(2,1)S(1)}, u32[]{:S(2)}, u32[]{:S(2)}) collective-permute-start(bf16[264,256]{1,0:T(8,128)(2,1)S(1)} %combine.21.refs_4_), channel_id=1, source_target_pairs={{0,2},{1,3},{2,0},{3,1},{4,6},{5,7},{6,4},{7,5},{8,10},{9,11},{10,... | collective-permute-start | bytes 405512 | tf_op jit(solution)/shard_map/ppermute | solution.py:40
  19.0 11.8 %collective-permute-start.5 = (bf16[264,256]{1,0:T(8,128)(2,1)S(1)}, bf16[264,256]{1,0:T(8,128)(2,1)S(1)}, u32[]{:S(2)}, u32[]{:S(2)}) collective-permute-start(bf16[264,256]{1,0:T(8,128)(2,1)S(1)} %combine.20.refs_2_), channel_id=1, source_target_pairs={{0,2},{1,3},{2,0},{3,1},{4,6},{5,7},{6,4},{7,5},{8,10},{9,11},{10,... | collective-permute-start | bytes 405512 | tf_op jit(solution)/shard_map/ppermute | solution.py:40
  23.7 19.2 %collective-permute-start.9 = (bf16[520,256]{1,0:T(8,128)(2,1)S(1)}, bf16[520,256]{1,0:T(8,128)(2,1)S(1)}, u32[]{:S(2)}, u32[]{:S(2)}) collective-permute-start(bf16[520,256]{1,0:T(8,128)(2,1)S(1)} %combine.22.refs_3_), channel_id=1, source_target_pairs={{0,2},{1,3},{2,0},{3,1},{4,6},{5,7},{6,4},{7,5},{8,10},{9,11},{10,... | collective-permute-start | bytes 798728 | tf_op jit(solution)/shard_map/ppermute | solution.py:40
  31.0 3.5 %collective-permute-start.7 = (bf16[264,256]{1,0:T(8,128)(2,1)S(1)}, bf16[264,256]{1,0:T(8,128)(2,1)S(1)}, u32[]{:S(2)}, u32[]{:S(2)}) collective-permute-start(bf16[264,256]{1,0:T(8,128)(2,1)S(1)} %combine.25.refs_4_), channel_id=1, source_target_pairs={{0,4},{4,0},{8,12},{12,8},{1,5},{5,1},{9,13},{13,9},{2,6},{6,2},{1... | collective-permute-start | bytes 405512 | tf_op jit(solution)/shard_map/ppermute | solution.py:40
  31.1 3.6 %collective-permute-start.10 = (bf16[264,256]{1,0:T(8,128)(2,1)S(1)}, bf16[264,256]{1,0:T(8,128)(2,1)S(1)}, u32[]{:S(2)}, u32[]{:S(2)}) collective-permute-start(bf16[264,256]{1,0:T(8,128)(2,1)S(1)} %combine.23.refs_4_), channel_id=1, source_target_pairs={{0,4},{4,0},{8,12},{12,8},{1,5},{5,1},{9,13},{13,9},{2,6},{6,2},{1... | collective-permute-start | bytes 405512 | tf_op jit(solution)/shard_map/ppermute | solution.py:40
  31.6 18.5 %collective-permute-start.4 = (bf16[520,256]{1,0:T(8,128)(2,1)S(1)}, bf16[520,256]{1,0:T(8,128)(2,1)S(1)}, u32[]{:S(2)}, u32[]{:S(2)}) collective-permute-start(bf16[520,256]{1,0:T(8,128)(2,1)S(1)} %get-tuple-element.31.refs_2_), channel_id=1, source_target_pairs={{0,1},{1,0},{2,3},{3,2},{4,5},{5,4},{6,7},{7,6},{8,9},{9,8},{10,11... | collective-permute-start | bytes 798728 | tf_op jit(solution)/shard_map/ppermute | solution.py:40
  43.2 9.1 %copy-start.2 = (bf16[256,2048]{1,0:T(8,128)(2,1)S(1)}, bf16[256,2048]{1,0:T(8,128)(2,1)}, u32[]{:S(2)}) copy-start(bf16[256,2048]{1,0:T(8,128)(2,1)} %refs_3_.23) | copy-start | bytes 3145732
  43.2 7.0 %collective-permute-start.12 = (bf16[520,256]{1,0:T(8,128)(2,1)S(1)}, bf16[520,256]{1,0:T(8,128)(2,1)S(1)}, u32[]{:S(2)}, u32[]{:S(2)}) collective-permute-start(bf16[520,256]{1,0:T(8,128)(2,1)S(1)} %combine.28.refs_4_), channel_id=1, source_target_pairs={{0,4},{4,0},{8,12},{12,8},{1,5},{5,1},{9,13},{13,9},{2,6},{6,2},{1... | collective-permute-start | bytes 798728 | tf_op jit(solution)/shard_map/ppermute | solution.py:40
  43.3 14.8 %collective-permute-start.14 = (bf16[520,256]{1,0:T(8,128)(2,1)S(1)}, bf16[520,256]{1,0:T(8,128)(2,1)S(1)}, u32[]{:S(2)}, u32[]{:S(2)}) collective-permute-start(bf16[520,256]{1,0:T(8,128)(2,1)S(1)} %combine.24.refs_3_), channel_id=1, source_target_pairs={{0,2},{1,3},{2,0},{3,1},{4,6},{5,7},{6,4},{7,5},{8,10},{9,11},{10,... | collective-permute-start | bytes 798728 | tf_op jit(solution)/shard_map/ppermute | solution.py:40
  43.4 6.5 %collective-permute-start.8 = (bf16[264,256]{1,0:T(8,128)(2,1)S(1)}, bf16[264,256]{1,0:T(8,128)(2,1)S(1)}, u32[]{:S(2)}, u32[]{:S(2)}) collective-permute-start(bf16[264,256]{1,0:T(8,128)(2,1)S(1)} %combine.26.refs_4_), channel_id=1, source_target_pairs={{0,8},{4,12},{8,0},{12,4},{1,9},{5,13},{9,1},{13,5},{2,10},{6,14},... | collective-permute-start | bytes 405512 | tf_op jit(solution)/shard_map/ppermute | solution.py:40
  44.9 7.3 %collective-permute-start.15 = (bf16[264,256]{1,0:T(8,128)(2,1)S(1)}, bf16[264,256]{1,0:T(8,128)(2,1)S(1)}, u32[]{:S(2)}, u32[]{:S(2)}) collective-permute-start(bf16[264,256]{1,0:T(8,128)(2,1)S(1)} %combine.27.refs_3_), channel_id=1, source_target_pairs={{0,8},{4,12},{8,0},{12,4},{1,9},{5,13},{9,1},{13,5},{2,10},{6,14},... | collective-permute-start | bytes 405512 | tf_op jit(solution)/shard_map/ppermute | solution.py:40
  58.2 1.6 %collective-permute-start.16 = (bf16[520,256]{1,0:T(8,128)(2,1)S(1)}, bf16[520,256]{1,0:T(8,128)(2,1)S(1)}, u32[]{:S(2)}, u32[]{:S(2)}) collective-permute-start(bf16[520,256]{1,0:T(8,128)(2,1)S(1)} %combine.33.refs_4_), channel_id=1, source_target_pairs={{0,4},{4,0},{8,12},{12,8},{1,5},{5,1},{9,13},{13,9},{2,6},{6,2},{1... | collective-permute-start | bytes 798728 | tf_op jit(solution)/shard_map/ppermute | solution.py:40
  58.4 8.7 %collective-permute-start.13 = (bf16[520,256]{1,0:T(8,128)(2,1)S(1)}, bf16[520,256]{1,0:T(8,128)(2,1)S(1)}, u32[]{:S(2)}, u32[]{:S(2)}) collective-permute-start(bf16[520,256]{1,0:T(8,128)(2,1)S(1)} %combine.31.refs_4_), channel_id=1, source_target_pairs={{0,8},{4,12},{8,0},{12,4},{1,9},{5,13},{9,1},{13,5},{2,10},{6,14},... | collective-permute-start | bytes 798728 | tf_op jit(solution)/shard_map/ppermute | solution.py:40
  59.9 14.2 %collective-permute-start.11 = (bf16[520,256]{1,0:T(8,128)(2,1)S(1)}, bf16[520,256]{1,0:T(8,128)(2,1)S(1)}, u32[]{:S(2)}, u32[]{:S(2)}) collective-permute-start(bf16[520,256]{1,0:T(8,128)(2,1)S(1)} %combine.30.refs_4_), channel_id=1, source_target_pairs={{0,2},{1,3},{2,0},{3,1},{4,6},{5,7},{6,4},{7,5},{8,10},{9,11},{10,... | collective-permute-start | bytes 798728 | tf_op jit(solution)/shard_map/ppermute | solution.py:40
  74.3 1.6 %collective-permute-start.17 = (bf16[520,256]{1,0:T(8,128)(2,1)S(1)}, bf16[520,256]{1,0:T(8,128)(2,1)S(1)}, u32[]{:S(2)}, u32[]{:S(2)}) collective-permute-start(bf16[520,256]{1,0:T(8,128)(2,1)S(1)} %combine.36.refs_4_), channel_id=1, source_target_pairs={{0,4},{4,0},{8,12},{12,8},{1,5},{5,1},{9,13},{13,9},{2,6},{6,2},{1... | collective-permute-start | bytes 798728 | tf_op jit(solution)/shard_map/ppermute | solution.py:40
  74.4 9.3 %collective-permute-start.22 = (bf16[520,256]{1,0:T(8,128)(2,1)S(1)}, bf16[520,256]{1,0:T(8,128)(2,1)S(1)}, u32[]{:S(2)}, u32[]{:S(2)}) collective-permute-start(bf16[520,256]{1,0:T(8,128)(2,1)S(1)} %combine.34.refs_10_), channel_id=1, source_target_pairs={{0,8},{4,12},{8,0},{12,4},{1,9},{5,13},{9,1},{13,5},{2,10},{6,14},... | collective-permute-start | bytes 798728 | tf_op jit(solution)/shard_map/ppermute | solution.py:40
  75.0 15.7 %collective-permute-start.19 = (bf16[520,256]{1,0:T(8,128)(2,1)S(1)}, bf16[520,256]{1,0:T(8,128)(2,1)S(1)}, u32[]{:S(2)}, u32[]{:S(2)}) collective-permute-start(bf16[520,256]{1,0:T(8,128)(2,1)S(1)} %combine.35.refs_3_), channel_id=1, source_target_pairs={{0,1},{1,0},{2,3},{3,2},{4,5},{5,4},{6,7},{7,6},{8,9},{9,8},{10,11... | collective-permute-start | bytes 798728 | tf_op jit(solution)/shard_map/ppermute | solution.py:40
  76.1 15.2 %collective-permute-start.18 = (bf16[520,256]{1,0:T(8,128)(2,1)S(1)}, bf16[520,256]{1,0:T(8,128)(2,1)S(1)}, u32[]{:S(2)}, u32[]{:S(2)}) collective-permute-start(bf16[520,256]{1,0:T(8,128)(2,1)S(1)} %combine.37.refs_4_), channel_id=1, source_target_pairs={{0,8},{4,12},{8,0},{12,4},{1,9},{5,13},{9,1},{13,5},{2,10},{6,14},... | collective-permute-start | bytes 798728 | tf_op jit(solution)/shard_map/ppermute | solution.py:40
  76.8 10.4 %collective-permute-start.20 = (bf16[264,256]{1,0:T(8,128)(2,1)S(1)}, bf16[264,256]{1,0:T(8,128)(2,1)S(1)}, u32[]{:S(2)}, u32[]{:S(2)}) collective-permute-start(bf16[264,256]{1,0:T(8,128)(2,1)S(1)} %combine.29.refs_2_), channel_id=1, source_target_pairs={{0,1},{1,0},{2,3},{3,2},{4,5},{5,4},{6,7},{7,6},{8,9},{9,8},{10,11... | collective-permute-start | bytes 405512 | tf_op jit(solution)/shard_map/ppermute | solution.py:40
  78.8 11.2 %collective-permute-start.21 = (bf16[264,256]{1,0:T(8,128)(2,1)S(1)}, bf16[264,256]{1,0:T(8,128)(2,1)S(1)}, u32[]{:S(2)}, u32[]{:S(2)}) collective-permute-start(bf16[264,256]{1,0:T(8,128)(2,1)S(1)} %combine.32.refs_14_), channel_id=1, source_target_pairs={{0,1},{1,0},{2,3},{3,2},{4,5},{5,4},{6,7},{7,6},{8,9},{9,8},{10,11... | collective-permute-start | bytes 405512 | tf_op jit(solution)/shard_map/ppermute | solution.py:40
  83.9 11.8 %collective-permute-start.24 = (bf16[520,256]{1,0:T(8,128)(2,1)S(1)}, bf16[520,256]{1,0:T(8,128)(2,1)S(1)}, u32[]{:S(2)}, u32[]{:S(2)}) collective-permute-start(bf16[520,256]{1,0:T(8,128)(2,1)S(1)} %combine.38.refs_8_), channel_id=1, source_target_pairs={{0,1},{1,0},{2,3},{3,2},{4,5},{5,4},{6,7},{7,6},{8,9},{9,8},{10,11... | collective-permute-start | bytes 798728 | tf_op jit(solution)/shard_map/ppermute | solution.py:40
  91.6 9.0 %collective-permute-start.23 = (bf16[520,256]{1,0:T(8,128)(2,1)S(1)}, bf16[520,256]{1,0:T(8,128)(2,1)S(1)}, u32[]{:S(2)}, u32[]{:S(2)}) collective-permute-start(bf16[520,256]{1,0:T(8,128)(2,1)S(1)} %combine.39.refs_10_), channel_id=1, source_target_pairs={{0,1},{1,0},{2,3},{3,2},{4,5},{5,4},{6,7},{7,6},{8,9},{9,8},{10,11... | collective-permute-start | bytes 798728 | tf_op jit(solution)/shard_map/ppermute | solution.py:40
